TPU v7x, 256 devices: a whole 4x4x8 slice. The times are simulated.
256 devices in a mesh: dp: 4 (over z_lo), context: 64 (over z_hi, x, y, core).
Axes of the slice: x: 4, y: 4, z: 8 (z_hi: 2, z_lo: 4; z = z_hi * 4 + z_lo), core: 2. Of those that a mesh axis runs over, the one named last changes fastest.
Arguments:
- queries: bfloat16 [4, 12288, 4096], P('dp', 'context'), may hold values from -6 to 6
- key_rows: bfloat16 [4, 12288, 4096], P('dp', 'context'), may hold values from -6 to 6
- value_rows: bfloat16 [4, 12288, 4096], P('dp', 'context'), may hold values from -6 to 6
- out_grad: bfloat16 [4, 12288, 4096], P('dp', 'context'), may hold values from -16 to 16
- log_decay: float32 [4, 12288, 32], P('dp', 'context'), may hold values from -0.8 to 0
- norm_gain: float32 [4096], replicated, may hold values from 0.1 to 1.9
Outputs:
- query_grad: bfloat16 [4, 12288, 4096], P('dp', 'context')
- key_grad: bfloat16 [4, 12288, 4096], P('dp', 'context')
- value_grad: bfloat16 [4, 12288, 4096], P('dp', 'context')
- gain_grad: float32 [4096], P(('dp', 'context'))
All inputs are finite; a program needn't handle non-finite values.
Results may differ from a plain program's by a relative error of at most 0.0058.
Values sent between devices are 32-bit elements; how exact they have to be, the bound alone decides.
No kernel may reach another device: no remote copies, remote signals or barrier semaphores. Data moves between devices by JAX's collectives and lax.ppermute only.
A program may use at most 128 MiB of HBM per device.

v0:
```python
import functools
import math

import jax
import jax.numpy as jnp
from jax import lax
from jax.experimental import pallas as pl
from jax.experimental.pallas import tpu as pltpu
from jax.sharding import Mesh, PartitionSpec as P

EPSILON = 1e-06
HIGHEST = lax.Precision.HIGHEST
F32 = jnp.float32
BF16 = jnp.bfloat16
T = 192
HD = 128
GH = 8
GW = GH * HD
NG = 4
HALF = NG // 2
NC = 16
ALL = ("dp", "zh", "x", "y", "core")


def dot(a, b, ca, cb):
    return lax.dot_general(a, b, (((ca,), (cb,)), ((), ())), preferred_element_type=F32)


def lanes(j):
    return slice(j * HD, (j + 1) * HD)


def split_state(state, axis):
    high = state.astype(BF16)
    low = (state - high.astype(F32)).astype(BF16)
    return jnp.concatenate([high, low], axis)


def rows_by_state(rows, state):
    return dot(jnp.concatenate([rows, rows], 1), split_state(state, 0), 1, 0)


def rows_by_state_t(rows, state):
    return dot(jnp.concatenate([rows, rows], 1), split_state(state, 1), 1, 1)


def decay_table(col, row):
    row_ids = lax.broadcasted_iota(jnp.int32, (T, T), 0)
    col_ids = lax.broadcasted_iota(jnp.int32, (T, T), 1)
    return jnp.exp(jnp.where(row_ids >= col_ids, col - row, -jnp.inf))


def states_of(k_ref, v_ref, cum, s_ref):
    last = cum[T - 1 : T, :]
    shrink = jnp.exp(last - cum)
    for j in range(GH):
        late = (k_ref[:, lanes(j)].astype(F32) * shrink[:, j : j + 1]).astype(BF16)
        s_ref[j, :HD, :] = dot(late, v_ref[:, lanes(j)], 0, 0)
        s_ref[j, HD:, :] = jnp.broadcast_to(last[:, j : j + 1], (8, HD))


def state_first_kernel(c_ref, k_ref, v_ref, ld_ref, s_ref, col_ref, row_ref):
    i = pl.program_id(0)

    @pl.when(i == 0)
    def _():
        upper = (
            lax.broadcasted_iota(jnp.int32, (T, T), 0) <= lax.broadcasted_iota(jnp.int32, (T, T), 1)
        ).astype(F32)
        logs = ld_ref[...]
        row_ref[...] = lax.dot_general(
            logs, upper, (((1,), (0,)), ((), ())), precision=HIGHEST, preferred_element_type=F32
        )
        col = lax.dot_general(
            upper, logs, (((0,), (1,)), ((), ())), precision=HIGHEST, preferred_element_type=F32
        )
        for g in range(NG):
            col_ref[g] = col[:, g * GH : (g + 1) * GH]

    states_of(k_ref, v_ref, col_ref[(1 - c_ref[0]) * HALF + i], s_ref)


def state_second_kernel(c_ref, k_ref, v_ref, col_ref, s_ref):
    states_of(k_ref, v_ref, col_ref[c_ref[0] * HALF + pl.program_id(0)], s_ref)


def combine_kernel(upward, c_ref, own_ref, got_ref, lo_ref, lg_ref, p_ref):
    first = c_ref[0] == 0 if upward else c_ref[0] == 1
    for j in range(GH):
        log_own, log_got = lo_ref[j, 0:1, :], lg_ref[j, 0:1, :]
        scale_own = jnp.where(first, jnp.exp(log_got), 1.0)
        scale_got = jnp.where(first, 1.0, jnp.exp(log_own))
        p_ref[j, :HD, :] = scale_own * own_ref[j] + scale_got * got_ref[j]
        if upward:
            p_ref[j, HD:, :] = jnp.broadcast_to(log_own + log_got, (8, HD))


def total_kernel(upward, m_ref, l_ref, t_ref):
    run = jnp.zeros((HD, HD), F32)
    for i in range(NC) if upward else reversed(range(NC)):
        run = jnp.exp(l_ref[i, 0:1, :]) * run + m_ref[i]
    t_ref[...] = run


def scan_kernel(upward, m_ref, l_ref, t_ref, o_ref):
    run = t_ref[...]
    for i in range(NC) if upward else reversed(range(NC)):
        o_ref[i] = run
        run = jnp.exp(l_ref[i, 0:1, :]) * run + m_ref[i]


def send_kernel(upward, c_ref, d_ref, own_ref, lo_ref, o_ref):
    step_on = c_ref[0] == 0 if upward else c_ref[0] == 1
    for j in range(GH):
        scale = jnp.where(step_on, jnp.exp(lo_ref[j, 0:1, :]), 1.0)
        keep = jnp.where(step_on, 1.0, 0.0)
        o_ref[j] = scale * d_ref[j] + keep * own_ref[j]


def own_state(upward, c_ref, d_ref, got_ref, lg_ref, j):
    at_edge = c_ref[0] == 0 if upward else c_ref[0] == 1
    scale = jnp.where(at_edge, 1.0, jnp.exp(lg_ref[j, 0:1, :]))
    keep = jnp.where(at_edge, 0.0, 1.0)
    return scale * d_ref[j] + keep * got_ref[j]


def forward_kernel(own, c_ref, q_ref, k_ref, v_ref, col_ref, row_ref, fw_ref, in_ref):
    half = c_ref[0] if own else 1 - c_ref[0]
    cum = col_ref[half * HALF + pl.program_id(0)]
    for j in range(GH):
        decay = decay_table(cum[:, j : j + 1], row_ref[j : j + 1, :])
        scores = dot(q_ref[:, lanes(j)], k_ref[:, lanes(j)], 1, 1)
        weights = (scores * decay).astype(BF16)
        fw_ref[j] = weights
        in_ref[:, lanes(j)] = dot(weights, v_ref[:, lanes(j)], 1, 0)


def attend_group(q_ref, g_ref, gain_ref, cum, in_ref, state_at, att_ref, sq_ref, pr_ref):
    growth = jnp.exp(cum)
    squares = jnp.zeros((T, HD), F32)
    products = jnp.zeros((T, HD), F32)
    for j in range(GH):
        att = in_ref[:, lanes(j)] + growth[:, j : j + 1] * rows_by_state(q_ref[:, lanes(j)], state_at(j))
        att_ref[:, lanes(j)] = att
        squares += att * att
        products += att * (gain_ref[:, lanes(j)] * g_ref[:, lanes(j)].astype(F32))
    sq_ref[...] += squares
    pr_ref[...] += products


def attend_own_kernel(
    c_ref, q_ref, g_ref, gain_ref, col_ref, in_ref, d_ref, got_ref, lg_ref,
    att_ref, i_ref, sq_ref, pr_ref,
):
    @pl.when(pl.program_id(0) == 0)
    def _():
        sq_ref[...] = jnp.zeros_like(sq_ref)
        pr_ref[...] = jnp.zeros_like(pr_ref)

    def state_at(j):
        state = own_state(True, c_ref, d_ref, got_ref, lg_ref, j)
        i_ref[j] = state
        return state

    cum = col_ref[c_ref[0] * HALF + pl.program_id(0)]
    attend_group(q_ref, g_ref, gain_ref, cum, in_ref, state_at, att_ref, sq_ref, pr_ref)


def delta_group(q_ref, g_ref, gain_ref, cum, att_ref, inverse, mean, od_ref, m_ref, gt_ref):
    growth = jnp.exp(cum)
    for j in range(GH):
        grad = g_ref[:, lanes(j)].astype(F32)
        normed = att_ref[:, lanes(j)] * inverse
        delta = (inverse * (gain_ref[:, lanes(j)] * grad - normed * mean)).astype(BF16)
        od_ref[:, lanes(j)] = delta
        gt_ref[:, lanes(j)] = jnp.sum(grad * normed, axis=0, keepdims=True)
        early = (q_ref[:, lanes(j)].astype(F32) * growth[:, j : j + 1]).astype(BF16)
        m_ref[j] = dot(early, delta, 0, 0)


def attend_other_kernel(
    c_ref, q_ref, g_ref, gain_ref, col_ref, in_ref, i_ref, sq_in, pr_in,
    od_ref, m_ref, gt_ref, inv_ref, mean_ref, att_ref, sq_ref, pr_ref,
):
    step = pl.program_id(0)
    group = jnp.where(step < HALF, step, 2 * HALF - 1 - step)
    cum = col_ref[(1 - c_ref[0]) * HALF + group]

    @pl.when(step == 0)
    def _():
        sq_ref[...] = sq_in[...]
        pr_ref[...] = pr_in[...]

    @pl.when(step < HALF)
    def _():
        attend_group(
            q_ref, g_ref, gain_ref, cum, in_ref, lambda j: i_ref[j], att_ref.at[group], sq_ref, pr_ref
        )

    @pl.when(step == HALF)
    def _():
        features = NG * GW
        inverse = lax.rsqrt(jnp.sum(sq_ref[...], axis=1, keepdims=True) * (1.0 / features) + EPSILON)
        mean = inverse * (jnp.sum(pr_ref[...], axis=1, keepdims=True) * (1.0 / features))
        inv_ref[...] = jnp.broadcast_to(inverse, (T, HD))
        mean_ref[...] = jnp.broadcast_to(mean, (T, HD))

    @pl.when(step >= HALF)
    def _():
        delta_group(
            q_ref, g_ref, gain_ref, cum, att_ref.at[group], inv_ref[...], mean_ref[...],
            od_ref, m_ref, gt_ref,
        )


def delta_own_kernel(
    c_ref, q_ref, g_ref, gain_ref, col_ref, att_ref, inv_ref, mean_ref, od_ref, m_ref, gt_ref
):
    cum = col_ref[c_ref[0] * HALF + pl.program_id(0)]
    delta_group(
        q_ref, g_ref, gain_ref, cum, att_ref, inv_ref[...], mean_ref[...], od_ref, m_ref, gt_ref
    )


def backward_kernel(
    own, c_ref, od_ref, q_ref, k_ref, v_ref, fw_ref, col_ref, row_ref, i_ref, *rest
):
    qg_ref, ki_ref, vi_ref = rest[-3:]
    half = c_ref[0] if own else 1 - c_ref[0]
    cum = col_ref[half * HALF + pl.program_id(0)]
    growth = jnp.exp(cum)
    for j in range(GH):
        at = lanes(j)
        decay = decay_table(cum[:, j : j + 1], row_ref[j : j + 1, :])
        delta = od_ref[:, at]
        weights = (dot(delta, v_ref[:, at], 1, 1) * decay).astype(BF16)
        inter = growth[:, j : j + 1] * rows_by_state_t(delta, i_ref[j])
        qg_ref[:, at] = (dot(weights, k_ref[:, at], 1, 0) + inter).astype(BF16)
        ki_ref[:, at] = dot(weights, q_ref[:, at], 0, 0)
        vi_ref[:, at] = dot(fw_ref[j], delta, 0, 0)


def finish_group(k_ref, v_ref, cum, ki_ref, vi_ref, state_at, kg_ref, vg_ref):
    shrink = jnp.exp(cum[T - 1 : T, :] - cum)
    for j in range(GH):
        at = lanes(j)
        state = state_at(j)
        scale = shrink[:, j : j + 1]
        kg_ref[:, at] = (ki_ref[:, at] + scale * rows_by_state_t(v_ref[:, at], state)).astype(BF16)
        vg_ref[:, at] = (vi_ref[:, at] + scale * rows_by_state(k_ref[:, at], state)).astype(BF16)


def finish_own_kernel(
    c_ref, k_ref, v_ref, col_ref, ki_ref, vi_ref, d_ref, got_ref, lg_ref, kg_ref, vg_ref
):
    cum = col_ref[c_ref[0] * HALF + pl.program_id(0)]
    finish_group(
        k_ref, v_ref, cum, ki_ref, vi_ref,
        lambda j: own_state(False, c_ref, d_ref, got_ref, lg_ref, j), kg_ref, vg_ref,
    )


def finish_other_kernel(
    c_ref, k_ref, v_ref, col_ref, ki_ref, vi_ref, x_ref, kg_in, vg_in, kg_ref, vg_ref
):
    cum = col_ref[(1 - c_ref[0]) * HALF + pl.program_id(0)]
    finish_group(k_ref, v_ref, cum, ki_ref, vi_ref, lambda j: x_ref[j], kg_ref, vg_ref)


def call(kernel, name, grid, in_specs, out_specs, out_shape, args, flops, scratch=(), aliases=None):
    nbytes = sum(math.prod(s.shape) * s.dtype.itemsize for s in out_shape)
    nbytes += sum(math.prod(a.shape) * a.dtype.itemsize for a in args[1:])
    return pl.pallas_call(
        kernel,
        name=name,
        grid_spec=pltpu.PrefetchScalarGridSpec(
            num_scalar_prefetch=1,
            grid=grid,
            in_specs=in_specs,
            out_specs=out_specs,
            scratch_shapes=scratch,
        ),
        out_shape=out_shape,
        input_output_aliases=aliases or {},
        compiler_params=pltpu.CompilerParams(vmem_limit_bytes=24 << 20),
        cost_estimate=pl.CostEstimate(flops=flops, bytes_accessed=nbytes, transcendentals=0),
    )(*args)


def shape(dims, dtype=F32):
    return jax.ShapeDtypeStruct(dims, dtype)


def half_of(own, c_ref):
    return c_ref[0] if own else 1 - c_ref[0]


def wide(own, group=lambda i: i):
    return pl.BlockSpec((None, T, GW), lambda i, c: (0, 0, half_of(own, c) * HALF + group(i)))


def narrow(group=lambda i: i):
    return pl.BlockSpec((T, GW), lambda i, c: (0, group(i)))


def gain_block(own, group=lambda i: i):
    return pl.BlockSpec((1, GW), lambda i, c: (0, half_of(own, c) * HALF + group(i)))


def row_block(own):
    return pl.BlockSpec((GH, T), lambda i, c: (half_of(own, c) * HALF + i, 0))


def state_block(rows=HD, group=lambda i: i):
    return pl.BlockSpec((GH, rows, HD), lambda i, c: (group(i), 0, 0))


LOG_BLOCK = pl.BlockSpec((GH, 8, HD), lambda i, c: (i, HD // 8, 0))
COL_WHOLE = pl.BlockSpec((NG, T, GH), lambda i, c: (0, 0, 0))
STAT_WHOLE = pl.BlockSpec((T, HD), lambda i, c: (0, 0))
ANY = pl.BlockSpec(memory_space=pl.ANY)
STATES = shape((NC, HD, HD))
LOGGED = shape((NC, HD + 8, HD))
HALF_F32 = shape((T, HALF * GW))
HALF_BF16 = shape((T, HALF * GW), BF16)
WHOLE_BF16 = shape((1, T, NG * GW), BF16)
STAT = shape((T, HD))
GAIN_ROW = shape((1, HALF * GW))
MM = 2 * T * HD * HD * NC
SM = 2 * T * T * HD * NC


def swap_cores(values):
    return lax.ppermute(values, "core", [(0, 1), (1, 0)])


def chips_all_to_all(values):
    return lax.all_to_all(values, ("x", "y"), split_axis=0, concat_axis=0, tiled=True)


def scan_over_chips(upward, got, logs):
    whole_m = pl.BlockSpec((NC, HD, HD), lambda i: (0, 0, 0))
    whole_l = pl.BlockSpec((NC, 8, HD), lambda i: (0, HD // 8, 0))
    whole_t = pl.BlockSpec((HD, HD), lambda i: (0, 0))
    params = pltpu.CompilerParams(vmem_limit_bytes=24 << 20)
    total = pl.pallas_call(
        functools.partial(total_kernel, upward),
        name="half_total",
        grid=(1,),
        in_specs=[whole_m, whole_l],
        out_specs=whole_t,
        out_shape=shape((HD, HD)),
        compiler_params=params,
    )(got, logs)
    before = lax.ppermute(total, "zh", [(0, 1)] if upward else [(1, 0)])
    return pl.pallas_call(
        functools.partial(scan_kernel, upward),
        name="chip_scan",
        grid=(1,),
        in_specs=[whole_m, whole_l, whole_t],
        out_specs=whole_m,
        out_shape=STATES,
        compiler_params=params,
    )(got, logs, before)


def per_device(queries, key_rows, value_rows, out_grad, log_decay, norm_gain):
    core = lax.axis_index("core").astype(jnp.int32).reshape(1)
    q, k, v, g = queries, key_rows, value_rows, out_grad
    gain = norm_gain.reshape(1, NG * GW)
    logs = jnp.transpose(log_decay[0])

    sent, col, row = call(
        state_first_kernel, "states_other", (HALF,),
        [wide(False), wide(False), pl.BlockSpec((NG * GH, T), lambda i, c: (0, 0))],
        [state_block(HD + 8), COL_WHOLE, pl.BlockSpec((NG * GH, T), lambda i, c: (0, 0))],
        [LOGGED, shape((NG, T, GH)), shape((NG * GH, T))],
        (core, k, v, logs), MM,
    )
    got = swap_cores(sent)
    (own,) = call(
        state_second_kernel, "states_own", (HALF,),
        [wide(True), wide(True), COL_WHOLE], [state_block(HD + 8)], [LOGGED],
        (core, k, v, col), MM,
    )
    (chip_total,) = call(
        functools.partial(combine_kernel, True), "chip_total", (HALF,),
        [state_block(), state_block(), LOG_BLOCK, LOG_BLOCK], [state_block(HD + 8)], [LOGGED],
        (core, own, got, own, got), 0,
    )
    gathered = chips_all_to_all(chip_total)

    weights, inside = {}, {}
    for mine in (True, False):
        weights[mine], inside[mine] = call(
            functools.partial(forward_kernel, mine), "forward_inside", (HALF,),
            [wide(mine), wide(mine), wide(mine), COL_WHOLE, row_block(mine)],
            [pl.BlockSpec((GH, T, T), lambda i, c: (i, 0, 0)), narrow()],
            [shape((NC, T, T), BF16), HALF_F32],
            (core, q, k, v, col, row), 2 * SM,
        )

    scanned = chips_all_to_all(scan_over_chips(True, gathered, gathered))
    (onward,) = call(
        functools.partial(send_kernel, True), "onward", (HALF,),
        [state_block(), state_block(), LOG_BLOCK], [state_block()], [STATES],
        (core, scanned, own, own), 0,
    )
    state_other = swap_cores(onward)
    att_own, state_own, squares, products = call(
        attend_own_kernel, "attend_own", (HALF,),
        [wide(True), wide(True), gain_block(True), COL_WHOLE, narrow(), state_block(), state_block(),
         LOG_BLOCK],
        [narrow(), state_block(), STAT_WHOLE, STAT_WHOLE],
        [HALF_F32, STATES, STAT, STAT],
        (core, q, g, gain, col, inside[True], scanned, got, got), 2 * MM,
    )

    def turn(i):
        return jnp.where(i < HALF, i, 2 * HALF - 1 - i)

    def first(i):
        return jnp.minimum(i, HALF - 1)

    def second(i):
        return jnp.minimum(2 * HALF - 1 - i, HALF - 1)

    delta_other, moment_sent, gain_other, inverse, mean = call(
        attend_other_kernel, "attend_other", (2 * HALF,),
        [wide(False, turn), wide(False, turn), gain_block(False, turn), COL_WHOLE, narrow(first),
         state_block(HD, first), STAT_WHOLE, STAT_WHOLE],
        [narrow(second), state_block(HD, second), pl.BlockSpec((1, GW), lambda i, c: (0, second(i))),
         STAT_WHOLE, STAT_WHOLE],
        [HALF_BF16, STATES, GAIN_ROW, STAT, STAT],
        (core, q, g, gain, col, inside[False], state_other, squares, products), 3 * MM,
        scratch=[pltpu.VMEM((HALF, T, GW), F32), pltpu.VMEM((T, HD), F32), pltpu.VMEM((T, HD), F32)],
    )
    moment_got = swap_cores(moment_sent)
    delta_own, moment_own, gain_own = call(
        delta_own_kernel, "delta_own", (HALF,),
        [wide(True), wide(True), gain_block(True), COL_WHOLE, narrow(), STAT_WHOLE, STAT_WHOLE],
        [narrow(), state_block(), pl.BlockSpec((1, GW), lambda i, c: (0, i))],
        [HALF_BF16, STATES, GAIN_ROW],
        (core, q, g, gain, col, att_own, inverse, mean), MM,
    )
    (chip_moment,) = call(
        functools.partial(combine_kernel, False), "chip_moment", (HALF,),
        [state_block(), state_block(), LOG_BLOCK, LOG_BLOCK], [state_block()], [STATES],
        (core, moment_own, moment_got, own, got), 0,
    )
    gathered_back = chips_all_to_all(chip_moment)

    gain_halves = jnp.where(
        core[0] == 0,
        jnp.concatenate([gain_own, gain_other], 1),
        jnp.concatenate([gain_other, gain_own], 1),
    )
    members = lax.axis_size(ALL)
    gain_parts = lax.all_to_all(
        gain_halves.reshape(members, -1), ALL, split_axis=0, concat_axis=0, tiled=True
    )
    gain_grad = jnp.sum(gain_parts, axis=0) * (1.0 / math.sqrt(T * members))

    delta = {True: delta_own, False: delta_other}
    state = {True: state_own, False: state_other}
    query_grad, key_inside, value_inside = (), {}, {}
    for mine in (True, False):
        *query_grad, key_inside[mine], value_inside[mine] = call(
            functools.partial(backward_kernel, mine), "backward_inside", (HALF,),
            [narrow(), wide(mine), wide(mine), wide(mine),
             pl.BlockSpec((GH, T, T), lambda i, c: (i, 0, 0)), COL_WHOLE, row_block(mine), state_block()]
            + [ANY] * len(query_grad),
            [wide(mine), narrow(), narrow()],
            [WHOLE_BF16, HALF_F32, HALF_F32],
            (core, delta[mine], q, k, v, weights[mine], col, row, state[mine], *query_grad),
            4 * SM + 2 * MM,
            aliases={9: 0} if query_grad else None,
        )

    scanned_back = chips_all_to_all(scan_over_chips(False, gathered_back, gathered))
    (onward_back,) = call(
        functools.partial(send_kernel, False), "onward_back", (HALF,),
        [state_block(), state_block(), LOG_BLOCK], [state_block()], [STATES],
        (core, scanned_back, moment_own, own), 0,
    )
    later_other = swap_cores(onward_back)
    key_grad, value_grad = call(
        finish_own_kernel, "finish_own", (HALF,),
        [wide(True), wide(True), COL_WHOLE, narrow(), narrow(), state_block(), state_block(), LOG_BLOCK],
        [wide(True), wide(True)], [WHOLE_BF16, WHOLE_BF16],
        (core, k, v, col, key_inside[True], value_inside[True], scanned_back, moment_got, got), 4 * MM,
    )
    key_grad, value_grad = call(
        finish_other_kernel, "finish_other", (HALF,),
        [wide(False), wide(False), COL_WHOLE, narrow(), narrow(), state_block(), ANY, ANY],
        [wide(False), wide(False)], [WHOLE_BF16, WHOLE_BF16],
        (core, k, v, col, key_inside[False], value_inside[False], later_other, key_grad, value_grad),
        4 * MM, aliases={7: 0, 8: 1},
    )
    return query_grad[0], key_grad, value_grad, gain_grad


def solution(mesh):
    fine = Mesh(mesh.devices.reshape(4, 2, 4, 4, 2), ALL)
    rows = P("dp", ("zh", "x", "y", "core"), None)
    return jax.shard_map(
        per_device,
        mesh=fine,
        in_specs=(rows,) * 5 + (P(),),
        out_specs=(rows, rows, rows, P(ALL)),
        check_vma=False,
    )
```

profile of v0, /device:TPU:1, one launch (start us, length us, event | category | flops | bytes accessed | tf_op | source)
XLA Modules:
  0.0 179.8 jit_solution(16576204241260714199)
XLA Ops:
  2.0 1.4 copy-done.2
  4.2 2.4 %states_other.1 = (f32[16,136,128]{2,1,0:T(8,128)S(1)}, f32[4,192,8]{2,1,0:T(8,128)S(1)}, f32[32,192]{1,0:T(8,128)S(1)}) custom-call(s32[1]{0:T(128)} %bitcast.c_ref, bf16[1,192,4096]{2,1,0:T(8,128)(2,1)S(1)} %copy-done, bf16[1,192,4096]{2,1,0:T(8,128)(2,1)S(1)} %copy-done.2, f32[32,192]{1,0:T(8,128)S(1)} %bitcast.9), custom_call_target="tpu_custom_call" | custom-call | flops 100663296 | bytes 4333568 | tf_op jit(solution)/shard_map/states_other/pallas_call | solution.py:273
  6.6 3.3 %collective-permute-start = (f32[16,136,128]{2,1,0:T(8,128)S(1)}, f32[16,136,128]{2,1,0:T(8,128)S(1)}, u32[]{:S(2)}, u32[]{:S(2)}) collective-permute-start(f32[16,136,128]{2,1,0:T(8,128)S(1)} %get-tuple-element.36), channel_id=1, source_target_pairs={{0,1},{1,0},{2,3},{3,2},{4,5},{5,4},{6,7},{7,6},{8,9},{9,8},{10,11... | collective-permute-start | bytes 3342344 | tf_op jit(solution)/shard_map/ppermute | solution.py:334
  10.0 1.9 %states_own.1.own_ref.lo_ref = f32[16,136,128]{2,1,0:T(8,128)S(1)} custom-call(s32[1]{0:T(128)} %bitcast.c_ref, bf16[1,192,4096]{2,1,0:T(8,128)(2,1)S(1)} %copy-done, bf16[1,192,4096]{2,1,0:T(8,128)(2,1)S(1)} %copy-done.2, f32[4,192,8]{2,1,0:T(8,128)S(1)} %get-tuple-element.33.col_ref), custom_call_target="tpu_custom_call" | custom-call | flops 100663296 | bytes 4284416 | tf_op jit(solution)/shard_map/states_own/pallas_call | solution.py:273
  12.7 21.9 %all_to_all.26.m_ref.l_ref = f32[16,136,128]{2,1,0:T(8,128)S(1)} all-to-all(f32[16,136,128]{2,1,0:T(8,128)S(1)} %chip_total.1), channel_id=1, replica_groups=mesh['dp'=4,'zh'=2,'x'=4,'y'=4,'core'=2] {'x','y'}, dimensions={0} | all-to-all | bytes 2228224 | tf_op jit(solution)/shard_map/all_to_all | solution.py:338
  34.7 8.8 %collective-permute-start.1 = (f32[128,128]{1,0:T(8,128)S(1)}, f32[128,128]{1,0:T(8,128)S(1)}, u32[]{:S(2)}, u32[]{:S(2)}) collective-permute-start(f32[128,128]{1,0:T(8,128)S(1)} %half_total.2), channel_id=1, source_target_pairs={{0,32},{1,33},{2,34},{3,35},{4,36},{5,37},{6,38},{7,39},{8,40},{9,... | collective-permute-start | bytes 196616 | tf_op jit(solution)/shard_map/ppermute | solution.py:355
  45.0 17.1 %all_to_all.27.d_ref = f32[16,128,128]{2,1,0:T(8,128)S(1)} all-to-all(f32[16,128,128]{2,1,0:T(8,128)S(1)} %chip_scan.2), channel_id=1, replica_groups=mesh['dp'=4,'zh'=2,'x'=4,'y'=4,'core'=2] {'x','y'}, dimensions={0} | all-to-all | bytes 2097152 | tf_op jit(solution)/shard_map/all_to_all | solution.py:338
  62.3 4.3 %collective-permute-start.2 = (f32[16,128,128]{2,1,0:T(8,128)S(1)}, f32[16,128,128]{2,1,0:T(8,128)S(1)}, u32[]{:S(2)}, u32[]{:S(2)}) collective-permute-start(f32[16,128,128]{2,1,0:T(8,128)S(1)} %onward.1), channel_id=1, source_target_pairs={{0,1},{1,0},{2,3},{3,2},{4,5},{5,4},{6,7},{7,6},{8,9},{9,8},{10,11... | collective-permute-start | bytes 3145736 | tf_op jit(solution)/shard_map/ppermute | solution.py:334
  66.7 1.9 %forward_inside.3 = (bf16[16,192,192]{2,1,0:T(8,128)(2,1)S(1)}, f32[192,2048]{1,0:T(8,128)S(1)}) custom-call(s32[1]{0:T(128)} %bitcast.c_ref, bf16[1,192,4096]{2,1,0:T(8,128)(2,1)S(1)} %copy-done.4, bf16[1,192,4096]{2,1,0:T(8,128)(2,1)S(1)} %copy-done.1, bf16[1,192,4096]{2,1,0:T(8,128)(2,1)S(1)} %copy-done.3, f32[4,192,8]{2,1,0:T(8,128)S(1)} %get-tuple-element.33.col_ref, ...), custom_call_target="tpu_custom_call" | custom-call | flops 301989888 | bytes 7520256 | tf_op jit(solution)/shard_map/forward_inside/pallas_call | solution.py:273
  69.8 1.9 %forward_inside.2 = (bf16[16,192,192]{2,1,0:T(8,128)(2,1)S(1)}, f32[192,2048]{1,0:T(8,128)S(1)}) custom-call(s32[1]{0:T(128)} %bitcast.c_ref, bf16[1,192,4096]{2,1,0:T(8,128)(2,1)S(1)} %copy-done.4, bf16[1,192,4096]{2,1,0:T(8,128)(2,1)S(1)} %copy-done.1, bf16[1,192,4096]{2,1,0:T(8,128)(2,1)S(1)} %copy-done.3, f32[4,192,8]{2,1,0:T(8,128)S(1)} %get-tuple-element.33.col_ref, ...), custom_call_target="tpu_custom_call" | custom-call | flops 301989888 | bytes 7520256 | tf_op jit(solution)/shard_map/forward_inside/pallas_call | solution.py:273
  75.2 3.0 %attend_other.1 = (bf16[192,2048]{1,0:T(8,128)(2,1)S(1)}, f32[16,128,128]{2,1,0:T(8,128)S(1)}, f32[1,2048]{1,0:T(1,128)S(1)}, f32[192,128]{1,0:T(8,128)S(1)}, f32[192,128]{1,0:T(8,128)S(1)}) custom-call(s32[1]{0:T(128)} %bitcast.c_ref, bf16[1,192,4096]{2,1,0:T(8,128)(2,1)S(1)} %copy-done.4, bf16[1,192,4096]{2,1,0:T(8,128)(2,1)S(1)} %copy-done.8, ...), custom_call_target="tpu_custom_call" | custom-call | flops 301989888 | bytes 8044544 | tf_op jit(solution)/shard_map/attend_other/pallas_call | solution.py:273
  78.2 1.6 collective-permute-start.3
  79.8 1.7 delta_own.1
  83.1 19.0 %all_to_all.28.m_ref = f32[16,128,128]{2,1,0:T(8,128)S(1)} all-to-all(f32[16,128,128]{2,1,0:T(8,128)S(1)} %chip_moment.1), channel_id=1, replica_groups=mesh['dp'=4,'zh'=2,'x'=4,'y'=4,'core'=2] {'x','y'}, dimensions={0} | all-to-all | bytes 2097152 | tf_op jit(solution)/shard_map/all_to_all | solution.py:338
  103.5 7.6 %collective-permute-done.4.t_ref = f32[128,128]{1,0:T(8,128)S(1)} collective-permute-done((f32[128,128]{1,0:T(8,128)S(1)}, f32[128,128]{1,0:T(8,128)S(1)}, u32[]{:S(2)}, u32[]{:S(2)}) %collective-permute-start.4) | collective-permute-done | bytes 65568 | tf_op jit(solution)/shard_map/ppermute | solution.py:355
  111.2 16.7 %all_to_all.29.d_ref = f32[16,128,128]{2,1,0:T(8,128)S(1)} all-to-all(f32[16,128,128]{2,1,0:T(8,128)S(1)} %chip_scan.3), channel_id=1, replica_groups=mesh['dp'=4,'zh'=2,'x'=4,'y'=4,'core'=2] {'x','y'}, dimensions={0} | all-to-all | bytes 2097152 | tf_op jit(solution)/shard_map/all_to_all | solution.py:338
  129.3 4.9 %collective-permute-start.5 = (f32[16,128,128]{2,1,0:T(8,128)}, f32[16,128,128]{2,1,0:T(8,128)}, u32[]{:S(2)}, u32[]{:S(2)}) collective-permute-start(f32[16,128,128]{2,1,0:T(8,128)} %onward_back.1), channel_id=1, source_target_pairs={{0,1},{1,0},{2,3},{3,2},{4,5},{5,4},{6,7},{7,6},{8,9},{9,8},{10,11... | collective-permute-start | bytes 3145736 | tf_op jit(solution)/shard_map/ppermute | solution.py:334
  134.8 1.5 select_n.23
  136.3 6.9 %all-to-all-start.4 = ((f32[256,1,16]{2,1,0:T(1,128)}), f32[256,1,16]{2,1,0:T(1,128)}, u32[]{:S(2)}, u32[]{:S(2)}) async-start(f32[256,1,16]{2,1,0:T(1,128)} %bitcast.10), calls=%async_computation.4 | async-start | bytes 262144 | tf_op jit(solution)/shard_map/all_to_all | solution.py:459
  144.6 1.4 copy-done.18
  149.1 6.0 %backward_inside.2 = (bf16[1,192,4096]{2,1,0:T(8,128)(2,1)}, f32[192,2048]{1,0:T(8,128)S(1)}, f32[192,2048]{1,0:T(8,128)S(1)}) custom-call(s32[1]{0:T(128)} %bitcast.c_ref, bf16[192,2048]{1,0:T(8,128)(2,1)S(1)} %copy-done.32, bf16[1,192,4096]{2,1,0:T(8,128)(2,1)S(1)} %copy-done.5, bf16[1,192,4096]{2,1,0:T(8,128)(2,1)S(1)} %copy-done.1, ...), custom_call_target="tpu_custom_call" | custom-call | flops 805306368 | bytes 12500992 | tf_op jit(solution)/shard_map/backward_inside/pallas_call | solution.py:273
  157.5 6.0 %backward_inside.3 = (bf16[1,192,4096]{2,1,0:T(8,128)(2,1)}, f32[192,2048]{1,0:T(8,128)S(1)}, f32[192,2048]{1,0:T(8,128)S(1)}) custom-call(s32[1]{0:T(128)} %bitcast.c_ref, bf16[192,2048]{1,0:T(8,128)(2,1)S(1)} %copy-done.30, bf16[1,192,4096]{2,1,0:T(8,128)(2,1)S(1)} %copy-done.5, ...), custom_call_target="tpu_custom_call", output_to_operand_aliasing={{0}: (9, {})} | custom-call | flops 805306368 | bytes 14073856 | tf_op jit(solution)/shard_map/backward_inside/pallas_call | solution.py:273
  174.0 2.5 %finish_own.1 = (bf16[1,192,4096]{2,1,0:T(8,128)(2,1)}, bf16[1,192,4096]{2,1,0:T(8,128)(2,1)}) custom-call(s32[1]{0:T(128)} %bitcast.c_ref, bf16[1,192,4096]{2,1,0:T(8,128)(2,1)S(1)} %copy-done.1, bf16[1,192,4096]{2,1,0:T(8,128)(2,1)S(1)} %copy-done.3, f32[4,192,8]{2,1,0:T(8,128)S(1)} %get-tuple-element.33.col_ref, f32[192,2048]{1,0:T(8,128)S(1)} %copy-done.20, ...), custom_call_target="tpu_custom_call" | custom-call | flops 402653184 | bytes 12673024 | tf_op jit(solution)/shard_map/finish_own/pallas_call | solution.py:273
  176.5 3.3 %finish_other.1 = (bf16[1,192,4096]{2,1,0:T(8,128)(2,1)}, bf16[1,192,4096]{2,1,0:T(8,128)(2,1)}) custom-call(s32[1]{0:T(128)} %bitcast.c_ref, bf16[1,192,4096]{2,1,0:T(8,128)(2,1)S(1)} %copy-done.1, bf16[1,192,4096]{2,1,0:T(8,128)(2,1)S(1)} %copy-done.3, f32[4,192,8]{2,1,0:T(8,128)S(1)} %get-tuple-element.33.col_ref, ...), custom_call_target="tpu_custom_call", output_to_operand_aliasing={{0}: (7, {}), {1}: (8, {})} | custom-call | flops 402653184 | bytes 13656064 | tf_op jit(solution)/shard_map/finish_other/pallas_call | solution.py:273
  (91 shorter events, 31.9 us)
Async XLA Ops:
  0.6 1.4 copy-start
  6.6 62.0 %copy-start.33 = (f32[32,192]{1,0:T(8,128)}, f32[32,192]{1,0:T(8,128)S(1)}, u32[]{:S(2)}) copy-start(f32[32,192]{1,0:T(8,128)S(1)} %get-tuple-element.34.row_ref) | copy-start | bytes 73732
  6.6 5.7 %collective-permute-start = (f32[16,136,128]{2,1,0:T(8,128)S(1)}, f32[16,136,128]{2,1,0:T(8,128)S(1)}, u32[]{:S(2)}, u32[]{:S(2)}) collective-permute-start(f32[16,136,128]{2,1,0:T(8,128)S(1)} %get-tuple-element.36), channel_id=1, source_target_pairs={{0,1},{1,0},{2,3},{3,2},{4,5},{5,4},{6,7},{7,6},{8,9},{9,8},{10,11... | collective-permute-start | bytes 3342344 | tf_op jit(solution)/shard_map/ppermute | solution.py:334
  12.3 69.7 %copy-start.6 = (f32[16,136,128]{2,1,0:T(8,128)}, f32[16,136,128]{2,1,0:T(8,128)S(1)}, u32[]{:S(2)}) copy-start(f32[16,136,128]{2,1,0:T(8,128)S(1)} %collective-permute-done.got_ref.lg_ref) | copy-start | bytes 3342340
  34.7 10.1 %collective-permute-start.1 = (f32[128,128]{1,0:T(8,128)S(1)}, f32[128,128]{1,0:T(8,128)S(1)}, u32[]{:S(2)}, u32[]{:S(2)}) collective-permute-start(f32[128,128]{1,0:T(8,128)S(1)} %half_total.2), channel_id=1, source_target_pairs={{0,32},{1,33},{2,34},{3,35},{4,36},{5,37},{6,38},{7,39},{8,40},{9,... | collective-permute-start | bytes 196616 | tf_op jit(solution)/shard_map/ppermute | solution.py:355
  45.0 21.7 %copy-start.4 = (bf16[1,192,4096]{2,1,0:T(8,128)(2,1)S(1)}, bf16[1,192,4096]{2,1,0:T(8,128)(2,1)}, u32[]{:S(2)}) copy-start(bf16[1,192,4096]{2,1,0:T(8,128)(2,1)} %q_ref.13) | copy-start | bytes 4718596
  62.0 4.6 %copy-start.1 = (bf16[1,192,4096]{2,1,0:T(8,128)(2,1)S(1)}, bf16[1,192,4096]{2,1,0:T(8,128)(2,1)}, u32[]{:S(2)}) copy-start(bf16[1,192,4096]{2,1,0:T(8,128)(2,1)} %k_ref.15) | copy-start | bytes 4718596
  62.0 4.6 %copy-start.3 = (bf16[1,192,4096]{2,1,0:T(8,128)(2,1)S(1)}, bf16[1,192,4096]{2,1,0:T(8,128)(2,1)}, u32[]{:S(2)}) copy-start(bf16[1,192,4096]{2,1,0:T(8,128)(2,1)} %v_ref.15) | copy-start | bytes 4718596
  62.3 12.9 %collective-permute-start.2 = (f32[16,128,128]{2,1,0:T(8,128)S(1)}, f32[16,128,128]{2,1,0:T(8,128)S(1)}, u32[]{:S(2)}, u32[]{:S(2)}) collective-permute-start(f32[16,128,128]{2,1,0:T(8,128)S(1)} %onward.1), channel_id=1, source_target_pairs={{0,1},{1,0},{2,3},{3,2},{4,5},{5,4},{6,7},{7,6},{8,9},{9,8},{10,11... | collective-permute-start | bytes 3145736 | tf_op jit(solution)/shard_map/ppermute | solution.py:334
  69.8 3.1 %copy-start.8 = (bf16[1,192,4096]{2,1,0:T(8,128)(2,1)S(1)}, bf16[1,192,4096]{2,1,0:T(8,128)(2,1)}, u32[]{:S(2)}) copy-start(bf16[1,192,4096]{2,1,0:T(8,128)(2,1)} %g_ref.5) | copy-start | bytes 4718596
  69.8 3.1 %copy-start.35 = (f32[4096]{0:T(1024)S(1)}, f32[4096]{0:T(1024)}, u32[]{:S(2)}) copy-start(f32[4096]{0:T(1024)} %param.11) | copy-start | bytes 49156
  75.2 3.0 %copy-start.11 = (f32[16,128,128]{2,1,0:T(8,128)}, f32[16,128,128]{2,1,0:T(8,128)S(1)}, u32[]{:S(2)}) copy-start(f32[16,128,128]{2,1,0:T(8,128)S(1)} %collective-permute-done.2.i_ref) | copy-start | bytes 3145732
  78.2 3.3 %copy-start.29 = (bf16[192,2048]{1,0:T(8,128)(2,1)}, bf16[192,2048]{1,0:T(8,128)(2,1)S(1)}, u32[]{:S(2)}) copy-start(bf16[192,2048]{1,0:T(8,128)(2,1)S(1)} %get-tuple-element.40.od_ref) | copy-start | bytes 2359300
  78.2 3.9 %collective-permute-start.3 = (f32[16,128,128]{2,1,0:T(8,128)S(1)}, f32[16,128,128]{2,1,0:T(8,128)S(1)}, u32[]{:S(2)}, u32[]{:S(2)}) collective-permute-start(f32[16,128,128]{2,1,0:T(8,128)S(1)} %get-tuple-element.53), channel_id=1, source_target_pairs={{0,1},{1,0},{2,3},{3,2},{4,5},{5,4},{6,7},{7,6},{8,9},{9,8},{10,11... | collective-permute-start | bytes 3145736 | tf_op jit(solution)/shard_map/ppermute | solution.py:334
  102.2 8.9 %collective-permute-start.4 = (f32[128,128]{1,0:T(8,128)S(1)}, f32[128,128]{1,0:T(8,128)S(1)}, u32[]{:S(2)}, u32[]{:S(2)}) collective-permute-start(f32[128,128]{1,0:T(8,128)S(1)} %half_total.3), channel_id=1, source_target_pairs={{32,0},{33,1},{34,2},{35,3},{36,4},{37,5},{38,6},{39,7},{40,8},{41... | collective-permute-start | bytes 196616 | tf_op jit(solution)/shard_map/ppermute | solution.py:355
  129.3 47.2 %collective-permute-start.5 = (f32[16,128,128]{2,1,0:T(8,128)}, f32[16,128,128]{2,1,0:T(8,128)}, u32[]{:S(2)}, u32[]{:S(2)}) collective-permute-start(f32[16,128,128]{2,1,0:T(8,128)} %onward_back.1), channel_id=1, source_target_pairs={{0,1},{1,0},{2,3},{3,2},{4,5},{5,4},{6,7},{7,6},{8,9},{9,8},{10,11... | collective-permute-start | bytes 3145736 | tf_op jit(solution)/shard_map/ppermute | solution.py:334
  136.3 29.5 %all-to-all-start.4 = ((f32[256,1,16]{2,1,0:T(1,128)}), f32[256,1,16]{2,1,0:T(1,128)}, u32[]{:S(2)}, u32[]{:S(2)}) async-start(f32[256,1,16]{2,1,0:T(1,128)} %bitcast.10), calls=%async_computation.4 | async-start | bytes 262144 | tf_op jit(solution)/shard_map/all_to_all | solution.py:459
  143.2 1.4 copy-start.5
  144.6 1.4 copy-start.18
  149.1 8.3 %copy-start.12 = (f32[16,128,128]{2,1,0:T(8,128)S(1)}, f32[16,128,128]{2,1,0:T(8,128)}, u32[]{:S(2)}) copy-start(f32[16,128,128]{2,1,0:T(8,128)} %copy-done.11) | copy-start | bytes 3145732
  149.1 8.3 %copy-start.16 = (bf16[16,192,192]{2,1,0:T(8,128)(2,1)S(1)}, bf16[16,192,192]{2,1,0:T(8,128)(2,1)}, u32[]{:S(2)}) copy-start(bf16[16,192,192]{2,1,0:T(8,128)(2,1)} %copy-done.15) | copy-start | bytes 3538948
  149.1 8.4 %copy-start.30 = (bf16[192,2048]{1,0:T(8,128)(2,1)S(1)}, bf16[192,2048]{1,0:T(8,128)(2,1)}, u32[]{:S(2)}) copy-start(bf16[192,2048]{1,0:T(8,128)(2,1)} %copy-done.29) | copy-start | bytes 2359300
  174.0 2.5 %copy-start.24 = (f32[192,2048]{1,0:T(8,128)S(1)}, f32[192,2048]{1,0:T(8,128)}, u32[]{:S(2)}) copy-start(f32[192,2048]{1,0:T(8,128)} %copy-done.23) | copy-start | bytes 4718596
  174.0 2.5 %copy-start.26 = (f32[192,2048]{1,0:T(8,128)S(1)}, f32[192,2048]{1,0:T(8,128)}, u32[]{:S(2)}) copy-start(f32[192,2048]{1,0:T(8,128)} %copy-done.25) | copy-start | bytes 4718596
  (20 other events, 23.0 us)
where the time goes:
time: 181 us; the launch traced here: 180 us
  blocking collectives  74.7 us (41%)
  Pallas kernels  34.4 us (19%)
  starting transfers between devices  31.1 us (17%)
  local copies, waits for them, and re-layouts  26.4 us (15%)
  waiting for transfers between devices  9.96 us (6%)
  other arithmetic  2.35 us (1%)
    all_to_all x4, blocking collectives, chips_all_to_all(): lax.all_to_all(values, ('x', 'y'), split_axis=0, concat_axis=0, tiled=True)  74.7 us
    pallas_call x15, Pallas kernels, call(): pl.pallas_call(kernel, name=name, grid_spec=pltpu.PrefetchScalarGridSpec(...  34.1 us
    unnamed x74, local copies, waits for them, and re-layouts  24.9 us
    ppermute x4, starting transfers between devices, swap_cores(): return lax.ppermute(values, 'core', [(0, 1), (1, 0)])  14.1 us
    ppermute x2, starting transfers between devices, scan_over_chips(): before = lax.ppermute(total, 'zh', [(0, 1)] if upward else [(1, 0)])  10.1 us
    ppermute x2, waiting for transfers between devices, scan_over_chips(): before = lax.ppermute(total, 'zh', [(0, 1)] if upward else [(1, 0)])  8.93 us
    all_to_all x1, starting transfers between devices, per_device(): lax.all_to_all(gain_halves.reshape(members, -1), ALL, split_axis=0, conca...  6.89 us
  transfers between devices with their start and end apart: 7, of which 4 were waited for; matrix products, arithmetic and copies ran while one was open for 2% of the time, Pallas kernels for 13%

commit v1 on v0

--- a/solution.py
+++ b/solution.py
@@ -267,9 +267,20 @@
     finish_group(k_ref, v_ref, cum, ki_ref, vi_ref, lambda j: x_ref[j], kg_ref, vg_ref)
 
 
+class Free:
+    def __init__(self, array):
+        self.array = array
+
+
+def in_hbm(a):
+    return pltpu.with_memory_space_constraint(a, pltpu.HBM)
+
+
 def call(kernel, name, grid, in_specs, out_specs, out_shape, args, flops, scratch=(), aliases=None):
     nbytes = sum(math.prod(s.shape) * s.dtype.itemsize for s in out_shape)
-    nbytes += sum(math.prod(a.shape) * a.dtype.itemsize for a in args[1:])
+    nbytes += sum(math.prod(a.shape) * a.dtype.itemsize for a in args[1:] if not isinstance(a, Free))
+    args = [args[0]] + [a.array if isinstance(a, Free) else in_hbm(a) for a in args[1:]]
+    out_shape = [pltpu.HBM(s.shape, s.dtype) for s in out_shape]
     return pl.pallas_call(
         kernel,
         name=name,
@@ -282,7 +293,7 @@
         ),
         out_shape=out_shape,
         input_output_aliases=aliases or {},
-        compiler_params=pltpu.CompilerParams(vmem_limit_bytes=24 << 20),
+        compiler_params=pltpu.CompilerParams(vmem_limit_bytes=16 << 20),
         cost_estimate=pl.CostEstimate(flops=flops, bytes_accessed=nbytes, transcendentals=0),
     )(*args)
 
@@ -342,7 +353,7 @@
     whole_m = pl.BlockSpec((NC, HD, HD), lambda i: (0, 0, 0))
     whole_l = pl.BlockSpec((NC, 8, HD), lambda i: (0, HD // 8, 0))
     whole_t = pl.BlockSpec((HD, HD), lambda i: (0, 0))
-    params = pltpu.CompilerParams(vmem_limit_bytes=24 << 20)
+    params = pltpu.CompilerParams(vmem_limit_bytes=16 << 20)
     total = pl.pallas_call(
         functools.partial(total_kernel, upward),
         name="half_total",
@@ -359,7 +370,7 @@
         grid=(1,),
         in_specs=[whole_m, whole_l, whole_t],
         out_specs=whole_m,
-        out_shape=STATES,
+        out_shape=pltpu.HBM(STATES.shape, F32),
         compiler_params=params,
     )(got, logs, before)
 
@@ -386,7 +397,7 @@
     (chip_total,) = call(
         functools.partial(combine_kernel, True), "chip_total", (HALF,),
         [state_block(), state_block(), LOG_BLOCK, LOG_BLOCK], [state_block(HD + 8)], [LOGGED],
-        (core, own, got, own, got), 0,
+        (core, own, Free(got), own, Free(got)), 0,
     )
     gathered = chips_all_to_all(chip_total)
 
@@ -400,11 +411,14 @@
             (core, q, k, v, col, row), 2 * SM,
         )
 
+    gathered, inside[True], inside[False] = lax.optimization_barrier(
+        (gathered, inside[True], inside[False])
+    )
     scanned = chips_all_to_all(scan_over_chips(True, gathered, gathered))
     (onward,) = call(
         functools.partial(send_kernel, True), "onward", (HALF,),
         [state_block(), state_block(), LOG_BLOCK], [state_block()], [STATES],
-        (core, scanned, own, own), 0,
+        (core, Free(scanned), own, own), 0,
     )
     state_other = swap_cores(onward)
     att_own, state_own, squares, products = call(
@@ -413,7 +427,7 @@
          LOG_BLOCK],
         [narrow(), state_block(), STAT_WHOLE, STAT_WHOLE],
         [HALF_F32, STATES, STAT, STAT],
-        (core, q, g, gain, col, inside[True], scanned, got, got), 2 * MM,
+        (core, q, g, gain, col, inside[True], Free(scanned), Free(got), Free(got)), 2 * MM,
     )
 
     def turn(i):
@@ -432,7 +446,7 @@
         [narrow(second), state_block(HD, second), pl.BlockSpec((1, GW), lambda i, c: (0, second(i))),
          STAT_WHOLE, STAT_WHOLE],
         [HALF_BF16, STATES, GAIN_ROW, STAT, STAT],
-        (core, q, g, gain, col, inside[False], state_other, squares, products), 3 * MM,
+        (core, q, g, gain, col, inside[False], Free(state_other), squares, products), 3 * MM,
         scratch=[pltpu.VMEM((HALF, T, GW), F32), pltpu.VMEM((T, HD), F32), pltpu.VMEM((T, HD), F32)],
     )
     moment_got = swap_cores(moment_sent)
@@ -446,7 +460,7 @@
     (chip_moment,) = call(
         functools.partial(combine_kernel, False), "chip_moment", (HALF,),
         [state_block(), state_block(), LOG_BLOCK, LOG_BLOCK], [state_block()], [STATES],
-        (core, moment_own, moment_got, own, got), 0,
+        (core, moment_own, Free(moment_got), own, Free(got)), 0,
     )
     gathered_back = chips_all_to_all(chip_moment)
 
@@ -462,7 +476,7 @@
     gain_grad = jnp.sum(gain_parts, axis=0) * (1.0 / math.sqrt(T * members))
 
     delta = {True: delta_own, False: delta_other}
-    state = {True: state_own, False: state_other}
+    state = {True: state_own, False: Free(state_other)}
     query_grad, key_inside, value_inside = (), {}, {}
     for mine in (True, False):
         *query_grad, key_inside[mine], value_inside[mine] = call(
@@ -477,24 +491,28 @@
             aliases={9: 0} if query_grad else None,
         )
 
+    gathered_back, key_inside[True] = lax.optimization_barrier((gathered_back, key_inside[True]))
     scanned_back = chips_all_to_all(scan_over_chips(False, gathered_back, gathered))
+    scanned_back, key_inside[False], gain_grad = lax.optimization_barrier(
+        (scanned_back, key_inside[False], gain_grad)
+    )
     (onward_back,) = call(
         functools.partial(send_kernel, False), "onward_back", (HALF,),
         [state_block(), state_block(), LOG_BLOCK], [state_block()], [STATES],
-        (core, scanned_back, moment_own, own), 0,
+        (core, Free(scanned_back), moment_own, own), 0,
     )
     later_other = swap_cores(onward_back)
     key_grad, value_grad = call(
         finish_own_kernel, "finish_own", (HALF,),
         [wide(True), wide(True), COL_WHOLE, narrow(), narrow(), state_block(), state_block(), LOG_BLOCK],
         [wide(True), wide(True)], [WHOLE_BF16, WHOLE_BF16],
-        (core, k, v, col, key_inside[True], value_inside[True], scanned_back, moment_got, got), 4 * MM,
+        (core, k, v, col, key_inside[True], value_inside[True], Free(scanned_back), Free(moment_got), Free(got)), 4 * MM,
     )
     key_grad, value_grad = call(
         finish_other_kernel, "finish_other", (HALF,),
         [wide(False), wide(False), COL_WHOLE, narrow(), narrow(), state_block(), ANY, ANY],
         [wide(False), wide(False)], [WHOLE_BF16, WHOLE_BF16],
-        (core, k, v, col, key_inside[False], value_inside[False], later_other, key_grad, value_grad),
+        (core, k, v, col, key_inside[False], value_inside[False], Free(later_other), key_grad, value_grad),
         4 * MM, aliases={7: 0, 8: 1},
     )
     return query_grad[0], key_grad, value_grad, gain_grad

time: 181 us -> 169 us (0.934)
  blocking collectives: 74.7 us -> 17.9 us
  Pallas kernels: 34.4 us -> 65.2 us
  waiting for transfers between devices: 9.96 us -> 37 us
  local copies, waits for them, and re-layouts: 26.4 us -> 1.82 us
  starting transfers between devices: 31.1 us -> 45 us
    all_to_all x4 -> x1, blocking collectives: 74.7 us -> 17.9 us  [chips_all_to_all(): lax.all_to_all(values, ('x', 'y'), split_axis=0, concat_axis=0, tiled=True)]
    pallas_call x15, Pallas kernels: 34.1 us -> 62.9 us  [call(): pl.pallas_call(kernel, name=name, grid_spec=pltpu.PrefetchScalarGridSpec(...]
    unnamed x74 -> x12, local copies, waits for them, and re-layouts: 24.9 us -> 1.06 us
    all_to_all x0 -> x3, waiting for transfers between devices: none -> 23.7 us  [chips_all_to_all(): lax.all_to_all(values, ('x', 'y'), split_axis=0, concat_axis=0, tiled=True)]
    all_to_all x0 -> x3, starting transfers between devices: none -> 12.3 us  [chips_all_to_all(): lax.all_to_all(values, ('x', 'y'), split_axis=0, concat_axis=0, tiled=True)]
    all_to_all x1, waiting for transfers between devices: 0.01 us -> 12.1 us  [per_device(): lax.all_to_all(gain_halves.reshape(members, -1), ALL, split_axis=0, conca...]
    ppermute x2, waiting for transfers between devices: 8.93 us -> 1.31 us  [scan_over_chips(): before = lax.ppermute(total, 'zh', [(0, 1)] if upward else [(1, 0)])]
    all_to_all x1, starting transfers between devices: 6.89 us -> 12.7 us  [per_device(): lax.all_to_all(gain_halves.reshape(members, -1), ALL, split_axis=0, conca...]
  transfers between devices with their start and end apart: 7 -> 10, of which waited for: 4 -> 5; matrix products, arithmetic and copies ran while one was open for 2% -> 1% of each run, Pallas kernels for 13% -> 25%
where the time goes in v1:
time: 169 us
  Pallas kernels  65.2 us (39%)
  starting transfers between devices  45 us (27%)
  waiting for transfers between devices  37 us (22%)
  blocking collectives  17.9 us (11%)
  local copies, waits for them, and re-layouts  1.82 us (1%)
    pallas_call x15, Pallas kernels, call(): pl.pallas_call(kernel, name=name, grid_spec=pltpu.PrefetchScalarGridSpec(...  62.9 us
    all_to_all x3, waiting for transfers between devices, chips_all_to_all(): lax.all_to_all(values, ('x', 'y'), split_axis=0, concat_axis=0, tiled=True)  23.7 us
    all_to_all x1, blocking collectives, chips_all_to_all(): lax.all_to_all(values, ('x', 'y'), split_axis=0, concat_axis=0, tiled=True)  17.9 us
    all_to_all x1, starting transfers between devices, per_device(): lax.all_to_all(gain_halves.reshape(members, -1), ALL, split_axis=0, conca...  12.7 us
    all_to_all x3, starting transfers between devices, chips_all_to_all(): lax.all_to_all(values, ('x', 'y'), split_axis=0, concat_axis=0, tiled=True)  12.3 us
    all_to_all x1, waiting for transfers between devices, per_device(): lax.all_to_all(gain_halves.reshape(members, -1), ALL, split_axis=0, conca...  12.1 us
    ppermute x2, starting transfers between devices, scan_over_chips(): before = lax.ppermute(total, 'zh', [(0, 1)] if upward else [(1, 0)])  10.1 us
    ppermute x4, starting transfers between devices, swap_cores(): return lax.ppermute(values, 'core', [(0, 1), (1, 0)])  9.86 us
  transfers between devices with their start and end apart: 10, of which 5 were waited for; matrix products, arithmetic and copies ran while one was open for 1% of the time, Pallas kernels for 25%

profile of v1, /device:TPU:1, one launch (start us, length us, event | category | flops | bytes accessed | tf_op | source)
XLA Modules:
  0.0 168.6 jit_solution(13090867291598691292)
XLA Ops:
  0.6 4.2 %states_other.1 = (f32[16,136,128]{2,1,0:T(8,128)}, f32[4,192,8]{2,1,0:T(8,128)}, f32[32,192]{1,0:T(8,128)}) custom-call(s32[1]{0:T(128)} %bitcast.c_ref, bf16[1,192,4096]{2,1,0:T(8,128)(2,1)} %k_ref.15, bf16[1,192,4096]{2,1,0:T(8,128)(2,1)} %v_ref.15, f32[32,192]{1,0:T(8,128)} %bitcast.10), custom_call_target="tpu_custom_call" | custom-call | flops 100663296 | bytes 4333568 | tf_op jit(solution)/shard_map/states_other/pallas_call | solution.py:284
  4.9 3.2 %collective-permute-start = (f32[16,136,128]{2,1,0:T(8,128)}, f32[16,136,128]{2,1,0:T(8,128)S(1)}, u32[]{:S(2)}, u32[]{:S(2)}) collective-permute-start(f32[16,136,128]{2,1,0:T(8,128)} %get-tuple-element.42), channel_id=1, source_target_pairs={{0,1},{1,0},{2,3},{3,2},{4,5},{5,4},{6,7},{7,6},{8,9},{9,8},{10,11... | collective-permute-start | bytes 3342344 | tf_op jit(solution)/shard_map/ppermute | solution.py:345
  8.1 3.8 %states_own.1.own_ref.lo_ref = f32[16,136,128]{2,1,0:T(8,128)} custom-call(s32[1]{0:T(128)} %bitcast.c_ref, bf16[1,192,4096]{2,1,0:T(8,128)(2,1)} %k_ref.15, bf16[1,192,4096]{2,1,0:T(8,128)(2,1)} %v_ref.15, f32[4,192,8]{2,1,0:T(8,128)} %get-tuple-element.41.col_ref), custom_call_target="tpu_custom_call" | custom-call | flops 100663296 | bytes 4284416 | tf_op jit(solution)/shard_map/states_own/pallas_call | solution.py:284
  14.0 5.0 %all-to-all-start = ((f32[16,136,128]{2,1,0:T(8,128)}), f32[16,136,128]{2,1,0:T(8,128)S(1)}, u32[]{:S(2)}, u32[]{:S(2)}) async-start(f32[16,136,128]{2,1,0:T(8,128)} %chip_total.1), calls=%async_computation | async-start | bytes 2228224 | tf_op jit(solution)/shard_map/all_to_all | solution.py:349
  19.1 4.2 %forward_inside.2 = (bf16[16,192,192]{2,1,0:T(8,128)(2,1)}, f32[192,2048]{1,0:T(8,128)}) custom-call(s32[1]{0:T(128)} %bitcast.c_ref, bf16[1,192,4096]{2,1,0:T(8,128)(2,1)} %q_ref.13, bf16[1,192,4096]{2,1,0:T(8,128)(2,1)} %k_ref.15, bf16[1,192,4096]{2,1,0:T(8,128)(2,1)} %v_ref.15, f32[4,192,8]{2,1,0:T(8,128)} %get-tuple-element.41.col_ref, ...), custom_call_target="tpu_custom_call" | custom-call | flops 301989888 | bytes 7520256 | tf_op jit(solution)/shard_map/forward_inside/pallas_call | solution.py:284
  23.3 4.2 %forward_inside.3 = (bf16[16,192,192]{2,1,0:T(8,128)(2,1)}, f32[192,2048]{1,0:T(8,128)}) custom-call(s32[1]{0:T(128)} %bitcast.c_ref, bf16[1,192,4096]{2,1,0:T(8,128)(2,1)} %q_ref.13, bf16[1,192,4096]{2,1,0:T(8,128)(2,1)} %k_ref.15, bf16[1,192,4096]{2,1,0:T(8,128)(2,1)} %v_ref.15, f32[4,192,8]{2,1,0:T(8,128)} %get-tuple-element.41.col_ref, ...), custom_call_target="tpu_custom_call" | custom-call | flops 301989888 | bytes 7520256 | tf_op jit(solution)/shard_map/forward_inside/pallas_call | solution.py:284
  27.5 9.3 %all-to-all-done.m_ref.l_ref = f32[16,136,128]{2,1,0:T(8,128)S(1)} async-done(((f32[16,136,128]{2,1,0:T(8,128)}), f32[16,136,128]{2,1,0:T(8,128)S(1)}, u32[]{:S(2)}, u32[]{:S(2)}) %all-to-all-start) | async-done | bytes 1114144 | tf_op jit(solution)/shard_map/all_to_all | solution.py:349
  36.9 8.8 %collective-permute-start.1 = (f32[128,128]{1,0:T(8,128)S(1)}, f32[128,128]{1,0:T(8,128)S(1)}, u32[]{:S(2)}, u32[]{:S(2)}) collective-permute-start(f32[128,128]{1,0:T(8,128)S(1)} %half_total.2), channel_id=1, source_target_pairs={{0,32},{1,33},{2,34},{3,35},{4,36},{5,37},{6,38},{7,39},{8,40},{9,... | collective-permute-start | bytes 196616 | tf_op jit(solution)/shard_map/ppermute | solution.py:366
  48.1 17.9 %all_to_all.26.d_ref = f32[16,128,128]{2,1,0:T(8,128)S(1)} all-to-all(f32[16,128,128]{2,1,0:T(8,128)} %chip_scan.2), channel_id=1, replica_groups=mesh['dp'=4,'zh'=2,'x'=4,'y'=4,'core'=2] {'x','y'}, dimensions={0} | all-to-all | bytes 2097152 | tf_op jit(solution)/shard_map/all_to_all | solution.py:349
  68.1 3.7 %collective-permute-start.2 = (f32[16,128,128]{2,1,0:T(8,128)}, f32[16,128,128]{2,1,0:T(8,128)S(1)}, u32[]{:S(2)}, u32[]{:S(2)}) collective-permute-start(f32[16,128,128]{2,1,0:T(8,128)} %onward.1), channel_id=1, source_target_pairs={{0,1},{1,0},{2,3},{3,2},{4,5},{5,4},{6,7},{7,6},{8,9},{9,8},{10,11... | collective-permute-start | bytes 3145736 | tf_op jit(solution)/shard_map/ppermute | solution.py:345
  71.9 3.4 %attend_own.1 = (f32[192,2048]{1,0:T(8,128)}, f32[16,128,128]{2,1,0:T(8,128)}, f32[192,128]{1,0:T(8,128)}, f32[192,128]{1,0:T(8,128)}) custom-call(s32[1]{0:T(128)} %bitcast.c_ref, bf16[1,192,4096]{2,1,0:T(8,128)(2,1)} %q_ref.13, bf16[1,192,4096]{2,1,0:T(8,128)(2,1)} %g_ref.5, f32[1,4096]{1,0:T(1,128)} %bitcast.7, f32[4,192,8]{2,1,0:T(8,128)} %get-tuple-element.41.col_ref, ...), custom_call_target="tpu_custom_call" | custom-call | flops 201326592 | bytes 7577600 | tf_op jit(solution)/shard_map/attend_own/pallas_call | solution.py:284
  75.3 5.9 %attend_other.1 = (bf16[192,2048]{1,0:T(8,128)(2,1)}, f32[16,128,128]{2,1,0:T(8,128)}, f32[1,2048]{1,0:T(1,128)}, f32[192,128]{1,0:T(8,128)}, f32[192,128]{1,0:T(8,128)}) custom-call(s32[1]{0:T(128)} %bitcast.c_ref, bf16[1,192,4096]{2,1,0:T(8,128)(2,1)} %q_ref.13, bf16[1,192,4096]{2,1,0:T(8,128)(2,1)} %g_ref.5, f32[1,4096]{1,0:T(1,128)} %bitcast.8, ...), custom_call_target="tpu_custom_call" | custom-call | flops 301989888 | bytes 6995968 | tf_op jit(solution)/shard_map/attend_other/pallas_call | solution.py:284
  81.3 3.9 %delta_own.1 = (bf16[192,2048]{1,0:T(8,128)(2,1)}, f32[16,128,128]{2,1,0:T(8,128)}, f32[1,2048]{1,0:T(1,128)}) custom-call(s32[1]{0:T(128)} %bitcast.c_ref, bf16[1,192,4096]{2,1,0:T(8,128)(2,1)} %q_ref.13, bf16[1,192,4096]{2,1,0:T(8,128)(2,1)} %g_ref.5, f32[1,4096]{1,0:T(1,128)} %bitcast.9, f32[4,192,8]{2,1,0:T(8,128)} %get-tuple-element.41.col_ref, ...), custom_call_target="tpu_custom_call" | custom-call | flops 100663296 | bytes 6799360 | tf_op jit(solution)/shard_map/delta_own/pallas_call | solution.py:284
  88.4 3.7 %all-to-all-start.2 = ((f32[16,128,128]{2,1,0:T(8,128)}), f32[16,128,128]{2,1,0:T(8,128)S(1)}, u32[]{:S(2)}, u32[]{:S(2)}) async-start(f32[16,128,128]{2,1,0:T(8,128)} %chip_moment.1), calls=%async_computation.2 | async-start | bytes 2097152 | tf_op jit(solution)/shard_map/all_to_all | solution.py:349
  92.1 8.5 %backward_inside.2 = (bf16[1,192,4096]{2,1,0:T(8,128)(2,1)}, f32[192,2048]{1,0:T(8,128)}, f32[192,2048]{1,0:T(8,128)}) custom-call(s32[1]{0:T(128)} %bitcast.c_ref, bf16[192,2048]{1,0:T(8,128)(2,1)} %get-tuple-element.56.od_ref, bf16[1,192,4096]{2,1,0:T(8,128)(2,1)} %q_ref.13, bf16[1,192,4096]{2,1,0:T(8,128)(2,1)} %k_ref.15, bf16[1,192,4096]{2,1,0:T(8,128)(2,1)} %v_ref.15, ...), custom_call_target="tpu_custom_call" | custom-call | flops 805306368 | bytes 12500992 | tf_op jit(solution)/shard_map/backward_inside/pallas_call | solution.py:284
  100.6 7.5 %all-to-all-done.2.m_ref = f32[16,128,128]{2,1,0:T(8,128)S(1)} async-done(((f32[16,128,128]{2,1,0:T(8,128)}), f32[16,128,128]{2,1,0:T(8,128)S(1)}, u32[]{:S(2)}, u32[]{:S(2)}) %all-to-all-start.2) | async-done | bytes 1048608 | tf_op jit(solution)/shard_map/all_to_all | solution.py:349
  110.3 12.7 %all-to-all-start.4 = ((f32[256,1,16]{2,1,0:T(1,128)}), f32[256,1,16]{2,1,0:T(1,128)S(1)}, u32[]{:S(2)}, u32[]{:S(2)}) async-start(f32[256,1,16]{2,1,0:T(1,128)} %bitcast.6), calls=%async_computation.4 | async-start | bytes 262144 | tf_op jit(solution)/shard_map/all_to_all | solution.py:473
  124.1 12.1 %all-to-all-done.4 = f32[256,1,16]{2,1,0:T(1,128)S(1)} async-done(((f32[256,1,16]{2,1,0:T(1,128)}), f32[256,1,16]{2,1,0:T(1,128)S(1)}, u32[]{:S(2)}, u32[]{:S(2)}) %all-to-all-start.4) | async-done | bytes 16416 | tf_op jit(solution)/shard_map/all_to_all | solution.py:473
  136.2 3.7 %all-to-all-start.3 = ((f32[16,128,128]{2,1,0:T(8,128)}), f32[16,128,128]{2,1,0:T(8,128)S(1)}, u32[]{:S(2)}, u32[]{:S(2)}) async-start(f32[16,128,128]{2,1,0:T(8,128)} %chip_scan.3), calls=%async_computation.3 | async-start | bytes 2097152 | tf_op jit(solution)/shard_map/all_to_all | solution.py:349
  139.8 8.3 %backward_inside.3 = (bf16[1,192,4096]{2,1,0:T(8,128)(2,1)}, f32[192,2048]{1,0:T(8,128)}, f32[192,2048]{1,0:T(8,128)}) custom-call(s32[1]{0:T(128)} %bitcast.c_ref, bf16[192,2048]{1,0:T(8,128)(2,1)} %get-tuple-element.51.od_ref, bf16[1,192,4096]{2,1,0:T(8,128)(2,1)} %q_ref.13, bf16[1,192,4096]{2,1,0:T(8,128)(2,1)} %k_ref.15, ...), custom_call_target="tpu_custom_call", output_to_operand_aliasing={{0}: (9, {})} | custom-call | flops 805306368 | bytes 13025280 | tf_op jit(solution)/shard_map/backward_inside/pallas_call | solution.py:284
  148.9 6.8 %all-to-all-done.3.d_ref = f32[16,128,128]{2,1,0:T(8,128)S(1)} async-done(((f32[16,128,128]{2,1,0:T(8,128)}), f32[16,128,128]{2,1,0:T(8,128)S(1)}, u32[]{:S(2)}, u32[]{:S(2)}) %all-to-all-start.3) | async-done | bytes 1048608 | tf_op jit(solution)/shard_map/all_to_all | solution.py:349
  157.9 2.8 %collective-permute-start.5 = (f32[16,128,128]{2,1,0:T(8,128)}, f32[16,128,128]{2,1,0:T(8,128)S(1)}, u32[]{:S(2)}, u32[]{:S(2)}) collective-permute-start(f32[16,128,128]{2,1,0:T(8,128)} %onward_back.1), channel_id=1, source_target_pairs={{0,1},{1,0},{2,3},{3,2},{4,5},{5,4},{6,7},{7,6},{8,9},{9,8},{10,11... | collective-permute-start | bytes 3145736 | tf_op jit(solution)/shard_map/ppermute | solution.py:345
  160.7 4.0 %finish_own.1 = (bf16[1,192,4096]{2,1,0:T(8,128)(2,1)}, bf16[1,192,4096]{2,1,0:T(8,128)(2,1)}) custom-call(s32[1]{0:T(128)} %bitcast.c_ref, bf16[1,192,4096]{2,1,0:T(8,128)(2,1)} %k_ref.15, bf16[1,192,4096]{2,1,0:T(8,128)(2,1)} %v_ref.15, f32[4,192,8]{2,1,0:T(8,128)} %get-tuple-element.41.col_ref, f32[192,2048]{1,0:T(8,128)} %get-tuple-element.71.ki_ref, ...), custom_call_target="tpu_custom_call" | custom-call | flops 402653184 | bytes 9461760 | tf_op jit(solution)/shard_map/finish_own/pallas_call | solution.py:284
  164.6 4.0 %finish_other.1 = (bf16[1,192,4096]{2,1,0:T(8,128)(2,1)}, bf16[1,192,4096]{2,1,0:T(8,128)(2,1)}) custom-call(s32[1]{0:T(128)} %bitcast.c_ref, bf16[1,192,4096]{2,1,0:T(8,128)(2,1)} %k_ref.15, bf16[1,192,4096]{2,1,0:T(8,128)(2,1)} %v_ref.15, f32[4,192,8]{2,1,0:T(8,128)} %get-tuple-element.41.col_ref, ...), custom_call_target="tpu_custom_call", output_to_operand_aliasing={{0}: (7, {}), {1}: (8, {})} | custom-call | flops 402653184 | bytes 12607488 | tf_op jit(solution)/shard_map/finish_other/pallas_call | solution.py:284
  (32 shorter events, 16.2 us)
Async XLA Ops:
  4.9 7.0 %collective-permute-start = (f32[16,136,128]{2,1,0:T(8,128)}, f32[16,136,128]{2,1,0:T(8,128)S(1)}, u32[]{:S(2)}, u32[]{:S(2)}) collective-permute-start(f32[16,136,128]{2,1,0:T(8,128)} %get-tuple-element.42), channel_id=1, source_target_pairs={{0,1},{1,0},{2,3},{3,2},{4,5},{5,4},{6,7},{7,6},{8,9},{9,8},{10,11... | collective-permute-start | bytes 3342344 | tf_op jit(solution)/shard_map/ppermute | solution.py:345
  14.0 22.8 %all-to-all-start = ((f32[16,136,128]{2,1,0:T(8,128)}), f32[16,136,128]{2,1,0:T(8,128)S(1)}, u32[]{:S(2)}, u32[]{:S(2)}) async-start(f32[16,136,128]{2,1,0:T(8,128)} %chip_total.1), calls=%async_computation | async-start | bytes 2228224 | tf_op jit(solution)/shard_map/all_to_all | solution.py:349
  36.9 10.1 %collective-permute-start.1 = (f32[128,128]{1,0:T(8,128)S(1)}, f32[128,128]{1,0:T(8,128)S(1)}, u32[]{:S(2)}, u32[]{:S(2)}) collective-permute-start(f32[128,128]{1,0:T(8,128)S(1)} %half_total.2), channel_id=1, source_target_pairs={{0,32},{1,33},{2,34},{3,35},{4,36},{5,37},{6,38},{7,39},{8,40},{9,... | collective-permute-start | bytes 196616 | tf_op jit(solution)/shard_map/ppermute | solution.py:366
  68.1 7.2 %collective-permute-start.2 = (f32[16,128,128]{2,1,0:T(8,128)}, f32[16,128,128]{2,1,0:T(8,128)S(1)}, u32[]{:S(2)}, u32[]{:S(2)}) collective-permute-start(f32[16,128,128]{2,1,0:T(8,128)} %onward.1), channel_id=1, source_target_pairs={{0,1},{1,0},{2,3},{3,2},{4,5},{5,4},{6,7},{7,6},{8,9},{9,8},{10,11... | collective-permute-start | bytes 3145736 | tf_op jit(solution)/shard_map/ppermute | solution.py:345
  75.3 5.9 %copy-start = (f32[16,128,128]{2,1,0:T(8,128)}, f32[16,128,128]{2,1,0:T(8,128)S(1)}, u32[]{:S(2)}) copy-start(f32[16,128,128]{2,1,0:T(8,128)S(1)} %collective-permute-done.2.i_ref) | copy-start | bytes 3145732
  81.2 4.1 %collective-permute-start.3 = (f32[16,128,128]{2,1,0:T(8,128)}, f32[16,128,128]{2,1,0:T(8,128)S(1)}, u32[]{:S(2)}, u32[]{:S(2)}) collective-permute-start(f32[16,128,128]{2,1,0:T(8,128)} %get-tuple-element.62), channel_id=1, source_target_pairs={{0,1},{1,0},{2,3},{3,2},{4,5},{5,4},{6,7},{7,6},{8,9},{9,8},{10,11... | collective-permute-start | bytes 3145736 | tf_op jit(solution)/shard_map/ppermute | solution.py:345
  87.4 1.0 copy-start.2
  88.4 19.7 %all-to-all-start.2 = ((f32[16,128,128]{2,1,0:T(8,128)}), f32[16,128,128]{2,1,0:T(8,128)S(1)}, u32[]{:S(2)}, u32[]{:S(2)}) async-start(f32[16,128,128]{2,1,0:T(8,128)} %chip_moment.1), calls=%async_computation.2 | async-start | bytes 2097152 | tf_op jit(solution)/shard_map/all_to_all | solution.py:349
  100.5 8.9 %copy-start.4 = (f32[1,2048]{1,0:T(1,128)S(1)}, f32[1,2048]{1,0:T(1,128)}, u32[]{:S(2)}) copy-start(f32[1,2048]{1,0:T(1,128)} %get-tuple-element.67) | copy-start | bytes 24580
  100.5 9.0 %copy-start.5 = (f32[1,2048]{1,0:T(1,128)S(1)}, f32[1,2048]{1,0:T(1,128)}, u32[]{:S(2)}) copy-start(f32[1,2048]{1,0:T(1,128)} %get-tuple-element.66) | copy-start | bytes 24580
  108.2 14.8 %collective-permute-start.4 = (f32[128,128]{1,0:T(8,128)S(1)}, f32[128,128]{1,0:T(8,128)S(1)}, u32[]{:S(2)}, u32[]{:S(2)}) collective-permute-start(f32[128,128]{1,0:T(8,128)S(1)} %half_total.3), channel_id=1, source_target_pairs={{32,0},{33,1},{34,2},{35,3},{36,4},{37,5},{38,6},{39,7},{40,8},{41... | collective-permute-start | bytes 196616 | tf_op jit(solution)/shard_map/ppermute | solution.py:366
  110.3 25.8 %all-to-all-start.4 = ((f32[256,1,16]{2,1,0:T(1,128)}), f32[256,1,16]{2,1,0:T(1,128)S(1)}, u32[]{:S(2)}, u32[]{:S(2)}) async-start(f32[256,1,16]{2,1,0:T(1,128)} %bitcast.6), calls=%async_computation.4 | async-start | bytes 262144 | tf_op jit(solution)/shard_map/all_to_all | solution.py:473
  124.1 15.7 %copy-start.1 = (f32[16,128,128]{2,1,0:T(8,128)S(1)}, f32[16,128,128]{2,1,0:T(8,128)}, u32[]{:S(2)}) copy-start(f32[16,128,128]{2,1,0:T(8,128)} %copy-done) | copy-start | bytes 3145732
  136.2 19.6 %all-to-all-start.3 = ((f32[16,128,128]{2,1,0:T(8,128)}), f32[16,128,128]{2,1,0:T(8,128)S(1)}, u32[]{:S(2)}, u32[]{:S(2)}) async-start(f32[16,128,128]{2,1,0:T(8,128)} %chip_scan.3), calls=%async_computation.3 | async-start | bytes 2097152 | tf_op jit(solution)/shard_map/all_to_all | solution.py:349
  155.7 4.9 %copy-start.3 = (f32[16,128,128]{2,1,0:T(8,128)S(1)}, f32[16,128,128]{2,1,0:T(8,128)}, u32[]{:S(2)}) copy-start(f32[16,128,128]{2,1,0:T(8,128)} %copy-done.2) | copy-start | bytes 3145732
  157.9 6.7 %collective-permute-start.5 = (f32[16,128,128]{2,1,0:T(8,128)}, f32[16,128,128]{2,1,0:T(8,128)S(1)}, u32[]{:S(2)}, u32[]{:S(2)}) collective-permute-start(f32[16,128,128]{2,1,0:T(8,128)} %onward_back.1), channel_id=1, source_target_pairs={{0,1},{1,0},{2,3},{3,2},{4,5},{5,4},{6,7},{7,6},{8,9},{9,8},{10,11... | collective-permute-start | bytes 3145736 | tf_op jit(solution)/shard_map/ppermute | solution.py:345

commit v2 on v1

--- a/solution.py
+++ b/solution.py
@@ -84,7 +84,7 @@
     states_of(k_ref, v_ref, col_ref[c_ref[0] * HALF + pl.program_id(0)], s_ref)
 
 
-def combine_kernel(upward, c_ref, own_ref, got_ref, lo_ref, lg_ref, p_ref):
+def combine_kernel(upward, c_ref, own_ref, got_ref, lo_ref, lg_ref, p_ref, kept_ref=None):
     first = c_ref[0] == 0 if upward else c_ref[0] == 1
     for j in range(GH):
         log_own, log_got = lo_ref[j, 0:1, :], lg_ref[j, 0:1, :]
@@ -93,23 +93,52 @@
         p_ref[j, :HD, :] = scale_own * own_ref[j] + scale_got * got_ref[j]
         if upward:
             p_ref[j, HD:, :] = jnp.broadcast_to(log_own + log_got, (8, HD))
-
-
-def total_kernel(upward, m_ref, l_ref, t_ref):
+        else:
+            kept_ref[j] = got_ref[j]
+
+
+def total_kernel(upward, c_ref, m_ref, l_ref, *rest):
     run = jnp.zeros((HD, HD), F32)
     for i in range(NC) if upward else reversed(range(NC)):
         run = jnp.exp(l_ref[i, 0:1, :]) * run + m_ref[i]
-    t_ref[...] = run
-
-
-def scan_kernel(upward, m_ref, l_ref, t_ref, o_ref):
-    run = t_ref[...]
+    t_ref = rest[-1]
+    t_ref[:HD, :] = run
+    if not upward:
+        t_ref[HD:, :] = rest[0][...]
+
+
+def scan_kernel(upward, c_ref, m_ref, l_ref, t_ref, *rest):
+    o_ref = rest[-1]
+    run = t_ref[:HD, :]
+    if not upward:
+        run = jnp.where(c_ref[2] == 0, run, 0.0)
+        both = rest[0][...] + t_ref[HD:, :]
     for i in range(NC) if upward else reversed(range(NC)):
-        o_ref[i] = run
+        o_ref[i, :HD, :] = run
         run = jnp.exp(l_ref[i, 0:1, :]) * run + m_ref[i]
-
-
-def send_kernel(upward, c_ref, d_ref, own_ref, lo_ref, o_ref):
+        if not upward:
+            x = i // 4
+            row = jnp.where(c_ref[2] == 0, both[x : x + 1, :], both[4 + x : 5 + x, :])
+            o_ref[i, HD:, :] = jnp.broadcast_to(row, (8, HD))
+
+
+def send_kernel(upward, c_ref, d_ref, own_ref, lo_ref, *rest):
+    if upward:
+        (o_ref,) = rest
+    else:
+        gains_ref, o_ref, sum_ref = rest
+        part = gains_ref[0]
+        for j in range(1, GH):
+            part += gains_ref[j]
+
+        @pl.when(pl.program_id(0) == 0)
+        def _():
+            sum_ref[...] = part
+
+        @pl.when(pl.program_id(0) > 0)
+        def _():
+            sum_ref[...] += part
+
     step_on = c_ref[0] == 0 if upward else c_ref[0] == 1
     for j in range(GH):
         scale = jnp.where(step_on, jnp.exp(lo_ref[j, 0:1, :]), 1.0)
@@ -173,7 +202,7 @@
         normed = att_ref[:, lanes(j)] * inverse
         delta = (inverse * (gain_ref[:, lanes(j)] * grad - normed * mean)).astype(BF16)
         od_ref[:, lanes(j)] = delta
-        gt_ref[:, lanes(j)] = jnp.sum(grad * normed, axis=0, keepdims=True)
+        gt_ref[j : j + 1, :] = jnp.sum(grad * normed, axis=0, keepdims=True)
         early = (q_ref[:, lanes(j)].astype(F32) * growth[:, j : j + 1]).astype(BF16)
         m_ref[j] = dot(early, delta, 0, 0)
 
@@ -214,12 +243,13 @@
 
 
 def delta_own_kernel(
-    c_ref, q_ref, g_ref, gain_ref, col_ref, att_ref, inv_ref, mean_ref, od_ref, m_ref, gt_ref
+    c_ref, q_ref, g_ref, gain_ref, col_ref, att_ref, inv_ref, mean_ref, gt_in, od_ref, m_ref, gt_ref, kept_ref
 ):
     cum = col_ref[c_ref[0] * HALF + pl.program_id(0)]
     delta_group(
         q_ref, g_ref, gain_ref, cum, att_ref, inv_ref[...], mean_ref[...], od_ref, m_ref, gt_ref
     )
+    kept_ref[...] = m_ref[...]
 
 
 def backward_kernel(
@@ -277,10 +307,8 @@
 
 
 def call(kernel, name, grid, in_specs, out_specs, out_shape, args, flops, scratch=(), aliases=None):
-    nbytes = sum(math.prod(s.shape) * s.dtype.itemsize for s in out_shape)
-    nbytes += sum(math.prod(a.shape) * a.dtype.itemsize for a in args[1:] if not isinstance(a, Free))
-    args = [args[0]] + [a.array if isinstance(a, Free) else in_hbm(a) for a in args[1:]]
-    out_shape = [pltpu.HBM(s.shape, s.dtype) for s in out_shape]
+    bare = [a.array if isinstance(a, Free) else a for a in [*args[1:], *out_shape]]
+    nbytes = sum(math.prod(a.shape) * a.dtype.itemsize for a in bare)
     return pl.pallas_call(
         kernel,
         name=name,
@@ -291,11 +319,11 @@
             out_specs=out_specs,
             scratch_shapes=scratch,
         ),
-        out_shape=out_shape,
+        out_shape=[s.array if isinstance(s, Free) else pltpu.HBM(s.shape, s.dtype) for s in out_shape],
         input_output_aliases=aliases or {},
         compiler_params=pltpu.CompilerParams(vmem_limit_bytes=16 << 20),
         cost_estimate=pl.CostEstimate(flops=flops, bytes_accessed=nbytes, transcendentals=0),
-    )(*args)
+    )(args[0], *[a.array if isinstance(a, Free) else in_hbm(a) for a in args[1:]])
 
 
 def shape(dims, dtype=F32):
@@ -320,6 +348,13 @@
 
 def row_block(own):
     return pl.BlockSpec((GH, T), lambda i, c: (half_of(own, c) * HALF + i, 0))
+
+
+def gains_block(own, group=lambda i: i):
+    return pl.BlockSpec(
+        (None, GH, HD),
+        lambda i, c: (jnp.bitwise_xor(half_of(own, c) * HALF + group(i), c[1]), 0, 0),
+    )
 
 
 def state_block(rows=HD, group=lambda i: i):
@@ -336,7 +371,7 @@
 HALF_BF16 = shape((T, HALF * GW), BF16)
 WHOLE_BF16 = shape((1, T, NG * GW), BF16)
 STAT = shape((T, HD))
-GAIN_ROW = shape((1, HALF * GW))
+GAINS = shape((NG, GH, HD))
 MM = 2 * T * HD * HD * NC
 SM = 2 * T * T * HD * NC
 
@@ -349,34 +384,29 @@
     return lax.all_to_all(values, ("x", "y"), split_axis=0, concat_axis=0, tiled=True)
 
 
-def scan_over_chips(upward, got, logs):
-    whole_m = pl.BlockSpec((NC, HD, HD), lambda i: (0, 0, 0))
-    whole_l = pl.BlockSpec((NC, 8, HD), lambda i: (0, HD // 8, 0))
-    whole_t = pl.BlockSpec((HD, HD), lambda i: (0, 0))
-    params = pltpu.CompilerParams(vmem_limit_bytes=16 << 20)
-    total = pl.pallas_call(
-        functools.partial(total_kernel, upward),
-        name="half_total",
-        grid=(1,),
-        in_specs=[whole_m, whole_l],
-        out_specs=whole_t,
-        out_shape=shape((HD, HD)),
-        compiler_params=params,
-    )(got, logs)
-    before = lax.ppermute(total, "zh", [(0, 1)] if upward else [(1, 0)])
-    return pl.pallas_call(
-        functools.partial(scan_kernel, upward),
-        name="chip_scan",
-        grid=(1,),
-        in_specs=[whole_m, whole_l, whole_t],
-        out_specs=whole_m,
-        out_shape=pltpu.HBM(STATES.shape, F32),
-        compiler_params=params,
-    )(got, logs, before)
+def scan_over_chips(upward, place, got, logs, gains=None):
+    whole_m = pl.BlockSpec((NC, HD, HD), lambda i, c: (0, 0, 0))
+    whole_l = pl.BlockSpec((NC, 8, HD), lambda i, c: (0, HD // 8, 0))
+    rows = HD if upward else HD + 8
+    whole_t = pl.BlockSpec((rows, HD), lambda i, c: (0, 0))
+    more = [] if upward else [Free(gains)]
+    more_specs = [pl.BlockSpec((8, HD), lambda i, c: (0, 0))] * len(more)
+    (total,) = call(
+        functools.partial(total_kernel, upward), "half_total", (1,),
+        [whole_m, whole_l] + more_specs, [whole_t], [Free(shape((rows, HD)))],
+        (place, Free(got), Free(logs), *more), 0,
+    )
+    before = lax.ppermute(total, "zh", [(0, 1)] if upward else [(0, 1), (1, 0)])
+    return call(
+        functools.partial(scan_kernel, upward), "chip_scan", (1,),
+        [whole_m, whole_l, whole_t] + more_specs,
+        [pl.BlockSpec((NC, rows, HD), lambda i, c: (0, 0, 0))], [shape((NC, rows, HD))],
+        (place, Free(got), Free(logs), Free(before), *more), 0,
+    )[0]
 
 
 def per_device(queries, key_rows, value_rows, out_grad, log_decay, norm_gain):
-    core = lax.axis_index("core").astype(jnp.int32).reshape(1)
+    core = jnp.stack([lax.axis_index(a).astype(jnp.int32) for a in ("core", "dp", "zh")])
     q, k, v, g = queries, key_rows, value_rows, out_grad
     gain = norm_gain.reshape(1, NG * GW)
     logs = jnp.transpose(log_decay[0])
@@ -385,19 +415,19 @@
         state_first_kernel, "states_other", (HALF,),
         [wide(False), wide(False), pl.BlockSpec((NG * GH, T), lambda i, c: (0, 0))],
         [state_block(HD + 8), COL_WHOLE, pl.BlockSpec((NG * GH, T), lambda i, c: (0, 0))],
-        [LOGGED, shape((NG, T, GH)), shape((NG * GH, T))],
+        [Free(LOGGED), shape((NG, T, GH)), shape((NG * GH, T))],
         (core, k, v, logs), MM,
     )
     got = swap_cores(sent)
     (own,) = call(
         state_second_kernel, "states_own", (HALF,),
-        [wide(True), wide(True), COL_WHOLE], [state_block(HD + 8)], [LOGGED],
+        [wide(True), wide(True), COL_WHOLE], [state_block(HD + 8)], [Free(LOGGED)],
         (core, k, v, col), MM,
     )
     (chip_total,) = call(
         functools.partial(combine_kernel, True), "chip_total", (HALF,),
         [state_block(), state_block(), LOG_BLOCK, LOG_BLOCK], [state_block(HD + 8)], [LOGGED],
-        (core, own, Free(got), own, Free(got)), 0,
+        (core, Free(own), Free(got), Free(own), Free(got)), 0,
     )
     gathered = chips_all_to_all(chip_total)
 
@@ -414,11 +444,11 @@
     gathered, inside[True], inside[False] = lax.optimization_barrier(
         (gathered, inside[True], inside[False])
     )
-    scanned = chips_all_to_all(scan_over_chips(True, gathered, gathered))
+    scanned = chips_all_to_all(scan_over_chips(True, core, gathered, gathered))
     (onward,) = call(
         functools.partial(send_kernel, True), "onward", (HALF,),
-        [state_block(), state_block(), LOG_BLOCK], [state_block()], [STATES],
-        (core, Free(scanned), own, own), 0,
+        [state_block(), state_block(), LOG_BLOCK], [state_block()], [Free(STATES)],
+        (core, Free(scanned), Free(own), Free(own)), 0,
     )
     state_other = swap_cores(onward)
     att_own, state_own, squares, products = call(
@@ -426,7 +456,7 @@
         [wide(True), wide(True), gain_block(True), COL_WHOLE, narrow(), state_block(), state_block(),
          LOG_BLOCK],
         [narrow(), state_block(), STAT_WHOLE, STAT_WHOLE],
-        [HALF_F32, STATES, STAT, STAT],
+        [Free(HALF_F32), STATES, Free(STAT), Free(STAT)],
         (core, q, g, gain, col, inside[True], Free(scanned), Free(got), Free(got)), 2 * MM,
     )
 
@@ -439,41 +469,34 @@
     def second(i):
         return jnp.minimum(2 * HALF - 1 - i, HALF - 1)
 
-    delta_other, moment_sent, gain_other, inverse, mean = call(
+    delta_other, moment_sent, gains, inverse, mean = call(
         attend_other_kernel, "attend_other", (2 * HALF,),
         [wide(False, turn), wide(False, turn), gain_block(False, turn), COL_WHOLE, narrow(first),
          state_block(HD, first), STAT_WHOLE, STAT_WHOLE],
-        [narrow(second), state_block(HD, second), pl.BlockSpec((1, GW), lambda i, c: (0, second(i))),
-         STAT_WHOLE, STAT_WHOLE],
-        [HALF_BF16, STATES, GAIN_ROW, STAT, STAT],
-        (core, q, g, gain, col, inside[False], Free(state_other), squares, products), 3 * MM,
+        [narrow(second), state_block(HD, second), gains_block(False, second), STAT_WHOLE, STAT_WHOLE],
+        [HALF_BF16, Free(STATES), GAINS, Free(STAT), Free(STAT)],
+        (core, q, g, gain, col, inside[False], Free(state_other), Free(squares), Free(products)), 3 * MM,
         scratch=[pltpu.VMEM((HALF, T, GW), F32), pltpu.VMEM((T, HD), F32), pltpu.VMEM((T, HD), F32)],
     )
     moment_got = swap_cores(moment_sent)
-    delta_own, moment_own, gain_own = call(
+    delta_own, moment_own, gains, moment_own_kept = call(
         delta_own_kernel, "delta_own", (HALF,),
-        [wide(True), wide(True), gain_block(True), COL_WHOLE, narrow(), STAT_WHOLE, STAT_WHOLE],
-        [narrow(), state_block(), pl.BlockSpec((1, GW), lambda i, c: (0, i))],
-        [HALF_BF16, STATES, GAIN_ROW],
-        (core, q, g, gain, col, att_own, inverse, mean), MM,
-    )
-    (chip_moment,) = call(
+        [wide(True), wide(True), gain_block(True), COL_WHOLE, narrow(), STAT_WHOLE, STAT_WHOLE, ANY],
+        [narrow(), state_block(), gains_block(True), state_block()],
+        [HALF_BF16, Free(STATES), GAINS, STATES],
+        (core, q, g, gain, col, Free(att_own), Free(inverse), Free(mean), gains), MM,
+        aliases={8: 2},
+    )
+    chip_moment, moment_got_kept = call(
         functools.partial(combine_kernel, False), "chip_moment", (HALF,),
-        [state_block(), state_block(), LOG_BLOCK, LOG_BLOCK], [state_block()], [STATES],
-        (core, moment_own, Free(moment_got), own, Free(got)), 0,
+        [state_block(), state_block(), LOG_BLOCK, LOG_BLOCK], [state_block()] * 2, [STATES] * 2,
+        (core, Free(moment_own), Free(moment_got), Free(own), Free(got)), 0,
     )
     gathered_back = chips_all_to_all(chip_moment)
 
-    gain_halves = jnp.where(
-        core[0] == 0,
-        jnp.concatenate([gain_own, gain_other], 1),
-        jnp.concatenate([gain_other, gain_own], 1),
-    )
-    members = lax.axis_size(ALL)
-    gain_parts = lax.all_to_all(
-        gain_halves.reshape(members, -1), ALL, split_axis=0, concat_axis=0, tiled=True
-    )
-    gain_grad = jnp.sum(gain_parts, axis=0) * (1.0 / math.sqrt(T * members))
+    collected = gains[0]
+    for distance in range(1, NG):
+        collected += lax.ppermute(gains[distance], "dp", [(i, i ^ distance) for i in range(NG)])
 
     delta = {True: delta_own, False: delta_other}
     state = {True: state_own, False: Free(state_other)}
@@ -492,21 +515,21 @@
         )
 
     gathered_back, key_inside[True] = lax.optimization_barrier((gathered_back, key_inside[True]))
-    scanned_back = chips_all_to_all(scan_over_chips(False, gathered_back, gathered))
-    scanned_back, key_inside[False], gain_grad = lax.optimization_barrier(
-        (scanned_back, key_inside[False], gain_grad)
-    )
-    (onward_back,) = call(
+    scanned_back = chips_all_to_all(scan_over_chips(False, core, gathered_back, gathered, collected))
+    scanned_back, key_inside[False] = lax.optimization_barrier((scanned_back, key_inside[False]))
+    onward_back, collected = call(
         functools.partial(send_kernel, False), "onward_back", (HALF,),
-        [state_block(), state_block(), LOG_BLOCK], [state_block()], [STATES],
-        (core, Free(scanned_back), moment_own, own), 0,
+        [state_block(), state_block(), LOG_BLOCK, LOG_BLOCK],
+        [state_block(), pl.BlockSpec((8, HD), lambda i, c: (0, 0))],
+        [Free(STATES), Free(shape((8, HD)))],
+        (core, Free(scanned_back), moment_own_kept, Free(own), Free(scanned_back)), 0,
     )
     later_other = swap_cores(onward_back)
     key_grad, value_grad = call(
         finish_own_kernel, "finish_own", (HALF,),
         [wide(True), wide(True), COL_WHOLE, narrow(), narrow(), state_block(), state_block(), LOG_BLOCK],
         [wide(True), wide(True)], [WHOLE_BF16, WHOLE_BF16],
-        (core, k, v, col, key_inside[True], value_inside[True], Free(scanned_back), Free(moment_got), Free(got)), 4 * MM,
+        (core, k, v, col, key_inside[True], value_inside[True], Free(scanned_back), moment_got_kept, Free(got)), 4 * MM,
     )
     key_grad, value_grad = call(
         finish_other_kernel, "finish_other", (HALF,),
@@ -515,6 +538,10 @@
         (core, k, v, col, key_inside[False], value_inside[False], Free(later_other), key_grad, value_grad),
         4 * MM, aliases={7: 0, 8: 1},
     )
+    collected = (collected + swap_cores(collected))[0]
+    at = lax.axis_index("y") * 32 + lax.axis_index("core") * 16
+    positions = T * lax.axis_size(ALL)
+    gain_grad = lax.dynamic_slice_in_dim(collected, at, 16) * (1.0 / math.sqrt(positions))
     return query_grad[0], key_grad, value_grad, gain_grad
 
 

time: 169 us -> 157 us (0.929)
  waiting for transfers between devices: 37 us -> 19.5 us
  Pallas kernels: 65.2 us -> 73 us
  starting transfers between devices: 45 us -> 42.9 us
    all_to_all x1 -> x0, starting transfers between devices: 12.7 us -> none  [per_device(): lax.all_to_all(gain_halves.reshape(members, -1), ALL, split_axis=0, conca...]
    all_to_all x1 -> x0, waiting for transfers between devices: 12.1 us -> none  [per_device(): lax.all_to_all(gain_halves.reshape(members, -1), ALL, split_axis=0, conca...]
    pallas_call x15 -> x19, Pallas kernels: 62.9 us -> 73 us  [call(): pl.pallas_call(kernel, name=name, grid_spec=pltpu.PrefetchScalarGridSpec(...]
    ppermute x2 -> x5, starting transfers between devices: 10.1 us -> 18.3 us  [the longest x2 14.6 us: scan_over_chips(): before = lax.ppermute(total, 'zh', [(0, 1)] if upward else [(0, 1), (1, 0)])]
    all_to_all x3, waiting for transfers between devices: 23.7 us -> 16.4 us  [chips_all_to_all(): lax.all_to_all(values, ('x', 'y'), split_axis=0, concat_axis=0, tiled=True)]
    pallas_call x4 -> x0, Pallas kernels: 2.3 us -> none  [the longest x2 2.12 us: scan_over_chips(): pl.pallas_call(functools.partial(scan_kernel, upward), name='chip_scan',...]
    ppermute x2 -> x5, waiting for transfers between devices: 1.31 us -> 3.02 us  [the longest x2 3.01 us: scan_over_chips(): before = lax.ppermute(total, 'zh', [(0, 1)] if upward else [(0, 1), (1, 0)])]
    ppermute x4 -> x5, starting transfers between devices: 9.86 us -> 10.7 us  [swap_cores(): return lax.ppermute(values, 'core', [(0, 1), (1, 0)])]
  transfers between devices with their start and end apart: 10 -> 13, of which waited for: 5 -> 5; matrix products, arithmetic and copies ran while one was open for 1% -> 0% of each run, Pallas kernels for 25% -> 28%
where the time goes in v2:
time: 157 us; the launch traced here: 156 us
  Pallas kernels  73 us (46%)
  starting transfers between devices  42.9 us (27%)
  waiting for transfers between devices  19.5 us (12%)
  blocking collectives  18.1 us (12%)
    pallas_call x19, Pallas kernels, call(): pl.pallas_call(kernel, name=name, grid_spec=pltpu.PrefetchScalarGridSpec(...  73 us
    all_to_all x1, blocking collectives, chips_all_to_all(): lax.all_to_all(values, ('x', 'y'), split_axis=0, concat_axis=0, tiled=True)  18.1 us
    all_to_all x3, waiting for transfers between devices, chips_all_to_all(): lax.all_to_all(values, ('x', 'y'), split_axis=0, concat_axis=0, tiled=True)  16.4 us
    ppermute x2, starting transfers between devices, scan_over_chips(): before = lax.ppermute(total, 'zh', [(0, 1)] if upward else [(0, 1), (1, 0)])  14.6 us
    all_to_all x3, starting transfers between devices, chips_all_to_all(): lax.all_to_all(values, ('x', 'y'), split_axis=0, concat_axis=0, tiled=True)  13.9 us
    ppermute x5, starting transfers between devices, swap_cores(): return lax.ppermute(values, 'core', [(0, 1), (1, 0)])  10.7 us
    ppermute x3, starting transfers between devices, per_device(): lax.ppermute(gains[distance], 'dp', [(i, i ^ distance) for i in range(NG)])  3.63 us
  transfers between devices with their start and end apart: 13, of which 5 were waited for; matrix products, arithmetic and copies ran while one was open for 0% of the time, Pallas kernels for 28%

profile of v2, /device:TPU:1, one launch (start us, length us, event | category | flops | bytes accessed | tf_op | source)
XLA Modules:
  0.0 156.1 jit_solution(12812674688705526837)
XLA Ops:
  0.7 4.4 %states_other.1 = (f32[16,136,128]{2,1,0:T(8,128)S(1)}, f32[4,192,8]{2,1,0:T(8,128)}, f32[32,192]{1,0:T(8,128)}) custom-call(s32[3]{0:T(128)S(1)} %pad_add_fusion.c_ref, bf16[1,192,4096]{2,1,0:T(8,128)(2,1)} %k_ref.15, bf16[1,192,4096]{2,1,0:T(8,128)(2,1)} %v_ref.15, f32[32,192]{1,0:T(8,128)} %bitcast.24), custom_call_target="tpu_custom_call" | custom-call | flops 100663296 | bytes 4333568 | tf_op jit(solution)/shard_map/states_other/pallas_call | solution.py:312
  5.1 3.2 %collective-permute-start = (f32[16,136,128]{2,1,0:T(8,128)S(1)}, f32[16,136,128]{2,1,0:T(8,128)S(1)}, u32[]{:S(2)}, u32[]{:S(2)}) collective-permute-start(f32[16,136,128]{2,1,0:T(8,128)S(1)} %get-tuple-element.46), channel_id=1, source_target_pairs={{0,1},{1,0},{2,3},{3,2},{4,5},{5,4},{6,7},{7,6},{8,9},{9,8},{10,11... | collective-permute-start | bytes 3342344 | tf_op jit(solution)/shard_map/ppermute | solution.py:380
  8.3 3.5 %states_own.1.own_ref.lo_ref = f32[16,136,128]{2,1,0:T(8,128)S(1)} custom-call(s32[3]{0:T(128)S(1)} %pad_add_fusion.c_ref, bf16[1,192,4096]{2,1,0:T(8,128)(2,1)} %k_ref.15, bf16[1,192,4096]{2,1,0:T(8,128)(2,1)} %v_ref.15, f32[4,192,8]{2,1,0:T(8,128)} %get-tuple-element.45.col_ref), custom_call_target="tpu_custom_call" | custom-call | flops 100663296 | bytes 4284416 | tf_op jit(solution)/shard_map/states_own/pallas_call | solution.py:312
  13.7 5.0 %all-to-all-start = ((f32[16,136,128]{2,1,0:T(8,128)}), f32[16,136,128]{2,1,0:T(8,128)S(1)}, u32[]{:S(2)}, u32[]{:S(2)}) async-start(f32[16,136,128]{2,1,0:T(8,128)} %chip_total.1), calls=%async_computation | async-start | bytes 2228224 | tf_op jit(solution)/shard_map/all_to_all | solution.py:384
  18.8 4.8 %forward_inside.2 = (bf16[16,192,192]{2,1,0:T(8,128)(2,1)}, f32[192,2048]{1,0:T(8,128)}) custom-call(s32[3]{0:T(128)S(1)} %pad_add_fusion.c_ref, bf16[1,192,4096]{2,1,0:T(8,128)(2,1)} %q_ref.13, bf16[1,192,4096]{2,1,0:T(8,128)(2,1)} %k_ref.15, bf16[1,192,4096]{2,1,0:T(8,128)(2,1)} %v_ref.15, f32[4,192,8]{2,1,0:T(8,128)} %get-tuple-element.45.col_ref, ...), custom_call_target="tpu_custom_call" | custom-call | flops 301989888 | bytes 7520256 | tf_op jit(solution)/shard_map/forward_inside/pallas_call | solution.py:312
  23.6 4.8 %forward_inside.3 = (bf16[16,192,192]{2,1,0:T(8,128)(2,1)}, f32[192,2048]{1,0:T(8,128)}) custom-call(s32[3]{0:T(128)S(1)} %pad_add_fusion.c_ref, bf16[1,192,4096]{2,1,0:T(8,128)(2,1)} %q_ref.13, bf16[1,192,4096]{2,1,0:T(8,128)(2,1)} %k_ref.15, bf16[1,192,4096]{2,1,0:T(8,128)(2,1)} %v_ref.15, f32[4,192,8]{2,1,0:T(8,128)} %get-tuple-element.45.col_ref, ...), custom_call_target="tpu_custom_call" | custom-call | flops 301989888 | bytes 7520256 | tf_op jit(solution)/shard_map/forward_inside/pallas_call | solution.py:312
  28.4 8.2 %all-to-all-done.m_ref.l_ref = f32[16,136,128]{2,1,0:T(8,128)S(1)} async-done(((f32[16,136,128]{2,1,0:T(8,128)}), f32[16,136,128]{2,1,0:T(8,128)S(1)}, u32[]{:S(2)}, u32[]{:S(2)}) %all-to-all-start) | async-done | bytes 1114144 | tf_op jit(solution)/shard_map/all_to_all | solution.py:384
  37.2 8.8 %collective-permute-start.1 = (f32[128,128]{1,0:T(8,128)S(1)}, f32[128,128]{1,0:T(8,128)S(1)}, u32[]{:S(2)}, u32[]{:S(2)}) collective-permute-start(f32[128,128]{1,0:T(8,128)S(1)} %half_total.2), channel_id=1, source_target_pairs={{0,32},{1,33},{2,34},{3,35},{4,36},{5,37},{6,38},{7,39},{8,40},{9,... | collective-permute-start | bytes 196616 | tf_op jit(solution)/shard_map/ppermute | solution.py:399
  49.0 18.1 %all_to_all.20.d_ref = f32[16,128,128]{2,1,0:T(8,128)S(1)} all-to-all(f32[16,128,128]{2,1,0:T(8,128)} %chip_scan.2), channel_id=1, replica_groups=mesh['dp'=4,'zh'=2,'x'=4,'y'=4,'core'=2] {'x','y'}, dimensions={0} | all-to-all | bytes 2097152 | tf_op jit(solution)/shard_map/all_to_all | solution.py:384
  67.9 3.7 %collective-permute-start.2 = (f32[16,128,128]{2,1,0:T(8,128)S(1)}, f32[16,128,128]{2,1,0:T(8,128)S(1)}, u32[]{:S(2)}, u32[]{:S(2)}) collective-permute-start(f32[16,128,128]{2,1,0:T(8,128)S(1)} %onward.1), channel_id=1, source_target_pairs={{0,1},{1,0},{2,3},{3,2},{4,5},{5,4},{6,7},{7,6},{8,9},{9,8},{10,11... | collective-permute-start | bytes 3145736 | tf_op jit(solution)/shard_map/ppermute | solution.py:380
  71.6 4.0 %attend_own.1 = (f32[192,2048]{1,0:T(8,128)S(1)}, f32[16,128,128]{2,1,0:T(8,128)}, f32[192,128]{1,0:T(8,128)S(1)}, f32[192,128]{1,0:T(8,128)S(1)}) custom-call(s32[3]{0:T(128)S(1)} %pad_add_fusion.c_ref, bf16[1,192,4096]{2,1,0:T(8,128)(2,1)} %q_ref.13, bf16[1,192,4096]{2,1,0:T(8,128)(2,1)} %g_ref.5, f32[1,4096]{1,0:T(1,128)} %bitcast.21, ...), custom_call_target="tpu_custom_call" | custom-call | flops 201326592 | bytes 10854400 | tf_op jit(solution)/shard_map/attend_own/pallas_call | solution.py:312
  75.6 5.9 %attend_other.1 = (bf16[192,2048]{1,0:T(8,128)(2,1)}, f32[16,128,128]{2,1,0:T(8,128)S(1)}, f32[4,8,128]{2,1,0:T(8,128)}, f32[192,128]{1,0:T(8,128)S(1)}, f32[192,128]{1,0:T(8,128)S(1)}) custom-call(s32[3]{0:T(128)S(1)} %pad_add_fusion.c_ref, bf16[1,192,4096]{2,1,0:T(8,128)(2,1)} %q_ref.13, bf16[1,192,4096]{2,1,0:T(8,128)(2,1)} %g_ref.5, f32[1,4096]{1,0:T(1,128)} %bitcast.22, ...), custom_call_target="tpu_custom_call" | custom-call | flops 301989888 | bytes 8052736 | tf_op jit(solution)/shard_map/attend_other/pallas_call | solution.py:312
  81.5 4.1 %delta_own.1 = (bf16[192,2048]{1,0:T(8,128)(2,1)}, f32[16,128,128]{2,1,0:T(8,128)S(1)}, f32[4,8,128]{2,1,0:T(8,128)}, f32[16,128,128]{2,1,0:T(8,128)}) custom-call(s32[3]{0:T(128)S(1)} %pad_add_fusion.c_ref, bf16[1,192,4096]{2,1,0:T(8,128)(2,1)} %q_ref.13, bf16[1,192,4096]{2,1,0:T(8,128)(2,1)} %g_ref.5, ...), custom_call_target="tpu_custom_call", output_to_operand_aliasing={{2}: (8, {})} | custom-call | flops 100663296 | bytes 7872512 | tf_op jit(solution)/shard_map/delta_own/pallas_call | solution.py:312
  87.6 4.5 %all-to-all-start.2 = ((f32[16,128,128]{2,1,0:T(8,128)}), f32[16,128,128]{2,1,0:T(8,128)}, u32[]{:S(2)}, u32[]{:S(2)}) async-start(f32[16,128,128]{2,1,0:T(8,128)} %get-tuple-element.68), calls=%async_computation.2 | async-start | bytes 2097152 | tf_op jit(solution)/shard_map/all_to_all | solution.py:384
  95.7 9.0 %backward_inside.2 = (bf16[1,192,4096]{2,1,0:T(8,128)(2,1)}, f32[192,2048]{1,0:T(8,128)}, f32[192,2048]{1,0:T(8,128)}) custom-call(s32[3]{0:T(128)S(1)} %pad_add_fusion.c_ref, bf16[192,2048]{1,0:T(8,128)(2,1)} %get-tuple-element.61.od_ref, bf16[1,192,4096]{2,1,0:T(8,128)(2,1)} %q_ref.13, bf16[1,192,4096]{2,1,0:T(8,128)(2,1)} %k_ref.15, ...), custom_call_target="tpu_custom_call" | custom-call | flops 805306368 | bytes 12500992 | tf_op jit(solution)/shard_map/backward_inside/pallas_call | solution.py:312
  104.8 3.2 %all-to-all-done.2.m_ref = f32[16,128,128]{2,1,0:T(8,128)} async-done(((f32[16,128,128]{2,1,0:T(8,128)}), f32[16,128,128]{2,1,0:T(8,128)}, u32[]{:S(2)}, u32[]{:S(2)}) %all-to-all-start.2) | async-done | bytes 1048608 | tf_op jit(solution)/shard_map/all_to_all | solution.py:384
  109.9 5.8 %collective-permute-start.7 = (f32[136,128]{1,0:T(8,128)S(1)}, f32[136,128]{1,0:T(8,128)S(1)}, u32[]{:S(2)}, u32[]{:S(2)}) collective-permute-start(f32[136,128]{1,0:T(8,128)S(1)} %half_total.3), channel_id=1, source_target_pairs={{0,32},{32,0},{1,33},{33,1},{2,34},{34,2},{3,35},{35,3},{4,36},{36... | collective-permute-start | bytes 208904 | tf_op jit(solution)/shard_map/ppermute | solution.py:399
  117.4 2.8 %chip_scan.3 = f32[16,136,128]{2,1,0:T(8,128)} custom-call(s32[3]{0:T(128)S(1)} %pad_add_fusion.c_ref, f32[16,128,128]{2,1,0:T(8,128)} %all-to-all-done.2.m_ref, f32[16,136,128]{2,1,0:T(8,128)S(1)} %all-to-all-done.m_ref.l_ref, f32[136,128]{1,0:T(8,128)S(1)} %collective-permute-done.7.t_ref, f32[8,128]{1,0:T(8,128)S(1)} %fusion.1.rest_0_), custom_call_target="tpu_custom_call" | custom-call | bytes 3350528 | tf_op jit(solution)/shard_map/chip_scan/pallas_call | solution.py:312
  120.2 4.4 %all-to-all-start.3 = ((f32[16,136,128]{2,1,0:T(8,128)}), f32[16,136,128]{2,1,0:T(8,128)S(1)}, u32[]{:S(2)}, u32[]{:S(2)}) async-start(f32[16,136,128]{2,1,0:T(8,128)} %chip_scan.3), calls=%async_computation.3 | async-start | bytes 2228224 | tf_op jit(solution)/shard_map/all_to_all | solution.py:384
  125.9 8.9 %backward_inside.3 = (bf16[1,192,4096]{2,1,0:T(8,128)(2,1)}, f32[192,2048]{1,0:T(8,128)}, f32[192,2048]{1,0:T(8,128)}) custom-call(s32[3]{0:T(128)S(1)} %pad_add_fusion.c_ref, bf16[192,2048]{1,0:T(8,128)(2,1)} %get-tuple-element.55.od_ref, bf16[1,192,4096]{2,1,0:T(8,128)(2,1)} %q_ref.13, ...), custom_call_target="tpu_custom_call", output_to_operand_aliasing={{0}: (9, {})} | custom-call | flops 805306368 | bytes 14073856 | tf_op jit(solution)/shard_map/backward_inside/pallas_call | solution.py:312
  134.8 5.0 %all-to-all-done.3.d_ref.rest_0_ = f32[16,136,128]{2,1,0:T(8,128)S(1)} async-done(((f32[16,136,128]{2,1,0:T(8,128)}), f32[16,136,128]{2,1,0:T(8,128)S(1)}, u32[]{:S(2)}, u32[]{:S(2)}) %all-to-all-start.3) | async-done | bytes 1114144 | tf_op jit(solution)/shard_map/all_to_all | solution.py:384
  142.4 3.7 %collective-permute-start.8 = (f32[16,128,128]{2,1,0:T(8,128)}, f32[16,128,128]{2,1,0:T(8,128)S(1)}, u32[]{:S(2)}, u32[]{:S(2)}) collective-permute-start(f32[16,128,128]{2,1,0:T(8,128)} %get-tuple-element.77), channel_id=1, source_target_pairs={{0,1},{1,0},{2,3},{3,2},{4,5},{5,4},{6,7},{7,6},{8,9},{9,8},{10,11... | collective-permute-start | bytes 3145736 | tf_op jit(solution)/shard_map/ppermute | solution.py:380
  146.1 4.8 %finish_own.1 = (bf16[1,192,4096]{2,1,0:T(8,128)(2,1)}, bf16[1,192,4096]{2,1,0:T(8,128)(2,1)}) custom-call(s32[3]{0:T(128)S(1)} %pad_add_fusion.c_ref, bf16[1,192,4096]{2,1,0:T(8,128)(2,1)} %k_ref.15, bf16[1,192,4096]{2,1,0:T(8,128)(2,1)} %v_ref.15, f32[4,192,8]{2,1,0:T(8,128)} %get-tuple-element.45.col_ref, f32[192,2048]{1,0:T(8,128)} %get-tuple-element.78.ki_ref, ...), custom_call_target="tpu_custom_call" | custom-call | flops 402653184 | bytes 12738560 | tf_op jit(solution)/shard_map/finish_own/pallas_call | solution.py:312
  151.6 4.5 %finish_other.1 = (bf16[1,192,4096]{2,1,0:T(8,128)(2,1)}, bf16[1,192,4096]{2,1,0:T(8,128)(2,1)}) custom-call(s32[3]{0:T(128)S(1)} %pad_add_fusion.c_ref, bf16[1,192,4096]{2,1,0:T(8,128)(2,1)} %k_ref.15, bf16[1,192,4096]{2,1,0:T(8,128)(2,1)} %v_ref.15, f32[4,192,8]{2,1,0:T(8,128)} %get-tuple-element.45.col_ref, ...), custom_call_target="tpu_custom_call", output_to_operand_aliasing={{0}: (7, {}), {1}: (8, {})} | custom-call | flops 402653184 | bytes 13656064 | tf_op jit(solution)/shard_map/finish_other/pallas_call | solution.py:312
  (34 shorter events, 20.2 us)
Async XLA Ops:
  5.1 6.8 %collective-permute-start = (f32[16,136,128]{2,1,0:T(8,128)S(1)}, f32[16,136,128]{2,1,0:T(8,128)S(1)}, u32[]{:S(2)}, u32[]{:S(2)}) collective-permute-start(f32[16,136,128]{2,1,0:T(8,128)S(1)} %get-tuple-element.46), channel_id=1, source_target_pairs={{0,1},{1,0},{2,3},{3,2},{4,5},{5,4},{6,7},{7,6},{8,9},{9,8},{10,11... | collective-permute-start | bytes 3342344 | tf_op jit(solution)/shard_map/ppermute | solution.py:380
  13.7 22.8 %all-to-all-start = ((f32[16,136,128]{2,1,0:T(8,128)}), f32[16,136,128]{2,1,0:T(8,128)S(1)}, u32[]{:S(2)}, u32[]{:S(2)}) async-start(f32[16,136,128]{2,1,0:T(8,128)} %chip_total.1), calls=%async_computation | async-start | bytes 2228224 | tf_op jit(solution)/shard_map/all_to_all | solution.py:384
  37.2 10.1 %collective-permute-start.1 = (f32[128,128]{1,0:T(8,128)S(1)}, f32[128,128]{1,0:T(8,128)S(1)}, u32[]{:S(2)}, u32[]{:S(2)}) collective-permute-start(f32[128,128]{1,0:T(8,128)S(1)} %half_total.2), channel_id=1, source_target_pairs={{0,32},{1,33},{2,34},{3,35},{4,36},{5,37},{6,38},{7,39},{8,40},{9,... | collective-permute-start | bytes 196616 | tf_op jit(solution)/shard_map/ppermute | solution.py:399
  67.9 7.7 %collective-permute-start.2 = (f32[16,128,128]{2,1,0:T(8,128)S(1)}, f32[16,128,128]{2,1,0:T(8,128)S(1)}, u32[]{:S(2)}, u32[]{:S(2)}) collective-permute-start(f32[16,128,128]{2,1,0:T(8,128)S(1)} %onward.1), channel_id=1, source_target_pairs={{0,1},{1,0},{2,3},{3,2},{4,5},{5,4},{6,7},{7,6},{8,9},{9,8},{10,11... | collective-permute-start | bytes 3145736 | tf_op jit(solution)/shard_map/ppermute | solution.py:380
  75.6 5.9 %copy-start = (f32[16,128,128]{2,1,0:T(8,128)}, f32[16,128,128]{2,1,0:T(8,128)S(1)}, u32[]{:S(2)}) copy-start(f32[16,128,128]{2,1,0:T(8,128)S(1)} %collective-permute-done.2.i_ref) | copy-start | bytes 3145732
  81.4 4.2 %collective-permute-start.3 = (f32[16,128,128]{2,1,0:T(8,128)S(1)}, f32[16,128,128]{2,1,0:T(8,128)S(1)}, u32[]{:S(2)}, u32[]{:S(2)}) collective-permute-start(f32[16,128,128]{2,1,0:T(8,128)S(1)} %get-tuple-element.67), channel_id=1, source_target_pairs={{0,1},{1,0},{2,3},{3,2},{4,5},{5,4},{6,7},{7,6},{8,9},{9,8},{10,11... | collective-permute-start | bytes 3145736 | tf_op jit(solution)/shard_map/ppermute | solution.py:380
  87.6 4.5 %copy-start.2 = (f32[4,8,128]{2,1,0:T(8,128)S(1)}, f32[4,8,128]{2,1,0:T(8,128)}, u32[]{:S(2)}) copy-start(f32[4,8,128]{2,1,0:T(8,128)} %get-tuple-element.71) | copy-start | bytes 49156
  87.6 20.4 %all-to-all-start.2 = ((f32[16,128,128]{2,1,0:T(8,128)}), f32[16,128,128]{2,1,0:T(8,128)}, u32[]{:S(2)}, u32[]{:S(2)}) async-start(f32[16,128,128]{2,1,0:T(8,128)} %get-tuple-element.68), calls=%async_computation.2 | async-start | bytes 2097152 | tf_op jit(solution)/shard_map/all_to_all | solution.py:384
  92.1 12.7 %collective-permute-start.4 = (f32[8,128]{1,0:T(8,128)S(1)}, f32[8,128]{1,0:T(8,128)S(1)}, u32[]{:S(2)}, u32[]{:S(2)}) collective-permute-start(f32[8,128]{1,0:T(8,128)S(1)} %get-tuple-element.86), channel_id=1, source_target_pairs={{0,64},{64,0},{128,192},{192,128},{1,65},{65,1},{129,193},{193,129... | collective-permute-start | bytes 12296 | tf_op jit(solution)/shard_map/ppermute | solution.py:499
  92.9 11.8 %collective-permute-start.5 = (f32[8,128]{1,0:T(8,128)S(1)}, f32[8,128]{1,0:T(8,128)S(1)}, u32[]{:S(2)}, u32[]{:S(2)}) collective-permute-start(f32[8,128]{1,0:T(8,128)S(1)} %get-tuple-element.88), channel_id=1, source_target_pairs={{0,128},{64,192},{128,0},{192,64},{1,129},{65,193},{129,1},{193,65... | collective-permute-start | bytes 12296 | tf_op jit(solution)/shard_map/ppermute | solution.py:499
  94.1 10.7 %collective-permute-start.6 = (f32[8,128]{1,0:T(8,128)S(1)}, f32[8,128]{1,0:T(8,128)S(1)}, u32[]{:S(2)}, u32[]{:S(2)}) collective-permute-start(f32[8,128]{1,0:T(8,128)S(1)} %get-tuple-element.87), channel_id=1, source_target_pairs={{0,192},{64,128},{128,64},{192,0},{1,193},{65,129},{129,65},{193,1... | collective-permute-start | bytes 12296 | tf_op jit(solution)/shard_map/ppermute | solution.py:499
  109.9 7.5 %collective-permute-start.7 = (f32[136,128]{1,0:T(8,128)S(1)}, f32[136,128]{1,0:T(8,128)S(1)}, u32[]{:S(2)}, u32[]{:S(2)}) collective-permute-start(f32[136,128]{1,0:T(8,128)S(1)} %half_total.3), channel_id=1, source_target_pairs={{0,32},{32,0},{1,33},{33,1},{2,34},{34,2},{3,35},{35,3},{4,36},{36... | collective-permute-start | bytes 208904 | tf_op jit(solution)/shard_map/ppermute | solution.py:399
  120.2 19.5 %all-to-all-start.3 = ((f32[16,136,128]{2,1,0:T(8,128)}), f32[16,136,128]{2,1,0:T(8,128)S(1)}, u32[]{:S(2)}, u32[]{:S(2)}) async-start(f32[16,136,128]{2,1,0:T(8,128)} %chip_scan.3), calls=%async_computation.3 | async-start | bytes 2228224 | tf_op jit(solution)/shard_map/all_to_all | solution.py:384
  124.7 1.2 copy-start.1
  142.4 9.1 %collective-permute-start.8 = (f32[16,128,128]{2,1,0:T(8,128)}, f32[16,128,128]{2,1,0:T(8,128)S(1)}, u32[]{:S(2)}, u32[]{:S(2)}) collective-permute-start(f32[16,128,128]{2,1,0:T(8,128)} %get-tuple-element.77), channel_id=1, source_target_pairs={{0,1},{1,0},{2,3},{3,2},{4,5},{5,4},{6,7},{7,6},{8,9},{9,8},{10,11... | collective-permute-start | bytes 3145736 | tf_op jit(solution)/shard_map/ppermute | solution.py:380
  146.1 4.8 %collective-permute-start.9 = (f32[8,128]{1,0:T(8,128)S(1)}, f32[8,128]{1,0:T(8,128)S(1)}, u32[]{:S(2)}, u32[]{:S(2)}) collective-permute-start(f32[8,128]{1,0:T(8,128)S(1)} %get-tuple-element.85), channel_id=1, source_target_pairs={{0,1},{1,0},{2,3},{3,2},{4,5},{5,4},{6,7},{7,6},{8,9},{9,8},{10,11... | collective-permute-start | bytes 12296 | tf_op jit(solution)/shard_map/ppermute | solution.py:380

commit v3 on v2

--- a/solution.py
+++ b/solution.py
@@ -50,13 +50,12 @@
     return jnp.exp(jnp.where(row_ids >= col_ids, col - row, -jnp.inf))
 
 
-def states_of(k_ref, v_ref, cum, s_ref):
+def states_of(k_ref, v_ref, cum, store):
     last = cum[T - 1 : T, :]
     shrink = jnp.exp(last - cum)
     for j in range(GH):
         late = (k_ref[:, lanes(j)].astype(F32) * shrink[:, j : j + 1]).astype(BF16)
-        s_ref[j, :HD, :] = dot(late, v_ref[:, lanes(j)], 0, 0)
-        s_ref[j, HD:, :] = jnp.broadcast_to(last[:, j : j + 1], (8, HD))
+        store(j, dot(late, v_ref[:, lanes(j)], 0, 0), jnp.broadcast_to(last[:, j : j + 1], (8, HD)))
 
 
 def state_first_kernel(c_ref, k_ref, v_ref, ld_ref, s_ref, col_ref, row_ref):
@@ -77,24 +76,33 @@
         for g in range(NG):
             col_ref[g] = col[:, g * GH : (g + 1) * GH]
 
-    states_of(k_ref, v_ref, col_ref[(1 - c_ref[0]) * HALF + i], s_ref)
-
-
-def state_second_kernel(c_ref, k_ref, v_ref, col_ref, s_ref):
-    states_of(k_ref, v_ref, col_ref[c_ref[0] * HALF + pl.program_id(0)], s_ref)
-
-
-def combine_kernel(upward, c_ref, own_ref, got_ref, lo_ref, lg_ref, p_ref, kept_ref=None):
+    def store(j, state, log):
+        s_ref[j, :HD, :] = state
+        s_ref[j, HD:, :] = log
+
+    states_of(k_ref, v_ref, col_ref[(1 - c_ref[0]) * HALF + i], store)
+
+
+def state_second_kernel(c_ref, k_ref, v_ref, col_ref, s_ref, kept_ref, l_ref):
+    def store(j, state, log):
+        s_ref[j] = state
+        kept_ref[j] = state
+        l_ref[j] = log
+
+    states_of(k_ref, v_ref, col_ref[c_ref[0] * HALF + pl.program_id(0)], store)
+
+
+def combine_kernel(upward, c_ref, own_ref, got_ref, lo_ref, lg_ref, p_ref, kept_ref, log_ref=None):
     first = c_ref[0] == 0 if upward else c_ref[0] == 1
     for j in range(GH):
         log_own, log_got = lo_ref[j, 0:1, :], lg_ref[j, 0:1, :]
         scale_own = jnp.where(first, jnp.exp(log_got), 1.0)
         scale_got = jnp.where(first, 1.0, jnp.exp(log_own))
         p_ref[j, :HD, :] = scale_own * own_ref[j] + scale_got * got_ref[j]
+        kept_ref[j] = got_ref[j]
         if upward:
-            p_ref[j, HD:, :] = jnp.broadcast_to(log_own + log_got, (8, HD))
-        else:
-            kept_ref[j] = got_ref[j]
+            p_ref[j, HD:, :] = lo_ref[j] + lg_ref[j]
+            log_ref[j] = lg_ref[j]
 
 
 def total_kernel(upward, c_ref, m_ref, l_ref, *rest):
@@ -108,11 +116,14 @@
 
 
 def scan_kernel(upward, c_ref, m_ref, l_ref, t_ref, *rest):
-    o_ref = rest[-1]
+    if upward:
+        o_ref, log_ref = rest
+        log_ref[...] = l_ref[...]
+    else:
+        gain_ref, o_ref = rest
+        both = gain_ref[...] + t_ref[HD:, :]
     run = t_ref[:HD, :]
-    if not upward:
-        run = jnp.where(c_ref[2] == 0, run, 0.0)
-        both = rest[0][...] + t_ref[HD:, :]
+    run = jnp.where(c_ref[2] == (1 if upward else 0), run, 0.0)
     for i in range(NC) if upward else reversed(range(NC)):
         o_ref[i, :HD, :] = run
         run = jnp.exp(l_ref[i, 0:1, :]) * run + m_ref[i]
@@ -122,11 +133,13 @@
             o_ref[i, HD:, :] = jnp.broadcast_to(row, (8, HD))
 
 
-def send_kernel(upward, c_ref, d_ref, own_ref, lo_ref, *rest):
+def hand_on_kernel(
+    upward, c_ref, d_ref, own_ref, got_ref, lo_ref, lg_ref, *rest
+):
     if upward:
-        (o_ref,) = rest
+        send_ref, state_ref = rest
     else:
-        gains_ref, o_ref, sum_ref = rest
+        gains_ref, send_ref, state_ref, sum_ref = rest
         part = gains_ref[0]
         for j in range(1, GH):
             part += gains_ref[j]
@@ -139,18 +152,17 @@
         def _():
             sum_ref[...] += part
 
-    step_on = c_ref[0] == 0 if upward else c_ref[0] == 1
-    for j in range(GH):
-        scale = jnp.where(step_on, jnp.exp(lo_ref[j, 0:1, :]), 1.0)
-        keep = jnp.where(step_on, 1.0, 0.0)
-        o_ref[j] = scale * d_ref[j] + keep * own_ref[j]
-
-
-def own_state(upward, c_ref, d_ref, got_ref, lg_ref, j):
-    at_edge = c_ref[0] == 0 if upward else c_ref[0] == 1
-    scale = jnp.where(at_edge, 1.0, jnp.exp(lg_ref[j, 0:1, :]))
-    keep = jnp.where(at_edge, 0.0, 1.0)
-    return scale * d_ref[j] + keep * got_ref[j]
+    at_edge = c_ref[0] == (0 if upward else 1)
+    for j in range(GH):
+        edge = d_ref[j]
+        send_ref[j] = (
+            jnp.where(at_edge, jnp.exp(lo_ref[j, 0:1, :]), 1.0) * edge
+            + jnp.where(at_edge, 1.0, 0.0) * own_ref[j]
+        )
+        state_ref[j] = (
+            jnp.where(at_edge, 1.0, jnp.exp(lg_ref[j, 0:1, :])) * edge
+            + jnp.where(at_edge, 0.0, 1.0) * got_ref[j]
+        )
 
 
 def forward_kernel(own, c_ref, q_ref, k_ref, v_ref, col_ref, row_ref, fw_ref, in_ref):
@@ -178,8 +190,7 @@
 
 
 def attend_own_kernel(
-    c_ref, q_ref, g_ref, gain_ref, col_ref, in_ref, d_ref, got_ref, lg_ref,
-    att_ref, i_ref, sq_ref, pr_ref,
+    c_ref, q_ref, g_ref, gain_ref, col_ref, in_ref, x_ref, att_ref, i_ref, sq_ref, pr_ref
 ):
     @pl.when(pl.program_id(0) == 0)
     def _():
@@ -187,9 +198,8 @@
         pr_ref[...] = jnp.zeros_like(pr_ref)
 
     def state_at(j):
-        state = own_state(True, c_ref, d_ref, got_ref, lg_ref, j)
-        i_ref[j] = state
-        return state
+        i_ref[j] = x_ref[j]
+        return x_ref[j]
 
     cum = col_ref[c_ref[0] * HALF + pl.program_id(0)]
     attend_group(q_ref, g_ref, gain_ref, cum, in_ref, state_at, att_ref, sq_ref, pr_ref)
@@ -270,31 +280,15 @@
         vi_ref[:, at] = dot(fw_ref[j], delta, 0, 0)
 
 
-def finish_group(k_ref, v_ref, cum, ki_ref, vi_ref, state_at, kg_ref, vg_ref):
+def finish_kernel(own, c_ref, k_ref, v_ref, col_ref, ki_ref, vi_ref, x_ref, *rest):
+    cum = col_ref[half_of(own, c_ref) * HALF + pl.program_id(0)]
     shrink = jnp.exp(cum[T - 1 : T, :] - cum)
+    kg_ref, vg_ref = rest[-2:]
     for j in range(GH):
         at = lanes(j)
-        state = state_at(j)
         scale = shrink[:, j : j + 1]
-        kg_ref[:, at] = (ki_ref[:, at] + scale * rows_by_state_t(v_ref[:, at], state)).astype(BF16)
-        vg_ref[:, at] = (vi_ref[:, at] + scale * rows_by_state(k_ref[:, at], state)).astype(BF16)
-
-
-def finish_own_kernel(
-    c_ref, k_ref, v_ref, col_ref, ki_ref, vi_ref, d_ref, got_ref, lg_ref, kg_ref, vg_ref
-):
-    cum = col_ref[c_ref[0] * HALF + pl.program_id(0)]
-    finish_group(
-        k_ref, v_ref, cum, ki_ref, vi_ref,
-        lambda j: own_state(False, c_ref, d_ref, got_ref, lg_ref, j), kg_ref, vg_ref,
-    )
-
-
-def finish_other_kernel(
-    c_ref, k_ref, v_ref, col_ref, ki_ref, vi_ref, x_ref, kg_in, vg_in, kg_ref, vg_ref
-):
-    cum = col_ref[(1 - c_ref[0]) * HALF + pl.program_id(0)]
-    finish_group(k_ref, v_ref, cum, ki_ref, vi_ref, lambda j: x_ref[j], kg_ref, vg_ref)
+        kg_ref[:, at] = (ki_ref[:, at] + scale * rows_by_state_t(v_ref[:, at], x_ref[j])).astype(BF16)
+        vg_ref[:, at] = (vi_ref[:, at] + scale * rows_by_state(k_ref[:, at], x_ref[j])).astype(BF16)
 
 
 class Free:
@@ -361,12 +355,14 @@
     return pl.BlockSpec((GH, rows, HD), lambda i, c: (group(i), 0, 0))
 
 
-LOG_BLOCK = pl.BlockSpec((GH, 8, HD), lambda i, c: (i, HD // 8, 0))
+LOG_BLOCK = pl.BlockSpec((GH, 8, HD), lambda i, c: (i, 0, 0))
+LOG_TAIL = pl.BlockSpec((GH, 8, HD), lambda i, c: (i, HD // 8, 0))
 COL_WHOLE = pl.BlockSpec((NG, T, GH), lambda i, c: (0, 0, 0))
 STAT_WHOLE = pl.BlockSpec((T, HD), lambda i, c: (0, 0))
 ANY = pl.BlockSpec(memory_space=pl.ANY)
 STATES = shape((NC, HD, HD))
 LOGGED = shape((NC, HD + 8, HD))
+LOGS = shape((NC, 8, HD))
 HALF_F32 = shape((T, HALF * GW))
 HALF_BF16 = shape((T, HALF * GW), BF16)
 WHOLE_BF16 = shape((1, T, NG * GW), BF16)
@@ -386,7 +382,8 @@
 
 def scan_over_chips(upward, place, got, logs, gains=None):
     whole_m = pl.BlockSpec((NC, HD, HD), lambda i, c: (0, 0, 0))
-    whole_l = pl.BlockSpec((NC, 8, HD), lambda i, c: (0, HD // 8, 0))
+    whole_l = pl.BlockSpec((NC, 8, HD), lambda i, c: (0, HD // 8 if upward else 0, 0))
+    logs_out = pl.BlockSpec((NC, 8, HD), lambda i, c: (0, 0, 0))
     rows = HD if upward else HD + 8
     whole_t = pl.BlockSpec((rows, HD), lambda i, c: (0, 0))
     more = [] if upward else [Free(gains)]
@@ -396,13 +393,13 @@
         [whole_m, whole_l] + more_specs, [whole_t], [Free(shape((rows, HD)))],
         (place, Free(got), Free(logs), *more), 0,
     )
-    before = lax.ppermute(total, "zh", [(0, 1)] if upward else [(0, 1), (1, 0)])
+    before = lax.ppermute(total, "zh", [(0, 1), (1, 0)])
+    outs = [pl.BlockSpec((NC, rows, HD), lambda i, c: (0, 0, 0))] + [logs_out] * upward
     return call(
         functools.partial(scan_kernel, upward), "chip_scan", (1,),
-        [whole_m, whole_l, whole_t] + more_specs,
-        [pl.BlockSpec((NC, rows, HD), lambda i, c: (0, 0, 0))], [shape((NC, rows, HD))],
+        [whole_m, whole_l, whole_t] + more_specs, outs, [shape((NC, rows, HD)), LOGS][: len(outs)],
         (place, Free(got), Free(logs), Free(before), *more), 0,
-    )[0]
+    )
 
 
 def per_device(queries, key_rows, value_rows, out_grad, log_decay, norm_gain):
@@ -419,15 +416,17 @@
         (core, k, v, logs), MM,
     )
     got = swap_cores(sent)
-    (own,) = call(
+    own, own_kept, log_own = call(
         state_second_kernel, "states_own", (HALF,),
-        [wide(True), wide(True), COL_WHOLE], [state_block(HD + 8)], [Free(LOGGED)],
+        [wide(True), wide(True), COL_WHOLE],
+        [state_block(), state_block(), LOG_BLOCK], [Free(STATES), STATES, LOGS],
         (core, k, v, col), MM,
     )
-    (chip_total,) = call(
+    chip_total, got_kept, log_got = call(
         functools.partial(combine_kernel, True), "chip_total", (HALF,),
-        [state_block(), state_block(), LOG_BLOCK, LOG_BLOCK], [state_block(HD + 8)], [LOGGED],
-        (core, Free(own), Free(got), Free(own), Free(got)), 0,
+        [state_block(), state_block(), LOG_BLOCK, LOG_TAIL],
+        [state_block(HD + 8), state_block(), LOG_BLOCK], [LOGGED, STATES, LOGS],
+        (core, Free(own), Free(got), Free(log_own), Free(got)), 0,
     )
     gathered = chips_all_to_all(chip_total)
 
@@ -444,20 +443,20 @@
     gathered, inside[True], inside[False] = lax.optimization_barrier(
         (gathered, inside[True], inside[False])
     )
-    scanned = chips_all_to_all(scan_over_chips(True, core, gathered, gathered))
-    (onward,) = call(
-        functools.partial(send_kernel, True), "onward", (HALF,),
-        [state_block(), state_block(), LOG_BLOCK], [state_block()], [Free(STATES)],
-        (core, Free(scanned), Free(own), Free(own)), 0,
+    before_chips, log_chips = scan_over_chips(True, core, gathered, gathered)
+    scanned = chips_all_to_all(before_chips)
+    onward, state_here = call(
+        functools.partial(hand_on_kernel, True), "onward", (HALF,),
+        [state_block()] * 3 + [LOG_BLOCK] * 2, [state_block()] * 2, [Free(STATES)] * 2,
+        (core, Free(scanned), Free(own_kept), Free(got_kept), Free(log_own), Free(log_got)), 0,
     )
     state_other = swap_cores(onward)
     att_own, state_own, squares, products = call(
         attend_own_kernel, "attend_own", (HALF,),
-        [wide(True), wide(True), gain_block(True), COL_WHOLE, narrow(), state_block(), state_block(),
-         LOG_BLOCK],
+        [wide(True), wide(True), gain_block(True), COL_WHOLE, narrow(), state_block()],
         [narrow(), state_block(), STAT_WHOLE, STAT_WHOLE],
         [Free(HALF_F32), STATES, Free(STAT), Free(STAT)],
-        (core, q, g, gain, col, inside[True], Free(scanned), Free(got), Free(got)), 2 * MM,
+        (core, Free(q), Free(g), gain, col, Free(inside[True]), Free(state_here)), 2 * MM,
     )
 
     def turn(i):
@@ -475,7 +474,7 @@
          state_block(HD, first), STAT_WHOLE, STAT_WHOLE],
         [narrow(second), state_block(HD, second), gains_block(False, second), STAT_WHOLE, STAT_WHOLE],
         [HALF_BF16, Free(STATES), GAINS, Free(STAT), Free(STAT)],
-        (core, q, g, gain, col, inside[False], Free(state_other), Free(squares), Free(products)), 3 * MM,
+        (core, Free(q), Free(g), gain, col, Free(inside[False]), Free(state_other), Free(squares), Free(products)), 3 * MM,
         scratch=[pltpu.VMEM((HALF, T, GW), F32), pltpu.VMEM((T, HD), F32), pltpu.VMEM((T, HD), F32)],
     )
     moment_got = swap_cores(moment_sent)
@@ -484,13 +483,13 @@
         [wide(True), wide(True), gain_block(True), COL_WHOLE, narrow(), STAT_WHOLE, STAT_WHOLE, ANY],
         [narrow(), state_block(), gains_block(True), state_block()],
         [HALF_BF16, Free(STATES), GAINS, STATES],
-        (core, q, g, gain, col, Free(att_own), Free(inverse), Free(mean), gains), MM,
+        (core, Free(q), Free(g), gain, col, Free(att_own), Free(inverse), Free(mean), gains), MM,
         aliases={8: 2},
     )
     chip_moment, moment_got_kept = call(
         functools.partial(combine_kernel, False), "chip_moment", (HALF,),
         [state_block(), state_block(), LOG_BLOCK, LOG_BLOCK], [state_block()] * 2, [STATES] * 2,
-        (core, Free(moment_own), Free(moment_got), Free(own), Free(got)), 0,
+        (core, Free(moment_own), Free(moment_got), Free(log_own), Free(log_got)), 0,
     )
     gathered_back = chips_all_to_all(chip_moment)
 
@@ -515,29 +514,29 @@
         )
 
     gathered_back, key_inside[True] = lax.optimization_barrier((gathered_back, key_inside[True]))
-    scanned_back = chips_all_to_all(scan_over_chips(False, core, gathered_back, gathered, collected))
+    (after_chips,) = scan_over_chips(False, core, gathered_back, log_chips, collected)
+    scanned_back = chips_all_to_all(after_chips)
     scanned_back, key_inside[False] = lax.optimization_barrier((scanned_back, key_inside[False]))
-    onward_back, collected = call(
-        functools.partial(send_kernel, False), "onward_back", (HALF,),
-        [state_block(), state_block(), LOG_BLOCK, LOG_BLOCK],
-        [state_block(), pl.BlockSpec((8, HD), lambda i, c: (0, 0))],
-        [Free(STATES), Free(shape((8, HD)))],
-        (core, Free(scanned_back), moment_own_kept, Free(own), Free(scanned_back)), 0,
+    onward_back, later_here, collected = call(
+        functools.partial(hand_on_kernel, False), "onward_back", (HALF,),
+        [state_block()] * 3 + [LOG_BLOCK] * 2 + [LOG_TAIL],
+        [state_block(), state_block(), pl.BlockSpec((8, HD), lambda i, c: (0, 0))],
+        [Free(STATES), Free(STATES), Free(shape((8, HD)))],
+        (core, Free(scanned_back), moment_own_kept, moment_got_kept, Free(log_own),
+         Free(log_got), Free(scanned_back)), 0,
     )
     later_other = swap_cores(onward_back)
-    key_grad, value_grad = call(
-        finish_own_kernel, "finish_own", (HALF,),
-        [wide(True), wide(True), COL_WHOLE, narrow(), narrow(), state_block(), state_block(), LOG_BLOCK],
-        [wide(True), wide(True)], [WHOLE_BF16, WHOLE_BF16],
-        (core, k, v, col, key_inside[True], value_inside[True], Free(scanned_back), moment_got_kept, Free(got)), 4 * MM,
-    )
-    key_grad, value_grad = call(
-        finish_other_kernel, "finish_other", (HALF,),
-        [wide(False), wide(False), COL_WHOLE, narrow(), narrow(), state_block(), ANY, ANY],
-        [wide(False), wide(False)], [WHOLE_BF16, WHOLE_BF16],
-        (core, k, v, col, key_inside[False], value_inside[False], Free(later_other), key_grad, value_grad),
-        4 * MM, aliases={7: 0, 8: 1},
-    )
+    later = {True: later_here, False: later_other}
+    grads = ()
+    for mine in (True, False):
+        grads = call(
+            functools.partial(finish_kernel, mine), "finish", (HALF,),
+            [wide(mine), wide(mine), COL_WHOLE, narrow(), narrow(), state_block()] + [ANY] * len(grads),
+            [wide(mine)] * 2, [WHOLE_BF16] * 2,
+            (core, k, v, col, key_inside[mine], value_inside[mine],
+             Free(later[mine]), *grads), 4 * MM, aliases={7: 0, 8: 1} if grads else None,
+        )
+    key_grad, value_grad = grads
     collected = (collected + swap_cores(collected))[0]
     at = lax.axis_index("y") * 32 + lax.axis_index("core") * 16
     positions = T * lax.axis_size(ALL)

time: 157 us -> 155 us (0.987)
  waiting for transfers between devices: 19.5 us -> 23.5 us
  starting transfers between devices: 42.9 us -> 39.9 us
  Pallas kernels: 73 us -> 70.3 us
    all_to_all x3, waiting for transfers between devices: 16.4 us -> 19.9 us  [chips_all_to_all(): lax.all_to_all(values, ('x', 'y'), split_axis=0, concat_axis=0, tiled=True)]
    pallas_call x19, Pallas kernels: 73 us -> 70.3 us  [call(): pl.pallas_call(kernel, name=name, grid_spec=pltpu.PrefetchScalarGridSpec(...]
    ppermute x2, starting transfers between devices: 14.6 us -> 12.4 us  [scan_over_chips(): before = lax.ppermute(total, 'zh', [(0, 1), (1, 0)])]
where the time goes in v3:
time: 155 us; the launch traced here: 154 us
  Pallas kernels  70.3 us (45%)
  starting transfers between devices  39.9 us (26%)
  waiting for transfers between devices  23.5 us (15%)
  blocking collectives  18.1 us (12%)
    pallas_call x19, Pallas kernels, call(): pl.pallas_call(kernel, name=name, grid_spec=pltpu.PrefetchScalarGridSpec(...  70.3 us
    all_to_all x3, waiting for transfers between devices, chips_all_to_all(): lax.all_to_all(values, ('x', 'y'), split_axis=0, concat_axis=0, tiled=True)  19.9 us
    all_to_all x1, blocking collectives, chips_all_to_all(): lax.all_to_all(values, ('x', 'y'), split_axis=0, concat_axis=0, tiled=True)  18.1 us
    all_to_all x3, starting transfers between devices, chips_all_to_all(): lax.all_to_all(values, ('x', 'y'), split_axis=0, concat_axis=0, tiled=True)  12.5 us
    ppermute x2, starting transfers between devices, scan_over_chips(): before = lax.ppermute(total, 'zh', [(0, 1), (1, 0)])  12.4 us
    ppermute x5, starting transfers between devices, swap_cores(): return lax.ppermute(values, 'core', [(0, 1), (1, 0)])  11.4 us
    ppermute x3, starting transfers between devices, per_device(): lax.ppermute(gains[distance], 'dp', [(i, i ^ distance) for i in range(NG)])  3.63 us
    ppermute x2, waiting for transfers between devices, scan_over_chips(): before = lax.ppermute(total, 'zh', [(0, 1), (1, 0)])  3.56 us
  transfers between devices with their start and end apart: 13, of which 5 were waited for; matrix products, arithmetic and copies ran while one was open for 0% of the time, Pallas kernels for 28%

profile of v3, /device:TPU:1, one launch (start us, length us, event | category | flops | bytes accessed | tf_op | source)
XLA Modules:
  0.0 154.1 jit_solution(13329890677333921257)
XLA Ops:
  0.7 4.4 %states_other.1 = (f32[16,136,128]{2,1,0:T(8,128)S(1)}, f32[4,192,8]{2,1,0:T(8,128)}, f32[32,192]{1,0:T(8,128)}) custom-call(s32[3]{0:T(128)S(1)} %pad_add_fusion.c_ref, bf16[1,192,4096]{2,1,0:T(8,128)(2,1)} %k_ref.15, bf16[1,192,4096]{2,1,0:T(8,128)(2,1)} %v_ref.15, f32[32,192]{1,0:T(8,128)} %bitcast.24), custom_call_target="tpu_custom_call" | custom-call | flops 100663296 | bytes 4333568 | tf_op jit(solution)/shard_map/states_other/pallas_call | solution.py:306
  5.1 3.2 %collective-permute-start = (f32[16,136,128]{2,1,0:T(8,128)S(1)}, f32[16,136,128]{2,1,0:T(8,128)S(1)}, u32[]{:S(2)}, u32[]{:S(2)}) collective-permute-start(f32[16,136,128]{2,1,0:T(8,128)S(1)} %get-tuple-element.58), channel_id=1, source_target_pairs={{0,1},{1,0},{2,3},{3,2},{4,5},{5,4},{6,7},{7,6},{8,9},{9,8},{10,11... | collective-permute-start | bytes 3342344 | tf_op jit(solution)/shard_map/ppermute | solution.py:376
  8.3 4.3 %states_own.1 = (f32[16,128,128]{2,1,0:T(8,128)S(1)}, f32[16,128,128]{2,1,0:T(8,128)}, f32[16,8,128]{2,1,0:T(8,128)}) custom-call(s32[3]{0:T(128)S(1)} %pad_add_fusion.c_ref, bf16[1,192,4096]{2,1,0:T(8,128)(2,1)} %k_ref.15, bf16[1,192,4096]{2,1,0:T(8,128)(2,1)} %v_ref.15, f32[4,192,8]{2,1,0:T(8,128)} %get-tuple-element.56.col_ref), custom_call_target="tpu_custom_call" | custom-call | flops 100663296 | bytes 5332992 | tf_op jit(solution)/shard_map/states_own/pallas_call | solution.py:306
  15.6 5.0 %all-to-all-start = ((f32[16,136,128]{2,1,0:T(8,128)}), f32[16,136,128]{2,1,0:T(8,128)S(1)}, u32[]{:S(2)}, u32[]{:S(2)}) async-start(f32[16,136,128]{2,1,0:T(8,128)} %get-tuple-element.60), calls=%async_computation | async-start | bytes 2228224 | tf_op jit(solution)/shard_map/all_to_all | solution.py:380
  20.6 4.8 %forward_inside.2 = (bf16[16,192,192]{2,1,0:T(8,128)(2,1)}, f32[192,2048]{1,0:T(8,128)}) custom-call(s32[3]{0:T(128)S(1)} %pad_add_fusion.c_ref, bf16[1,192,4096]{2,1,0:T(8,128)(2,1)} %q_ref.13, bf16[1,192,4096]{2,1,0:T(8,128)(2,1)} %k_ref.15, bf16[1,192,4096]{2,1,0:T(8,128)(2,1)} %v_ref.15, f32[4,192,8]{2,1,0:T(8,128)} %get-tuple-element.56.col_ref, ...), custom_call_target="tpu_custom_call" | custom-call | flops 301989888 | bytes 7520256 | tf_op jit(solution)/shard_map/forward_inside/pallas_call | solution.py:306
  25.4 4.8 %forward_inside.3 = (bf16[16,192,192]{2,1,0:T(8,128)(2,1)}, f32[192,2048]{1,0:T(8,128)}) custom-call(s32[3]{0:T(128)S(1)} %pad_add_fusion.c_ref, bf16[1,192,4096]{2,1,0:T(8,128)(2,1)} %q_ref.13, bf16[1,192,4096]{2,1,0:T(8,128)(2,1)} %k_ref.15, bf16[1,192,4096]{2,1,0:T(8,128)(2,1)} %v_ref.15, f32[4,192,8]{2,1,0:T(8,128)} %get-tuple-element.56.col_ref, ...), custom_call_target="tpu_custom_call" | custom-call | flops 301989888 | bytes 7520256 | tf_op jit(solution)/shard_map/forward_inside/pallas_call | solution.py:306
  30.2 8.2 %all-to-all-done.m_ref.l_ref = f32[16,136,128]{2,1,0:T(8,128)S(1)} async-done(((f32[16,136,128]{2,1,0:T(8,128)}), f32[16,136,128]{2,1,0:T(8,128)S(1)}, u32[]{:S(2)}, u32[]{:S(2)}) %all-to-all-start) | async-done | bytes 1114144 | tf_op jit(solution)/shard_map/all_to_all | solution.py:380
  39.0 7.0 %collective-permute-start.1 = (f32[128,128]{1,0:T(8,128)S(1)}, f32[128,128]{1,0:T(8,128)S(1)}, u32[]{:S(2)}, u32[]{:S(2)}) collective-permute-start(f32[128,128]{1,0:T(8,128)S(1)} %half_total.2), channel_id=1, source_target_pairs={{0,32},{32,0},{1,33},{33,1},{2,34},{34,2},{3,35},{35,3},{4,36},{36... | collective-permute-start | bytes 196616 | tf_op jit(solution)/shard_map/ppermute | solution.py:396
  49.4 18.1 %all_to_all.20.d_ref = f32[16,128,128]{2,1,0:T(8,128)S(1)} all-to-all(f32[16,128,128]{2,1,0:T(8,128)} %get-tuple-element.66), channel_id=1, replica_groups=mesh['dp'=4,'zh'=2,'x'=4,'y'=4,'core'=2] {'x','y'}, dimensions={0} | all-to-all | bytes 2097152 | tf_op jit(solution)/shard_map/all_to_all | solution.py:380
  68.3 3.8 %collective-permute-start.2 = (f32[16,128,128]{2,1,0:T(8,128)S(1)}, f32[16,128,128]{2,1,0:T(8,128)S(1)}, u32[]{:S(2)}, u32[]{:S(2)}) collective-permute-start(f32[16,128,128]{2,1,0:T(8,128)S(1)} %get-tuple-element.70), channel_id=1, source_target_pairs={{0,1},{1,0},{2,3},{3,2},{4,5},{5,4},{6,7},{7,6},{8,9},{9,8},{10,11... | collective-permute-start | bytes 3145736 | tf_op jit(solution)/shard_map/ppermute | solution.py:376
  72.2 3.5 %attend_own.1 = (f32[192,2048]{1,0:T(8,128)S(1)}, f32[16,128,128]{2,1,0:T(8,128)}, f32[192,128]{1,0:T(8,128)S(1)}, f32[192,128]{1,0:T(8,128)S(1)}) custom-call(s32[3]{0:T(128)S(1)} %pad_add_fusion.c_ref, bf16[1,192,4096]{2,1,0:T(8,128)(2,1)S(1)} %copy-done, bf16[1,192,4096]{2,1,0:T(8,128)(2,1)S(1)} %copy-done.1, f32[1,4096]{1,0:T(1,128)} %bitcast.21, ...), custom_call_target="tpu_custom_call" | custom-call | flops 201326592 | bytes 8626176 | tf_op jit(solution)/shard_map/attend_own/pallas_call | solution.py:306
  75.7 5.3 %attend_other.1 = (bf16[192,2048]{1,0:T(8,128)(2,1)}, f32[16,128,128]{2,1,0:T(8,128)S(1)}, f32[4,8,128]{2,1,0:T(8,128)}, f32[192,128]{1,0:T(8,128)S(1)}, f32[192,128]{1,0:T(8,128)S(1)}) custom-call(s32[3]{0:T(128)S(1)} %pad_add_fusion.c_ref, bf16[1,192,4096]{2,1,0:T(8,128)(2,1)S(1)} %copy-done, bf16[1,192,4096]{2,1,0:T(8,128)(2,1)S(1)} %copy-done.1, ...), custom_call_target="tpu_custom_call" | custom-call | flops 301989888 | bytes 8052736 | tf_op jit(solution)/shard_map/attend_other/pallas_call | solution.py:306
  81.9 3.9 %delta_own.1 = (bf16[192,2048]{1,0:T(8,128)(2,1)}, f32[16,128,128]{2,1,0:T(8,128)S(1)}, f32[4,8,128]{2,1,0:T(8,128)}, f32[16,128,128]{2,1,0:T(8,128)}) custom-call(s32[3]{0:T(128)S(1)} %pad_add_fusion.c_ref, bf16[1,192,4096]{2,1,0:T(8,128)(2,1)S(1)} %copy-done, bf16[1,192,4096]{2,1,0:T(8,128)(2,1)S(1)} %copy-done.1, ...), custom_call_target="tpu_custom_call", output_to_operand_aliasing={{2}: (8, {})} | custom-call | flops 100663296 | bytes 7872512 | tf_op jit(solution)/shard_map/delta_own/pallas_call | solution.py:306
  87.8 3.8 %all-to-all-start.2 = ((f32[16,128,128]{2,1,0:T(8,128)}), f32[16,128,128]{2,1,0:T(8,128)S(1)}, u32[]{:S(2)}, u32[]{:S(2)}) async-start(f32[16,128,128]{2,1,0:T(8,128)} %get-tuple-element.88), calls=%async_computation.2 | async-start | bytes 2097152 | tf_op jit(solution)/shard_map/all_to_all | solution.py:380
  95.3 9.0 %backward_inside.2 = (bf16[1,192,4096]{2,1,0:T(8,128)(2,1)}, f32[192,2048]{1,0:T(8,128)}, f32[192,2048]{1,0:T(8,128)}) custom-call(s32[3]{0:T(128)S(1)} %pad_add_fusion.c_ref, bf16[192,2048]{1,0:T(8,128)(2,1)} %get-tuple-element.81.od_ref, bf16[1,192,4096]{2,1,0:T(8,128)(2,1)} %q_ref.13, bf16[1,192,4096]{2,1,0:T(8,128)(2,1)} %k_ref.15, ...), custom_call_target="tpu_custom_call" | custom-call | flops 805306368 | bytes 12500992 | tf_op jit(solution)/shard_map/backward_inside/pallas_call | solution.py:306
  104.3 5.2 %all-to-all-done.2.m_ref = f32[16,128,128]{2,1,0:T(8,128)S(1)} async-done(((f32[16,128,128]{2,1,0:T(8,128)}), f32[16,128,128]{2,1,0:T(8,128)S(1)}, u32[]{:S(2)}, u32[]{:S(2)}) %all-to-all-start.2) | async-done | bytes 1048608 | tf_op jit(solution)/shard_map/all_to_all | solution.py:380
  110.1 5.4 %collective-permute-start.7 = (f32[136,128]{1,0:T(8,128)S(1)}, f32[136,128]{1,0:T(8,128)S(1)}, u32[]{:S(2)}, u32[]{:S(2)}) collective-permute-start(f32[136,128]{1,0:T(8,128)S(1)} %half_total.3), channel_id=1, source_target_pairs={{0,32},{32,0},{1,33},{33,1},{2,34},{34,2},{3,35},{35,3},{4,36},{36... | collective-permute-start | bytes 208904 | tf_op jit(solution)/shard_map/ppermute | solution.py:396
  119.0 3.7 %all-to-all-start.3 = ((f32[16,136,128]{2,1,0:T(8,128)}), f32[16,136,128]{2,1,0:T(8,128)S(1)}, u32[]{:S(2)}, u32[]{:S(2)}) async-start(f32[16,136,128]{2,1,0:T(8,128)} %chip_scan.3), calls=%async_computation.3 | async-start | bytes 2228224 | tf_op jit(solution)/shard_map/all_to_all | solution.py:380
  122.7 8.8 %backward_inside.3 = (bf16[1,192,4096]{2,1,0:T(8,128)(2,1)}, f32[192,2048]{1,0:T(8,128)}, f32[192,2048]{1,0:T(8,128)}) custom-call(s32[3]{0:T(128)S(1)} %pad_add_fusion.c_ref, bf16[192,2048]{1,0:T(8,128)(2,1)} %get-tuple-element.75.od_ref, bf16[1,192,4096]{2,1,0:T(8,128)(2,1)} %q_ref.13, ...), custom_call_target="tpu_custom_call", output_to_operand_aliasing={{0}: (9, {})} | custom-call | flops 805306368 | bytes 14073856 | tf_op jit(solution)/shard_map/backward_inside/pallas_call | solution.py:306
  131.5 6.5 %all-to-all-done.3.d_ref.rest_0_ = f32[16,136,128]{2,1,0:T(8,128)S(1)} async-done(((f32[16,136,128]{2,1,0:T(8,128)}), f32[16,136,128]{2,1,0:T(8,128)S(1)}, u32[]{:S(2)}, u32[]{:S(2)}) %all-to-all-start.3) | async-done | bytes 1114144 | tf_op jit(solution)/shard_map/all_to_all | solution.py:380
  138.0 3.0 %onward_back.1 = (f32[16,128,128]{2,1,0:T(8,128)}, f32[16,128,128]{2,1,0:T(8,128)S(1)}, f32[8,128]{1,0:T(8,128)S(1)}) custom-call(s32[3]{0:T(128)S(1)} %pad_add_fusion.c_ref, f32[16,136,128]{2,1,0:T(8,128)S(1)} %all-to-all-done.3.d_ref.rest_0_, f32[16,128,128]{2,1,0:T(8,128)} %get-tuple-element.97.own_ref, f32[16,128,128]{2,1,0:T(8,128)} %get-tuple-element.98.got_ref, ...), custom_call_target="tpu_custom_call" | custom-call | bytes 6557696 | tf_op jit(solution)/shard_map/onward_back/pallas_call | solution.py:306
  141.1 3.4 %collective-permute-start.8 = (f32[16,128,128]{2,1,0:T(8,128)}, f32[16,128,128]{2,1,0:T(8,128)S(1)}, u32[]{:S(2)}, u32[]{:S(2)}) collective-permute-start(f32[16,128,128]{2,1,0:T(8,128)} %get-tuple-element.99), channel_id=1, source_target_pairs={{0,1},{1,0},{2,3},{3,2},{4,5},{5,4},{6,7},{7,6},{8,9},{9,8},{10,11... | collective-permute-start | bytes 3145736 | tf_op jit(solution)/shard_map/ppermute | solution.py:376
  144.4 4.5 %finish.2 = (bf16[1,192,4096]{2,1,0:T(8,128)(2,1)}, bf16[1,192,4096]{2,1,0:T(8,128)(2,1)}) custom-call(s32[3]{0:T(128)S(1)} %pad_add_fusion.c_ref, bf16[1,192,4096]{2,1,0:T(8,128)(2,1)} %k_ref.15, bf16[1,192,4096]{2,1,0:T(8,128)(2,1)} %v_ref.15, f32[4,192,8]{2,1,0:T(8,128)} %get-tuple-element.56.col_ref, f32[192,2048]{1,0:T(8,128)} %get-tuple-element.100.ki_ref, ...), custom_call_target="tpu_custom_call" | custom-call | flops 402653184 | bytes 10510336 | tf_op jit(solution)/shard_map/finish/pallas_call | solution.py:306
  149.6 4.5 %finish.3 = (bf16[1,192,4096]{2,1,0:T(8,128)(2,1)}, bf16[1,192,4096]{2,1,0:T(8,128)(2,1)}) custom-call(s32[3]{0:T(128)S(1)} %pad_add_fusion.c_ref, bf16[1,192,4096]{2,1,0:T(8,128)(2,1)} %k_ref.15, bf16[1,192,4096]{2,1,0:T(8,128)(2,1)} %v_ref.15, f32[4,192,8]{2,1,0:T(8,128)} %get-tuple-element.56.col_ref, ...), custom_call_target="tpu_custom_call", output_to_operand_aliasing={{0}: (7, {}), {1}: (8, {})} | custom-call | flops 402653184 | bytes 13656064 | tf_op jit(solution)/shard_map/finish/pallas_call | solution.py:306
  (50 shorter events, 19.0 us)
Async XLA Ops:
  5.1 7.6 %collective-permute-start = (f32[16,136,128]{2,1,0:T(8,128)S(1)}, f32[16,136,128]{2,1,0:T(8,128)S(1)}, u32[]{:S(2)}, u32[]{:S(2)}) collective-permute-start(f32[16,136,128]{2,1,0:T(8,128)S(1)} %get-tuple-element.58), channel_id=1, source_target_pairs={{0,1},{1,0},{2,3},{3,2},{4,5},{5,4},{6,7},{7,6},{8,9},{9,8},{10,11... | collective-permute-start | bytes 3342344 | tf_op jit(solution)/shard_map/ppermute | solution.py:376
  12.7 0.8 copy-start.4
  15.6 22.8 %all-to-all-start = ((f32[16,136,128]{2,1,0:T(8,128)}), f32[16,136,128]{2,1,0:T(8,128)S(1)}, u32[]{:S(2)}, u32[]{:S(2)}) async-start(f32[16,136,128]{2,1,0:T(8,128)} %get-tuple-element.60), calls=%async_computation | async-start | bytes 2228224 | tf_op jit(solution)/shard_map/all_to_all | solution.py:380
  39.0 8.7 %collective-permute-start.1 = (f32[128,128]{1,0:T(8,128)S(1)}, f32[128,128]{1,0:T(8,128)S(1)}, u32[]{:S(2)}, u32[]{:S(2)}) collective-permute-start(f32[128,128]{1,0:T(8,128)S(1)} %half_total.2), channel_id=1, source_target_pairs={{0,32},{32,0},{1,33},{33,1},{2,34},{34,2},{3,35},{35,3},{4,36},{36... | collective-permute-start | bytes 196616 | tf_op jit(solution)/shard_map/ppermute | solution.py:396
  47.8 19.7 %copy-start.6 = (f32[16,128,128]{2,1,0:T(8,128)S(1)}, f32[16,128,128]{2,1,0:T(8,128)}, u32[]{:S(2)}) copy-start(f32[16,128,128]{2,1,0:T(8,128)} %get-tuple-element.67.own_ref) | copy-start | bytes 3145732
  47.8 19.7 %copy-start.7 = (f32[16,128,128]{2,1,0:T(8,128)S(1)}, f32[16,128,128]{2,1,0:T(8,128)}, u32[]{:S(2)}) copy-start(f32[16,128,128]{2,1,0:T(8,128)} %get-tuple-element.68.got_ref) | copy-start | bytes 3145732
  49.4 18.1 %copy-start.5 = (f32[16,8,128]{2,1,0:T(8,128)S(1)}, f32[16,8,128]{2,1,0:T(8,128)}, u32[]{:S(2)}) copy-start(f32[16,8,128]{2,1,0:T(8,128)} %get-tuple-element.59.lo_ref) | copy-start | bytes 196612
  49.4 18.1 %copy-start.8 = (f32[16,8,128]{2,1,0:T(8,128)S(1)}, f32[16,8,128]{2,1,0:T(8,128)}, u32[]{:S(2)}) copy-start(f32[16,8,128]{2,1,0:T(8,128)} %get-tuple-element.69.lg_ref) | copy-start | bytes 196612
  49.4 22.8 %copy-start.3 = (f32[192,2048]{1,0:T(8,128)S(1)}, f32[192,2048]{1,0:T(8,128)}, u32[]{:S(2)}) copy-start(f32[192,2048]{1,0:T(8,128)} %get-tuple-element.71.in_ref) | copy-start | bytes 4718596
  67.5 4.7 %copy-start = (bf16[1,192,4096]{2,1,0:T(8,128)(2,1)S(1)}, bf16[1,192,4096]{2,1,0:T(8,128)(2,1)}, u32[]{:S(2)}) copy-start(bf16[1,192,4096]{2,1,0:T(8,128)(2,1)} %q_ref.13) | copy-start | bytes 4718596
  67.5 4.7 %copy-start.1 = (bf16[1,192,4096]{2,1,0:T(8,128)(2,1)S(1)}, bf16[1,192,4096]{2,1,0:T(8,128)(2,1)}, u32[]{:S(2)}) copy-start(bf16[1,192,4096]{2,1,0:T(8,128)(2,1)} %g_ref.5) | copy-start | bytes 4718596
  68.3 7.4 %collective-permute-start.2 = (f32[16,128,128]{2,1,0:T(8,128)S(1)}, f32[16,128,128]{2,1,0:T(8,128)S(1)}, u32[]{:S(2)}, u32[]{:S(2)}) collective-permute-start(f32[16,128,128]{2,1,0:T(8,128)S(1)} %get-tuple-element.70), channel_id=1, source_target_pairs={{0,1},{1,0},{2,3},{3,2},{4,5},{5,4},{6,7},{7,6},{8,9},{9,8},{10,11... | collective-permute-start | bytes 3145736 | tf_op jit(solution)/shard_map/ppermute | solution.py:376
  72.2 3.5 %copy-start.2 = (f32[192,2048]{1,0:T(8,128)S(1)}, f32[192,2048]{1,0:T(8,128)}, u32[]{:S(2)}) copy-start(f32[192,2048]{1,0:T(8,128)} %get-tuple-element.64.in_ref) | copy-start | bytes 4718596
  81.1 4.8 %collective-permute-start.3 = (f32[16,128,128]{2,1,0:T(8,128)S(1)}, f32[16,128,128]{2,1,0:T(8,128)S(1)}, u32[]{:S(2)}, u32[]{:S(2)}) collective-permute-start(f32[16,128,128]{2,1,0:T(8,128)S(1)} %get-tuple-element.87), channel_id=1, source_target_pairs={{0,1},{1,0},{2,3},{3,2},{4,5},{5,4},{6,7},{7,6},{8,9},{9,8},{10,11... | collective-permute-start | bytes 3145736 | tf_op jit(solution)/shard_map/ppermute | solution.py:376
  87.8 3.8 %copy-start.10 = (f32[4,8,128]{2,1,0:T(8,128)S(1)}, f32[4,8,128]{2,1,0:T(8,128)}, u32[]{:S(2)}) copy-start(f32[4,8,128]{2,1,0:T(8,128)} %get-tuple-element.92) | copy-start | bytes 49156
  87.8 21.7 %all-to-all-start.2 = ((f32[16,128,128]{2,1,0:T(8,128)}), f32[16,128,128]{2,1,0:T(8,128)S(1)}, u32[]{:S(2)}, u32[]{:S(2)}) async-start(f32[16,128,128]{2,1,0:T(8,128)} %get-tuple-element.88), calls=%async_computation.2 | async-start | bytes 2097152 | tf_op jit(solution)/shard_map/all_to_all | solution.py:380
  91.6 12.6 %collective-permute-start.4 = (f32[8,128]{1,0:T(8,128)S(1)}, f32[8,128]{1,0:T(8,128)S(1)}, u32[]{:S(2)}, u32[]{:S(2)}) collective-permute-start(f32[8,128]{1,0:T(8,128)S(1)} %get-tuple-element.108), channel_id=1, source_target_pairs={{0,64},{64,0},{128,192},{192,128},{1,65},{65,1},{129,193},{193,129... | collective-permute-start | bytes 12296 | tf_op jit(solution)/shard_map/ppermute | solution.py:498
  92.4 11.9 %collective-permute-start.5 = (f32[8,128]{1,0:T(8,128)S(1)}, f32[8,128]{1,0:T(8,128)S(1)}, u32[]{:S(2)}, u32[]{:S(2)}) collective-permute-start(f32[8,128]{1,0:T(8,128)S(1)} %get-tuple-element.110), channel_id=1, source_target_pairs={{0,128},{64,192},{128,0},{192,64},{1,129},{65,193},{129,1},{193,65... | collective-permute-start | bytes 12296 | tf_op jit(solution)/shard_map/ppermute | solution.py:498
  94.9 9.4 %collective-permute-start.6 = (f32[8,128]{1,0:T(8,128)S(1)}, f32[8,128]{1,0:T(8,128)S(1)}, u32[]{:S(2)}, u32[]{:S(2)}) collective-permute-start(f32[8,128]{1,0:T(8,128)S(1)} %get-tuple-element.109), channel_id=1, source_target_pairs={{0,192},{64,128},{128,64},{192,0},{1,193},{65,129},{129,65},{193,1... | collective-permute-start | bytes 12296 | tf_op jit(solution)/shard_map/ppermute | solution.py:498
  95.3 14.2 %copy-start.9 = (f32[16,8,128]{2,1,0:T(8,128)S(1)}, f32[16,8,128]{2,1,0:T(8,128)}, u32[]{:S(2)}) copy-start(f32[16,8,128]{2,1,0:T(8,128)} %get-tuple-element.91.l_ref) | copy-start | bytes 196612
  110.1 7.2 %collective-permute-start.7 = (f32[136,128]{1,0:T(8,128)S(1)}, f32[136,128]{1,0:T(8,128)S(1)}, u32[]{:S(2)}, u32[]{:S(2)}) collective-permute-start(f32[136,128]{1,0:T(8,128)S(1)} %half_total.3), channel_id=1, source_target_pairs={{0,32},{32,0},{1,33},{33,1},{2,34},{34,2},{3,35},{35,3},{4,36},{36... | collective-permute-start | bytes 208904 | tf_op jit(solution)/shard_map/ppermute | solution.py:396
  119.0 19.1 %all-to-all-start.3 = ((f32[16,136,128]{2,1,0:T(8,128)}), f32[16,136,128]{2,1,0:T(8,128)S(1)}, u32[]{:S(2)}, u32[]{:S(2)}) async-start(f32[16,136,128]{2,1,0:T(8,128)} %chip_scan.3), calls=%async_computation.3 | async-start | bytes 2228224 | tf_op jit(solution)/shard_map/all_to_all | solution.py:380
  141.1 8.5 %collective-permute-start.8 = (f32[16,128,128]{2,1,0:T(8,128)}, f32[16,128,128]{2,1,0:T(8,128)S(1)}, u32[]{:S(2)}, u32[]{:S(2)}) collective-permute-start(f32[16,128,128]{2,1,0:T(8,128)} %get-tuple-element.99), channel_id=1, source_target_pairs={{0,1},{1,0},{2,3},{3,2},{4,5},{5,4},{6,7},{7,6},{8,9},{9,8},{10,11... | collective-permute-start | bytes 3145736 | tf_op jit(solution)/shard_map/ppermute | solution.py:376
  144.4 4.5 %collective-permute-start.9 = (f32[8,128]{1,0:T(8,128)S(1)}, f32[8,128]{1,0:T(8,128)S(1)}, u32[]{:S(2)}, u32[]{:S(2)}) collective-permute-start(f32[8,128]{1,0:T(8,128)S(1)} %get-tuple-element.107), channel_id=1, source_target_pairs={{0,1},{1,0},{2,3},{3,2},{4,5},{5,4},{6,7},{7,6},{8,9},{9,8},{10,11... | collective-permute-start | bytes 12296 | tf_op jit(solution)/shard_map/ppermute | solution.py:376

commit v4 on v3

v4 whole, which is shorter than its diff:
```python
import functools
import math

import jax
import jax.numpy as jnp
from jax import lax
from jax.experimental import pallas as pl
from jax.experimental.pallas import tpu as pltpu
from jax.sharding import Mesh, PartitionSpec as P

EPSILON = 1e-06
HIGHEST = lax.Precision.HIGHEST
F32 = jnp.float32
BF16 = jnp.bfloat16
T = 192
HD = 128
GH = 8
FH = 4
GW = GH * HD
NG = 4
HALF = NG // 2
NC = 16
ALL = ("dp", "zh", "x", "y", "core")


def dot(a, b, ca, cb):
    return lax.dot_general(a, b, (((ca,), (cb,)), ((), ())), preferred_element_type=F32)


def lanes(j):
    return slice(j * HD, (j + 1) * HD)


def split_state(state, axis):
    high = state.astype(BF16)
    low = (state - high.astype(F32)).astype(BF16)
    return jnp.concatenate([high, low], axis)


def rows_by_state(rows, state):
    return dot(jnp.concatenate([rows, rows], 1), split_state(state, 0), 1, 0)


def rows_by_state_t(rows, state):
    return dot(jnp.concatenate([rows, rows], 1), split_state(state, 1), 1, 1)


def columns(row_ref, heads=GH):
    cum = jnp.transpose(row_ref[...])
    if heads == GH:
        return cum
    return jnp.where(pl.program_id(0) % 2 == 0, cum[:, :heads], cum[:, heads:])


def decay_table(col, row):
    row_ids = lax.broadcasted_iota(jnp.int32, (T, T), 0)
    col_ids = lax.broadcasted_iota(jnp.int32, (T, T), 1)
    return jnp.exp(jnp.where(row_ids >= col_ids, col - row, -jnp.inf))


def states_of(k_ref, v_ref, row_ref, store):
    cum = columns(row_ref, FH)
    last = cum[T - 1 : T, :]
    shrink = jnp.exp(last - cum)
    for j in range(FH):
        late = (k_ref[:, lanes(j)].astype(F32) * shrink[:, j : j + 1]).astype(BF16)
        store(j, dot(late, v_ref[:, lanes(j)], 0, 0), jnp.broadcast_to(last[:, j : j + 1], (8, HD)))


def state_first_kernel(c_ref, k_ref, v_ref, ld_ref, s_ref, row_ref):
    i = pl.program_id(0)

    @pl.when(i == 0)
    def _():
        upper = (
            lax.broadcasted_iota(jnp.int32, (T, T), 0) <= lax.broadcasted_iota(jnp.int32, (T, T), 1)
        ).astype(F32)
        logs = ld_ref[...]
        row_ref[...] = lax.dot_general(
            logs, upper, (((1,), (0,)), ((), ())), precision=HIGHEST, preferred_element_type=F32
        )

    def store(j, state, log):
        s_ref[j, :HD, :] = state
        s_ref[j, HD:, :] = log

    group = (1 - c_ref[0]) * HALF + i // 2
    states_of(k_ref, v_ref, row_ref.at[pl.ds(pl.multiple_of(group * GH, GH), GH)], store)


def state_second_kernel(c_ref, k_ref, v_ref, row_ref, s_ref, l_ref):
    def store(j, state, log):
        s_ref[j] = state
        l_ref[j] = log

    states_of(k_ref, v_ref, row_ref, store)


def combine_kernel(upward, c_ref, own_ref, got_ref, lo_ref, lg_ref, p_ref, log_ref=None):
    first = c_ref[0] == 0 if upward else c_ref[0] == 1
    for j in range(GH):
        log_own, log_got = lo_ref[j, 0:1, :], lg_ref[j, 0:1, :]
        scale_own = jnp.where(first, jnp.exp(log_got), 1.0)
        scale_got = jnp.where(first, 1.0, jnp.exp(log_own))
        p_ref[j, :HD, :] = scale_own * own_ref[j] + scale_got * got_ref[j]
        if upward:
            p_ref[j, HD:, :] = lo_ref[j] + lg_ref[j]
            log_ref[j] = lg_ref[j]


def total_kernel(upward, c_ref, m_ref, l_ref, *rest):
    run = jnp.zeros((HD, HD), F32)
    for i in range(NC) if upward else reversed(range(NC)):
        run = jnp.exp(l_ref[i, 0:1, :]) * run + m_ref[i]
    t_ref = rest[-1]
    t_ref[:HD, :] = run
    if not upward:
        t_ref[HD:, :] = rest[0][...]


def scan_kernel(upward, c_ref, m_ref, l_ref, t_ref, *rest):
    if upward:
        o_ref, log_ref = rest
        log_ref[...] = l_ref[...]
    else:
        gain_ref, o_ref = rest
        both = gain_ref[...] + t_ref[HD:, :]
    run = t_ref[:HD, :]
    run = jnp.where(c_ref[2] == (1 if upward else 0), run, 0.0)
    for i in range(NC) if upward else reversed(range(NC)):
        o_ref[i, :HD, :] = run
        run = jnp.exp(l_ref[i, 0:1, :]) * run + m_ref[i]
        if not upward:
            x = i // 4
            row = jnp.where(c_ref[2] == 0, both[x : x + 1, :], both[4 + x : 5 + x, :])
            o_ref[i, HD:, :] = jnp.broadcast_to(row, (8, HD))


def hand_on_kernel(
    upward, c_ref, d_ref, own_ref, got_ref, lo_ref, lg_ref, *rest
):
    if upward:
        send_ref, state_ref = rest
    else:
        gains_ref, send_ref, state_ref, sum_ref = rest
        part = gains_ref[0]
        for j in range(1, GH):
            part += gains_ref[j]

        @pl.when(pl.program_id(0) == 0)
        def _():
            sum_ref[...] = part

        @pl.when(pl.program_id(0) > 0)
        def _():
            sum_ref[...] += part

    at_edge = c_ref[0] == (0 if upward else 1)
    for j in range(GH):
        edge = d_ref[j]
        send_ref[j] = (
            jnp.where(at_edge, jnp.exp(lo_ref[j, 0:1, :]), 1.0) * edge
            + jnp.where(at_edge, 1.0, 0.0) * own_ref[j]
        )
        state_ref[j] = (
            jnp.where(at_edge, 1.0, jnp.exp(lg_ref[j, 0:1, :])) * edge
            + jnp.where(at_edge, 0.0, 1.0) * got_ref[j]
        )


def forward_kernel(c_ref, q_ref, k_ref, v_ref, row_ref, fw_ref, in_ref):
    cum = columns(row_ref)
    for j in range(GH):
        decay = decay_table(cum[:, j : j + 1], row_ref[j : j + 1, :])
        scores = dot(q_ref[:, lanes(j)], k_ref[:, lanes(j)], 1, 1)
        weights = (scores * decay).astype(BF16)
        fw_ref[j] = weights
        in_ref[:, lanes(j)] = dot(weights, v_ref[:, lanes(j)], 1, 0)


def attend_group(q_ref, g_ref, gain_ref, cum, in_ref, x_ref, att_ref, sq_ref, pr_ref):
    growth = jnp.exp(cum)
    squares = jnp.zeros((T, HD), F32)
    products = jnp.zeros((T, HD), F32)
    for j in range(GH):
        att = in_ref[:, lanes(j)] + growth[:, j : j + 1] * rows_by_state(q_ref[:, lanes(j)], x_ref[j])
        att_ref[:, lanes(j)] = att
        squares += att * att
        products += att * (gain_ref[:, lanes(j)] * g_ref[:, lanes(j)].astype(F32))
    sq_ref[...] += squares
    pr_ref[...] += products


def attend_own_kernel(
    c_ref, q_ref, g_ref, gain_ref, row_ref, in_ref, x_ref, att_ref, sq_ref, pr_ref
):
    @pl.when(pl.program_id(0) == 0)
    def _():
        sq_ref[...] = jnp.zeros_like(sq_ref)
        pr_ref[...] = jnp.zeros_like(pr_ref)

    attend_group(
        q_ref, g_ref, gain_ref, columns(row_ref), in_ref, x_ref, att_ref, sq_ref, pr_ref
    )


def delta_group(q_ref, g_ref, gain_ref, cum, att_ref, inverse, mean, od_ref, m_ref, gt_ref):
    growth = jnp.exp(cum)
    for j in range(GH):
        grad = g_ref[:, lanes(j)].astype(F32)
        normed = att_ref[:, lanes(j)] * inverse
        delta = (inverse * (gain_ref[:, lanes(j)] * grad - normed * mean)).astype(BF16)
        od_ref[:, lanes(j)] = delta
        gt_ref[j : j + 1, :] = jnp.sum(grad * normed, axis=0, keepdims=True)
        early = (q_ref[:, lanes(j)].astype(F32) * growth[:, j : j + 1]).astype(BF16)
        m_ref[j] = dot(early, delta, 0, 0)


def attend_other_kernel(
    c_ref, q_ref, g_ref, gain_ref, row_ref, in_ref, i_ref, sq_in, pr_in,
    od_ref, m_ref, gt_ref, inv_ref, mean_ref, att_ref, sq_ref, pr_ref,
):
    step = pl.program_id(0)
    group = jnp.where(step < HALF, step, 2 * HALF - 1 - step)
    cum = columns(row_ref)

    @pl.when(step == 0)
    def _():
        sq_ref[...] = sq_in[...]
        pr_ref[...] = pr_in[...]

    @pl.when(step < HALF)
    def _():
        attend_group(
            q_ref, g_ref, gain_ref, cum, in_ref, i_ref, att_ref.at[group], sq_ref, pr_ref
        )

    @pl.when(step == HALF)
    def _():
        features = NG * GW
        inverse = lax.rsqrt(jnp.sum(sq_ref[...], axis=1, keepdims=True) * (1.0 / features) + EPSILON)
        mean = inverse * (jnp.sum(pr_ref[...], axis=1, keepdims=True) * (1.0 / features))
        inv_ref[...] = jnp.broadcast_to(inverse, (T, HD))
        mean_ref[...] = jnp.broadcast_to(mean, (T, HD))

    @pl.when(step >= HALF)
    def _():
        delta_group(
            q_ref, g_ref, gain_ref, cum, att_ref.at[group], inv_ref[...], mean_ref[...],
            od_ref, m_ref, gt_ref,
        )


def delta_own_kernel(
    c_ref, q_ref, g_ref, gain_ref, row_ref, att_ref, inv_ref, mean_ref, gt_in, od_ref, m_ref, gt_ref
):
    delta_group(
        q_ref, g_ref, gain_ref, columns(row_ref), att_ref, inv_ref[...], mean_ref[...], od_ref, m_ref, gt_ref
    )


def backward_kernel(
    c_ref, od_ref, q_ref, k_ref, v_ref, fw_ref, row_ref, i_ref, *rest
):
    qg_ref, ki_ref, vi_ref = rest[-3:]
    cum = columns(row_ref)
    growth = jnp.exp(cum)
    for j in range(GH):
        at = lanes(j)
        decay = decay_table(cum[:, j : j + 1], row_ref[j : j + 1, :])
        delta = od_ref[:, at]
        weights = (dot(delta, v_ref[:, at], 1, 1) * decay).astype(BF16)
        inter = growth[:, j : j + 1] * rows_by_state_t(delta, i_ref[j])
        qg_ref[:, at] = (dot(weights, k_ref[:, at], 1, 0) + inter).astype(BF16)
        ki_ref[:, at] = dot(weights, q_ref[:, at], 0, 0)
        vi_ref[:, at] = dot(fw_ref[j], delta, 0, 0)


def finish_kernel(c_ref, k_ref, v_ref, row_ref, ki_ref, vi_ref, x_ref, *rest):
    cum = columns(row_ref, FH)
    shrink = jnp.exp(cum[T - 1 : T, :] - cum)
    kg_ref, vg_ref = rest[-2:]
    for j in range(FH):
        at = lanes(j)
        scale = shrink[:, j : j + 1]
        kg_ref[:, at] = (ki_ref[:, at] + scale * rows_by_state_t(v_ref[:, at], x_ref[j])).astype(BF16)
        vg_ref[:, at] = (vi_ref[:, at] + scale * rows_by_state(k_ref[:, at], x_ref[j])).astype(BF16)


class Kept:
    def __init__(self, array):
        self.array = array
        self.shape, self.dtype = array.shape, array.dtype


def in_hbm(a):
    return pltpu.with_memory_space_constraint(a.array, pltpu.HBM) if isinstance(a, Kept) else a


def call(
    kernel, name, grid, in_specs, out_specs, out_shape, args, flops, scratch=(), aliases=None, kept=False
):
    place, *args = args
    nbytes = sum(math.prod(a.shape) * a.dtype.itemsize for a in [*args, *out_shape])
    if kept:
        args, out_shape = [Kept(a) for a in args], [Kept(s) for s in out_shape]
    return pl.pallas_call(
        kernel,
        name=name,
        grid_spec=pltpu.PrefetchScalarGridSpec(
            num_scalar_prefetch=1,
            grid=grid,
            in_specs=in_specs,
            out_specs=out_specs,
            scratch_shapes=scratch,
        ),
        out_shape=[pltpu.HBM(s.shape, s.dtype) if isinstance(s, Kept) else s for s in out_shape],
        input_output_aliases=aliases or {},
        compiler_params=pltpu.CompilerParams(vmem_limit_bytes=16 << 20),
        cost_estimate=pl.CostEstimate(flops=flops, bytes_accessed=nbytes, transcendentals=0),
    )(place, *[in_hbm(a) for a in args])


def shape(dims, dtype=F32):
    return jax.ShapeDtypeStruct(dims, dtype)


def half_of(own, c_ref):
    return c_ref[0] if own else 1 - c_ref[0]


def wide(own, group=lambda i: i):
    return pl.BlockSpec((None, T, GW), lambda i, c: (0, 0, half_of(own, c) * HALF + group(i)))


def narrow(group=lambda i: i):
    return pl.BlockSpec((T, GW), lambda i, c: (0, group(i)))


def fine(own):
    return pl.BlockSpec((None, T, FH * HD), lambda i, c: (0, 0, half_of(own, c) * (NC // FH) + i))


FINE_NARROW = pl.BlockSpec((T, FH * HD), lambda i, c: (0, i))


def fine_block(rows=HD):
    return pl.BlockSpec((FH, rows, HD), lambda i, c: (i, 0, 0))


def gain_block(own, group=lambda i: i):
    return pl.BlockSpec((1, GW), lambda i, c: (0, half_of(own, c) * HALF + group(i)))


def row_block(own, group=lambda i: i):
    return pl.BlockSpec((GH, T), lambda i, c: (half_of(own, c) * HALF + group(i), 0))


def gains_block(own, group=lambda i: i):
    return pl.BlockSpec(
        (None, GH, HD),
        lambda i, c: (jnp.bitwise_xor(half_of(own, c) * HALF + group(i), c[1]), 0, 0),
    )


def state_block(rows=HD, group=lambda i: i):
    return pl.BlockSpec((GH, rows, HD), lambda i, c: (group(i), 0, 0))


LOG_BLOCK = pl.BlockSpec((GH, 8, HD), lambda i, c: (i, 0, 0))
LOG_TAIL = pl.BlockSpec((GH, 8, HD), lambda i, c: (i, HD // 8, 0))
STAT_WHOLE = pl.BlockSpec((T, HD), lambda i, c: (0, 0))
ANY = pl.BlockSpec(memory_space=pl.ANY)
STATES = shape((NC, HD, HD))
LOGGED = shape((NC, HD + 8, HD))
LOGS = shape((NC, 8, HD))
HALF_F32 = shape((T, HALF * GW))
HALF_BF16 = shape((T, HALF * GW), BF16)
WHOLE_BF16 = shape((1, T, NG * GW), BF16)
STAT = shape((T, HD))
GAINS = shape((NG, GH, HD))
MM = 2 * T * HD * HD * NC
SM = 2 * T * T * HD * NC


def swap_cores(values):
    return lax.ppermute(values, "core", [(0, 1), (1, 0)])


def chips_all_to_all(values):
    return lax.all_to_all(values, ("x", "y"), split_axis=0, concat_axis=0, tiled=True)


def scan_over_chips(upward, place, got, logs, gains=None):
    whole_m = pl.BlockSpec((NC, HD, HD), lambda i, c: (0, 0, 0))
    whole_l = pl.BlockSpec((NC, 8, HD), lambda i, c: (0, HD // 8 if upward else 0, 0))
    logs_out = pl.BlockSpec((NC, 8, HD), lambda i, c: (0, 0, 0))
    rows = HD if upward else HD + 8
    whole_t = pl.BlockSpec((rows, HD), lambda i, c: (0, 0))
    more = [] if upward else [gains]
    more_specs = [pl.BlockSpec((8, HD), lambda i, c: (0, 0))] * len(more)
    (total,) = call(
        functools.partial(total_kernel, upward), "half_total", (1,),
        [whole_m, whole_l] + more_specs, [whole_t], [shape((rows, HD))],
        (place, got, logs, *more), 0,
    )
    before = lax.ppermute(total, "zh", [(0, 1), (1, 0)])
    outs = [pl.BlockSpec((NC, rows, HD), lambda i, c: (0, 0, 0))] + [logs_out] * upward
    return call(
        functools.partial(scan_kernel, upward), "chip_scan", (1,),
        [whole_m, whole_l, whole_t] + more_specs, outs, [Kept(shape((NC, rows, HD))), LOGS][: len(outs)],
        (place, got, logs, before, *more), 0,
    )


def per_device(queries, key_rows, value_rows, out_grad, log_decay, norm_gain):
    core = jnp.stack([lax.axis_index(a).astype(jnp.int32) for a in ("core", "dp", "zh")])
    q, k, v, g = queries, key_rows, value_rows, out_grad
    gain = norm_gain.reshape(1, NG * GW)
    logs = jnp.transpose(log_decay[0])

    whole_rows = pl.BlockSpec((NG * GH, T), lambda i, c: (0, 0))
    sent, row = call(
        state_first_kernel, "states_other", (NC // FH,),
        [fine(False), fine(False), whole_rows], [fine_block(HD + 8), whole_rows],
        [LOGGED, shape((NG * GH, T))], (core, Kept(k), Kept(v), logs), MM,
    )
    got = swap_cores(sent)
    own, log_own = call(
        state_second_kernel, "states_own", (NC // FH,),
        [fine(True), fine(True), row_block(True, lambda i: i // 2)], [fine_block(), fine_block(8)],
        [STATES, LOGS],
        (core, Kept(k), Kept(v), row), MM,
    )
    chip_total, log_got = call(
        functools.partial(combine_kernel, True), "chip_total", (HALF,),
        [state_block(), state_block(), LOG_BLOCK, LOG_TAIL],
        [state_block(HD + 8), LOG_BLOCK], [Kept(LOGGED), LOGS],
        (core, own, got, log_own, got), 0,
    )
    gathered = chips_all_to_all(chip_total)

    weights, inside = {}, {}
    for mine in (True, False):
        weights[mine], inside[mine] = call(
            forward_kernel, "forward_inside", (HALF,),
            [wide(mine), wide(mine), wide(mine), row_block(mine)],
            [pl.BlockSpec((GH, T, T), lambda i, c: (i, 0, 0)), narrow()],
            [shape((NC, T, T), BF16), HALF_F32],
            (core, q, k, v, row), 2 * SM, kept=True,
        )

    gathered, inside[True], inside[False] = lax.optimization_barrier(
        (gathered, inside[True], inside[False])
    )
    before_chips, log_chips = scan_over_chips(True, core, gathered, gathered)
    scanned = chips_all_to_all(before_chips)
    onward, state_here = call(
        functools.partial(hand_on_kernel, True), "onward", (HALF,),
        [state_block()] * 3 + [LOG_BLOCK] * 2, [state_block()] * 2, [STATES] * 2,
        (core, scanned, own, got, log_own, log_got), 0,
    )
    state_other = swap_cores(onward)
    att_own, squares, products = call(
        attend_own_kernel, "attend_own", (HALF,),
        [wide(True), wide(True), gain_block(True), row_block(True), narrow(), state_block()],
        [narrow(), STAT_WHOLE, STAT_WHOLE], [HALF_F32, STAT, STAT],
        (core, q, g, gain, row, inside[True], state_here), 2 * MM,
    )

    def turn(i):
        return jnp.where(i < HALF, i, 2 * HALF - 1 - i)

    def first(i):
        return jnp.minimum(i, HALF - 1)

    def second(i):
        return jnp.minimum(2 * HALF - 1 - i, HALF - 1)

    delta_other, moment_sent, gains, inverse, mean = call(
        attend_other_kernel, "attend_other", (2 * HALF,),
        [wide(False, turn), wide(False, turn), gain_block(False, turn), row_block(False, turn), narrow(first),
         state_block(HD, first), STAT_WHOLE, STAT_WHOLE],
        [narrow(second), state_block(HD, second), gains_block(False, second), STAT_WHOLE, STAT_WHOLE],
        [HALF_BF16, STATES, Kept(GAINS), STAT, STAT],
        (core, q, g, gain, row, inside[False], state_other, squares, products), 3 * MM,
        scratch=[pltpu.VMEM((HALF, T, GW), F32), pltpu.VMEM((T, HD), F32), pltpu.VMEM((T, HD), F32)],
    )
    moment_got = swap_cores(moment_sent)
    delta_own, moment_own, gains = call(
        delta_own_kernel, "delta_own", (HALF,),
        [wide(True), wide(True), gain_block(True), row_block(True), narrow(), STAT_WHOLE, STAT_WHOLE, ANY],
        [narrow(), state_block(), gains_block(True)],
        [HALF_BF16, STATES, Kept(GAINS)],
        (core, q, g, gain, row, att_own, inverse, mean, Kept(gains)), MM,
        aliases={8: 2},
    )
    (chip_moment,) = call(
        functools.partial(combine_kernel, False), "chip_moment", (HALF,),
        [state_block(), state_block(), LOG_BLOCK, LOG_BLOCK], [state_block()], [Kept(STATES)],
        (core, moment_own, moment_got, log_own, log_got), 0,
    )
    gathered_back = chips_all_to_all(chip_moment)

    collected = gains[0]
    for distance in range(1, NG):
        collected += lax.ppermute(gains[distance], "dp", [(i, i ^ distance) for i in range(NG)])

    delta = {True: delta_own, False: delta_other}
    state = {True: state_here, False: state_other}
    query_grad, key_inside, value_inside = (), {}, {}
    for mine in (True, False):
        *query_grad, key_inside[mine], value_inside[mine] = call(
            backward_kernel, "backward_inside", (HALF,),
            [narrow(), wide(mine), wide(mine), wide(mine),
             pl.BlockSpec((GH, T, T), lambda i, c: (i, 0, 0)), row_block(mine), state_block()]
            + [ANY] * len(query_grad),
            [wide(mine), narrow(), narrow()],
            [WHOLE_BF16, HALF_F32, HALF_F32],
            (core, delta[mine], q, k, v, weights[mine], row, state[mine], *query_grad),
            4 * SM + 2 * MM, aliases={8: 0} if query_grad else None, kept=True,
        )

    gathered_back, key_inside[True] = lax.optimization_barrier((gathered_back, key_inside[True]))
    (after_chips,) = scan_over_chips(False, core, gathered_back, log_chips, collected)
    scanned_back = chips_all_to_all(after_chips)
    scanned_back, key_inside[False] = lax.optimization_barrier((scanned_back, key_inside[False]))
    onward_back, later_here, collected = call(
        functools.partial(hand_on_kernel, False), "onward_back", (HALF,),
        [state_block()] * 3 + [LOG_BLOCK] * 2 + [LOG_TAIL],
        [state_block(), state_block(), pl.BlockSpec((8, HD), lambda i, c: (0, 0))],
        [STATES, STATES, shape((8, HD))],
        (core, scanned_back, Kept(moment_own), Kept(moment_got), log_own,
         log_got, scanned_back), 0,
    )
    later_other = swap_cores(onward_back)
    later = {True: later_here, False: later_other}
    grads = ()
    for mine in (True, False):
        grads = call(
            finish_kernel, "finish", (NC // FH,),
            [fine(mine), fine(mine), row_block(mine, lambda i: i // 2), FINE_NARROW, FINE_NARROW,
             fine_block()] + [ANY] * len(grads),
            [fine(mine)] * 2, [Kept(WHOLE_BF16)] * 2,
            (core, Kept(k), Kept(v), row, Kept(key_inside[mine]), Kept(value_inside[mine]),
             later[mine], *[Kept(a) for a in grads]), 4 * MM, aliases={7: 0, 8: 1} if grads else None,
        )
    key_grad, value_grad = grads
    collected = (collected + swap_cores(collected))[0]
    at = lax.axis_index("y") * 32 + lax.axis_index("core") * 16
    positions = T * lax.axis_size(ALL)
    gain_grad = lax.dynamic_slice_in_dim(collected, at, 16) * (1.0 / math.sqrt(positions))
    return query_grad[0], key_grad, value_grad, gain_grad


def solution(mesh):
    fine = Mesh(mesh.devices.reshape(4, 2, 4, 4, 2), ALL)
    rows = P("dp", ("zh", "x", "y", "core"), None)
    return jax.shard_map(
        per_device,
        mesh=fine,
        in_specs=(rows,) * 5 + (P(),),
        out_specs=(rows, rows, rows, P(ALL)),
        check_vma=False,
    )
```

time: 155 us -> 157 us (1.013)
  local copies, waits for them, and re-layouts: 0.88 us -> 3.66 us
    unnamed x22 -> x36, local copies, waits for them, and re-layouts: 0.87 us -> 3.65 us
  transfers between devices with their start and end apart: 13 -> 13, of which waited for: 5 -> 6; matrix products, arithmetic and copies ran while one was open for 0% -> 0% of each run, Pallas kernels for 28% -> 27%
where the time goes in v4:
time: 157 us
  Pallas kernels  69.3 us (44%)
  starting transfers between devices  39.6 us (25%)
  waiting for transfers between devices  24.4 us (16%)
  blocking collectives  18 us (11%)
  local copies, waits for them, and re-layouts  3.66 us (2%)
    pallas_call x19, Pallas kernels, call(): pl.pallas_call(kernel, name=name, grid_spec=pltpu.PrefetchScalarGridSpec(...  69.3 us
    all_to_all x3, waiting for transfers between devices, chips_all_to_all(): lax.all_to_all(values, ('x', 'y'), split_axis=0, concat_axis=0, tiled=True)  20.6 us
    all_to_all x1, blocking collectives, chips_all_to_all(): lax.all_to_all(values, ('x', 'y'), split_axis=0, concat_axis=0, tiled=True)  18 us
    all_to_all x3, starting transfers between devices, chips_all_to_all(): lax.all_to_all(values, ('x', 'y'), split_axis=0, concat_axis=0, tiled=True)  12.5 us
    ppermute x2, starting transfers between devices, scan_over_chips(): before = lax.ppermute(total, 'zh', [(0, 1), (1, 0)])  12.4 us
    ppermute x5, starting transfers between devices, swap_cores(): return lax.ppermute(values, 'core', [(0, 1), (1, 0)])  11.1 us
    unnamed x36, local copies, waits for them, and re-layouts  3.65 us
    ppermute x3, starting transfers between devices, per_device(): lax.ppermute(gains[distance], 'dp', [(i, i ^ distance) for i in range(NG)])  3.64 us
  transfers between devices with their start and end apart: 13, of which 6 were waited for; matrix products, arithmetic and copies ran while one was open for 0% of the time, Pallas kernels for 27%

profile of v4, /device:TPU:1, one launch (start us, length us, event | category | flops | bytes accessed | tf_op | source)
XLA Modules:
  0.0 156.6 jit_solution(2379143504937117102)
XLA Ops:
  1.5 4.9 %states_other.1 = (f32[16,136,128]{2,1,0:T(8,128)S(1)}, f32[32,192]{1,0:T(8,128)S(1)}) custom-call(s32[3]{0:T(128)S(1)} %pad_add_fusion.c_ref, bf16[1,192,4096]{2,1,0:T(8,128)(2,1)} %k_ref.15, bf16[1,192,4096]{2,1,0:T(8,128)(2,1)} %v_ref.15, f32[32,192]{1,0:T(8,128)S(1)} %bitcast.24), custom_call_target="tpu_custom_call" | custom-call | flops 100663296 | bytes 4308992 | tf_op jit(solution)/shard_map/states_other/pallas_call | solution.py:307
  6.4 3.3 %collective-permute-start = (f32[16,136,128]{2,1,0:T(8,128)S(1)}, f32[16,136,128]{2,1,0:T(8,128)S(1)}, u32[]{:S(2)}, u32[]{:S(2)}) collective-permute-start(f32[16,136,128]{2,1,0:T(8,128)S(1)} %get-tuple-element.51), channel_id=1, source_target_pairs={{0,1},{1,0},{2,3},{3,2},{4,5},{5,4},{6,7},{7,6},{8,9},{9,8},{10,11... | collective-permute-start | bytes 3342344 | tf_op jit(solution)/shard_map/ppermute | solution.py:387
  9.7 4.7 %states_own.1 = (f32[16,128,128]{2,1,0:T(8,128)S(1)}, f32[16,8,128]{2,1,0:T(8,128)S(1)}) custom-call(s32[3]{0:T(128)S(1)} %pad_add_fusion.c_ref, bf16[1,192,4096]{2,1,0:T(8,128)(2,1)} %k_ref.15, bf16[1,192,4096]{2,1,0:T(8,128)(2,1)} %v_ref.15, f32[32,192]{1,0:T(8,128)S(1)} %get-tuple-element.49.row_ref), custom_call_target="tpu_custom_call" | custom-call | flops 100663296 | bytes 4284416 | tf_op jit(solution)/shard_map/states_own/pallas_call | solution.py:307
  16.2 5.0 %all-to-all-start = ((f32[16,136,128]{2,1,0:T(8,128)}), f32[16,136,128]{2,1,0:T(8,128)S(1)}, u32[]{:S(2)}, u32[]{:S(2)}) async-start(f32[16,136,128]{2,1,0:T(8,128)} %get-tuple-element.53), calls=%async_computation | async-start | bytes 2228224 | tf_op jit(solution)/shard_map/all_to_all | solution.py:391
  21.3 4.7 %forward_inside.2 = (bf16[16,192,192]{2,1,0:T(8,128)(2,1)}, f32[192,2048]{1,0:T(8,128)}) custom-call(s32[3]{0:T(128)S(1)} %pad_add_fusion.c_ref, bf16[1,192,4096]{2,1,0:T(8,128)(2,1)} %q_ref.13, bf16[1,192,4096]{2,1,0:T(8,128)(2,1)} %k_ref.15, bf16[1,192,4096]{2,1,0:T(8,128)(2,1)} %v_ref.15, f32[32,192]{1,0:T(8,128)} %copy-done.8), custom_call_target="tpu_custom_call" | custom-call | flops 301989888 | bytes 7495680 | tf_op jit(solution)/shard_map/forward_inside/pallas_call | solution.py:307
  26.0 4.7 %forward_inside.3 = (bf16[16,192,192]{2,1,0:T(8,128)(2,1)}, f32[192,2048]{1,0:T(8,128)}) custom-call(s32[3]{0:T(128)S(1)} %pad_add_fusion.c_ref, bf16[1,192,4096]{2,1,0:T(8,128)(2,1)} %q_ref.13, bf16[1,192,4096]{2,1,0:T(8,128)(2,1)} %k_ref.15, bf16[1,192,4096]{2,1,0:T(8,128)(2,1)} %v_ref.15, f32[32,192]{1,0:T(8,128)} %copy-done.8), custom_call_target="tpu_custom_call" | custom-call | flops 301989888 | bytes 7495680 | tf_op jit(solution)/shard_map/forward_inside/pallas_call | solution.py:307
  30.6 8.4 %all-to-all-done.m_ref.l_ref = f32[16,136,128]{2,1,0:T(8,128)S(1)} async-done(((f32[16,136,128]{2,1,0:T(8,128)}), f32[16,136,128]{2,1,0:T(8,128)S(1)}, u32[]{:S(2)}, u32[]{:S(2)}) %all-to-all-start) | async-done | bytes 1114144 | tf_op jit(solution)/shard_map/all_to_all | solution.py:391
  39.7 7.0 %collective-permute-start.1 = (f32[128,128]{1,0:T(8,128)S(1)}, f32[128,128]{1,0:T(8,128)S(1)}, u32[]{:S(2)}, u32[]{:S(2)}) collective-permute-start(f32[128,128]{1,0:T(8,128)S(1)} %half_total.2), channel_id=1, source_target_pairs={{0,32},{32,0},{1,33},{33,1},{2,34},{34,2},{3,35},{35,3},{4,36},{36... | collective-permute-start | bytes 196616 | tf_op jit(solution)/shard_map/ppermute | solution.py:407
  50.1 18.0 %all_to_all.20.d_ref = f32[16,128,128]{2,1,0:T(8,128)S(1)} all-to-all(f32[16,128,128]{2,1,0:T(8,128)} %get-tuple-element.58), channel_id=1, replica_groups=mesh['dp'=4,'zh'=2,'x'=4,'y'=4,'core'=2] {'x','y'}, dimensions={0} | all-to-all | bytes 2097152 | tf_op jit(solution)/shard_map/all_to_all | solution.py:391
  69.1 3.8 %collective-permute-start.2 = (f32[16,128,128]{2,1,0:T(8,128)S(1)}, f32[16,128,128]{2,1,0:T(8,128)S(1)}, u32[]{:S(2)}, u32[]{:S(2)}) collective-permute-start(f32[16,128,128]{2,1,0:T(8,128)S(1)} %get-tuple-element.60), channel_id=1, source_target_pairs={{0,1},{1,0},{2,3},{3,2},{4,5},{5,4},{6,7},{7,6},{8,9},{9,8},{10,11... | collective-permute-start | bytes 3145736 | tf_op jit(solution)/shard_map/ppermute | solution.py:387
  75.2 4.6 %attend_other.1 = (bf16[192,2048]{1,0:T(8,128)(2,1)S(1)}, f32[16,128,128]{2,1,0:T(8,128)S(1)}, f32[4,8,128]{2,1,0:T(8,128)}, f32[192,128]{1,0:T(8,128)S(1)}, f32[192,128]{1,0:T(8,128)S(1)}) custom-call(s32[3]{0:T(128)S(1)} %pad_add_fusion.c_ref, bf16[1,192,4096]{2,1,0:T(8,128)(2,1)S(1)} %copy-done, bf16[1,192,4096]{2,1,0:T(8,128)(2,1)S(1)} %copy-done.1, ...), custom_call_target="tpu_custom_call" | custom-call | flops 301989888 | bytes 8052736 | tf_op jit(solution)/shard_map/attend_other/pallas_call | solution.py:307
  81.3 3.4 %delta_own.1 = (bf16[192,2048]{1,0:T(8,128)(2,1)S(1)}, f32[16,128,128]{2,1,0:T(8,128)S(1)}, f32[4,8,128]{2,1,0:T(8,128)}) custom-call(s32[3]{0:T(128)S(1)} %pad_add_fusion.c_ref, bf16[1,192,4096]{2,1,0:T(8,128)(2,1)S(1)} %copy-done, bf16[1,192,4096]{2,1,0:T(8,128)(2,1)S(1)} %copy-done.1, f32[1,4096]{1,0:T(1,128)S(1)} %bitcast.23, ...), custom_call_target="tpu_custom_call", output_to_operand_aliasing={{2}: (8, {})} | custom-call | flops 100663296 | bytes 6823936 | tf_op jit(solution)/shard_map/delta_own/pallas_call | solution.py:307
  88.2 3.8 %all-to-all-start.2 = ((f32[16,128,128]{2,1,0:T(8,128)}), f32[16,128,128]{2,1,0:T(8,128)S(1)}, u32[]{:S(2)}, u32[]{:S(2)}) async-start(f32[16,128,128]{2,1,0:T(8,128)} %chip_moment.1), calls=%async_computation.2 | async-start | bytes 2097152 | tf_op jit(solution)/shard_map/all_to_all | solution.py:391
  92.1 2.9 %collective-permute-start.6 = (f32[8,128]{1,0:T(8,128)S(1)}, f32[8,128]{1,0:T(8,128)S(1)}, u32[]{:S(2)}, u32[]{:S(2)}) collective-permute-start(f32[8,128]{1,0:T(8,128)S(1)} %get-tuple-element.95), channel_id=1, source_target_pairs={{0,192},{64,128},{128,64},{192,0},{1,193},{65,129},{129,65},{193,1... | collective-permute-start | bytes 12296 | tf_op jit(solution)/shard_map/ppermute | solution.py:507
  95.7 8.7 %backward_inside.2 = (bf16[1,192,4096]{2,1,0:T(8,128)(2,1)}, f32[192,2048]{1,0:T(8,128)}, f32[192,2048]{1,0:T(8,128)}) custom-call(s32[3]{0:T(128)S(1)} %pad_add_fusion.c_ref, bf16[192,2048]{1,0:T(8,128)(2,1)} %copy-done.14, bf16[1,192,4096]{2,1,0:T(8,128)(2,1)} %q_ref.13, bf16[1,192,4096]{2,1,0:T(8,128)(2,1)} %k_ref.15, bf16[1,192,4096]{2,1,0:T(8,128)(2,1)} %v_ref.15, ...), custom_call_target="tpu_custom_call" | custom-call | flops 805306368 | bytes 12476416 | tf_op jit(solution)/shard_map/backward_inside/pallas_call | solution.py:307
  104.4 5.5 %all-to-all-done.2.m_ref = f32[16,128,128]{2,1,0:T(8,128)S(1)} async-done(((f32[16,128,128]{2,1,0:T(8,128)}), f32[16,128,128]{2,1,0:T(8,128)S(1)}, u32[]{:S(2)}, u32[]{:S(2)}) %all-to-all-start.2) | async-done | bytes 1048608 | tf_op jit(solution)/shard_map/all_to_all | solution.py:391
  110.5 5.4 %collective-permute-start.7 = (f32[136,128]{1,0:T(8,128)S(1)}, f32[136,128]{1,0:T(8,128)S(1)}, u32[]{:S(2)}, u32[]{:S(2)}) collective-permute-start(f32[136,128]{1,0:T(8,128)S(1)} %half_total.3), channel_id=1, source_target_pairs={{0,32},{32,0},{1,33},{33,1},{2,34},{34,2},{3,35},{35,3},{4,36},{36... | collective-permute-start | bytes 208904 | tf_op jit(solution)/shard_map/ppermute | solution.py:407
  119.4 3.7 %all-to-all-start.3 = ((f32[16,136,128]{2,1,0:T(8,128)}), f32[16,136,128]{2,1,0:T(8,128)S(1)}, u32[]{:S(2)}, u32[]{:S(2)}) async-start(f32[16,136,128]{2,1,0:T(8,128)} %chip_scan.3), calls=%async_computation.3 | async-start | bytes 2228224 | tf_op jit(solution)/shard_map/all_to_all | solution.py:391
  123.1 8.7 %backward_inside.3 = (bf16[1,192,4096]{2,1,0:T(8,128)(2,1)}, f32[192,2048]{1,0:T(8,128)}, f32[192,2048]{1,0:T(8,128)}) custom-call(s32[3]{0:T(128)S(1)} %pad_add_fusion.c_ref, bf16[192,2048]{1,0:T(8,128)(2,1)} %copy-done.13, bf16[1,192,4096]{2,1,0:T(8,128)(2,1)} %q_ref.13, bf16[1,192,4096]{2,1,0:T(8,128)(2,1)} %k_ref.15, ...), custom_call_target="tpu_custom_call", output_to_operand_aliasing={{0}: (8, {})} | custom-call | flops 805306368 | bytes 14049280 | tf_op jit(solution)/shard_map/backward_inside/pallas_call | solution.py:307
  131.8 6.6 %all-to-all-done.3.d_ref.rest_0_ = f32[16,136,128]{2,1,0:T(8,128)S(1)} async-done(((f32[16,136,128]{2,1,0:T(8,128)}), f32[16,136,128]{2,1,0:T(8,128)S(1)}, u32[]{:S(2)}, u32[]{:S(2)}) %all-to-all-start.3) | async-done | bytes 1114144 | tf_op jit(solution)/shard_map/all_to_all | solution.py:391
  138.4 3.0 %onward_back.1 = (f32[16,128,128]{2,1,0:T(8,128)}, f32[16,128,128]{2,1,0:T(8,128)S(1)}, f32[8,128]{1,0:T(8,128)S(1)}) custom-call(s32[3]{0:T(128)S(1)} %pad_add_fusion.c_ref, f32[16,136,128]{2,1,0:T(8,128)S(1)} %all-to-all-done.3.d_ref.rest_0_, f32[16,128,128]{2,1,0:T(8,128)} %copy-done.3, f32[16,128,128]{2,1,0:T(8,128)} %copy-done.2, ...), custom_call_target="tpu_custom_call" | custom-call | bytes 6557696 | tf_op jit(solution)/shard_map/onward_back/pallas_call | solution.py:307
  141.4 3.4 %collective-permute-start.8 = (f32[16,128,128]{2,1,0:T(8,128)}, f32[16,128,128]{2,1,0:T(8,128)S(1)}, u32[]{:S(2)}, u32[]{:S(2)}) collective-permute-start(f32[16,128,128]{2,1,0:T(8,128)} %get-tuple-element.85), channel_id=1, source_target_pairs={{0,1},{1,0},{2,3},{3,2},{4,5},{5,4},{6,7},{7,6},{8,9},{9,8},{10,11... | collective-permute-start | bytes 3145736 | tf_op jit(solution)/shard_map/ppermute | solution.py:387
  144.8 5.6 %finish.2 = (bf16[1,192,4096]{2,1,0:T(8,128)(2,1)}, bf16[1,192,4096]{2,1,0:T(8,128)(2,1)}) custom-call(s32[3]{0:T(128)S(1)} %pad_add_fusion.c_ref, bf16[1,192,4096]{2,1,0:T(8,128)(2,1)} %k_ref.15, bf16[1,192,4096]{2,1,0:T(8,128)(2,1)} %v_ref.15, f32[32,192]{1,0:T(8,128)S(1)} %copy-done.10, f32[192,2048]{1,0:T(8,128)} %get-tuple-element.86.ki_ref, ...), custom_call_target="tpu_custom_call" | custom-call | flops 402653184 | bytes 10510336 | tf_op jit(solution)/shard_map/finish/pallas_call | solution.py:307
  151.0 5.6 %finish.3 = (bf16[1,192,4096]{2,1,0:T(8,128)(2,1)}, bf16[1,192,4096]{2,1,0:T(8,128)(2,1)}) custom-call(s32[3]{0:T(128)S(1)} %pad_add_fusion.c_ref, bf16[1,192,4096]{2,1,0:T(8,128)(2,1)} %k_ref.15, bf16[1,192,4096]{2,1,0:T(8,128)(2,1)} %v_ref.15, f32[32,192]{1,0:T(8,128)S(1)} %copy-done.10, ...), custom_call_target="tpu_custom_call", output_to_operand_aliasing={{0}: (7, {}), {1}: (8, {})} | custom-call | flops 402653184 | bytes 13656064 | tf_op jit(solution)/shard_map/finish/pallas_call | solution.py:307
  (64 shorter events, 20.2 us)
Async XLA Ops:
  6.4 8.1 %copy-start.8 = (f32[32,192]{1,0:T(8,128)}, f32[32,192]{1,0:T(8,128)S(1)}, u32[]{:S(2)}) copy-start(f32[32,192]{1,0:T(8,128)S(1)} %get-tuple-element.49.row_ref) | copy-start | bytes 73732
  6.4 8.1 %collective-permute-start = (f32[16,136,128]{2,1,0:T(8,128)S(1)}, f32[16,136,128]{2,1,0:T(8,128)S(1)}, u32[]{:S(2)}, u32[]{:S(2)}) collective-permute-start(f32[16,136,128]{2,1,0:T(8,128)S(1)} %get-tuple-element.51), channel_id=1, source_target_pairs={{0,1},{1,0},{2,3},{3,2},{4,5},{5,4},{6,7},{7,6},{8,9},{9,8},{10,11... | collective-permute-start | bytes 3342344 | tf_op jit(solution)/shard_map/ppermute | solution.py:387
  16.2 22.8 %all-to-all-start = ((f32[16,136,128]{2,1,0:T(8,128)}), f32[16,136,128]{2,1,0:T(8,128)S(1)}, u32[]{:S(2)}, u32[]{:S(2)}) async-start(f32[16,136,128]{2,1,0:T(8,128)} %get-tuple-element.53), calls=%async_computation | async-start | bytes 2228224 | tf_op jit(solution)/shard_map/all_to_all | solution.py:391
  39.7 8.7 %collective-permute-start.1 = (f32[128,128]{1,0:T(8,128)S(1)}, f32[128,128]{1,0:T(8,128)S(1)}, u32[]{:S(2)}, u32[]{:S(2)}) collective-permute-start(f32[128,128]{1,0:T(8,128)S(1)} %half_total.2), channel_id=1, source_target_pairs={{0,32},{32,0},{1,33},{33,1},{2,34},{34,2},{3,35},{35,3},{4,36},{36... | collective-permute-start | bytes 196616 | tf_op jit(solution)/shard_map/ppermute | solution.py:407
  48.4 24.5 %copy-start.12 = (f32[192,2048]{1,0:T(8,128)S(1)}, f32[192,2048]{1,0:T(8,128)}, u32[]{:S(2)}) copy-start(f32[192,2048]{1,0:T(8,128)} %get-tuple-element.61.in_ref) | copy-start | bytes 4718596
  50.1 18.0 %copy-start.6 = (f32[16,128,128]{2,1,0:T(8,128)S(1)}, f32[16,128,128]{2,1,0:T(8,128)}, u32[]{:S(2)}) copy-start(f32[16,128,128]{2,1,0:T(8,128)} %copy-done.5) | copy-start | bytes 3145732
  68.1 4.8 %copy-start = (bf16[1,192,4096]{2,1,0:T(8,128)(2,1)S(1)}, bf16[1,192,4096]{2,1,0:T(8,128)(2,1)}, u32[]{:S(2)}) copy-start(bf16[1,192,4096]{2,1,0:T(8,128)(2,1)} %q_ref.13) | copy-start | bytes 4718596
  68.1 4.8 %copy-start.1 = (bf16[1,192,4096]{2,1,0:T(8,128)(2,1)S(1)}, bf16[1,192,4096]{2,1,0:T(8,128)(2,1)}, u32[]{:S(2)}) copy-start(bf16[1,192,4096]{2,1,0:T(8,128)(2,1)} %g_ref.5) | copy-start | bytes 4718596
  68.1 4.8 %copy-start.9 = (f32[32,192]{1,0:T(8,128)S(1)}, f32[32,192]{1,0:T(8,128)}, u32[]{:S(2)}) copy-start(f32[32,192]{1,0:T(8,128)} %copy-done.8) | copy-start | bytes 73732
  68.1 4.8 %copy-start.15 = (f32[4096]{0:T(1024)S(1)}, f32[4096]{0:T(1024)}, u32[]{:S(2)}) copy-start(f32[4096]{0:T(1024)} %param.11) | copy-start | bytes 49156
  69.1 5.8 %copy-start.7 = (f32[16,128,128]{2,1,0:T(8,128)}, f32[16,128,128]{2,1,0:T(8,128)S(1)}, u32[]{:S(2)}) copy-start(f32[16,128,128]{2,1,0:T(8,128)S(1)} %get-tuple-element.62.x_ref.i_ref) | copy-start | bytes 3145732
  69.1 6.1 %collective-permute-start.2 = (f32[16,128,128]{2,1,0:T(8,128)S(1)}, f32[16,128,128]{2,1,0:T(8,128)S(1)}, u32[]{:S(2)}, u32[]{:S(2)}) collective-permute-start(f32[16,128,128]{2,1,0:T(8,128)S(1)} %get-tuple-element.60), channel_id=1, source_target_pairs={{0,1},{1,0},{2,3},{3,2},{4,5},{5,4},{6,7},{7,6},{8,9},{9,8},{10,11... | collective-permute-start | bytes 3145736 | tf_op jit(solution)/shard_map/ppermute | solution.py:387
  75.2 4.6 %copy-start.4 = (f32[16,128,128]{2,1,0:T(8,128)}, f32[16,128,128]{2,1,0:T(8,128)S(1)}, u32[]{:S(2)}) copy-start(f32[16,128,128]{2,1,0:T(8,128)S(1)} %collective-permute-done.2.i_ref) | copy-start | bytes 3145732
  80.7 4.8 %collective-permute-start.3 = (f32[16,128,128]{2,1,0:T(8,128)S(1)}, f32[16,128,128]{2,1,0:T(8,128)S(1)}, u32[]{:S(2)}, u32[]{:S(2)}) collective-permute-start(f32[16,128,128]{2,1,0:T(8,128)S(1)} %get-tuple-element.76), channel_id=1, source_target_pairs={{0,1},{1,0},{2,3},{3,2},{4,5},{5,4},{6,7},{7,6},{8,9},{9,8},{10,11... | collective-permute-start | bytes 3145736 | tf_op jit(solution)/shard_map/ppermute | solution.py:387
  88.2 3.8 %copy-start.17 = (f32[4,8,128]{2,1,0:T(8,128)S(1)}, f32[4,8,128]{2,1,0:T(8,128)}, u32[]{:S(2)}) copy-start(f32[4,8,128]{2,1,0:T(8,128)} %get-tuple-element.80) | copy-start | bytes 49156
  88.2 21.7 %all-to-all-start.2 = ((f32[16,128,128]{2,1,0:T(8,128)}), f32[16,128,128]{2,1,0:T(8,128)S(1)}, u32[]{:S(2)}, u32[]{:S(2)}) async-start(f32[16,128,128]{2,1,0:T(8,128)} %chip_moment.1), calls=%async_computation.2 | async-start | bytes 2097152 | tf_op jit(solution)/shard_map/all_to_all | solution.py:391
  92.1 12.3 %collective-permute-start.6 = (f32[8,128]{1,0:T(8,128)S(1)}, f32[8,128]{1,0:T(8,128)S(1)}, u32[]{:S(2)}, u32[]{:S(2)}) collective-permute-start(f32[8,128]{1,0:T(8,128)S(1)} %get-tuple-element.95), channel_id=1, source_target_pairs={{0,192},{64,128},{128,64},{192,0},{1,193},{65,129},{129,65},{193,1... | collective-permute-start | bytes 12296 | tf_op jit(solution)/shard_map/ppermute | solution.py:507
  95.0 9.4 %collective-permute-start.5 = (f32[8,128]{1,0:T(8,128)S(1)}, f32[8,128]{1,0:T(8,128)S(1)}, u32[]{:S(2)}, u32[]{:S(2)}) collective-permute-start(f32[8,128]{1,0:T(8,128)S(1)} %get-tuple-element.96), channel_id=1, source_target_pairs={{0,128},{64,192},{128,0},{192,64},{1,129},{65,193},{129,1},{193,65... | collective-permute-start | bytes 12296 | tf_op jit(solution)/shard_map/ppermute | solution.py:507
  95.0 9.4 %collective-permute-start.4 = (f32[8,128]{1,0:T(8,128)S(1)}, f32[8,128]{1,0:T(8,128)S(1)}, u32[]{:S(2)}, u32[]{:S(2)}) collective-permute-start(f32[8,128]{1,0:T(8,128)S(1)} %get-tuple-element.94), channel_id=1, source_target_pairs={{0,64},{64,0},{128,192},{192,128},{1,65},{65,1},{129,193},{193,129... | collective-permute-start | bytes 12296 | tf_op jit(solution)/shard_map/ppermute | solution.py:507
  110.5 7.2 %collective-permute-start.7 = (f32[136,128]{1,0:T(8,128)S(1)}, f32[136,128]{1,0:T(8,128)S(1)}, u32[]{:S(2)}, u32[]{:S(2)}) collective-permute-start(f32[136,128]{1,0:T(8,128)S(1)} %half_total.3), channel_id=1, source_target_pairs={{0,32},{32,0},{1,33},{33,1},{2,34},{34,2},{3,35},{35,3},{4,36},{36... | collective-permute-start | bytes 208904 | tf_op jit(solution)/shard_map/ppermute | solution.py:407
  119.4 19.1 %all-to-all-start.3 = ((f32[16,136,128]{2,1,0:T(8,128)}), f32[16,136,128]{2,1,0:T(8,128)S(1)}, u32[]{:S(2)}, u32[]{:S(2)}) async-start(f32[16,136,128]{2,1,0:T(8,128)} %chip_scan.3), calls=%async_computation.3 | async-start | bytes 2228224 | tf_op jit(solution)/shard_map/all_to_all | solution.py:391
  138.4 6.4 %copy-start.10 = (f32[32,192]{1,0:T(8,128)S(1)}, f32[32,192]{1,0:T(8,128)}, u32[]{:S(2)}) copy-start(f32[32,192]{1,0:T(8,128)} %copy-done.8) | copy-start | bytes 73732
  141.4 9.6 %collective-permute-start.8 = (f32[16,128,128]{2,1,0:T(8,128)}, f32[16,128,128]{2,1,0:T(8,128)S(1)}, u32[]{:S(2)}, u32[]{:S(2)}) collective-permute-start(f32[16,128,128]{2,1,0:T(8,128)} %get-tuple-element.85), channel_id=1, source_target_pairs={{0,1},{1,0},{2,3},{3,2},{4,5},{5,4},{6,7},{7,6},{8,9},{9,8},{10,11... | collective-permute-start | bytes 3145736 | tf_op jit(solution)/shard_map/ppermute | solution.py:387
  144.8 5.6 %collective-permute-start.9 = (f32[8,128]{1,0:T(8,128)S(1)}, f32[8,128]{1,0:T(8,128)S(1)}, u32[]{:S(2)}, u32[]{:S(2)}) collective-permute-start(f32[8,128]{1,0:T(8,128)S(1)} %get-tuple-element.93), channel_id=1, source_target_pairs={{0,1},{1,0},{2,3},{3,2},{4,5},{5,4},{6,7},{7,6},{8,9},{9,8},{10,11... | collective-permute-start | bytes 12296 | tf_op jit(solution)/shard_map/ppermute | solution.py:387
  (7 other events, 9.3 us)

commit v5 on v4

--- a/solution.py
+++ b/solution.py
@@ -15,7 +15,7 @@
 T = 192
 HD = 128
 GH = 8
-FH = 4
+FH = 8
 GW = GH * HD
 NG = 4
 HALF = NG // 2
@@ -84,7 +84,7 @@
         s_ref[j, :HD, :] = state
         s_ref[j, HD:, :] = log
 
-    group = (1 - c_ref[0]) * HALF + i // 2
+    group = (1 - c_ref[0]) * HALF + i
     states_of(k_ref, v_ref, row_ref.at[pl.ds(pl.multiple_of(group * GH, GH), GH)], store)
 
 
@@ -252,11 +252,12 @@
 
 
 def delta_own_kernel(
-    c_ref, q_ref, g_ref, gain_ref, row_ref, att_ref, inv_ref, mean_ref, gt_in, od_ref, m_ref, gt_ref
+    c_ref, q_ref, g_ref, gain_ref, row_ref, att_ref, inv_ref, mean_ref, od_ref, m_ref, gt_ref, kept_ref
 ):
     delta_group(
         q_ref, g_ref, gain_ref, columns(row_ref), att_ref, inv_ref[...], mean_ref[...], od_ref, m_ref, gt_ref
     )
+    kept_ref[...] = m_ref[...]
 
 
 def backward_kernel(
@@ -298,12 +299,10 @@
 
 
 def call(
-    kernel, name, grid, in_specs, out_specs, out_shape, args, flops, scratch=(), aliases=None, kept=False
+    kernel, name, grid, in_specs, out_specs, out_shape, args, flops, scratch=(), aliases=None
 ):
     place, *args = args
     nbytes = sum(math.prod(a.shape) * a.dtype.itemsize for a in [*args, *out_shape])
-    if kept:
-        args, out_shape = [Kept(a) for a in args], [Kept(s) for s in out_shape]
     return pl.pallas_call(
         kernel,
         name=name,
@@ -356,11 +355,8 @@
     return pl.BlockSpec((GH, T), lambda i, c: (half_of(own, c) * HALF + group(i), 0))
 
 
-def gains_block(own, group=lambda i: i):
-    return pl.BlockSpec(
-        (None, GH, HD),
-        lambda i, c: (jnp.bitwise_xor(half_of(own, c) * HALF + group(i), c[1]), 0, 0),
-    )
+def gains_block(group=lambda i: i):
+    return pl.BlockSpec((None, GH, HD), lambda i, c: (jnp.bitwise_xor(group(i), c[1] % 2), 0, 0))
 
 
 def state_block(rows=HD, group=lambda i: i):
@@ -378,7 +374,7 @@
 HALF_BF16 = shape((T, HALF * GW), BF16)
 WHOLE_BF16 = shape((1, T, NG * GW), BF16)
 STAT = shape((T, HD))
-GAINS = shape((NG, GH, HD))
+GAINS = shape((HALF, GH, HD))
 MM = 2 * T * HD * HD * NC
 SM = 2 * T * T * HD * NC
 
@@ -428,7 +424,7 @@
     got = swap_cores(sent)
     own, log_own = call(
         state_second_kernel, "states_own", (NC // FH,),
-        [fine(True), fine(True), row_block(True, lambda i: i // 2)], [fine_block(), fine_block(8)],
+        [fine(True), fine(True), row_block(True)], [fine_block(), fine_block(8)],
         [STATES, LOGS],
         (core, Kept(k), Kept(v), row), MM,
     )
@@ -446,8 +442,8 @@
             forward_kernel, "forward_inside", (HALF,),
             [wide(mine), wide(mine), wide(mine), row_block(mine)],
             [pl.BlockSpec((GH, T, T), lambda i, c: (i, 0, 0)), narrow()],
-            [shape((NC, T, T), BF16), HALF_F32],
-            (core, q, k, v, row), 2 * SM, kept=True,
+            [Kept(shape((NC, T, T), BF16)), Kept(HALF_F32)],
+            (core, Kept(q), Kept(k), Kept(v), row), 2 * SM,
         )
 
     gathered, inside[True], inside[False] = lax.optimization_barrier(
@@ -477,23 +473,22 @@
     def second(i):
         return jnp.minimum(2 * HALF - 1 - i, HALF - 1)
 
-    delta_other, moment_sent, gains, inverse, mean = call(
+    delta_other, moment_sent, gains_other, inverse, mean = call(
         attend_other_kernel, "attend_other", (2 * HALF,),
         [wide(False, turn), wide(False, turn), gain_block(False, turn), row_block(False, turn), narrow(first),
          state_block(HD, first), STAT_WHOLE, STAT_WHOLE],
-        [narrow(second), state_block(HD, second), gains_block(False, second), STAT_WHOLE, STAT_WHOLE],
-        [HALF_BF16, STATES, Kept(GAINS), STAT, STAT],
+        [narrow(second), state_block(HD, second), gains_block(second), STAT_WHOLE, STAT_WHOLE],
+        [Kept(HALF_BF16), STATES, GAINS, STAT, STAT],
         (core, q, g, gain, row, inside[False], state_other, squares, products), 3 * MM,
         scratch=[pltpu.VMEM((HALF, T, GW), F32), pltpu.VMEM((T, HD), F32), pltpu.VMEM((T, HD), F32)],
     )
     moment_got = swap_cores(moment_sent)
-    delta_own, moment_own, gains = call(
+    delta_own, moment_own, gains_own, moment_kept = call(
         delta_own_kernel, "delta_own", (HALF,),
-        [wide(True), wide(True), gain_block(True), row_block(True), narrow(), STAT_WHOLE, STAT_WHOLE, ANY],
-        [narrow(), state_block(), gains_block(True)],
-        [HALF_BF16, STATES, Kept(GAINS)],
-        (core, q, g, gain, row, att_own, inverse, mean, Kept(gains)), MM,
-        aliases={8: 2},
+        [wide(True), wide(True), gain_block(True), row_block(True), narrow(), STAT_WHOLE, STAT_WHOLE],
+        [narrow(), state_block(), gains_block(), state_block()],
+        [Kept(HALF_BF16), STATES, GAINS, Kept(STATES)],
+        (core, q, g, gain, row, att_own, inverse, mean), MM,
     )
     (chip_moment,) = call(
         functools.partial(combine_kernel, False), "chip_moment", (HALF,),
@@ -502,6 +497,8 @@
     )
     gathered_back = chips_all_to_all(chip_moment)
 
+    near = core[0] == core[1] // 2
+    gains = [*jnp.where(near, gains_own, gains_other), *jnp.where(near, gains_other, gains_own)]
     collected = gains[0]
     for distance in range(1, NG):
         collected += lax.ppermute(gains[distance], "dp", [(i, i ^ distance) for i in range(NG)])
@@ -516,9 +513,10 @@
              pl.BlockSpec((GH, T, T), lambda i, c: (i, 0, 0)), row_block(mine), state_block()]
             + [ANY] * len(query_grad),
             [wide(mine), narrow(), narrow()],
-            [WHOLE_BF16, HALF_F32, HALF_F32],
-            (core, delta[mine], q, k, v, weights[mine], row, state[mine], *query_grad),
-            4 * SM + 2 * MM, aliases={8: 0} if query_grad else None, kept=True,
+            [Kept(WHOLE_BF16), Kept(HALF_F32), Kept(HALF_F32)],
+            (core, Kept(delta[mine]), Kept(q), Kept(k), Kept(v), Kept(weights[mine]), row, state[mine],
+             *[Kept(a) for a in query_grad]),
+            4 * SM + 2 * MM, aliases={8: 0} if query_grad else None,
         )
 
     gathered_back, key_inside[True] = lax.optimization_barrier((gathered_back, key_inside[True]))
@@ -530,7 +528,7 @@
         [state_block()] * 3 + [LOG_BLOCK] * 2 + [LOG_TAIL],
         [state_block(), state_block(), pl.BlockSpec((8, HD), lambda i, c: (0, 0))],
         [STATES, STATES, shape((8, HD))],
-        (core, scanned_back, Kept(moment_own), Kept(moment_got), log_own,
+        (core, scanned_back, Kept(moment_kept), Kept(moment_got), log_own,
          log_got, scanned_back), 0,
     )
     later_other = swap_cores(onward_back)
@@ -539,7 +537,7 @@
     for mine in (True, False):
         grads = call(
             finish_kernel, "finish", (NC // FH,),
-            [fine(mine), fine(mine), row_block(mine, lambda i: i // 2), FINE_NARROW, FINE_NARROW,
+            [fine(mine), fine(mine), row_block(mine), FINE_NARROW, FINE_NARROW,
              fine_block()] + [ANY] * len(grads),
             [fine(mine)] * 2, [Kept(WHOLE_BF16)] * 2,
             (core, Kept(k), Kept(v), row, Kept(key_inside[mine]), Kept(value_inside[mine]),

time: 157 us -> 150 us (0.955)
  Pallas kernels: 69.3 us -> 64.8 us
  local copies, waits for them, and re-layouts: 3.66 us -> 2.04 us
    pallas_call x19, Pallas kernels: 69.3 us -> 64.8 us  [call(): pl.pallas_call(kernel, name=name, grid_spec=pltpu.PrefetchScalarGridSpec(...]
    unnamed x36 -> x26, local copies, waits for them, and re-layouts: 3.65 us -> 2.03 us
where the time goes in v5:
time: 150 us
  Pallas kernels  64.8 us (43%)
  starting transfers between devices  39.2 us (26%)
  waiting for transfers between devices  23.9 us (16%)
  blocking collectives  18 us (12%)
  local copies, waits for them, and re-layouts  2.04 us (1%)
    pallas_call x19, Pallas kernels, call(): pl.pallas_call(kernel, name=name, grid_spec=pltpu.PrefetchScalarGridSpec(...  64.8 us
    all_to_all x3, waiting for transfers between devices, chips_all_to_all(): lax.all_to_all(values, ('x', 'y'), split_axis=0, concat_axis=0, tiled=True)  20.1 us
    all_to_all x1, blocking collectives, chips_all_to_all(): lax.all_to_all(values, ('x', 'y'), split_axis=0, concat_axis=0, tiled=True)  18 us
    all_to_all x3, starting transfers between devices, chips_all_to_all(): lax.all_to_all(values, ('x', 'y'), split_axis=0, concat_axis=0, tiled=True)  12.5 us
    ppermute x2, starting transfers between devices, scan_over_chips(): before = lax.ppermute(total, 'zh', [(0, 1), (1, 0)])  12.4 us
    ppermute x5, starting transfers between devices, swap_cores(): return lax.ppermute(values, 'core', [(0, 1), (1, 0)])  11.1 us
    ppermute x2, waiting for transfers between devices, scan_over_chips(): before = lax.ppermute(total, 'zh', [(0, 1), (1, 0)])  3.55 us
    ppermute x3, starting transfers between devices, per_device(): lax.ppermute(gains[distance], 'dp', [(i, i ^ distance) for i in range(NG)])  3.2 us
  transfers between devices with their start and end apart: 13, of which 6 were waited for; matrix products, arithmetic and copies ran while one was open for 0% of the time, Pallas kernels for 27%

profile of v5, /device:TPU:1, one launch (start us, length us, event | category | flops | bytes accessed | tf_op | source)
XLA Modules:
  0.0 149.6 jit_solution(37884238529816295)
XLA Ops:
  1.5 4.0 %states_other.1 = (f32[16,136,128]{2,1,0:T(8,128)S(1)}, f32[32,192]{1,0:T(8,128)S(1)}) custom-call(s32[3]{0:T(128)S(1)} %pad_add_fusion.c_ref, bf16[1,192,4096]{2,1,0:T(8,128)(2,1)} %k_ref.15, bf16[1,192,4096]{2,1,0:T(8,128)(2,1)} %v_ref.15, f32[32,192]{1,0:T(8,128)S(1)} %bitcast.26), custom_call_target="tpu_custom_call" | custom-call | flops 100663296 | bytes 4308992 | tf_op jit(solution)/shard_map/states_other/pallas_call | solution.py:306
  5.4 3.3 %collective-permute-start = (f32[16,136,128]{2,1,0:T(8,128)S(1)}, f32[16,136,128]{2,1,0:T(8,128)S(1)}, u32[]{:S(2)}, u32[]{:S(2)}) collective-permute-start(f32[16,136,128]{2,1,0:T(8,128)S(1)} %get-tuple-element.52), channel_id=1, source_target_pairs={{0,1},{1,0},{2,3},{3,2},{4,5},{5,4},{6,7},{7,6},{8,9},{9,8},{10,11... | collective-permute-start | bytes 3342344 | tf_op jit(solution)/shard_map/ppermute | solution.py:383
  8.8 3.7 %states_own.1 = (f32[16,128,128]{2,1,0:T(8,128)S(1)}, f32[16,8,128]{2,1,0:T(8,128)S(1)}) custom-call(s32[3]{0:T(128)S(1)} %pad_add_fusion.c_ref, bf16[1,192,4096]{2,1,0:T(8,128)(2,1)} %k_ref.15, bf16[1,192,4096]{2,1,0:T(8,128)(2,1)} %v_ref.15, f32[32,192]{1,0:T(8,128)S(1)} %get-tuple-element.50.row_ref), custom_call_target="tpu_custom_call" | custom-call | flops 100663296 | bytes 4284416 | tf_op jit(solution)/shard_map/states_own/pallas_call | solution.py:306
  14.3 5.0 %all-to-all-start = ((f32[16,136,128]{2,1,0:T(8,128)}), f32[16,136,128]{2,1,0:T(8,128)S(1)}, u32[]{:S(2)}, u32[]{:S(2)}) async-start(f32[16,136,128]{2,1,0:T(8,128)} %get-tuple-element.54), calls=%async_computation | async-start | bytes 2228224 | tf_op jit(solution)/shard_map/all_to_all | solution.py:387
  19.3 4.7 %forward_inside.2 = (bf16[16,192,192]{2,1,0:T(8,128)(2,1)}, f32[192,2048]{1,0:T(8,128)}) custom-call(s32[3]{0:T(128)S(1)} %pad_add_fusion.c_ref, bf16[1,192,4096]{2,1,0:T(8,128)(2,1)} %q_ref.13, bf16[1,192,4096]{2,1,0:T(8,128)(2,1)} %k_ref.15, bf16[1,192,4096]{2,1,0:T(8,128)(2,1)} %v_ref.15, f32[32,192]{1,0:T(8,128)S(1)} %get-tuple-element.50.row_ref), custom_call_target="tpu_custom_call" | custom-call | flops 301989888 | bytes 7495680 | tf_op jit(solution)/shard_map/forward_inside/pallas_call | solution.py:306
  24.0 4.7 %forward_inside.3 = (bf16[16,192,192]{2,1,0:T(8,128)(2,1)}, f32[192,2048]{1,0:T(8,128)}) custom-call(s32[3]{0:T(128)S(1)} %pad_add_fusion.c_ref, bf16[1,192,4096]{2,1,0:T(8,128)(2,1)} %q_ref.13, bf16[1,192,4096]{2,1,0:T(8,128)(2,1)} %k_ref.15, bf16[1,192,4096]{2,1,0:T(8,128)(2,1)} %v_ref.15, f32[32,192]{1,0:T(8,128)S(1)} %get-tuple-element.50.row_ref), custom_call_target="tpu_custom_call" | custom-call | flops 301989888 | bytes 7495680 | tf_op jit(solution)/shard_map/forward_inside/pallas_call | solution.py:306
  28.7 8.4 %all-to-all-done.m_ref.l_ref = f32[16,136,128]{2,1,0:T(8,128)S(1)} async-done(((f32[16,136,128]{2,1,0:T(8,128)}), f32[16,136,128]{2,1,0:T(8,128)S(1)}, u32[]{:S(2)}, u32[]{:S(2)}) %all-to-all-start) | async-done | bytes 1114144 | tf_op jit(solution)/shard_map/all_to_all | solution.py:387
  37.8 7.0 %collective-permute-start.1 = (f32[128,128]{1,0:T(8,128)S(1)}, f32[128,128]{1,0:T(8,128)S(1)}, u32[]{:S(2)}, u32[]{:S(2)}) collective-permute-start(f32[128,128]{1,0:T(8,128)S(1)} %half_total.2), channel_id=1, source_target_pairs={{0,32},{32,0},{1,33},{33,1},{2,34},{34,2},{3,35},{35,3},{4,36},{36... | collective-permute-start | bytes 196616 | tf_op jit(solution)/shard_map/ppermute | solution.py:403
  48.1 18.0 %all_to_all.20.d_ref = f32[16,128,128]{2,1,0:T(8,128)S(1)} all-to-all(f32[16,128,128]{2,1,0:T(8,128)} %get-tuple-element.59), channel_id=1, replica_groups=mesh['dp'=4,'zh'=2,'x'=4,'y'=4,'core'=2] {'x','y'}, dimensions={0} | all-to-all | bytes 2097152 | tf_op jit(solution)/shard_map/all_to_all | solution.py:387
  67.1 3.8 %collective-permute-start.2 = (f32[16,128,128]{2,1,0:T(8,128)S(1)}, f32[16,128,128]{2,1,0:T(8,128)S(1)}, u32[]{:S(2)}, u32[]{:S(2)}) collective-permute-start(f32[16,128,128]{2,1,0:T(8,128)S(1)} %get-tuple-element.61), channel_id=1, source_target_pairs={{0,1},{1,0},{2,3},{3,2},{4,5},{5,4},{6,7},{7,6},{8,9},{9,8},{10,11... | collective-permute-start | bytes 3145736 | tf_op jit(solution)/shard_map/ppermute | solution.py:383
  71.0 2.0 %attend_own.1 = (f32[192,2048]{1,0:T(8,128)S(1)}, f32[192,128]{1,0:T(8,128)S(1)}, f32[192,128]{1,0:T(8,128)S(1)}) custom-call(s32[3]{0:T(128)S(1)} %pad_add_fusion.c_ref, bf16[1,192,4096]{2,1,0:T(8,128)(2,1)S(1)} %copy-done, bf16[1,192,4096]{2,1,0:T(8,128)(2,1)S(1)} %copy-done.1, f32[1,4096]{1,0:T(1,128)S(1)} %bitcast.23, ...), custom_call_target="tpu_custom_call" | custom-call | flops 201326592 | bytes 7577600 | tf_op jit(solution)/shard_map/attend_own/pallas_call | solution.py:306
  73.2 4.7 %attend_other.1 = (bf16[192,2048]{1,0:T(8,128)(2,1)}, f32[16,128,128]{2,1,0:T(8,128)S(1)}, f32[2,8,128]{2,1,0:T(8,128)S(1)}, f32[192,128]{1,0:T(8,128)S(1)}, f32[192,128]{1,0:T(8,128)S(1)}) custom-call(s32[3]{0:T(128)S(1)} %pad_add_fusion.c_ref, bf16[1,192,4096]{2,1,0:T(8,128)(2,1)S(1)} %copy-done, bf16[1,192,4096]{2,1,0:T(8,128)(2,1)S(1)} %copy-done.1, ...), custom_call_target="tpu_custom_call" | custom-call | flops 301989888 | bytes 8044544 | tf_op jit(solution)/shard_map/attend_other/pallas_call | solution.py:306
  78.5 3.5 %delta_own.1 = (bf16[192,2048]{1,0:T(8,128)(2,1)}, f32[16,128,128]{2,1,0:T(8,128)S(1)}, f32[2,8,128]{2,1,0:T(8,128)S(1)}, f32[16,128,128]{2,1,0:T(8,128)}) custom-call(s32[3]{0:T(128)S(1)} %pad_add_fusion.c_ref, bf16[1,192,4096]{2,1,0:T(8,128)(2,1)S(1)} %copy-done, bf16[1,192,4096]{2,1,0:T(8,128)(2,1)S(1)} %copy-done.1, f32[1,4096]{1,0:T(1,128)S(1)} %bitcast.25, ...), custom_call_target="tpu_custom_call" | custom-call | flops 100663296 | bytes 7847936 | tf_op jit(solution)/shard_map/delta_own/pallas_call | solution.py:306
  83.6 3.7 %all-to-all-start.2 = ((f32[16,128,128]{2,1,0:T(8,128)}), f32[16,128,128]{2,1,0:T(8,128)S(1)}, u32[]{:S(2)}, u32[]{:S(2)}) async-start(f32[16,128,128]{2,1,0:T(8,128)} %chip_moment.1), calls=%async_computation.2 | async-start | bytes 2097152 | tf_op jit(solution)/shard_map/all_to_all | solution.py:387
  91.8 8.5 %backward_inside.2 = (bf16[1,192,4096]{2,1,0:T(8,128)(2,1)}, f32[192,2048]{1,0:T(8,128)}, f32[192,2048]{1,0:T(8,128)}) custom-call(s32[3]{0:T(128)S(1)} %pad_add_fusion.c_ref, bf16[192,2048]{1,0:T(8,128)(2,1)} %get-tuple-element.71.od_ref, bf16[1,192,4096]{2,1,0:T(8,128)(2,1)} %q_ref.13, bf16[1,192,4096]{2,1,0:T(8,128)(2,1)} %k_ref.15, ...), custom_call_target="tpu_custom_call" | custom-call | flops 805306368 | bytes 12476416 | tf_op jit(solution)/shard_map/backward_inside/pallas_call | solution.py:306
  100.3 4.9 %all-to-all-done.2.m_ref = f32[16,128,128]{2,1,0:T(8,128)S(1)} async-done(((f32[16,128,128]{2,1,0:T(8,128)}), f32[16,128,128]{2,1,0:T(8,128)S(1)}, u32[]{:S(2)}, u32[]{:S(2)}) %all-to-all-start.2) | async-done | bytes 1048608 | tf_op jit(solution)/shard_map/all_to_all | solution.py:387
  105.8 5.4 %collective-permute-start.7 = (f32[136,128]{1,0:T(8,128)S(1)}, f32[136,128]{1,0:T(8,128)S(1)}, u32[]{:S(2)}, u32[]{:S(2)}) collective-permute-start(f32[136,128]{1,0:T(8,128)S(1)} %half_total.3), channel_id=1, source_target_pairs={{0,32},{32,0},{1,33},{33,1},{2,34},{34,2},{3,35},{35,3},{4,36},{36... | collective-permute-start | bytes 208904 | tf_op jit(solution)/shard_map/ppermute | solution.py:403
  114.6 3.8 %all-to-all-start.3 = ((f32[16,136,128]{2,1,0:T(8,128)}), f32[16,136,128]{2,1,0:T(8,128)S(1)}, u32[]{:S(2)}, u32[]{:S(2)}) async-start(f32[16,136,128]{2,1,0:T(8,128)} %chip_scan.3), calls=%async_computation.3 | async-start | bytes 2228224 | tf_op jit(solution)/shard_map/all_to_all | solution.py:387
  118.5 8.5 %backward_inside.3 = (bf16[1,192,4096]{2,1,0:T(8,128)(2,1)}, f32[192,2048]{1,0:T(8,128)}, f32[192,2048]{1,0:T(8,128)}) custom-call(s32[3]{0:T(128)S(1)} %pad_add_fusion.c_ref, bf16[192,2048]{1,0:T(8,128)(2,1)} %get-tuple-element.66.od_ref, bf16[1,192,4096]{2,1,0:T(8,128)(2,1)} %q_ref.13, ...), custom_call_target="tpu_custom_call", output_to_operand_aliasing={{0}: (8, {})} | custom-call | flops 805306368 | bytes 14049280 | tf_op jit(solution)/shard_map/backward_inside/pallas_call | solution.py:306
  127.0 6.8 %all-to-all-done.3.d_ref.rest_0_ = f32[16,136,128]{2,1,0:T(8,128)S(1)} async-done(((f32[16,136,128]{2,1,0:T(8,128)}), f32[16,136,128]{2,1,0:T(8,128)S(1)}, u32[]{:S(2)}, u32[]{:S(2)}) %all-to-all-start.3) | async-done | bytes 1114144 | tf_op jit(solution)/shard_map/all_to_all | solution.py:387
  133.8 3.0 %onward_back.1 = (f32[16,128,128]{2,1,0:T(8,128)}, f32[16,128,128]{2,1,0:T(8,128)S(1)}, f32[8,128]{1,0:T(8,128)S(1)}) custom-call(s32[3]{0:T(128)S(1)} %pad_add_fusion.c_ref, f32[16,136,128]{2,1,0:T(8,128)S(1)} %all-to-all-done.3.d_ref.rest_0_, f32[16,128,128]{2,1,0:T(8,128)} %get-tuple-element.86.own_ref, f32[16,128,128]{2,1,0:T(8,128)} %copy-done.2, ...), custom_call_target="tpu_custom_call" | custom-call | bytes 6557696 | tf_op jit(solution)/shard_map/onward_back/pallas_call | solution.py:306
  136.8 3.4 %collective-permute-start.8 = (f32[16,128,128]{2,1,0:T(8,128)}, f32[16,128,128]{2,1,0:T(8,128)S(1)}, u32[]{:S(2)}, u32[]{:S(2)}) collective-permute-start(f32[16,128,128]{2,1,0:T(8,128)} %get-tuple-element.87), channel_id=1, source_target_pairs={{0,1},{1,0},{2,3},{3,2},{4,5},{5,4},{6,7},{7,6},{8,9},{9,8},{10,11... | collective-permute-start | bytes 3145736 | tf_op jit(solution)/shard_map/ppermute | solution.py:383
  140.2 4.4 %finish.2 = (bf16[1,192,4096]{2,1,0:T(8,128)(2,1)}, bf16[1,192,4096]{2,1,0:T(8,128)(2,1)}) custom-call(s32[3]{0:T(128)S(1)} %pad_add_fusion.c_ref, bf16[1,192,4096]{2,1,0:T(8,128)(2,1)} %k_ref.15, bf16[1,192,4096]{2,1,0:T(8,128)(2,1)} %v_ref.15, f32[32,192]{1,0:T(8,128)S(1)} %get-tuple-element.50.row_ref, f32[192,2048]{1,0:T(8,128)} %get-tuple-element.88.ki_ref, ...), custom_call_target="tpu_custom_call" | custom-call | flops 402653184 | bytes 10510336 | tf_op jit(solution)/shard_map/finish/pallas_call | solution.py:306
  145.2 4.4 %finish.3 = (bf16[1,192,4096]{2,1,0:T(8,128)(2,1)}, bf16[1,192,4096]{2,1,0:T(8,128)(2,1)}) custom-call(s32[3]{0:T(128)S(1)} %pad_add_fusion.c_ref, bf16[1,192,4096]{2,1,0:T(8,128)(2,1)} %k_ref.15, bf16[1,192,4096]{2,1,0:T(8,128)(2,1)} %v_ref.15, f32[32,192]{1,0:T(8,128)S(1)} %get-tuple-element.50.row_ref, ...), custom_call_target="tpu_custom_call", output_to_operand_aliasing={{0}: (7, {}), {1}: (8, {})} | custom-call | flops 402653184 | bytes 13656064 | tf_op jit(solution)/shard_map/finish/pallas_call | solution.py:306
  (56 shorter events, 19.1 us)
Async XLA Ops:
  5.4 7.1 %collective-permute-start = (f32[16,136,128]{2,1,0:T(8,128)S(1)}, f32[16,136,128]{2,1,0:T(8,128)S(1)}, u32[]{:S(2)}, u32[]{:S(2)}) collective-permute-start(f32[16,136,128]{2,1,0:T(8,128)S(1)} %get-tuple-element.52), channel_id=1, source_target_pairs={{0,1},{1,0},{2,3},{3,2},{4,5},{5,4},{6,7},{7,6},{8,9},{9,8},{10,11... | collective-permute-start | bytes 3342344 | tf_op jit(solution)/shard_map/ppermute | solution.py:383
  12.5 1.8 %copy-start.5 = (f32[16,128,128]{2,1,0:T(8,128)}, f32[16,128,128]{2,1,0:T(8,128)S(1)}, u32[]{:S(2)}) copy-start(f32[16,128,128]{2,1,0:T(8,128)S(1)} %get-tuple-element.51.own_ref) | copy-start | bytes 3145732
  14.3 22.8 %all-to-all-start = ((f32[16,136,128]{2,1,0:T(8,128)}), f32[16,136,128]{2,1,0:T(8,128)S(1)}, u32[]{:S(2)}, u32[]{:S(2)}) async-start(f32[16,136,128]{2,1,0:T(8,128)} %get-tuple-element.54), calls=%async_computation | async-start | bytes 2228224 | tf_op jit(solution)/shard_map/all_to_all | solution.py:387
  37.8 8.7 %collective-permute-start.1 = (f32[128,128]{1,0:T(8,128)S(1)}, f32[128,128]{1,0:T(8,128)S(1)}, u32[]{:S(2)}, u32[]{:S(2)}) collective-permute-start(f32[128,128]{1,0:T(8,128)S(1)} %half_total.2), channel_id=1, source_target_pairs={{0,32},{32,0},{1,33},{33,1},{2,34},{34,2},{3,35},{35,3},{4,36},{36... | collective-permute-start | bytes 196616 | tf_op jit(solution)/shard_map/ppermute | solution.py:403
  46.5 24.5 %copy-start.10 = (f32[192,2048]{1,0:T(8,128)S(1)}, f32[192,2048]{1,0:T(8,128)}, u32[]{:S(2)}) copy-start(f32[192,2048]{1,0:T(8,128)} %get-tuple-element.62.in_ref) | copy-start | bytes 4718596
  48.1 18.0 %copy-start.6 = (f32[16,128,128]{2,1,0:T(8,128)S(1)}, f32[16,128,128]{2,1,0:T(8,128)}, u32[]{:S(2)}) copy-start(f32[16,128,128]{2,1,0:T(8,128)} %copy-done.5) | copy-start | bytes 3145732
  66.1 4.8 %copy-start = (bf16[1,192,4096]{2,1,0:T(8,128)(2,1)S(1)}, bf16[1,192,4096]{2,1,0:T(8,128)(2,1)}, u32[]{:S(2)}) copy-start(bf16[1,192,4096]{2,1,0:T(8,128)(2,1)} %q_ref.13) | copy-start | bytes 4718596
  66.1 4.8 %copy-start.1 = (bf16[1,192,4096]{2,1,0:T(8,128)(2,1)S(1)}, bf16[1,192,4096]{2,1,0:T(8,128)(2,1)}, u32[]{:S(2)}) copy-start(bf16[1,192,4096]{2,1,0:T(8,128)(2,1)} %g_ref.5) | copy-start | bytes 4718596
  66.1 4.8 %copy-start.11 = (f32[4096]{0:T(1024)S(1)}, f32[4096]{0:T(1024)}, u32[]{:S(2)}) copy-start(f32[4096]{0:T(1024)} %param.11) | copy-start | bytes 49156
  67.1 5.9 %copy-start.7 = (f32[16,128,128]{2,1,0:T(8,128)}, f32[16,128,128]{2,1,0:T(8,128)S(1)}, u32[]{:S(2)}) copy-start(f32[16,128,128]{2,1,0:T(8,128)S(1)} %get-tuple-element.63.x_ref.i_ref) | copy-start | bytes 3145732
  67.1 6.1 %collective-permute-start.2 = (f32[16,128,128]{2,1,0:T(8,128)S(1)}, f32[16,128,128]{2,1,0:T(8,128)S(1)}, u32[]{:S(2)}, u32[]{:S(2)}) collective-permute-start(f32[16,128,128]{2,1,0:T(8,128)S(1)} %get-tuple-element.61), channel_id=1, source_target_pairs={{0,1},{1,0},{2,3},{3,2},{4,5},{5,4},{6,7},{7,6},{8,9},{9,8},{10,11... | collective-permute-start | bytes 3145736 | tf_op jit(solution)/shard_map/ppermute | solution.py:383
  71.0 2.3 %copy-start.9 = (f32[192,2048]{1,0:T(8,128)S(1)}, f32[192,2048]{1,0:T(8,128)}, u32[]{:S(2)}) copy-start(f32[192,2048]{1,0:T(8,128)} %get-tuple-element.57.in_ref) | copy-start | bytes 4718596
  73.2 4.7 %copy-start.3 = (f32[16,128,128]{2,1,0:T(8,128)}, f32[16,128,128]{2,1,0:T(8,128)S(1)}, u32[]{:S(2)}) copy-start(f32[16,128,128]{2,1,0:T(8,128)S(1)} %collective-permute-done.2.i_ref) | copy-start | bytes 3145732
  78.0 4.0 %collective-permute-start.3 = (f32[16,128,128]{2,1,0:T(8,128)S(1)}, f32[16,128,128]{2,1,0:T(8,128)S(1)}, u32[]{:S(2)}, u32[]{:S(2)}) collective-permute-start(f32[16,128,128]{2,1,0:T(8,128)S(1)} %get-tuple-element.76), channel_id=1, source_target_pairs={{0,1},{1,0},{2,3},{3,2},{4,5},{5,4},{6,7},{7,6},{8,9},{9,8},{10,11... | collective-permute-start | bytes 3145736 | tf_op jit(solution)/shard_map/ppermute | solution.py:383
  82.0 1.6 %copy-start.2 = (f32[16,128,128]{2,1,0:T(8,128)}, f32[16,128,128]{2,1,0:T(8,128)S(1)}, u32[]{:S(2)}) copy-start(f32[16,128,128]{2,1,0:T(8,128)S(1)} %collective-permute-done.3.got_ref) | copy-start | bytes 3145732
  83.6 21.5 %all-to-all-start.2 = ((f32[16,128,128]{2,1,0:T(8,128)}), f32[16,128,128]{2,1,0:T(8,128)S(1)}, u32[]{:S(2)}, u32[]{:S(2)}) async-start(f32[16,128,128]{2,1,0:T(8,128)} %chip_moment.1), calls=%async_computation.2 | async-start | bytes 2097152 | tf_op jit(solution)/shard_map/all_to_all | solution.py:387
  87.3 12.9 %collective-permute-start.5 = (f32[8,128]{1,0:T(8,128)S(1)}, f32[8,128]{1,0:T(8,128)S(1)}, u32[]{:S(2)}, u32[]{:S(2)}) collective-permute-start(f32[8,128]{1,0:T(8,128)S(1)} %get-tuple-element.98), channel_id=1, source_target_pairs={{0,128},{64,192},{128,0},{192,64},{1,129},{65,193},{129,1},{193,65... | collective-permute-start | bytes 12296 | tf_op jit(solution)/shard_map/ppermute | solution.py:504
  88.8 11.5 %collective-permute-start.6 = (f32[8,128]{1,0:T(8,128)S(1)}, f32[8,128]{1,0:T(8,128)S(1)}, u32[]{:S(2)}, u32[]{:S(2)}) collective-permute-start(f32[8,128]{1,0:T(8,128)S(1)} %get-tuple-element.99), channel_id=1, source_target_pairs={{0,192},{64,128},{128,64},{192,0},{1,193},{65,129},{129,65},{193,1... | collective-permute-start | bytes 12296 | tf_op jit(solution)/shard_map/ppermute | solution.py:504
  90.4 9.9 %collective-permute-start.4 = (f32[8,128]{1,0:T(8,128)S(1)}, f32[8,128]{1,0:T(8,128)S(1)}, u32[]{:S(2)}, u32[]{:S(2)}) collective-permute-start(f32[8,128]{1,0:T(8,128)S(1)} %slice_bitcast_fusion.2), channel_id=1, source_target_pairs={{0,64},{64,0},{128,192},{192,128},{1,65},{65,1},{129,193},{193,129... | collective-permute-start | bytes 12296 | tf_op jit(solution)/shard_map/ppermute | solution.py:504
  105.8 7.2 %collective-permute-start.7 = (f32[136,128]{1,0:T(8,128)S(1)}, f32[136,128]{1,0:T(8,128)S(1)}, u32[]{:S(2)}, u32[]{:S(2)}) collective-permute-start(f32[136,128]{1,0:T(8,128)S(1)} %half_total.3), channel_id=1, source_target_pairs={{0,32},{32,0},{1,33},{33,1},{2,34},{34,2},{3,35},{35,3},{4,36},{36... | collective-permute-start | bytes 208904 | tf_op jit(solution)/shard_map/ppermute | solution.py:403
  114.6 3.8 %copy-start.4 = (f32[16,128,128]{2,1,0:T(8,128)S(1)}, f32[16,128,128]{2,1,0:T(8,128)}, u32[]{:S(2)}) copy-start(f32[16,128,128]{2,1,0:T(8,128)} %copy-done.3) | copy-start | bytes 3145732
  114.6 19.2 %all-to-all-start.3 = ((f32[16,136,128]{2,1,0:T(8,128)}), f32[16,136,128]{2,1,0:T(8,128)S(1)}, u32[]{:S(2)}, u32[]{:S(2)}) async-start(f32[16,136,128]{2,1,0:T(8,128)} %chip_scan.3), calls=%async_computation.3 | async-start | bytes 2228224 | tf_op jit(solution)/shard_map/all_to_all | solution.py:387
  136.8 8.4 %collective-permute-start.8 = (f32[16,128,128]{2,1,0:T(8,128)}, f32[16,128,128]{2,1,0:T(8,128)S(1)}, u32[]{:S(2)}, u32[]{:S(2)}) collective-permute-start(f32[16,128,128]{2,1,0:T(8,128)} %get-tuple-element.87), channel_id=1, source_target_pairs={{0,1},{1,0},{2,3},{3,2},{4,5},{5,4},{6,7},{7,6},{8,9},{9,8},{10,11... | collective-permute-start | bytes 3145736 | tf_op jit(solution)/shard_map/ppermute | solution.py:383
  140.2 4.4 %collective-permute-start.9 = (f32[8,128]{1,0:T(8,128)S(1)}, f32[8,128]{1,0:T(8,128)S(1)}, u32[]{:S(2)}, u32[]{:S(2)}) collective-permute-start(f32[8,128]{1,0:T(8,128)S(1)} %get-tuple-element.95), channel_id=1, source_target_pairs={{0,1},{1,0},{2,3},{3,2},{4,5},{5,4},{6,7},{7,6},{8,9},{9,8},{10,11... | collective-permute-start | bytes 12296 | tf_op jit(solution)/shard_map/ppermute | solution.py:383
  (2 other events, 2.0 us)

commit v6 on v5

--- a/solution.py
+++ b/solution.py
@@ -15,7 +15,6 @@
 T = 192
 HD = 128
 GH = 8
-FH = 8
 GW = GH * HD
 NG = 4
 HALF = NG // 2
@@ -45,11 +44,8 @@
     return dot(jnp.concatenate([rows, rows], 1), split_state(state, 1), 1, 1)
 
 
-def columns(row_ref, heads=GH):
-    cum = jnp.transpose(row_ref[...])
-    if heads == GH:
-        return cum
-    return jnp.where(pl.program_id(0) % 2 == 0, cum[:, :heads], cum[:, heads:])
+def columns(row_ref):
+    return jnp.transpose(row_ref[...])
 
 
 def decay_table(col, row):
@@ -58,13 +54,18 @@
     return jnp.exp(jnp.where(row_ids >= col_ids, col - row, -jnp.inf))
 
 
+def scaled_columns(x, factors):
+    return (jnp.transpose(x).astype(F32) * factors).astype(BF16)
+
+
 def states_of(k_ref, v_ref, row_ref, store):
-    cum = columns(row_ref, FH)
-    last = cum[T - 1 : T, :]
-    shrink = jnp.exp(last - cum)
-    for j in range(FH):
-        late = (k_ref[:, lanes(j)].astype(F32) * shrink[:, j : j + 1]).astype(BF16)
-        store(j, dot(late, v_ref[:, lanes(j)], 0, 0), jnp.broadcast_to(last[:, j : j + 1], (8, HD)))
+    rows = row_ref[...]
+    last = rows[:, T - 1 : T]
+    shrink = jnp.exp(last - rows)
+    for j in range(GH):
+        late = scaled_columns(k_ref[:, lanes(j)], shrink[j : j + 1, :])
+        log = jnp.broadcast_to(last[j : j + 1, :], (8, HD))
+        store(j, dot(late, v_ref[:, lanes(j)], 1, 0), log)
 
 
 def state_first_kernel(c_ref, k_ref, v_ref, ld_ref, s_ref, row_ref):
@@ -96,13 +97,14 @@
     states_of(k_ref, v_ref, row_ref, store)
 
 
-def combine_kernel(upward, c_ref, own_ref, got_ref, lo_ref, lg_ref, p_ref, log_ref=None):
+def combine_kernel(upward, c_ref, own_ref, got_ref, lo_ref, lg_ref, p_ref, kept_ref, log_ref=None):
     first = c_ref[0] == 0 if upward else c_ref[0] == 1
     for j in range(GH):
         log_own, log_got = lo_ref[j, 0:1, :], lg_ref[j, 0:1, :]
         scale_own = jnp.where(first, jnp.exp(log_got), 1.0)
         scale_got = jnp.where(first, 1.0, jnp.exp(log_own))
         p_ref[j, :HD, :] = scale_own * own_ref[j] + scale_got * got_ref[j]
+        kept_ref[j] = jnp.where(first, own_ref[j], got_ref[j])
         if upward:
             p_ref[j, HD:, :] = lo_ref[j] + lg_ref[j]
             log_ref[j] = lg_ref[j]
@@ -136,9 +138,7 @@
             o_ref[i, HD:, :] = jnp.broadcast_to(row, (8, HD))
 
 
-def hand_on_kernel(
-    upward, c_ref, d_ref, own_ref, got_ref, lo_ref, lg_ref, *rest
-):
+def hand_on_kernel(upward, c_ref, d_ref, kept_ref, lo_ref, lg_ref, *rest):
     if upward:
         send_ref, state_ref = rest
     else:
@@ -158,14 +158,9 @@
     at_edge = c_ref[0] == (0 if upward else 1)
     for j in range(GH):
         edge = d_ref[j]
-        send_ref[j] = (
-            jnp.where(at_edge, jnp.exp(lo_ref[j, 0:1, :]), 1.0) * edge
-            + jnp.where(at_edge, 1.0, 0.0) * own_ref[j]
-        )
-        state_ref[j] = (
-            jnp.where(at_edge, 1.0, jnp.exp(lg_ref[j, 0:1, :])) * edge
-            + jnp.where(at_edge, 0.0, 1.0) * got_ref[j]
-        )
+        passed = jnp.exp(jnp.where(at_edge, lo_ref[j, 0:1, :], lg_ref[j, 0:1, :])) * edge + kept_ref[j]
+        send_ref[j] = jnp.where(at_edge, passed, edge)
+        state_ref[j] = jnp.where(at_edge, edge, passed)
 
 
 def forward_kernel(c_ref, q_ref, k_ref, v_ref, row_ref, fw_ref, in_ref):
@@ -204,16 +199,16 @@
     )
 
 
-def delta_group(q_ref, g_ref, gain_ref, cum, att_ref, inverse, mean, od_ref, m_ref, gt_ref):
-    growth = jnp.exp(cum)
+def delta_group(q_ref, g_ref, gain_ref, row_ref, att_ref, inverse, mean, od_ref, m_ref, gt_ref):
+    growth = jnp.exp(row_ref[...])
     for j in range(GH):
         grad = g_ref[:, lanes(j)].astype(F32)
         normed = att_ref[:, lanes(j)] * inverse
         delta = (inverse * (gain_ref[:, lanes(j)] * grad - normed * mean)).astype(BF16)
         od_ref[:, lanes(j)] = delta
         gt_ref[j : j + 1, :] = jnp.sum(grad * normed, axis=0, keepdims=True)
-        early = (q_ref[:, lanes(j)].astype(F32) * growth[:, j : j + 1]).astype(BF16)
-        m_ref[j] = dot(early, delta, 0, 0)
+        early = scaled_columns(q_ref[:, lanes(j)], growth[j : j + 1, :])
+        m_ref[j] = dot(early, delta, 1, 0)
 
 
 def attend_other_kernel(
@@ -222,7 +217,6 @@
 ):
     step = pl.program_id(0)
     group = jnp.where(step < HALF, step, 2 * HALF - 1 - step)
-    cum = columns(row_ref)
 
     @pl.when(step == 0)
     def _():
@@ -232,7 +226,7 @@
     @pl.when(step < HALF)
     def _():
         attend_group(
-            q_ref, g_ref, gain_ref, cum, in_ref, i_ref, att_ref.at[group], sq_ref, pr_ref
+            q_ref, g_ref, gain_ref, columns(row_ref), in_ref, i_ref, att_ref.at[group], sq_ref, pr_ref
         )
 
     @pl.when(step == HALF)
@@ -246,18 +240,17 @@
     @pl.when(step >= HALF)
     def _():
         delta_group(
-            q_ref, g_ref, gain_ref, cum, att_ref.at[group], inv_ref[...], mean_ref[...],
+            q_ref, g_ref, gain_ref, row_ref, att_ref.at[group], inv_ref[...], mean_ref[...],
             od_ref, m_ref, gt_ref,
         )
 
 
 def delta_own_kernel(
-    c_ref, q_ref, g_ref, gain_ref, row_ref, att_ref, inv_ref, mean_ref, od_ref, m_ref, gt_ref, kept_ref
+    c_ref, q_ref, g_ref, gain_ref, row_ref, att_ref, inv_ref, mean_ref, od_ref, m_ref, gt_ref
 ):
     delta_group(
-        q_ref, g_ref, gain_ref, columns(row_ref), att_ref, inv_ref[...], mean_ref[...], od_ref, m_ref, gt_ref
-    )
-    kept_ref[...] = m_ref[...]
+        q_ref, g_ref, gain_ref, row_ref, att_ref, inv_ref[...], mean_ref[...], od_ref, m_ref, gt_ref
+    )
 
 
 def backward_kernel(
@@ -278,10 +271,10 @@
 
 
 def finish_kernel(c_ref, k_ref, v_ref, row_ref, ki_ref, vi_ref, x_ref, *rest):
-    cum = columns(row_ref, FH)
+    cum = columns(row_ref)
     shrink = jnp.exp(cum[T - 1 : T, :] - cum)
     kg_ref, vg_ref = rest[-2:]
-    for j in range(FH):
+    for j in range(GH):
         at = lanes(j)
         scale = shrink[:, j : j + 1]
         kg_ref[:, at] = (ki_ref[:, at] + scale * rows_by_state_t(v_ref[:, at], x_ref[j])).astype(BF16)
@@ -336,17 +329,6 @@
     return pl.BlockSpec((T, GW), lambda i, c: (0, group(i)))
 
 
-def fine(own):
-    return pl.BlockSpec((None, T, FH * HD), lambda i, c: (0, 0, half_of(own, c) * (NC // FH) + i))
-
-
-FINE_NARROW = pl.BlockSpec((T, FH * HD), lambda i, c: (0, i))
-
-
-def fine_block(rows=HD):
-    return pl.BlockSpec((FH, rows, HD), lambda i, c: (i, 0, 0))
-
-
 def gain_block(own, group=lambda i: i):
     return pl.BlockSpec((1, GW), lambda i, c: (0, half_of(own, c) * HALF + group(i)))
 
@@ -417,21 +399,20 @@
 
     whole_rows = pl.BlockSpec((NG * GH, T), lambda i, c: (0, 0))
     sent, row = call(
-        state_first_kernel, "states_other", (NC // FH,),
-        [fine(False), fine(False), whole_rows], [fine_block(HD + 8), whole_rows],
-        [LOGGED, shape((NG * GH, T))], (core, Kept(k), Kept(v), logs), MM,
+        state_first_kernel, "states_other", (HALF,),
+        [wide(False), wide(False), whole_rows], [state_block(HD + 8), whole_rows],
+        [LOGGED, shape((NG * GH, T))], (core, Kept(k), Kept(v), Kept(logs)), MM,
     )
     got = swap_cores(sent)
     own, log_own = call(
-        state_second_kernel, "states_own", (NC // FH,),
-        [fine(True), fine(True), row_block(True)], [fine_block(), fine_block(8)],
-        [STATES, LOGS],
+        state_second_kernel, "states_own", (HALF,),
+        [wide(True), wide(True), row_block(True)], [state_block(), LOG_BLOCK], [STATES, LOGS],
         (core, Kept(k), Kept(v), row), MM,
     )
-    chip_total, log_got = call(
+    chip_total, kept_state, log_got = call(
         functools.partial(combine_kernel, True), "chip_total", (HALF,),
         [state_block(), state_block(), LOG_BLOCK, LOG_TAIL],
-        [state_block(HD + 8), LOG_BLOCK], [Kept(LOGGED), LOGS],
+        [state_block(HD + 8), state_block(), LOG_BLOCK], [Kept(LOGGED), Kept(STATES), LOGS],
         (core, own, got, log_own, got), 0,
     )
     gathered = chips_all_to_all(chip_total)
@@ -453,8 +434,8 @@
     scanned = chips_all_to_all(before_chips)
     onward, state_here = call(
         functools.partial(hand_on_kernel, True), "onward", (HALF,),
-        [state_block()] * 3 + [LOG_BLOCK] * 2, [state_block()] * 2, [STATES] * 2,
-        (core, scanned, own, got, log_own, log_got), 0,
+        [state_block()] * 2 + [LOG_BLOCK] * 2, [state_block()] * 2, [STATES] * 2,
+        (core, scanned, kept_state, log_own, log_got), 0,
     )
     state_other = swap_cores(onward)
     att_own, squares, products = call(
@@ -483,16 +464,15 @@
         scratch=[pltpu.VMEM((HALF, T, GW), F32), pltpu.VMEM((T, HD), F32), pltpu.VMEM((T, HD), F32)],
     )
     moment_got = swap_cores(moment_sent)
-    delta_own, moment_own, gains_own, moment_kept = call(
+    delta_own, moment_own, gains_own = call(
         delta_own_kernel, "delta_own", (HALF,),
         [wide(True), wide(True), gain_block(True), row_block(True), narrow(), STAT_WHOLE, STAT_WHOLE],
-        [narrow(), state_block(), gains_block(), state_block()],
-        [Kept(HALF_BF16), STATES, GAINS, Kept(STATES)],
+        [narrow(), state_block(), gains_block()], [Kept(HALF_BF16), STATES, GAINS],
         (core, q, g, gain, row, att_own, inverse, mean), MM,
     )
-    (chip_moment,) = call(
+    chip_moment, kept_moment = call(
         functools.partial(combine_kernel, False), "chip_moment", (HALF,),
-        [state_block(), state_block(), LOG_BLOCK, LOG_BLOCK], [state_block()], [Kept(STATES)],
+        [state_block(), state_block(), LOG_BLOCK, LOG_BLOCK], [state_block()] * 2, [Kept(STATES)] * 2,
         (core, moment_own, moment_got, log_own, log_got), 0,
     )
     gathered_back = chips_all_to_all(chip_moment)
@@ -525,21 +505,20 @@
     scanned_back, key_inside[False] = lax.optimization_barrier((scanned_back, key_inside[False]))
     onward_back, later_here, collected = call(
         functools.partial(hand_on_kernel, False), "onward_back", (HALF,),
-        [state_block()] * 3 + [LOG_BLOCK] * 2 + [LOG_TAIL],
+        [state_block()] * 2 + [LOG_BLOCK] * 2 + [LOG_TAIL],
         [state_block(), state_block(), pl.BlockSpec((8, HD), lambda i, c: (0, 0))],
         [STATES, STATES, shape((8, HD))],
-        (core, scanned_back, Kept(moment_kept), Kept(moment_got), log_own,
-         log_got, scanned_back), 0,
+        (core, scanned_back, Kept(kept_moment), log_own, log_got, scanned_back), 0,
     )
     later_other = swap_cores(onward_back)
     later = {True: later_here, False: later_other}
     grads = ()
     for mine in (True, False):
         grads = call(
-            finish_kernel, "finish", (NC // FH,),
-            [fine(mine), fine(mine), row_block(mine), FINE_NARROW, FINE_NARROW,
-             fine_block()] + [ANY] * len(grads),
-            [fine(mine)] * 2, [Kept(WHOLE_BF16)] * 2,
+            finish_kernel, "finish", (HALF,),
+            [wide(mine), wide(mine), row_block(mine), narrow(), narrow(), state_block()]
+            + [ANY] * len(grads),
+            [wide(mine)] * 2, [Kept(WHOLE_BF16)] * 2,
             (core, Kept(k), Kept(v), row, Kept(key_inside[mine]), Kept(value_inside[mine]),
              later[mine], *[Kept(a) for a in grads]), 4 * MM, aliases={7: 0, 8: 1} if grads else None,
         )

time: 150 us -> 145 us (0.967)
  Pallas kernels: 64.8 us -> 61.2 us
  waiting for transfers between devices: 23.9 us -> 22 us
    pallas_call x19, Pallas kernels: 64.8 us -> 61.2 us  [call(): pl.pallas_call(kernel, name=name, grid_spec=pltpu.PrefetchScalarGridSpec(...]
    all_to_all x3, waiting for transfers between devices: 20.1 us -> 18.1 us  [chips_all_to_all(): lax.all_to_all(values, ('x', 'y'), split_axis=0, concat_axis=0, tiled=True)]
  transfers between devices with their start and end apart: 13 -> 13, of which waited for: 6 -> 6; matrix products, arithmetic and copies ran while one was open for 0% -> 0% of each run, Pallas kernels for 27% -> 26%
where the time goes in v6:
time: 145 us; the launch traced here: 144 us
  Pallas kernels  61.2 us (42%)
  starting transfers between devices  40.2 us (28%)
  waiting for transfers between devices  22 us (15%)
  blocking collectives  18.1 us (12%)
    pallas_call x19, Pallas kernels, call(): pl.pallas_call(kernel, name=name, grid_spec=pltpu.PrefetchScalarGridSpec(...  61.2 us
    all_to_all x3, waiting for transfers between devices, chips_all_to_all(): lax.all_to_all(values, ('x', 'y'), split_axis=0, concat_axis=0, tiled=True)  18.1 us
    all_to_all x1, blocking collectives, chips_all_to_all(): lax.all_to_all(values, ('x', 'y'), split_axis=0, concat_axis=0, tiled=True)  18.1 us
    ppermute x2, starting transfers between devices, scan_over_chips(): before = lax.ppermute(total, 'zh', [(0, 1), (1, 0)])  12.4 us
    all_to_all x3, starting transfers between devices, chips_all_to_all(): lax.all_to_all(values, ('x', 'y'), split_axis=0, concat_axis=0, tiled=True)  12.4 us
    ppermute x5, starting transfers between devices, swap_cores(): return lax.ppermute(values, 'core', [(0, 1), (1, 0)])  12.2 us
    ppermute x2, waiting for transfers between devices, scan_over_chips(): before = lax.ppermute(total, 'zh', [(0, 1), (1, 0)])  3.54 us
    ppermute x3, starting transfers between devices, per_device(): lax.ppermute(gains[distance], 'dp', [(i, i ^ distance) for i in range(NG)])  3.19 us
  transfers between devices with their start and end apart: 13, of which 6 were waited for; matrix products, arithmetic and copies ran while one was open for 0% of the time, Pallas kernels for 26%

profile of v6, /device:TPU:1, one launch (start us, length us, event | category | flops | bytes accessed | tf_op | source)
XLA Modules:
  0.0 144.2 jit_solution(8032588875880470937)
XLA Ops:
  0.7 2.7 %states_other.1 = (f32[16,136,128]{2,1,0:T(8,128)S(1)}, f32[32,192]{1,0:T(8,128)S(1)}) custom-call(s32[3]{0:T(128)S(1)} %pad_add_fusion.c_ref, bf16[1,192,4096]{2,1,0:T(8,128)(2,1)} %k_ref.15, bf16[1,192,4096]{2,1,0:T(8,128)(2,1)} %v_ref.15, f32[32,192]{1,0:T(8,128)} %bitcast.26), custom_call_target="tpu_custom_call" | custom-call | flops 100663296 | bytes 4308992 | tf_op jit(solution)/shard_map/states_other/pallas_call | solution.py:299
  3.4 3.3 %collective-permute-start = (f32[16,136,128]{2,1,0:T(8,128)S(1)}, f32[16,136,128]{2,1,0:T(8,128)S(1)}, u32[]{:S(2)}, u32[]{:S(2)}) collective-permute-start(f32[16,136,128]{2,1,0:T(8,128)S(1)} %get-tuple-element.54), channel_id=1, source_target_pairs={{0,1},{1,0},{2,3},{3,2},{4,5},{5,4},{6,7},{7,6},{8,9},{9,8},{10,11... | collective-permute-start | bytes 3342344 | tf_op jit(solution)/shard_map/ppermute | solution.py:365
  6.7 2.5 %states_own.1 = (f32[16,128,128]{2,1,0:T(8,128)S(1)}, f32[16,8,128]{2,1,0:T(8,128)S(1)}) custom-call(s32[3]{0:T(128)S(1)} %pad_add_fusion.c_ref, bf16[1,192,4096]{2,1,0:T(8,128)(2,1)} %k_ref.15, bf16[1,192,4096]{2,1,0:T(8,128)(2,1)} %v_ref.15, f32[32,192]{1,0:T(8,128)S(1)} %get-tuple-element.52.row_ref), custom_call_target="tpu_custom_call" | custom-call | flops 100663296 | bytes 4284416 | tf_op jit(solution)/shard_map/states_own/pallas_call | solution.py:299
  9.2 2.1 %chip_total.1 = (f32[16,136,128]{2,1,0:T(8,128)}, f32[16,128,128]{2,1,0:T(8,128)}, f32[16,8,128]{2,1,0:T(8,128)S(1)}) custom-call(s32[3]{0:T(128)S(1)} %pad_add_fusion.c_ref, f32[16,128,128]{2,1,0:T(8,128)S(1)} %get-tuple-element.53.own_ref, f32[16,136,128]{2,1,0:T(8,128)S(1)} %collective-permute-done.got_ref.lg_ref, ...), custom_call_target="tpu_custom_call" | custom-call | bytes 5570560 | tf_op jit(solution)/shard_map/chip_total/pallas_call | solution.py:299
  11.3 5.0 %all-to-all-start = ((f32[16,136,128]{2,1,0:T(8,128)}), f32[16,136,128]{2,1,0:T(8,128)S(1)}, u32[]{:S(2)}, u32[]{:S(2)}) async-start(f32[16,136,128]{2,1,0:T(8,128)} %get-tuple-element.56), calls=%async_computation | async-start | bytes 2228224 | tf_op jit(solution)/shard_map/all_to_all | solution.py:369
  16.4 4.7 %forward_inside.2 = (bf16[16,192,192]{2,1,0:T(8,128)(2,1)}, f32[192,2048]{1,0:T(8,128)}) custom-call(s32[3]{0:T(128)S(1)} %pad_add_fusion.c_ref, bf16[1,192,4096]{2,1,0:T(8,128)(2,1)} %q_ref.13, bf16[1,192,4096]{2,1,0:T(8,128)(2,1)} %k_ref.15, bf16[1,192,4096]{2,1,0:T(8,128)(2,1)} %v_ref.15, f32[32,192]{1,0:T(8,128)S(1)} %get-tuple-element.52.row_ref), custom_call_target="tpu_custom_call" | custom-call | flops 301989888 | bytes 7495680 | tf_op jit(solution)/shard_map/forward_inside/pallas_call | solution.py:299
  21.1 4.7 %forward_inside.3 = (bf16[16,192,192]{2,1,0:T(8,128)(2,1)}, f32[192,2048]{1,0:T(8,128)}) custom-call(s32[3]{0:T(128)S(1)} %pad_add_fusion.c_ref, bf16[1,192,4096]{2,1,0:T(8,128)(2,1)} %q_ref.13, bf16[1,192,4096]{2,1,0:T(8,128)(2,1)} %k_ref.15, bf16[1,192,4096]{2,1,0:T(8,128)(2,1)} %v_ref.15, f32[32,192]{1,0:T(8,128)S(1)} %get-tuple-element.52.row_ref), custom_call_target="tpu_custom_call" | custom-call | flops 301989888 | bytes 7495680 | tf_op jit(solution)/shard_map/forward_inside/pallas_call | solution.py:299
  25.8 7.1 %all-to-all-done.m_ref.l_ref = f32[16,136,128]{2,1,0:T(8,128)S(1)} async-done(((f32[16,136,128]{2,1,0:T(8,128)}), f32[16,136,128]{2,1,0:T(8,128)S(1)}, u32[]{:S(2)}, u32[]{:S(2)}) %all-to-all-start) | async-done | bytes 1114144 | tf_op jit(solution)/shard_map/all_to_all | solution.py:369
  33.4 7.0 %collective-permute-start.1 = (f32[128,128]{1,0:T(8,128)S(1)}, f32[128,128]{1,0:T(8,128)S(1)}, u32[]{:S(2)}, u32[]{:S(2)}) collective-permute-start(f32[128,128]{1,0:T(8,128)S(1)} %half_total.2), channel_id=1, source_target_pairs={{0,32},{32,0},{1,33},{33,1},{2,34},{34,2},{3,35},{35,3},{4,36},{36... | collective-permute-start | bytes 196616 | tf_op jit(solution)/shard_map/ppermute | solution.py:385
  43.8 18.1 %all_to_all.20.d_ref = f32[16,128,128]{2,1,0:T(8,128)S(1)} all-to-all(f32[16,128,128]{2,1,0:T(8,128)} %get-tuple-element.61), channel_id=1, replica_groups=mesh['dp'=4,'zh'=2,'x'=4,'y'=4,'core'=2] {'x','y'}, dimensions={0} | all-to-all | bytes 2097152 | tf_op jit(solution)/shard_map/all_to_all | solution.py:369
  62.7 5.0 %collective-permute-start.2 = (f32[16,128,128]{2,1,0:T(8,128)S(1)}, f32[16,128,128]{2,1,0:T(8,128)S(1)}, u32[]{:S(2)}, u32[]{:S(2)}) collective-permute-start(f32[16,128,128]{2,1,0:T(8,128)S(1)} %get-tuple-element.64), channel_id=1, source_target_pairs={{0,1},{1,0},{2,3},{3,2},{4,5},{5,4},{6,7},{7,6},{8,9},{9,8},{10,11... | collective-permute-start | bytes 3145736 | tf_op jit(solution)/shard_map/ppermute | solution.py:365
  70.0 4.1 %attend_other.1 = (bf16[192,2048]{1,0:T(8,128)(2,1)}, f32[16,128,128]{2,1,0:T(8,128)S(1)}, f32[2,8,128]{2,1,0:T(8,128)S(1)}, f32[192,128]{1,0:T(8,128)S(1)}, f32[192,128]{1,0:T(8,128)S(1)}) custom-call(s32[3]{0:T(128)S(1)} %pad_add_fusion.c_ref, bf16[1,192,4096]{2,1,0:T(8,128)(2,1)S(1)} %copy-done, bf16[1,192,4096]{2,1,0:T(8,128)(2,1)S(1)} %copy-done.1, ...), custom_call_target="tpu_custom_call" | custom-call | flops 301989888 | bytes 8044544 | tf_op jit(solution)/shard_map/attend_other/pallas_call | solution.py:299
  74.5 2.5 %delta_own.1 = (bf16[192,2048]{1,0:T(8,128)(2,1)}, f32[16,128,128]{2,1,0:T(8,128)S(1)}, f32[2,8,128]{2,1,0:T(8,128)S(1)}) custom-call(s32[3]{0:T(128)S(1)} %pad_add_fusion.c_ref, bf16[1,192,4096]{2,1,0:T(8,128)(2,1)S(1)} %copy-done, bf16[1,192,4096]{2,1,0:T(8,128)(2,1)S(1)} %copy-done.1, f32[1,4096]{1,0:T(1,128)S(1)} %bitcast.25, ...), custom_call_target="tpu_custom_call" | custom-call | flops 100663296 | bytes 6799360 | tf_op jit(solution)/shard_map/delta_own/pallas_call | solution.py:299
  79.0 3.7 %all-to-all-start.2 = ((f32[16,128,128]{2,1,0:T(8,128)}), f32[16,128,128]{2,1,0:T(8,128)S(1)}, u32[]{:S(2)}, u32[]{:S(2)}) async-start(f32[16,128,128]{2,1,0:T(8,128)} %get-tuple-element.80), calls=%async_computation.2 | async-start | bytes 2097152 | tf_op jit(solution)/shard_map/all_to_all | solution.py:369
  87.1 8.5 %backward_inside.2 = (bf16[1,192,4096]{2,1,0:T(8,128)(2,1)}, f32[192,2048]{1,0:T(8,128)}, f32[192,2048]{1,0:T(8,128)}) custom-call(s32[3]{0:T(128)S(1)} %pad_add_fusion.c_ref, bf16[192,2048]{1,0:T(8,128)(2,1)} %get-tuple-element.74.od_ref, bf16[1,192,4096]{2,1,0:T(8,128)(2,1)} %q_ref.13, bf16[1,192,4096]{2,1,0:T(8,128)(2,1)} %k_ref.15, ...), custom_call_target="tpu_custom_call" | custom-call | flops 805306368 | bytes 12476416 | tf_op jit(solution)/shard_map/backward_inside/pallas_call | solution.py:299
  95.6 4.4 %all-to-all-done.2.m_ref = f32[16,128,128]{2,1,0:T(8,128)S(1)} async-done(((f32[16,128,128]{2,1,0:T(8,128)}), f32[16,128,128]{2,1,0:T(8,128)S(1)}, u32[]{:S(2)}, u32[]{:S(2)}) %all-to-all-start.2) | async-done | bytes 1048608 | tf_op jit(solution)/shard_map/all_to_all | solution.py:369
  100.7 5.4 %collective-permute-start.7 = (f32[136,128]{1,0:T(8,128)S(1)}, f32[136,128]{1,0:T(8,128)S(1)}, u32[]{:S(2)}, u32[]{:S(2)}) collective-permute-start(f32[136,128]{1,0:T(8,128)S(1)} %half_total.3), channel_id=1, source_target_pairs={{0,32},{32,0},{1,33},{33,1},{2,34},{34,2},{3,35},{35,3},{4,36},{36... | collective-permute-start | bytes 208904 | tf_op jit(solution)/shard_map/ppermute | solution.py:385
  109.5 3.7 %all-to-all-start.3 = ((f32[16,136,128]{2,1,0:T(8,128)}), f32[16,136,128]{2,1,0:T(8,128)S(1)}, u32[]{:S(2)}, u32[]{:S(2)}) async-start(f32[16,136,128]{2,1,0:T(8,128)} %chip_scan.3), calls=%async_computation.3 | async-start | bytes 2228224 | tf_op jit(solution)/shard_map/all_to_all | solution.py:369
  113.3 8.6 %backward_inside.3 = (bf16[1,192,4096]{2,1,0:T(8,128)(2,1)}, f32[192,2048]{1,0:T(8,128)}, f32[192,2048]{1,0:T(8,128)}) custom-call(s32[3]{0:T(128)S(1)} %pad_add_fusion.c_ref, bf16[192,2048]{1,0:T(8,128)(2,1)} %get-tuple-element.69.od_ref, bf16[1,192,4096]{2,1,0:T(8,128)(2,1)} %q_ref.13, ...), custom_call_target="tpu_custom_call", output_to_operand_aliasing={{0}: (8, {})} | custom-call | flops 805306368 | bytes 14049280 | tf_op jit(solution)/shard_map/backward_inside/pallas_call | solution.py:299
  121.8 6.6 %all-to-all-done.3.d_ref.rest_0_ = f32[16,136,128]{2,1,0:T(8,128)S(1)} async-done(((f32[16,136,128]{2,1,0:T(8,128)}), f32[16,136,128]{2,1,0:T(8,128)S(1)}, u32[]{:S(2)}, u32[]{:S(2)}) %all-to-all-start.3) | async-done | bytes 1114144 | tf_op jit(solution)/shard_map/all_to_all | solution.py:369
  128.5 2.9 %onward_back.1 = (f32[16,128,128]{2,1,0:T(8,128)}, f32[16,128,128]{2,1,0:T(8,128)S(1)}, f32[8,128]{1,0:T(8,128)S(1)}) custom-call(s32[3]{0:T(128)S(1)} %pad_add_fusion.c_ref, f32[16,136,128]{2,1,0:T(8,128)S(1)} %all-to-all-done.3.d_ref.rest_0_, f32[16,128,128]{2,1,0:T(8,128)} %get-tuple-element.90.kept_ref, f32[16,8,128]{2,1,0:T(8,128)S(1)} %get-tuple-element.55.lo_ref, ...), custom_call_target="tpu_custom_call" | custom-call | bytes 5509120 | tf_op jit(solution)/shard_map/onward_back/pallas_call | solution.py:299
  131.3 3.6 %collective-permute-start.8 = (f32[16,128,128]{2,1,0:T(8,128)}, f32[16,128,128]{2,1,0:T(8,128)S(1)}, u32[]{:S(2)}, u32[]{:S(2)}) collective-permute-start(f32[16,128,128]{2,1,0:T(8,128)} %get-tuple-element.91), channel_id=1, source_target_pairs={{0,1},{1,0},{2,3},{3,2},{4,5},{5,4},{6,7},{7,6},{8,9},{9,8},{10,11... | collective-permute-start | bytes 3145736 | tf_op jit(solution)/shard_map/ppermute | solution.py:365
  134.9 4.4 %finish.2 = (bf16[1,192,4096]{2,1,0:T(8,128)(2,1)}, bf16[1,192,4096]{2,1,0:T(8,128)(2,1)}) custom-call(s32[3]{0:T(128)S(1)} %pad_add_fusion.c_ref, bf16[1,192,4096]{2,1,0:T(8,128)(2,1)} %k_ref.15, bf16[1,192,4096]{2,1,0:T(8,128)(2,1)} %v_ref.15, f32[32,192]{1,0:T(8,128)S(1)} %get-tuple-element.52.row_ref, f32[192,2048]{1,0:T(8,128)} %get-tuple-element.92.ki_ref, ...), custom_call_target="tpu_custom_call" | custom-call | flops 402653184 | bytes 10510336 | tf_op jit(solution)/shard_map/finish/pallas_call | solution.py:299
  139.8 4.4 %finish.3 = (bf16[1,192,4096]{2,1,0:T(8,128)(2,1)}, bf16[1,192,4096]{2,1,0:T(8,128)(2,1)}) custom-call(s32[3]{0:T(128)S(1)} %pad_add_fusion.c_ref, bf16[1,192,4096]{2,1,0:T(8,128)(2,1)} %k_ref.15, bf16[1,192,4096]{2,1,0:T(8,128)(2,1)} %v_ref.15, f32[32,192]{1,0:T(8,128)S(1)} %get-tuple-element.52.row_ref, ...), custom_call_target="tpu_custom_call", output_to_operand_aliasing={{0}: (7, {}), {1}: (8, {})} | custom-call | flops 402653184 | bytes 13656064 | tf_op jit(solution)/shard_map/finish/pallas_call | solution.py:299
  (46 shorter events, 18.6 us)
Async XLA Ops:
  3.4 5.8 %collective-permute-start = (f32[16,136,128]{2,1,0:T(8,128)S(1)}, f32[16,136,128]{2,1,0:T(8,128)S(1)}, u32[]{:S(2)}, u32[]{:S(2)}) collective-permute-start(f32[16,136,128]{2,1,0:T(8,128)S(1)} %get-tuple-element.54), channel_id=1, source_target_pairs={{0,1},{1,0},{2,3},{3,2},{4,5},{5,4},{6,7},{7,6},{8,9},{9,8},{10,11... | collective-permute-start | bytes 3342344 | tf_op jit(solution)/shard_map/ppermute | solution.py:365
  11.3 21.5 %all-to-all-start = ((f32[16,136,128]{2,1,0:T(8,128)}), f32[16,136,128]{2,1,0:T(8,128)S(1)}, u32[]{:S(2)}, u32[]{:S(2)}) async-start(f32[16,136,128]{2,1,0:T(8,128)} %get-tuple-element.56), calls=%async_computation | async-start | bytes 2228224 | tf_op jit(solution)/shard_map/all_to_all | solution.py:369
  33.4 8.7 %collective-permute-start.1 = (f32[128,128]{1,0:T(8,128)S(1)}, f32[128,128]{1,0:T(8,128)S(1)}, u32[]{:S(2)}, u32[]{:S(2)}) collective-permute-start(f32[128,128]{1,0:T(8,128)S(1)} %half_total.2), channel_id=1, source_target_pairs={{0,32},{32,0},{1,33},{33,1},{2,34},{34,2},{3,35},{35,3},{4,36},{36... | collective-permute-start | bytes 196616 | tf_op jit(solution)/shard_map/ppermute | solution.py:385
  42.2 25.5 %copy-start.5 = (f32[192,2048]{1,0:T(8,128)S(1)}, f32[192,2048]{1,0:T(8,128)}, u32[]{:S(2)}) copy-start(f32[192,2048]{1,0:T(8,128)} %get-tuple-element.65.in_ref) | copy-start | bytes 4718596
  43.8 18.1 %copy-start.6 = (f32[16,128,128]{2,1,0:T(8,128)S(1)}, f32[16,128,128]{2,1,0:T(8,128)}, u32[]{:S(2)}) copy-start(f32[16,128,128]{2,1,0:T(8,128)} %get-tuple-element.62.kept_ref) | copy-start | bytes 3145732
  43.8 23.9 %copy-start.1 = (bf16[1,192,4096]{2,1,0:T(8,128)(2,1)S(1)}, bf16[1,192,4096]{2,1,0:T(8,128)(2,1)}, u32[]{:S(2)}) copy-start(bf16[1,192,4096]{2,1,0:T(8,128)(2,1)} %g_ref.5) | copy-start | bytes 4718596
  61.9 5.8 %copy-start = (bf16[1,192,4096]{2,1,0:T(8,128)(2,1)S(1)}, bf16[1,192,4096]{2,1,0:T(8,128)(2,1)}, u32[]{:S(2)}) copy-start(bf16[1,192,4096]{2,1,0:T(8,128)(2,1)} %q_ref.13) | copy-start | bytes 4718596
  61.9 5.8 %copy-start.7 = (f32[4096]{0:T(1024)S(1)}, f32[4096]{0:T(1024)}, u32[]{:S(2)}) copy-start(f32[4096]{0:T(1024)} %param.11) | copy-start | bytes 49156
  62.6 7.0 %copy-start.2 = (f32[16,128,128]{2,1,0:T(8,128)}, f32[16,128,128]{2,1,0:T(8,128)S(1)}, u32[]{:S(2)}) copy-start(f32[16,128,128]{2,1,0:T(8,128)S(1)} %get-tuple-element.66.x_ref.i_ref) | copy-start | bytes 3145732
  62.7 7.3 %collective-permute-start.2 = (f32[16,128,128]{2,1,0:T(8,128)S(1)}, f32[16,128,128]{2,1,0:T(8,128)S(1)}, u32[]{:S(2)}, u32[]{:S(2)}) collective-permute-start(f32[16,128,128]{2,1,0:T(8,128)S(1)} %get-tuple-element.64), channel_id=1, source_target_pairs={{0,1},{1,0},{2,3},{3,2},{4,5},{5,4},{6,7},{7,6},{8,9},{9,8},{10,11... | collective-permute-start | bytes 3145736 | tf_op jit(solution)/shard_map/ppermute | solution.py:365
  67.7 2.3 %copy-start.4 = (f32[192,2048]{1,0:T(8,128)S(1)}, f32[192,2048]{1,0:T(8,128)}, u32[]{:S(2)}) copy-start(f32[192,2048]{1,0:T(8,128)} %get-tuple-element.59.in_ref) | copy-start | bytes 4718596
  74.1 2.9 %collective-permute-start.3 = (f32[16,128,128]{2,1,0:T(8,128)S(1)}, f32[16,128,128]{2,1,0:T(8,128)S(1)}, u32[]{:S(2)}, u32[]{:S(2)}) collective-permute-start(f32[16,128,128]{2,1,0:T(8,128)S(1)} %get-tuple-element.79), channel_id=1, source_target_pairs={{0,1},{1,0},{2,3},{3,2},{4,5},{5,4},{6,7},{7,6},{8,9},{9,8},{10,11... | collective-permute-start | bytes 3145736 | tf_op jit(solution)/shard_map/ppermute | solution.py:365
  79.0 21.1 %all-to-all-start.2 = ((f32[16,128,128]{2,1,0:T(8,128)}), f32[16,128,128]{2,1,0:T(8,128)S(1)}, u32[]{:S(2)}, u32[]{:S(2)}) async-start(f32[16,128,128]{2,1,0:T(8,128)} %get-tuple-element.80), calls=%async_computation.2 | async-start | bytes 2097152 | tf_op jit(solution)/shard_map/all_to_all | solution.py:369
  82.7 12.9 %collective-permute-start.5 = (f32[8,128]{1,0:T(8,128)S(1)}, f32[8,128]{1,0:T(8,128)S(1)}, u32[]{:S(2)}, u32[]{:S(2)}) collective-permute-start(f32[8,128]{1,0:T(8,128)S(1)} %get-tuple-element.102), channel_id=1, source_target_pairs={{0,128},{64,192},{128,0},{192,64},{1,129},{65,193},{129,1},{193,65... | collective-permute-start | bytes 12296 | tf_op jit(solution)/shard_map/ppermute | solution.py:484
  84.2 11.4 %collective-permute-start.6 = (f32[8,128]{1,0:T(8,128)S(1)}, f32[8,128]{1,0:T(8,128)S(1)}, u32[]{:S(2)}, u32[]{:S(2)}) collective-permute-start(f32[8,128]{1,0:T(8,128)S(1)} %get-tuple-element.103), channel_id=1, source_target_pairs={{0,192},{64,128},{128,64},{192,0},{1,193},{65,129},{129,65},{193,1... | collective-permute-start | bytes 12296 | tf_op jit(solution)/shard_map/ppermute | solution.py:484
  85.7 9.9 %collective-permute-start.4 = (f32[8,128]{1,0:T(8,128)S(1)}, f32[8,128]{1,0:T(8,128)S(1)}, u32[]{:S(2)}, u32[]{:S(2)}) collective-permute-start(f32[8,128]{1,0:T(8,128)S(1)} %slice_bitcast_fusion.2), channel_id=1, source_target_pairs={{0,64},{64,0},{128,192},{192,128},{1,65},{65,1},{129,193},{193,129... | collective-permute-start | bytes 12296 | tf_op jit(solution)/shard_map/ppermute | solution.py:484
  85.9 1.2 copy-start.3
  100.7 7.2 %collective-permute-start.7 = (f32[136,128]{1,0:T(8,128)S(1)}, f32[136,128]{1,0:T(8,128)S(1)}, u32[]{:S(2)}, u32[]{:S(2)}) collective-permute-start(f32[136,128]{1,0:T(8,128)S(1)} %half_total.3), channel_id=1, source_target_pairs={{0,32},{32,0},{1,33},{33,1},{2,34},{34,2},{3,35},{35,3},{4,36},{36... | collective-permute-start | bytes 208904 | tf_op jit(solution)/shard_map/ppermute | solution.py:385
  109.5 18.9 %all-to-all-start.3 = ((f32[16,136,128]{2,1,0:T(8,128)}), f32[16,136,128]{2,1,0:T(8,128)S(1)}, u32[]{:S(2)}, u32[]{:S(2)}) async-start(f32[16,136,128]{2,1,0:T(8,128)} %chip_scan.3), calls=%async_computation.3 | async-start | bytes 2228224 | tf_op jit(solution)/shard_map/all_to_all | solution.py:369
  131.3 8.5 %collective-permute-start.8 = (f32[16,128,128]{2,1,0:T(8,128)}, f32[16,128,128]{2,1,0:T(8,128)S(1)}, u32[]{:S(2)}, u32[]{:S(2)}) collective-permute-start(f32[16,128,128]{2,1,0:T(8,128)} %get-tuple-element.91), channel_id=1, source_target_pairs={{0,1},{1,0},{2,3},{3,2},{4,5},{5,4},{6,7},{7,6},{8,9},{9,8},{10,11... | collective-permute-start | bytes 3145736 | tf_op jit(solution)/shard_map/ppermute | solution.py:365
  134.9 4.4 %collective-permute-start.9 = (f32[8,128]{1,0:T(8,128)S(1)}, f32[8,128]{1,0:T(8,128)S(1)}, u32[]{:S(2)}, u32[]{:S(2)}) collective-permute-start(f32[8,128]{1,0:T(8,128)S(1)} %get-tuple-element.99), channel_id=1, source_target_pairs={{0,1},{1,0},{2,3},{3,2},{4,5},{5,4},{6,7},{7,6},{8,9},{9,8},{10,11... | collective-permute-start | bytes 12296 | tf_op jit(solution)/shard_map/ppermute | solution.py:365

commit v7 on v6

--- a/solution.py
+++ b/solution.py
@@ -18,6 +18,7 @@
 GW = GH * HD
 NG = 4
 HALF = NG // 2
+CH = 4
 NC = 16
 ALL = ("dp", "zh", "x", "y", "core")
 
@@ -169,7 +170,7 @@
         decay = decay_table(cum[:, j : j + 1], row_ref[j : j + 1, :])
         scores = dot(q_ref[:, lanes(j)], k_ref[:, lanes(j)], 1, 1)
         weights = (scores * decay).astype(BF16)
-        fw_ref[j] = weights
+        fw_ref[j] = jnp.transpose(weights)
         in_ref[:, lanes(j)] = dot(weights, v_ref[:, lanes(j)], 1, 0)
 
 
@@ -267,18 +268,54 @@
         inter = growth[:, j : j + 1] * rows_by_state_t(delta, i_ref[j])
         qg_ref[:, at] = (dot(weights, k_ref[:, at], 1, 0) + inter).astype(BF16)
         ki_ref[:, at] = dot(weights, q_ref[:, at], 0, 0)
-        vi_ref[:, at] = dot(fw_ref[j], delta, 0, 0)
-
-
-def finish_kernel(c_ref, k_ref, v_ref, row_ref, ki_ref, vi_ref, x_ref, *rest):
-    cum = columns(row_ref)
+        vi_ref[:, at] = dot(fw_ref[j], delta, 1, 0)
+
+
+def finish_kernel(own, c_ref, row_ref, k_hbm, v_hbm, ki_hbm, vi_hbm, x_hbm, *rest):
+    kg_hbm, vg_hbm, k_buf, v_buf, ki_buf, vi_buf, x_buf, kg_buf, vg_buf, in_sem, out_sem = rest[-11:]
+    half = half_of(own, c_ref)
+    pieces = NC // CH
+    width = CH * HD
+
+    def whole(n):
+        return pl.ds(pl.multiple_of(half * (NC * HD) + n * width, width), width)
+
+    def loads(n):
+        part, heads = pl.ds(n * width, width), pl.ds(n * CH, CH)
+        moves = [
+            (x_hbm.at[heads], x_buf.at[heads]),
+            (k_hbm.at[0, :, whole(n)], k_buf.at[:, part]),
+            (v_hbm.at[0, :, whole(n)], v_buf.at[:, part]),
+            (ki_hbm.at[:, part], ki_buf.at[:, part]),
+            (vi_hbm.at[:, part], vi_buf.at[:, part]),
+        ]
+        return [pltpu.make_async_copy(a, b, in_sem.at[n, i]) for i, (a, b) in enumerate(moves)]
+
+    def stores(n):
+        part = pl.ds(n * width, width)
+        moves = [(kg_buf.at[:, part], kg_hbm.at[0, :, whole(n)]), (vg_buf.at[:, part], vg_hbm.at[0, :, whole(n)])]
+        return [pltpu.make_async_copy(a, b, out_sem.at[n, i]) for i, (a, b) in enumerate(moves)]
+
+    for n in range(pieces):
+        for copy in loads(n):
+            copy.start()
+    cum = jnp.transpose(row_ref[...])
     shrink = jnp.exp(cum[T - 1 : T, :] - cum)
-    kg_ref, vg_ref = rest[-2:]
-    for j in range(GH):
-        at = lanes(j)
-        scale = shrink[:, j : j + 1]
-        kg_ref[:, at] = (ki_ref[:, at] + scale * rows_by_state_t(v_ref[:, at], x_ref[j])).astype(BF16)
-        vg_ref[:, at] = (vi_ref[:, at] + scale * rows_by_state(k_ref[:, at], x_ref[j])).astype(BF16)
+    for n in range(pieces):
+        for copy in loads(n):
+            copy.wait()
+        for j in range(n * CH, (n + 1) * CH):
+            at = lanes(j)
+            scale = shrink[:, j : j + 1]
+            key_part = scale * rows_by_state_t(v_buf[:, at], x_buf[j])
+            kg_buf[:, at] = (ki_buf[:, at] + key_part).astype(BF16)
+            value_part = scale * rows_by_state(k_buf[:, at], x_buf[j])
+            vg_buf[:, at] = (vi_buf[:, at] + value_part).astype(BF16)
+        for copy in stores(n):
+            copy.start()
+    for n in range(pieces):
+        for copy in stores(n):
+            copy.wait()
 
 
 class Kept:
@@ -507,20 +544,23 @@
         functools.partial(hand_on_kernel, False), "onward_back", (HALF,),
         [state_block()] * 2 + [LOG_BLOCK] * 2 + [LOG_TAIL],
         [state_block(), state_block(), pl.BlockSpec((8, HD), lambda i, c: (0, 0))],
-        [STATES, STATES, shape((8, HD))],
-        (core, scanned_back, Kept(kept_moment), log_own, log_got, scanned_back), 0,
+        [STATES, Kept(STATES), shape((8, HD))],
+        (core, scanned_back, kept_moment, log_own, log_got, scanned_back), 0,
     )
     later_other = swap_cores(onward_back)
     later = {True: later_here, False: later_other}
     grads = ()
     for mine in (True, False):
         grads = call(
-            finish_kernel, "finish", (HALF,),
-            [wide(mine), wide(mine), row_block(mine), narrow(), narrow(), state_block()]
-            + [ANY] * len(grads),
-            [wide(mine)] * 2, [Kept(WHOLE_BF16)] * 2,
-            (core, Kept(k), Kept(v), row, Kept(key_inside[mine]), Kept(value_inside[mine]),
-             later[mine], *[Kept(a) for a in grads]), 4 * MM, aliases={7: 0, 8: 1} if grads else None,
+            functools.partial(finish_kernel, mine), "finish", (1,),
+            [pl.BlockSpec((NC, T), lambda i, c, mine=mine: (half_of(mine, c), 0))] + [ANY] * (5 + len(grads)),
+            [ANY] * 2, [Kept(WHOLE_BF16)] * 2,
+            (core, row, Kept(k), Kept(v), Kept(key_inside[mine]), Kept(value_inside[mine]),
+             Kept(later[mine]) if mine else later[mine], *[Kept(a) for a in grads]), 4 * MM,
+            scratch=[pltpu.VMEM((T, NC * HD), BF16)] * 2 + [pltpu.VMEM((T, NC * HD), F32)] * 2
+            + [pltpu.VMEM((NC, HD, HD), F32)] + [pltpu.VMEM((T, NC * HD), BF16)] * 2
+            + [pltpu.SemaphoreType.DMA((NC // CH, 5)), pltpu.SemaphoreType.DMA((NC // CH, 2))],
+            aliases={7: 0, 8: 1} if grads else None,
         )
     key_grad, value_grad = grads
     collected = (collected + swap_cores(collected))[0]

time: 145 us -> 146 us (level)
  no operation moved by 1% of the time
where the time goes in v7:
time: 146 us; the launch traced here: 145 us
  Pallas kernels  60.3 us (41%)
  starting transfers between devices  40.2 us (28%)
  waiting for transfers between devices  22.6 us (15%)
  blocking collectives  18.1 us (12%)
  local copies, waits for them, and re-layouts  2.49 us (2%)
    pallas_call x19, Pallas kernels, call(): pl.pallas_call(kernel, name=name, grid_spec=pltpu.PrefetchScalarGridSpec(...  60.3 us
    all_to_all x3, waiting for transfers between devices, chips_all_to_all(): lax.all_to_all(values, ('x', 'y'), split_axis=0, concat_axis=0, tiled=True)  18.8 us
    all_to_all x1, blocking collectives, chips_all_to_all(): lax.all_to_all(values, ('x', 'y'), split_axis=0, concat_axis=0, tiled=True)  18.1 us
    ppermute x2, starting transfers between devices, scan_over_chips(): before = lax.ppermute(total, 'zh', [(0, 1), (1, 0)])  12.4 us
    all_to_all x3, starting transfers between devices, chips_all_to_all(): lax.all_to_all(values, ('x', 'y'), split_axis=0, concat_axis=0, tiled=True)  12.4 us
    ppermute x5, starting transfers between devices, swap_cores(): return lax.ppermute(values, 'core', [(0, 1), (1, 0)])  12.2 us
    ppermute x2, waiting for transfers between devices, scan_over_chips(): before = lax.ppermute(total, 'zh', [(0, 1), (1, 0)])  3.54 us
    ppermute x3, starting transfers between devices, per_device(): lax.ppermute(gains[distance], 'dp', [(i, i ^ distance) for i in range(NG)])  3.19 us
  transfers between devices with their start and end apart: 13, of which 6 were waited for; matrix products, arithmetic and copies ran while one was open for 0% of the time, Pallas kernels for 26%

profile of v7, /device:TPU:1, one launch (start us, length us, event | category | flops | bytes accessed | tf_op | source)
XLA Modules:
  0.0 145.4 jit_solution(10659755548136635185)
XLA Ops:
  0.7 2.7 %states_other.1 = (f32[16,136,128]{2,1,0:T(8,128)S(1)}, f32[32,192]{1,0:T(8,128)S(1)}) custom-call(s32[3]{0:T(128)S(1)} %pad_add_fusion.c_ref, bf16[1,192,4096]{2,1,0:T(8,128)(2,1)} %k_hbm.3, bf16[1,192,4096]{2,1,0:T(8,128)(2,1)} %v_hbm.3, f32[32,192]{1,0:T(8,128)} %bitcast.26), custom_call_target="tpu_custom_call" | custom-call | flops 100663296 | bytes 4308992 | tf_op jit(solution)/shard_map/states_other/pallas_call | solution.py:336
  3.4 3.3 %collective-permute-start = (f32[16,136,128]{2,1,0:T(8,128)S(1)}, f32[16,136,128]{2,1,0:T(8,128)S(1)}, u32[]{:S(2)}, u32[]{:S(2)}) collective-permute-start(f32[16,136,128]{2,1,0:T(8,128)S(1)} %get-tuple-element.54), channel_id=1, source_target_pairs={{0,1},{1,0},{2,3},{3,2},{4,5},{5,4},{6,7},{7,6},{8,9},{9,8},{10,11... | collective-permute-start | bytes 3342344 | tf_op jit(solution)/shard_map/ppermute | solution.py:402
  6.7 2.5 %states_own.1 = (f32[16,128,128]{2,1,0:T(8,128)S(1)}, f32[16,8,128]{2,1,0:T(8,128)S(1)}) custom-call(s32[3]{0:T(128)S(1)} %pad_add_fusion.c_ref, bf16[1,192,4096]{2,1,0:T(8,128)(2,1)} %k_hbm.3, bf16[1,192,4096]{2,1,0:T(8,128)(2,1)} %v_hbm.3, f32[32,192]{1,0:T(8,128)S(1)} %get-tuple-element.52.row_ref), custom_call_target="tpu_custom_call" | custom-call | flops 100663296 | bytes 4284416 | tf_op jit(solution)/shard_map/states_own/pallas_call | solution.py:336
  9.2 2.1 %chip_total.1 = (f32[16,136,128]{2,1,0:T(8,128)}, f32[16,128,128]{2,1,0:T(8,128)}, f32[16,8,128]{2,1,0:T(8,128)S(1)}) custom-call(s32[3]{0:T(128)S(1)} %pad_add_fusion.c_ref, f32[16,128,128]{2,1,0:T(8,128)S(1)} %get-tuple-element.53.own_ref, f32[16,136,128]{2,1,0:T(8,128)S(1)} %collective-permute-done.got_ref.lg_ref, ...), custom_call_target="tpu_custom_call" | custom-call | bytes 5570560 | tf_op jit(solution)/shard_map/chip_total/pallas_call | solution.py:336
  11.4 5.0 %all-to-all-start = ((f32[16,136,128]{2,1,0:T(8,128)}), f32[16,136,128]{2,1,0:T(8,128)S(1)}, u32[]{:S(2)}, u32[]{:S(2)}) async-start(f32[16,136,128]{2,1,0:T(8,128)} %get-tuple-element.56), calls=%async_computation | async-start | bytes 2228224 | tf_op jit(solution)/shard_map/all_to_all | solution.py:406
  16.4 4.6 %forward_inside.2 = (bf16[16,192,192]{2,1,0:T(8,128)(2,1)}, f32[192,2048]{1,0:T(8,128)}) custom-call(s32[3]{0:T(128)S(1)} %pad_add_fusion.c_ref, bf16[1,192,4096]{2,1,0:T(8,128)(2,1)} %q_ref.13, bf16[1,192,4096]{2,1,0:T(8,128)(2,1)} %k_hbm.3, bf16[1,192,4096]{2,1,0:T(8,128)(2,1)} %v_hbm.3, f32[32,192]{1,0:T(8,128)S(1)} %get-tuple-element.52.row_ref), custom_call_target="tpu_custom_call" | custom-call | flops 301989888 | bytes 7495680 | tf_op jit(solution)/shard_map/forward_inside/pallas_call | solution.py:336
  21.0 4.6 %forward_inside.3 = (bf16[16,192,192]{2,1,0:T(8,128)(2,1)}, f32[192,2048]{1,0:T(8,128)}) custom-call(s32[3]{0:T(128)S(1)} %pad_add_fusion.c_ref, bf16[1,192,4096]{2,1,0:T(8,128)(2,1)} %q_ref.13, bf16[1,192,4096]{2,1,0:T(8,128)(2,1)} %k_hbm.3, bf16[1,192,4096]{2,1,0:T(8,128)(2,1)} %v_hbm.3, f32[32,192]{1,0:T(8,128)S(1)} %get-tuple-element.52.row_ref), custom_call_target="tpu_custom_call" | custom-call | flops 301989888 | bytes 7495680 | tf_op jit(solution)/shard_map/forward_inside/pallas_call | solution.py:336
  25.6 7.3 %all-to-all-done.m_ref.l_ref = f32[16,136,128]{2,1,0:T(8,128)S(1)} async-done(((f32[16,136,128]{2,1,0:T(8,128)}), f32[16,136,128]{2,1,0:T(8,128)S(1)}, u32[]{:S(2)}, u32[]{:S(2)}) %all-to-all-start) | async-done | bytes 1114144 | tf_op jit(solution)/shard_map/all_to_all | solution.py:406
  33.5 7.0 %collective-permute-start.1 = (f32[128,128]{1,0:T(8,128)S(1)}, f32[128,128]{1,0:T(8,128)S(1)}, u32[]{:S(2)}, u32[]{:S(2)}) collective-permute-start(f32[128,128]{1,0:T(8,128)S(1)} %half_total.2), channel_id=1, source_target_pairs={{0,32},{32,0},{1,33},{33,1},{2,34},{34,2},{3,35},{35,3},{4,36},{36... | collective-permute-start | bytes 196616 | tf_op jit(solution)/shard_map/ppermute | solution.py:422
  43.8 18.1 %all_to_all.20.d_ref = f32[16,128,128]{2,1,0:T(8,128)S(1)} all-to-all(f32[16,128,128]{2,1,0:T(8,128)} %get-tuple-element.61), channel_id=1, replica_groups=mesh['dp'=4,'zh'=2,'x'=4,'y'=4,'core'=2] {'x','y'}, dimensions={0} | all-to-all | bytes 2097152 | tf_op jit(solution)/shard_map/all_to_all | solution.py:406
  62.7 5.0 %collective-permute-start.2 = (f32[16,128,128]{2,1,0:T(8,128)S(1)}, f32[16,128,128]{2,1,0:T(8,128)S(1)}, u32[]{:S(2)}, u32[]{:S(2)}) collective-permute-start(f32[16,128,128]{2,1,0:T(8,128)S(1)} %get-tuple-element.64), channel_id=1, source_target_pairs={{0,1},{1,0},{2,3},{3,2},{4,5},{5,4},{6,7},{7,6},{8,9},{9,8},{10,11... | collective-permute-start | bytes 3145736 | tf_op jit(solution)/shard_map/ppermute | solution.py:402
  70.0 4.2 %attend_other.1 = (bf16[192,2048]{1,0:T(8,128)(2,1)}, f32[16,128,128]{2,1,0:T(8,128)S(1)}, f32[2,8,128]{2,1,0:T(8,128)S(1)}, f32[192,128]{1,0:T(8,128)S(1)}, f32[192,128]{1,0:T(8,128)S(1)}) custom-call(s32[3]{0:T(128)S(1)} %pad_add_fusion.c_ref, bf16[1,192,4096]{2,1,0:T(8,128)(2,1)S(1)} %copy-done, bf16[1,192,4096]{2,1,0:T(8,128)(2,1)S(1)} %copy-done.1, ...), custom_call_target="tpu_custom_call" | custom-call | flops 301989888 | bytes 8044544 | tf_op jit(solution)/shard_map/attend_other/pallas_call | solution.py:336
  74.5 2.5 %delta_own.1 = (bf16[192,2048]{1,0:T(8,128)(2,1)}, f32[16,128,128]{2,1,0:T(8,128)S(1)}, f32[2,8,128]{2,1,0:T(8,128)S(1)}) custom-call(s32[3]{0:T(128)S(1)} %pad_add_fusion.c_ref, bf16[1,192,4096]{2,1,0:T(8,128)(2,1)S(1)} %copy-done, bf16[1,192,4096]{2,1,0:T(8,128)(2,1)S(1)} %copy-done.1, f32[1,4096]{1,0:T(1,128)S(1)} %bitcast.25, ...), custom_call_target="tpu_custom_call" | custom-call | flops 100663296 | bytes 6799360 | tf_op jit(solution)/shard_map/delta_own/pallas_call | solution.py:336
  79.0 3.7 %all-to-all-start.2 = ((f32[16,128,128]{2,1,0:T(8,128)}), f32[16,128,128]{2,1,0:T(8,128)S(1)}, u32[]{:S(2)}, u32[]{:S(2)}) async-start(f32[16,128,128]{2,1,0:T(8,128)} %get-tuple-element.80), calls=%async_computation.2 | async-start | bytes 2097152 | tf_op jit(solution)/shard_map/all_to_all | solution.py:406
  87.2 8.3 %backward_inside.2 = (bf16[1,192,4096]{2,1,0:T(8,128)(2,1)}, f32[192,2048]{1,0:T(8,128)}, f32[192,2048]{1,0:T(8,128)}) custom-call(s32[3]{0:T(128)S(1)} %pad_add_fusion.c_ref, bf16[192,2048]{1,0:T(8,128)(2,1)} %get-tuple-element.74.od_ref, bf16[1,192,4096]{2,1,0:T(8,128)(2,1)} %q_ref.13, bf16[1,192,4096]{2,1,0:T(8,128)(2,1)} %k_hbm.3, ...), custom_call_target="tpu_custom_call" | custom-call | flops 805306368 | bytes 12476416 | tf_op jit(solution)/shard_map/backward_inside/pallas_call | solution.py:336
  95.5 4.7 %all-to-all-done.2.m_ref = f32[16,128,128]{2,1,0:T(8,128)S(1)} async-done(((f32[16,128,128]{2,1,0:T(8,128)}), f32[16,128,128]{2,1,0:T(8,128)S(1)}, u32[]{:S(2)}, u32[]{:S(2)}) %all-to-all-start.2) | async-done | bytes 1048608 | tf_op jit(solution)/shard_map/all_to_all | solution.py:406
  100.8 5.4 %collective-permute-start.7 = (f32[136,128]{1,0:T(8,128)S(1)}, f32[136,128]{1,0:T(8,128)S(1)}, u32[]{:S(2)}, u32[]{:S(2)}) collective-permute-start(f32[136,128]{1,0:T(8,128)S(1)} %half_total.3), channel_id=1, source_target_pairs={{0,32},{32,0},{1,33},{33,1},{2,34},{34,2},{3,35},{35,3},{4,36},{36... | collective-permute-start | bytes 208904 | tf_op jit(solution)/shard_map/ppermute | solution.py:422
  109.6 3.7 %all-to-all-start.3 = ((f32[16,136,128]{2,1,0:T(8,128)}), f32[16,136,128]{2,1,0:T(8,128)S(1)}, u32[]{:S(2)}, u32[]{:S(2)}) async-start(f32[16,136,128]{2,1,0:T(8,128)} %chip_scan.3), calls=%async_computation.3 | async-start | bytes 2228224 | tf_op jit(solution)/shard_map/all_to_all | solution.py:406
  113.3 8.3 %backward_inside.3 = (bf16[1,192,4096]{2,1,0:T(8,128)(2,1)}, f32[192,2048]{1,0:T(8,128)}, f32[192,2048]{1,0:T(8,128)}) custom-call(s32[3]{0:T(128)S(1)} %pad_add_fusion.c_ref, bf16[192,2048]{1,0:T(8,128)(2,1)} %get-tuple-element.69.od_ref, bf16[1,192,4096]{2,1,0:T(8,128)(2,1)} %q_ref.13, ...), custom_call_target="tpu_custom_call", output_to_operand_aliasing={{0}: (8, {})} | custom-call | flops 805306368 | bytes 14049280 | tf_op jit(solution)/shard_map/backward_inside/pallas_call | solution.py:336
  121.6 6.9 %all-to-all-done.3.d_ref.rest_0_ = f32[16,136,128]{2,1,0:T(8,128)S(1)} async-done(((f32[16,136,128]{2,1,0:T(8,128)}), f32[16,136,128]{2,1,0:T(8,128)S(1)}, u32[]{:S(2)}, u32[]{:S(2)}) %all-to-all-start.3) | async-done | bytes 1114144 | tf_op jit(solution)/shard_map/all_to_all | solution.py:406
  129.7 2.2 %onward_back.1 = (f32[16,128,128]{2,1,0:T(8,128)}, f32[16,128,128]{2,1,0:T(8,128)}, f32[8,128]{1,0:T(8,128)S(1)}) custom-call(s32[3]{0:T(128)S(1)} %pad_add_fusion.c_ref, f32[16,136,128]{2,1,0:T(8,128)S(1)} %all-to-all-done.3.d_ref.rest_0_, f32[16,128,128]{2,1,0:T(8,128)S(1)} %copy-done.7, f32[16,8,128]{2,1,0:T(8,128)S(1)} %get-tuple-element.55.lo_ref, ...), custom_call_target="tpu_custom_call" | custom-call | bytes 5509120 | tf_op jit(solution)/shard_map/onward_back/pallas_call | solution.py:336
  131.9 3.6 %collective-permute-start.8 = (f32[16,128,128]{2,1,0:T(8,128)}, f32[16,128,128]{2,1,0:T(8,128)S(1)}, u32[]{:S(2)}, u32[]{:S(2)}) collective-permute-start(f32[16,128,128]{2,1,0:T(8,128)} %get-tuple-element.91), channel_id=1, source_target_pairs={{0,1},{1,0},{2,3},{3,2},{4,5},{5,4},{6,7},{7,6},{8,9},{9,8},{10,11... | collective-permute-start | bytes 3145736 | tf_op jit(solution)/shard_map/ppermute | solution.py:402
  135.4 4.7 %finish.2 = (bf16[1,192,4096]{2,1,0:T(8,128)(2,1)}, bf16[1,192,4096]{2,1,0:T(8,128)(2,1)}) custom-call(s32[3]{0:T(128)S(1)} %pad_add_fusion.c_ref, f32[32,192]{1,0:T(8,128)S(1)} %get-tuple-element.52.row_ref, bf16[1,192,4096]{2,1,0:T(8,128)(2,1)} %k_hbm.3, bf16[1,192,4096]{2,1,0:T(8,128)(2,1)} %v_hbm.3, f32[192,2048]{1,0:T(8,128)} %get-tuple-element.92.ki_hbm, ...), custom_call_target="tpu_custom_call" | custom-call | flops 402653184 | bytes 10510336 | tf_op jit(solution)/shard_map/finish/pallas_call | solution.py:336
  140.8 4.4 %finish.3 = (bf16[1,192,4096]{2,1,0:T(8,128)(2,1)}, bf16[1,192,4096]{2,1,0:T(8,128)(2,1)}) custom-call(s32[3]{0:T(128)S(1)} %pad_add_fusion.c_ref, f32[32,192]{1,0:T(8,128)S(1)} %get-tuple-element.52.row_ref, bf16[1,192,4096]{2,1,0:T(8,128)(2,1)} %k_hbm.3, bf16[1,192,4096]{2,1,0:T(8,128)(2,1)} %v_hbm.3, ...), custom_call_target="tpu_custom_call", output_to_operand_aliasing={{0}: (7, {}), {1}: (8, {})} | custom-call | flops 402653184 | bytes 13656064 | tf_op jit(solution)/shard_map/finish/pallas_call | solution.py:336
  (48 shorter events, 19.8 us)
Async XLA Ops:
  3.4 5.8 %collective-permute-start = (f32[16,136,128]{2,1,0:T(8,128)S(1)}, f32[16,136,128]{2,1,0:T(8,128)S(1)}, u32[]{:S(2)}, u32[]{:S(2)}) collective-permute-start(f32[16,136,128]{2,1,0:T(8,128)S(1)} %get-tuple-element.54), channel_id=1, source_target_pairs={{0,1},{1,0},{2,3},{3,2},{4,5},{5,4},{6,7},{7,6},{8,9},{9,8},{10,11... | collective-permute-start | bytes 3342344 | tf_op jit(solution)/shard_map/ppermute | solution.py:402
  11.4 21.5 %all-to-all-start = ((f32[16,136,128]{2,1,0:T(8,128)}), f32[16,136,128]{2,1,0:T(8,128)S(1)}, u32[]{:S(2)}, u32[]{:S(2)}) async-start(f32[16,136,128]{2,1,0:T(8,128)} %get-tuple-element.56), calls=%async_computation | async-start | bytes 2228224 | tf_op jit(solution)/shard_map/all_to_all | solution.py:406
  33.5 8.7 %collective-permute-start.1 = (f32[128,128]{1,0:T(8,128)S(1)}, f32[128,128]{1,0:T(8,128)S(1)}, u32[]{:S(2)}, u32[]{:S(2)}) collective-permute-start(f32[128,128]{1,0:T(8,128)S(1)} %half_total.2), channel_id=1, source_target_pairs={{0,32},{32,0},{1,33},{33,1},{2,34},{34,2},{3,35},{35,3},{4,36},{36... | collective-permute-start | bytes 196616 | tf_op jit(solution)/shard_map/ppermute | solution.py:422
  42.2 25.5 %copy-start.5 = (f32[192,2048]{1,0:T(8,128)S(1)}, f32[192,2048]{1,0:T(8,128)}, u32[]{:S(2)}) copy-start(f32[192,2048]{1,0:T(8,128)} %get-tuple-element.65.in_ref) | copy-start | bytes 4718596
  43.8 18.1 %copy-start.6 = (f32[16,128,128]{2,1,0:T(8,128)S(1)}, f32[16,128,128]{2,1,0:T(8,128)}, u32[]{:S(2)}) copy-start(f32[16,128,128]{2,1,0:T(8,128)} %get-tuple-element.62.kept_ref) | copy-start | bytes 3145732
  43.8 23.9 %copy-start.1 = (bf16[1,192,4096]{2,1,0:T(8,128)(2,1)S(1)}, bf16[1,192,4096]{2,1,0:T(8,128)(2,1)}, u32[]{:S(2)}) copy-start(bf16[1,192,4096]{2,1,0:T(8,128)(2,1)} %g_ref.5) | copy-start | bytes 4718596
  61.9 5.8 %copy-start = (bf16[1,192,4096]{2,1,0:T(8,128)(2,1)S(1)}, bf16[1,192,4096]{2,1,0:T(8,128)(2,1)}, u32[]{:S(2)}) copy-start(bf16[1,192,4096]{2,1,0:T(8,128)(2,1)} %q_ref.13) | copy-start | bytes 4718596
  61.9 5.8 %copy-start.8 = (f32[4096]{0:T(1024)S(1)}, f32[4096]{0:T(1024)}, u32[]{:S(2)}) copy-start(f32[4096]{0:T(1024)} %param.11) | copy-start | bytes 49156
  62.7 7.0 %copy-start.2 = (f32[16,128,128]{2,1,0:T(8,128)}, f32[16,128,128]{2,1,0:T(8,128)S(1)}, u32[]{:S(2)}) copy-start(f32[16,128,128]{2,1,0:T(8,128)S(1)} %get-tuple-element.66.x_ref.i_ref) | copy-start | bytes 3145732
  62.7 7.3 %collective-permute-start.2 = (f32[16,128,128]{2,1,0:T(8,128)S(1)}, f32[16,128,128]{2,1,0:T(8,128)S(1)}, u32[]{:S(2)}, u32[]{:S(2)}) collective-permute-start(f32[16,128,128]{2,1,0:T(8,128)S(1)} %get-tuple-element.64), channel_id=1, source_target_pairs={{0,1},{1,0},{2,3},{3,2},{4,5},{5,4},{6,7},{7,6},{8,9},{9,8},{10,11... | collective-permute-start | bytes 3145736 | tf_op jit(solution)/shard_map/ppermute | solution.py:402
  67.7 2.3 %copy-start.4 = (f32[192,2048]{1,0:T(8,128)S(1)}, f32[192,2048]{1,0:T(8,128)}, u32[]{:S(2)}) copy-start(f32[192,2048]{1,0:T(8,128)} %get-tuple-element.59.in_ref) | copy-start | bytes 4718596
  74.1 2.9 %collective-permute-start.3 = (f32[16,128,128]{2,1,0:T(8,128)S(1)}, f32[16,128,128]{2,1,0:T(8,128)S(1)}, u32[]{:S(2)}, u32[]{:S(2)}) collective-permute-start(f32[16,128,128]{2,1,0:T(8,128)S(1)} %get-tuple-element.79), channel_id=1, source_target_pairs={{0,1},{1,0},{2,3},{3,2},{4,5},{5,4},{6,7},{7,6},{8,9},{9,8},{10,11... | collective-permute-start | bytes 3145736 | tf_op jit(solution)/shard_map/ppermute | solution.py:402
  79.0 21.1 %all-to-all-start.2 = ((f32[16,128,128]{2,1,0:T(8,128)}), f32[16,128,128]{2,1,0:T(8,128)S(1)}, u32[]{:S(2)}, u32[]{:S(2)}) async-start(f32[16,128,128]{2,1,0:T(8,128)} %get-tuple-element.80), calls=%async_computation.2 | async-start | bytes 2097152 | tf_op jit(solution)/shard_map/all_to_all | solution.py:406
  82.7 12.7 %collective-permute-start.5 = (f32[8,128]{1,0:T(8,128)S(1)}, f32[8,128]{1,0:T(8,128)S(1)}, u32[]{:S(2)}, u32[]{:S(2)}) collective-permute-start(f32[8,128]{1,0:T(8,128)S(1)} %get-tuple-element.102), channel_id=1, source_target_pairs={{0,128},{64,192},{128,0},{192,64},{1,129},{65,193},{129,1},{193,65... | collective-permute-start | bytes 12296 | tf_op jit(solution)/shard_map/ppermute | solution.py:521
  84.2 11.2 %collective-permute-start.6 = (f32[8,128]{1,0:T(8,128)S(1)}, f32[8,128]{1,0:T(8,128)S(1)}, u32[]{:S(2)}, u32[]{:S(2)}) collective-permute-start(f32[8,128]{1,0:T(8,128)S(1)} %get-tuple-element.103), channel_id=1, source_target_pairs={{0,192},{64,128},{128,64},{192,0},{1,193},{65,129},{129,65},{193,1... | collective-permute-start | bytes 12296 | tf_op jit(solution)/shard_map/ppermute | solution.py:521
  85.7 9.7 %collective-permute-start.4 = (f32[8,128]{1,0:T(8,128)S(1)}, f32[8,128]{1,0:T(8,128)S(1)}, u32[]{:S(2)}, u32[]{:S(2)}) collective-permute-start(f32[8,128]{1,0:T(8,128)S(1)} %slice_bitcast_fusion.2), channel_id=1, source_target_pairs={{0,64},{64,0},{128,192},{192,128},{1,65},{65,1},{129,193},{193,129... | collective-permute-start | bytes 12296 | tf_op jit(solution)/shard_map/ppermute | solution.py:521
  85.9 1.2 copy-start.3
  100.8 7.2 %collective-permute-start.7 = (f32[136,128]{1,0:T(8,128)S(1)}, f32[136,128]{1,0:T(8,128)S(1)}, u32[]{:S(2)}, u32[]{:S(2)}) collective-permute-start(f32[136,128]{1,0:T(8,128)S(1)} %half_total.3), channel_id=1, source_target_pairs={{0,32},{32,0},{1,33},{33,1},{2,34},{34,2},{3,35},{35,3},{4,36},{36... | collective-permute-start | bytes 208904 | tf_op jit(solution)/shard_map/ppermute | solution.py:422
  109.6 18.9 %all-to-all-start.3 = ((f32[16,136,128]{2,1,0:T(8,128)}), f32[16,136,128]{2,1,0:T(8,128)S(1)}, u32[]{:S(2)}, u32[]{:S(2)}) async-start(f32[16,136,128]{2,1,0:T(8,128)} %chip_scan.3), calls=%async_computation.3 | async-start | bytes 2228224 | tf_op jit(solution)/shard_map/all_to_all | solution.py:406
  128.5 1.2 copy-start.7
  131.9 8.9 %collective-permute-start.8 = (f32[16,128,128]{2,1,0:T(8,128)}, f32[16,128,128]{2,1,0:T(8,128)S(1)}, u32[]{:S(2)}, u32[]{:S(2)}) collective-permute-start(f32[16,128,128]{2,1,0:T(8,128)} %get-tuple-element.91), channel_id=1, source_target_pairs={{0,1},{1,0},{2,3},{3,2},{4,5},{5,4},{6,7},{7,6},{8,9},{9,8},{10,11... | collective-permute-start | bytes 3145736 | tf_op jit(solution)/shard_map/ppermute | solution.py:402
  135.4 4.8 %collective-permute-start.9 = (f32[8,128]{1,0:T(8,128)S(1)}, f32[8,128]{1,0:T(8,128)S(1)}, u32[]{:S(2)}, u32[]{:S(2)}) collective-permute-start(f32[8,128]{1,0:T(8,128)S(1)} %get-tuple-element.99), channel_id=1, source_target_pairs={{0,1},{1,0},{2,3},{3,2},{4,5},{5,4},{6,7},{7,6},{8,9},{9,8},{10,11... | collective-permute-start | bytes 12296 | tf_op jit(solution)/shard_map/ppermute | solution.py:402

commit v8 on v6

--- a/solution.py
+++ b/solution.py
@@ -18,6 +18,7 @@
 GW = GH * HD
 NG = 4
 HALF = NG // 2
+DEVICES = 256
 NC = 16
 ALL = ("dp", "zh", "x", "y", "core")
 
@@ -122,20 +123,23 @@
 
 def scan_kernel(upward, c_ref, m_ref, l_ref, t_ref, *rest):
     if upward:
-        o_ref, log_ref = rest
+        o_hbm, log_ref, o_buf, sem = rest
         log_ref[...] = l_ref[...]
     else:
-        gain_ref, o_ref = rest
+        gain_ref, o_hbm, o_buf, sem = rest
         both = gain_ref[...] + t_ref[HD:, :]
-    run = t_ref[:HD, :]
-    run = jnp.where(c_ref[2] == (1 if upward else 0), run, 0.0)
+    run = jnp.where(c_ref[2] == (1 if upward else 0), t_ref[:HD, :], 0.0)
+    copies = [pltpu.make_async_copy(o_buf.at[i], o_hbm.at[i], sem.at[i]) for i in range(NC)]
     for i in range(NC) if upward else reversed(range(NC)):
-        o_ref[i, :HD, :] = run
-        run = jnp.exp(l_ref[i, 0:1, :]) * run + m_ref[i]
+        o_buf[i, :HD, :] = run
         if not upward:
             x = i // 4
             row = jnp.where(c_ref[2] == 0, both[x : x + 1, :], both[4 + x : 5 + x, :])
-            o_ref[i, HD:, :] = jnp.broadcast_to(row, (8, HD))
+            o_buf[i, HD:, :] = jnp.broadcast_to(row, (8, HD))
+        copies[i].start()
+        run = jnp.exp(l_ref[i, 0:1, :]) * run + m_ref[i]
+    for copy in copies:
+        copy.wait()
 
 
 def hand_on_kernel(upward, c_ref, d_ref, kept_ref, lo_ref, lg_ref, *rest):
@@ -169,7 +173,7 @@
         decay = decay_table(cum[:, j : j + 1], row_ref[j : j + 1, :])
         scores = dot(q_ref[:, lanes(j)], k_ref[:, lanes(j)], 1, 1)
         weights = (scores * decay).astype(BF16)
-        fw_ref[j] = weights
+        fw_ref[j] = jnp.transpose(weights)
         in_ref[:, lanes(j)] = dot(weights, v_ref[:, lanes(j)], 1, 0)
 
 
@@ -266,19 +270,25 @@
         weights = (dot(delta, v_ref[:, at], 1, 1) * decay).astype(BF16)
         inter = growth[:, j : j + 1] * rows_by_state_t(delta, i_ref[j])
         qg_ref[:, at] = (dot(weights, k_ref[:, at], 1, 0) + inter).astype(BF16)
-        ki_ref[:, at] = dot(weights, q_ref[:, at], 0, 0)
-        vi_ref[:, at] = dot(fw_ref[j], delta, 0, 0)
-
-
-def finish_kernel(c_ref, k_ref, v_ref, row_ref, ki_ref, vi_ref, x_ref, *rest):
+        ki_ref[:, at] = dot(weights, q_ref[:, at], 0, 0).astype(BF16)
+        vi_ref[:, at] = dot(fw_ref[j], delta, 1, 0).astype(BF16)
+
+
+def finish_kernel(own, c_ref, k_ref, v_ref, row_ref, ki_ref, vi_ref, x_ref, *rest):
     cum = columns(row_ref)
     shrink = jnp.exp(cum[T - 1 : T, :] - cum)
-    kg_ref, vg_ref = rest[-2:]
+    if own:
+        kg_ref, vg_ref = rest
+    else:
+        mine_ref, pair_ref, _, _, kg_ref, vg_ref, gain_ref = rest
+        total = (mine_ref[...] + pair_ref[...]) * (1.0 / math.sqrt(T * DEVICES))
+        at = c_ref[3] * 32 + c_ref[0] * 16
+        gain_ref[...] = pltpu.roll(total, lax.rem(HD - at, HD), 1)[0:1, :16]
     for j in range(GH):
         at = lanes(j)
         scale = shrink[:, j : j + 1]
-        kg_ref[:, at] = (ki_ref[:, at] + scale * rows_by_state_t(v_ref[:, at], x_ref[j])).astype(BF16)
-        vg_ref[:, at] = (vi_ref[:, at] + scale * rows_by_state(k_ref[:, at], x_ref[j])).astype(BF16)
+        kg_ref[:, at] = (ki_ref[:, at].astype(F32) + scale * rows_by_state_t(v_ref[:, at], x_ref[j])).astype(BF16)
+        vg_ref[:, at] = (vi_ref[:, at].astype(F32) + scale * rows_by_state(k_ref[:, at], x_ref[j])).astype(BF16)
 
 
 class Kept:
@@ -383,16 +393,17 @@
         (place, got, logs, *more), 0,
     )
     before = lax.ppermute(total, "zh", [(0, 1), (1, 0)])
-    outs = [pl.BlockSpec((NC, rows, HD), lambda i, c: (0, 0, 0))] + [logs_out] * upward
+    outs = [ANY] + [logs_out] * upward
     return call(
         functools.partial(scan_kernel, upward), "chip_scan", (1,),
         [whole_m, whole_l, whole_t] + more_specs, outs, [Kept(shape((NC, rows, HD))), LOGS][: len(outs)],
         (place, got, logs, before, *more), 0,
+        scratch=[pltpu.VMEM((NC, rows, HD), F32), pltpu.SemaphoreType.DMA((NC,))],
     )
 
 
 def per_device(queries, key_rows, value_rows, out_grad, log_decay, norm_gain):
-    core = jnp.stack([lax.axis_index(a).astype(jnp.int32) for a in ("core", "dp", "zh")])
+    core = jnp.stack([lax.axis_index(a).astype(jnp.int32) for a in ("core", "dp", "zh", "y")])
     q, k, v, g = queries, key_rows, value_rows, out_grad
     gain = norm_gain.reshape(1, NG * GW)
     logs = jnp.transpose(log_decay[0])
@@ -484,7 +495,7 @@
         collected += lax.ppermute(gains[distance], "dp", [(i, i ^ distance) for i in range(NG)])
 
     delta = {True: delta_own, False: delta_other}
-    state = {True: state_here, False: state_other}
+    state = {True: Kept(state_here), False: state_other}
     query_grad, key_inside, value_inside = (), {}, {}
     for mine in (True, False):
         *query_grad, key_inside[mine], value_inside[mine] = call(
@@ -493,7 +504,7 @@
              pl.BlockSpec((GH, T, T), lambda i, c: (i, 0, 0)), row_block(mine), state_block()]
             + [ANY] * len(query_grad),
             [wide(mine), narrow(), narrow()],
-            [Kept(WHOLE_BF16), Kept(HALF_F32), Kept(HALF_F32)],
+            [Kept(WHOLE_BF16), Kept(HALF_BF16), Kept(HALF_BF16)],
             (core, Kept(delta[mine]), Kept(q), Kept(k), Kept(v), Kept(weights[mine]), row, state[mine],
              *[Kept(a) for a in query_grad]),
             4 * SM + 2 * MM, aliases={8: 0} if query_grad else None,
@@ -511,23 +522,23 @@
         (core, scanned_back, Kept(kept_moment), log_own, log_got, scanned_back), 0,
     )
     later_other = swap_cores(onward_back)
-    later = {True: later_here, False: later_other}
-    grads = ()
-    for mine in (True, False):
-        grads = call(
-            finish_kernel, "finish", (HALF,),
-            [wide(mine), wide(mine), row_block(mine), narrow(), narrow(), state_block()]
-            + [ANY] * len(grads),
-            [wide(mine)] * 2, [Kept(WHOLE_BF16)] * 2,
-            (core, Kept(k), Kept(v), row, Kept(key_inside[mine]), Kept(value_inside[mine]),
-             later[mine], *[Kept(a) for a in grads]), 4 * MM, aliases={7: 0, 8: 1} if grads else None,
-        )
-    key_grad, value_grad = grads
-    collected = (collected + swap_cores(collected))[0]
-    at = lax.axis_index("y") * 32 + lax.axis_index("core") * 16
-    positions = T * lax.axis_size(ALL)
-    gain_grad = lax.dynamic_slice_in_dim(collected, at, 16) * (1.0 / math.sqrt(positions))
-    return query_grad[0], key_grad, value_grad, gain_grad
+    pair = swap_cores(collected)
+    inputs = [[wide(mine), wide(mine), row_block(mine), narrow(), narrow(), state_block()] for mine in (True, False)]
+    small = pl.BlockSpec((8, HD), lambda i, c: (0, 0))
+    grads = call(
+        functools.partial(finish_kernel, True), "finish_own", (HALF,),
+        inputs[0], [wide(True)] * 2, [Kept(WHOLE_BF16)] * 2,
+        (core, Kept(k), Kept(v), row, Kept(key_inside[True]), Kept(value_inside[True]), later_here), 4 * MM,
+    )
+    key_grad, value_grad, gain_grad = call(
+        functools.partial(finish_kernel, False), "finish_other", (HALF,),
+        inputs[1] + [small, small, ANY, ANY],
+        [wide(False)] * 2 + [pl.BlockSpec((1, 16), lambda i, c: (0, 0))],
+        [Kept(WHOLE_BF16)] * 2 + [Kept(shape((1, 16)))],
+        (core, Kept(k), Kept(v), row, Kept(key_inside[False]), Kept(value_inside[False]), later_other,
+         collected, pair, *[Kept(a) for a in grads]), 4 * MM, aliases={9: 0, 10: 1},
+    )
+    return query_grad[0], key_grad, value_grad, gain_grad.reshape(16)
 
 
 def solution(mesh):

time: 145 us -> 143 us (0.986)
  Pallas kernels: 61.2 us -> 58.6 us
  waiting for transfers between devices: 22 us -> 24.2 us
    pallas_call x19, Pallas kernels: 61.2 us -> 58.6 us  [call(): pl.pallas_call(kernel, name=name, grid_spec=pltpu.PrefetchScalarGridSpec(...]
    all_to_all x3, waiting for transfers between devices: 18.1 us -> 20.4 us  [chips_all_to_all(): lax.all_to_all(values, ('x', 'y'), split_axis=0, concat_axis=0, tiled=True)]
where the time goes in v8:
time: 143 us; the launch traced here: 142 us
  Pallas kernels  58.6 us (41%)
  starting transfers between devices  40.5 us (28%)
  waiting for transfers between devices  24.2 us (17%)
  blocking collectives  17.9 us (13%)
    pallas_call x19, Pallas kernels, call(): pl.pallas_call(kernel, name=name, grid_spec=pltpu.PrefetchScalarGridSpec(...  58.6 us
    all_to_all x3, waiting for transfers between devices, chips_all_to_all(): lax.all_to_all(values, ('x', 'y'), split_axis=0, concat_axis=0, tiled=True)  20.4 us
    all_to_all x1, blocking collectives, chips_all_to_all(): lax.all_to_all(values, ('x', 'y'), split_axis=0, concat_axis=0, tiled=True)  17.9 us
    ppermute x5, starting transfers between devices, swap_cores(): return lax.ppermute(values, 'core', [(0, 1), (1, 0)])  12.4 us
    ppermute x2, starting transfers between devices, scan_over_chips(): before = lax.ppermute(total, 'zh', [(0, 1), (1, 0)])  12.4 us
    all_to_all x3, starting transfers between devices, chips_all_to_all(): lax.all_to_all(values, ('x', 'y'), split_axis=0, concat_axis=0, tiled=True)  12.4 us
    ppermute x2, waiting for transfers between devices, scan_over_chips(): before = lax.ppermute(total, 'zh', [(0, 1), (1, 0)])  3.53 us
    ppermute x3, starting transfers between devices, per_device(): lax.ppermute(gains[distance], 'dp', [(i, i ^ distance) for i in range(NG)])  3.23 us
  transfers between devices with their start and end apart: 13, of which 6 were waited for; matrix products, arithmetic and copies ran while one was open for 0% of the time, Pallas kernels for 26%

profile of v8, /device:TPU:1, one launch (start us, length us, event | category | flops | bytes accessed | tf_op | source)
XLA Modules:
  0.0 142.3 jit_solution(10761838493458983031)
XLA Ops:
  0.7 2.7 %states_other.1 = (f32[16,136,128]{2,1,0:T(8,128)S(1)}, f32[32,192]{1,0:T(8,128)S(1)}) custom-call(s32[4]{0:T(128)S(1)} %pad_add_fusion.c_ref, bf16[1,192,4096]{2,1,0:T(8,128)(2,1)} %k_ref.15, bf16[1,192,4096]{2,1,0:T(8,128)(2,1)} %v_ref.15, f32[32,192]{1,0:T(8,128)} %bitcast.26), custom_call_target="tpu_custom_call" | custom-call | flops 100663296 | bytes 4308992 | tf_op jit(solution)/shard_map/states_other/pallas_call | solution.py:309
  3.4 3.3 %collective-permute-start = (f32[16,136,128]{2,1,0:T(8,128)S(1)}, f32[16,136,128]{2,1,0:T(8,128)S(1)}, u32[]{:S(2)}, u32[]{:S(2)}) collective-permute-start(f32[16,136,128]{2,1,0:T(8,128)S(1)} %get-tuple-element.55), channel_id=1, source_target_pairs={{0,1},{1,0},{2,3},{3,2},{4,5},{5,4},{6,7},{7,6},{8,9},{9,8},{10,11... | collective-permute-start | bytes 3342344 | tf_op jit(solution)/shard_map/ppermute | solution.py:375
  6.7 2.4 %states_own.1 = (f32[16,128,128]{2,1,0:T(8,128)S(1)}, f32[16,8,128]{2,1,0:T(8,128)S(1)}) custom-call(s32[4]{0:T(128)S(1)} %pad_add_fusion.c_ref, bf16[1,192,4096]{2,1,0:T(8,128)(2,1)} %k_ref.15, bf16[1,192,4096]{2,1,0:T(8,128)(2,1)} %v_ref.15, f32[32,192]{1,0:T(8,128)S(1)} %get-tuple-element.53.row_ref), custom_call_target="tpu_custom_call" | custom-call | flops 100663296 | bytes 4284416 | tf_op jit(solution)/shard_map/states_own/pallas_call | solution.py:309
  9.2 2.1 %chip_total.1 = (f32[16,136,128]{2,1,0:T(8,128)}, f32[16,128,128]{2,1,0:T(8,128)}, f32[16,8,128]{2,1,0:T(8,128)S(1)}) custom-call(s32[4]{0:T(128)S(1)} %pad_add_fusion.c_ref, f32[16,128,128]{2,1,0:T(8,128)S(1)} %get-tuple-element.54.own_ref, f32[16,136,128]{2,1,0:T(8,128)S(1)} %collective-permute-done.got_ref.lg_ref, ...), custom_call_target="tpu_custom_call" | custom-call | bytes 5570560 | tf_op jit(solution)/shard_map/chip_total/pallas_call | solution.py:309
  11.3 5.0 %all-to-all-start = ((f32[16,136,128]{2,1,0:T(8,128)}), f32[16,136,128]{2,1,0:T(8,128)S(1)}, u32[]{:S(2)}, u32[]{:S(2)}) async-start(f32[16,136,128]{2,1,0:T(8,128)} %get-tuple-element.57), calls=%async_computation | async-start | bytes 2228224 | tf_op jit(solution)/shard_map/all_to_all | solution.py:379
  16.3 4.6 %forward_inside.2 = (bf16[16,192,192]{2,1,0:T(8,128)(2,1)}, f32[192,2048]{1,0:T(8,128)}) custom-call(s32[4]{0:T(128)S(1)} %pad_add_fusion.c_ref, bf16[1,192,4096]{2,1,0:T(8,128)(2,1)} %q_ref.13, bf16[1,192,4096]{2,1,0:T(8,128)(2,1)} %k_ref.15, bf16[1,192,4096]{2,1,0:T(8,128)(2,1)} %v_ref.15, f32[32,192]{1,0:T(8,128)S(1)} %get-tuple-element.53.row_ref), custom_call_target="tpu_custom_call" | custom-call | flops 301989888 | bytes 7495680 | tf_op jit(solution)/shard_map/forward_inside/pallas_call | solution.py:309
  20.9 4.6 %forward_inside.3 = (bf16[16,192,192]{2,1,0:T(8,128)(2,1)}, f32[192,2048]{1,0:T(8,128)}) custom-call(s32[4]{0:T(128)S(1)} %pad_add_fusion.c_ref, bf16[1,192,4096]{2,1,0:T(8,128)(2,1)} %q_ref.13, bf16[1,192,4096]{2,1,0:T(8,128)(2,1)} %k_ref.15, bf16[1,192,4096]{2,1,0:T(8,128)(2,1)} %v_ref.15, f32[32,192]{1,0:T(8,128)S(1)} %get-tuple-element.53.row_ref), custom_call_target="tpu_custom_call" | custom-call | flops 301989888 | bytes 7495680 | tf_op jit(solution)/shard_map/forward_inside/pallas_call | solution.py:309
  25.5 7.3 %all-to-all-done.m_ref.l_ref = f32[16,136,128]{2,1,0:T(8,128)S(1)} async-done(((f32[16,136,128]{2,1,0:T(8,128)}), f32[16,136,128]{2,1,0:T(8,128)S(1)}, u32[]{:S(2)}, u32[]{:S(2)}) %all-to-all-start) | async-done | bytes 1114144 | tf_op jit(solution)/shard_map/all_to_all | solution.py:379
  33.4 7.0 %collective-permute-start.1 = (f32[128,128]{1,0:T(8,128)S(1)}, f32[128,128]{1,0:T(8,128)S(1)}, u32[]{:S(2)}, u32[]{:S(2)}) collective-permute-start(f32[128,128]{1,0:T(8,128)S(1)} %half_total.2), channel_id=1, source_target_pairs={{0,32},{32,0},{1,33},{33,1},{2,34},{34,2},{3,35},{35,3},{4,36},{36... | collective-permute-start | bytes 196616 | tf_op jit(solution)/shard_map/ppermute | solution.py:395
  43.9 17.9 %all_to_all.20.d_ref = f32[16,128,128]{2,1,0:T(8,128)S(1)} all-to-all(f32[16,128,128]{2,1,0:T(8,128)} %get-tuple-element.62), channel_id=1, replica_groups=mesh['dp'=4,'zh'=2,'x'=4,'y'=4,'core'=2] {'x','y'}, dimensions={0} | all-to-all | bytes 2097152 | tf_op jit(solution)/shard_map/all_to_all | solution.py:379
  62.6 5.0 %collective-permute-start.2 = (f32[16,128,128]{2,1,0:T(8,128)S(1)}, f32[16,128,128]{2,1,0:T(8,128)S(1)}, u32[]{:S(2)}, u32[]{:S(2)}) collective-permute-start(f32[16,128,128]{2,1,0:T(8,128)S(1)} %get-tuple-element.65), channel_id=1, source_target_pairs={{0,1},{1,0},{2,3},{3,2},{4,5},{5,4},{6,7},{7,6},{8,9},{9,8},{10,11... | collective-permute-start | bytes 3145736 | tf_op jit(solution)/shard_map/ppermute | solution.py:375
  69.9 4.1 %attend_other.1 = (bf16[192,2048]{1,0:T(8,128)(2,1)}, f32[16,128,128]{2,1,0:T(8,128)S(1)}, f32[2,8,128]{2,1,0:T(8,128)S(1)}, f32[192,128]{1,0:T(8,128)S(1)}, f32[192,128]{1,0:T(8,128)S(1)}) custom-call(s32[4]{0:T(128)S(1)} %pad_add_fusion.c_ref, bf16[1,192,4096]{2,1,0:T(8,128)(2,1)S(1)} %copy-done, bf16[1,192,4096]{2,1,0:T(8,128)(2,1)S(1)} %copy-done.1, ...), custom_call_target="tpu_custom_call" | custom-call | flops 301989888 | bytes 8044544 | tf_op jit(solution)/shard_map/attend_other/pallas_call | solution.py:309
  74.4 2.5 %delta_own.1 = (bf16[192,2048]{1,0:T(8,128)(2,1)}, f32[16,128,128]{2,1,0:T(8,128)S(1)}, f32[2,8,128]{2,1,0:T(8,128)S(1)}) custom-call(s32[4]{0:T(128)S(1)} %pad_add_fusion.c_ref, bf16[1,192,4096]{2,1,0:T(8,128)(2,1)S(1)} %copy-done, bf16[1,192,4096]{2,1,0:T(8,128)(2,1)S(1)} %copy-done.1, f32[1,4096]{1,0:T(1,128)S(1)} %bitcast.25, ...), custom_call_target="tpu_custom_call" | custom-call | flops 100663296 | bytes 6799360 | tf_op jit(solution)/shard_map/delta_own/pallas_call | solution.py:309
  76.9 2.0 %chip_moment.1 = (f32[16,128,128]{2,1,0:T(8,128)}, f32[16,128,128]{2,1,0:T(8,128)}) custom-call(s32[4]{0:T(128)S(1)} %pad_add_fusion.c_ref, f32[16,128,128]{2,1,0:T(8,128)S(1)} %get-tuple-element.79.own_ref, f32[16,128,128]{2,1,0:T(8,128)S(1)} %collective-permute-done.3.got_ref, f32[16,8,128]{2,1,0:T(8,128)S(1)} %get-tuple-element.56.lo_ref, ...), custom_call_target="tpu_custom_call" | custom-call | bytes 4325376 | tf_op jit(solution)/shard_map/chip_moment/pallas_call | solution.py:309
  78.9 3.7 %all-to-all-start.2 = ((f32[16,128,128]{2,1,0:T(8,128)}), f32[16,128,128]{2,1,0:T(8,128)S(1)}, u32[]{:S(2)}, u32[]{:S(2)}) async-start(f32[16,128,128]{2,1,0:T(8,128)} %get-tuple-element.81), calls=%async_computation.2 | async-start | bytes 2097152 | tf_op jit(solution)/shard_map/all_to_all | solution.py:379
  85.8 8.2 %backward_inside.2 = (bf16[1,192,4096]{2,1,0:T(8,128)(2,1)}, bf16[192,2048]{1,0:T(8,128)(2,1)}, bf16[192,2048]{1,0:T(8,128)(2,1)}) custom-call(s32[4]{0:T(128)S(1)} %pad_add_fusion.c_ref, bf16[192,2048]{1,0:T(8,128)(2,1)} %get-tuple-element.75.od_ref, bf16[1,192,4096]{2,1,0:T(8,128)(2,1)} %q_ref.13, bf16[1,192,4096]{2,1,0:T(8,128)(2,1)} %k_ref.15, ...), custom_call_target="tpu_custom_call" | custom-call | flops 805306368 | bytes 10903552 | tf_op jit(solution)/shard_map/backward_inside/pallas_call | solution.py:309
  94.0 6.0 %all-to-all-done.2.m_ref = f32[16,128,128]{2,1,0:T(8,128)S(1)} async-done(((f32[16,128,128]{2,1,0:T(8,128)}), f32[16,128,128]{2,1,0:T(8,128)S(1)}, u32[]{:S(2)}, u32[]{:S(2)}) %all-to-all-start.2) | async-done | bytes 1048608 | tf_op jit(solution)/shard_map/all_to_all | solution.py:379
  100.6 5.4 %collective-permute-start.7 = (f32[136,128]{1,0:T(8,128)S(1)}, f32[136,128]{1,0:T(8,128)S(1)}, u32[]{:S(2)}, u32[]{:S(2)}) collective-permute-start(f32[136,128]{1,0:T(8,128)S(1)} %half_total.3), channel_id=1, source_target_pairs={{0,32},{32,0},{1,33},{33,1},{2,34},{34,2},{3,35},{35,3},{4,36},{36... | collective-permute-start | bytes 208904 | tf_op jit(solution)/shard_map/ppermute | solution.py:395
  109.5 3.7 %all-to-all-start.3 = ((f32[16,136,128]{2,1,0:T(8,128)}), f32[16,136,128]{2,1,0:T(8,128)S(1)}, u32[]{:S(2)}, u32[]{:S(2)}) async-start(f32[16,136,128]{2,1,0:T(8,128)} %chip_scan.3), calls=%async_computation.3 | async-start | bytes 2228224 | tf_op jit(solution)/shard_map/all_to_all | solution.py:379
  113.3 8.0 %backward_inside.3 = (bf16[1,192,4096]{2,1,0:T(8,128)(2,1)}, bf16[192,2048]{1,0:T(8,128)(2,1)}, bf16[192,2048]{1,0:T(8,128)(2,1)}) custom-call(s32[4]{0:T(128)S(1)} %pad_add_fusion.c_ref, bf16[192,2048]{1,0:T(8,128)(2,1)} %get-tuple-element.70.od_ref, bf16[1,192,4096]{2,1,0:T(8,128)(2,1)} %q_ref.13, ...), custom_call_target="tpu_custom_call", output_to_operand_aliasing={{0}: (8, {})} | custom-call | flops 805306368 | bytes 12476416 | tf_op jit(solution)/shard_map/backward_inside/pallas_call | solution.py:309
  121.3 7.2 %all-to-all-done.3.d_ref.rest_0_ = f32[16,136,128]{2,1,0:T(8,128)S(1)} async-done(((f32[16,136,128]{2,1,0:T(8,128)}), f32[16,136,128]{2,1,0:T(8,128)S(1)}, u32[]{:S(2)}, u32[]{:S(2)}) %all-to-all-start.3) | async-done | bytes 1114144 | tf_op jit(solution)/shard_map/all_to_all | solution.py:379
  130.4 3.6 %collective-permute-start.8 = (f32[16,128,128]{2,1,0:T(8,128)S(1)}, f32[16,128,128]{2,1,0:T(8,128)S(1)}, u32[]{:S(2)}, u32[]{:S(2)}) collective-permute-start(f32[16,128,128]{2,1,0:T(8,128)S(1)} %get-tuple-element.92), channel_id=1, source_target_pairs={{0,1},{1,0},{2,3},{3,2},{4,5},{5,4},{6,7},{7,6},{8,9},{9,8},{10,11... | collective-permute-start | bytes 3145736 | tf_op jit(solution)/shard_map/ppermute | solution.py:375
  134.1 4.0 %finish_own.1 = (bf16[1,192,4096]{2,1,0:T(8,128)(2,1)}, bf16[1,192,4096]{2,1,0:T(8,128)(2,1)}) custom-call(s32[4]{0:T(128)S(1)} %pad_add_fusion.c_ref, bf16[1,192,4096]{2,1,0:T(8,128)(2,1)} %k_ref.15, bf16[1,192,4096]{2,1,0:T(8,128)(2,1)} %v_ref.15, f32[32,192]{1,0:T(8,128)S(1)} %get-tuple-element.53.row_ref, bf16[192,2048]{1,0:T(8,128)(2,1)} %get-tuple-element.94.ki_ref, ...), custom_call_target="tpu_custom_call" | custom-call | flops 402653184 | bytes 8937472 | tf_op jit(solution)/shard_map/finish_own/pallas_call | solution.py:309
  138.2 4.1 %finish_other.1 = (bf16[1,192,4096]{2,1,0:T(8,128)(2,1)}, bf16[1,192,4096]{2,1,0:T(8,128)(2,1)}, f32[1,16]{1,0:T(1,128)}) custom-call(s32[4]{0:T(128)S(1)} %pad_add_fusion.c_ref, bf16[1,192,4096]{2,1,0:T(8,128)(2,1)} %k_ref.15, bf16[1,192,4096]{2,1,0:T(8,128)(2,1)} %v_ref.15, ...), custom_call_target="tpu_custom_call", output_to_operand_aliasing={{0}: (9, {}), {1}: (10, {})} | custom-call | flops 402653184 | bytes 12091456 | tf_op jit(solution)/shard_map/finish_other/pallas_call | solution.py:309
  (41 shorter events, 17.0 us)
Async XLA Ops:
  3.4 5.8 %collective-permute-start = (f32[16,136,128]{2,1,0:T(8,128)S(1)}, f32[16,136,128]{2,1,0:T(8,128)S(1)}, u32[]{:S(2)}, u32[]{:S(2)}) collective-permute-start(f32[16,136,128]{2,1,0:T(8,128)S(1)} %get-tuple-element.55), channel_id=1, source_target_pairs={{0,1},{1,0},{2,3},{3,2},{4,5},{5,4},{6,7},{7,6},{8,9},{9,8},{10,11... | collective-permute-start | bytes 3342344 | tf_op jit(solution)/shard_map/ppermute | solution.py:375
  11.3 21.5 %all-to-all-start = ((f32[16,136,128]{2,1,0:T(8,128)}), f32[16,136,128]{2,1,0:T(8,128)S(1)}, u32[]{:S(2)}, u32[]{:S(2)}) async-start(f32[16,136,128]{2,1,0:T(8,128)} %get-tuple-element.57), calls=%async_computation | async-start | bytes 2228224 | tf_op jit(solution)/shard_map/all_to_all | solution.py:379
  33.4 8.7 %collective-permute-start.1 = (f32[128,128]{1,0:T(8,128)S(1)}, f32[128,128]{1,0:T(8,128)S(1)}, u32[]{:S(2)}, u32[]{:S(2)}) collective-permute-start(f32[128,128]{1,0:T(8,128)S(1)} %half_total.2), channel_id=1, source_target_pairs={{0,32},{32,0},{1,33},{33,1},{2,34},{34,2},{3,35},{35,3},{4,36},{36... | collective-permute-start | bytes 196616 | tf_op jit(solution)/shard_map/ppermute | solution.py:395
  42.1 25.5 %copy-start.4 = (f32[192,2048]{1,0:T(8,128)S(1)}, f32[192,2048]{1,0:T(8,128)}, u32[]{:S(2)}) copy-start(f32[192,2048]{1,0:T(8,128)} %get-tuple-element.66.in_ref) | copy-start | bytes 4718596
  43.8 18.0 %copy-start.5 = (f32[16,128,128]{2,1,0:T(8,128)S(1)}, f32[16,128,128]{2,1,0:T(8,128)}, u32[]{:S(2)}) copy-start(f32[16,128,128]{2,1,0:T(8,128)} %get-tuple-element.63.kept_ref) | copy-start | bytes 3145732
  43.8 23.8 %copy-start.1 = (bf16[1,192,4096]{2,1,0:T(8,128)(2,1)S(1)}, bf16[1,192,4096]{2,1,0:T(8,128)(2,1)}, u32[]{:S(2)}) copy-start(bf16[1,192,4096]{2,1,0:T(8,128)(2,1)} %g_ref.5) | copy-start | bytes 4718596
  61.8 5.8 %copy-start = (bf16[1,192,4096]{2,1,0:T(8,128)(2,1)S(1)}, bf16[1,192,4096]{2,1,0:T(8,128)(2,1)}, u32[]{:S(2)}) copy-start(bf16[1,192,4096]{2,1,0:T(8,128)(2,1)} %q_ref.13) | copy-start | bytes 4718596
  61.8 5.8 %copy-start.6 = (f32[4096]{0:T(1024)S(1)}, f32[4096]{0:T(1024)}, u32[]{:S(2)}) copy-start(f32[4096]{0:T(1024)} %param.11) | copy-start | bytes 49156
  62.6 7.0 %copy-start.2 = (f32[16,128,128]{2,1,0:T(8,128)}, f32[16,128,128]{2,1,0:T(8,128)S(1)}, u32[]{:S(2)}) copy-start(f32[16,128,128]{2,1,0:T(8,128)S(1)} %get-tuple-element.67.x_ref.i_ref) | copy-start | bytes 3145732
  62.6 7.3 %collective-permute-start.2 = (f32[16,128,128]{2,1,0:T(8,128)S(1)}, f32[16,128,128]{2,1,0:T(8,128)S(1)}, u32[]{:S(2)}, u32[]{:S(2)}) collective-permute-start(f32[16,128,128]{2,1,0:T(8,128)S(1)} %get-tuple-element.65), channel_id=1, source_target_pairs={{0,1},{1,0},{2,3},{3,2},{4,5},{5,4},{6,7},{7,6},{8,9},{9,8},{10,11... | collective-permute-start | bytes 3145736 | tf_op jit(solution)/shard_map/ppermute | solution.py:375
  67.6 2.3 %copy-start.3 = (f32[192,2048]{1,0:T(8,128)S(1)}, f32[192,2048]{1,0:T(8,128)}, u32[]{:S(2)}) copy-start(f32[192,2048]{1,0:T(8,128)} %get-tuple-element.60.in_ref) | copy-start | bytes 4718596
  74.0 2.9 %collective-permute-start.3 = (f32[16,128,128]{2,1,0:T(8,128)S(1)}, f32[16,128,128]{2,1,0:T(8,128)S(1)}, u32[]{:S(2)}, u32[]{:S(2)}) collective-permute-start(f32[16,128,128]{2,1,0:T(8,128)S(1)} %get-tuple-element.80), channel_id=1, source_target_pairs={{0,1},{1,0},{2,3},{3,2},{4,5},{5,4},{6,7},{7,6},{8,9},{9,8},{10,11... | collective-permute-start | bytes 3145736 | tf_op jit(solution)/shard_map/ppermute | solution.py:375
  78.9 21.1 %all-to-all-start.2 = ((f32[16,128,128]{2,1,0:T(8,128)}), f32[16,128,128]{2,1,0:T(8,128)S(1)}, u32[]{:S(2)}, u32[]{:S(2)}) async-start(f32[16,128,128]{2,1,0:T(8,128)} %get-tuple-element.81), calls=%async_computation.2 | async-start | bytes 2097152 | tf_op jit(solution)/shard_map/all_to_all | solution.py:379
  82.6 11.4 %collective-permute-start.5 = (f32[8,128]{1,0:T(8,128)S(1)}, f32[8,128]{1,0:T(8,128)S(1)}, u32[]{:S(2)}, u32[]{:S(2)}) collective-permute-start(f32[8,128]{1,0:T(8,128)S(1)} %get-tuple-element.104), channel_id=1, source_target_pairs={{0,128},{64,192},{128,0},{192,64},{1,129},{65,193},{129,1},{193,65... | collective-permute-start | bytes 12296 | tf_op jit(solution)/shard_map/ppermute | solution.py:495
  84.1 9.9 %collective-permute-start.6 = (f32[8,128]{1,0:T(8,128)S(1)}, f32[8,128]{1,0:T(8,128)S(1)}, u32[]{:S(2)}, u32[]{:S(2)}) collective-permute-start(f32[8,128]{1,0:T(8,128)S(1)} %get-tuple-element.105), channel_id=1, source_target_pairs={{0,192},{64,128},{128,64},{192,0},{1,193},{65,129},{129,65},{193,1... | collective-permute-start | bytes 12296 | tf_op jit(solution)/shard_map/ppermute | solution.py:495
  85.6 8.4 %collective-permute-start.4 = (f32[8,128]{1,0:T(8,128)S(1)}, f32[8,128]{1,0:T(8,128)S(1)}, u32[]{:S(2)}, u32[]{:S(2)}) collective-permute-start(f32[8,128]{1,0:T(8,128)S(1)} %slice_bitcast_fusion.2), channel_id=1, source_target_pairs={{0,64},{64,0},{128,192},{192,128},{1,65},{65,1},{129,193},{193,129... | collective-permute-start | bytes 12296 | tf_op jit(solution)/shard_map/ppermute | solution.py:495
  100.6 7.2 %collective-permute-start.7 = (f32[136,128]{1,0:T(8,128)S(1)}, f32[136,128]{1,0:T(8,128)S(1)}, u32[]{:S(2)}, u32[]{:S(2)}) collective-permute-start(f32[136,128]{1,0:T(8,128)S(1)} %half_total.3), channel_id=1, source_target_pairs={{0,32},{32,0},{1,33},{33,1},{2,34},{34,2},{3,35},{35,3},{4,36},{36... | collective-permute-start | bytes 208904 | tf_op jit(solution)/shard_map/ppermute | solution.py:395
  109.5 18.9 %all-to-all-start.3 = ((f32[16,136,128]{2,1,0:T(8,128)}), f32[16,136,128]{2,1,0:T(8,128)S(1)}, u32[]{:S(2)}, u32[]{:S(2)}) async-start(f32[16,136,128]{2,1,0:T(8,128)} %chip_scan.3), calls=%async_computation.3 | async-start | bytes 2228224 | tf_op jit(solution)/shard_map/all_to_all | solution.py:379
  130.4 7.8 %collective-permute-start.8 = (f32[16,128,128]{2,1,0:T(8,128)S(1)}, f32[16,128,128]{2,1,0:T(8,128)S(1)}, u32[]{:S(2)}, u32[]{:S(2)}) collective-permute-start(f32[16,128,128]{2,1,0:T(8,128)S(1)} %get-tuple-element.92), channel_id=1, source_target_pairs={{0,1},{1,0},{2,3},{3,2},{4,5},{5,4},{6,7},{7,6},{8,9},{9,8},{10,11... | collective-permute-start | bytes 3145736 | tf_op jit(solution)/shard_map/ppermute | solution.py:375
  134.0 4.1 %collective-permute-start.9 = (f32[8,128]{1,0:T(8,128)S(1)}, f32[8,128]{1,0:T(8,128)S(1)}, u32[]{:S(2)}, u32[]{:S(2)}) collective-permute-start(f32[8,128]{1,0:T(8,128)S(1)} %get-tuple-element.93.rest_0_), channel_id=1, source_target_pairs={{0,1},{1,0},{2,3},{3,2},{4,5},{5,4},{6,7},{7,6},{8,9},{9,8},{10,11... | collective-permute-start | bytes 12296 | tf_op jit(solution)/shard_map/ppermute | solution.py:375

commit v9 on v8

--- a/solution.py
+++ b/solution.py
@@ -167,7 +167,10 @@
         state_ref[j] = jnp.where(at_edge, edge, passed)
 
 
-def forward_kernel(c_ref, q_ref, k_ref, v_ref, row_ref, fw_ref, in_ref):
+def forward_kernel(c_ref, q_ref, k_ref, v_ref, row_ref, *rest):
+    fw_ref, in_ref = rest[-2:]
+    if len(rest) > 2:
+        rest[1][...] = rest[0][...]
     cum = columns(row_ref)
     for j in range(GH):
         decay = decay_table(cum[:, j : j + 1], row_ref[j : j + 1, :])
@@ -423,20 +426,23 @@
     chip_total, kept_state, log_got = call(
         functools.partial(combine_kernel, True), "chip_total", (HALF,),
         [state_block(), state_block(), LOG_BLOCK, LOG_TAIL],
-        [state_block(HD + 8), state_block(), LOG_BLOCK], [Kept(LOGGED), Kept(STATES), LOGS],
+        [state_block(HD + 8), state_block(), LOG_BLOCK], [Kept(LOGGED), STATES, LOGS],
         (core, own, got, log_own, got), 0,
     )
     gathered = chips_all_to_all(chip_total)
 
     weights, inside = {}, {}
     for mine in (True, False):
-        weights[mine], inside[mine] = call(
+        carried = [kept_state] if mine else []
+        *moved, weights[mine], inside[mine] = call(
             forward_kernel, "forward_inside", (HALF,),
-            [wide(mine), wide(mine), wide(mine), row_block(mine)],
-            [pl.BlockSpec((GH, T, T), lambda i, c: (i, 0, 0)), narrow()],
-            [Kept(shape((NC, T, T), BF16)), Kept(HALF_F32)],
-            (core, Kept(q), Kept(k), Kept(v), row), 2 * SM,
+            [wide(mine), wide(mine), wide(mine), row_block(mine)] + [state_block()] * len(carried),
+            [state_block()] * len(carried) + [pl.BlockSpec((GH, T, T), lambda i, c: (i, 0, 0)), narrow()],
+            [Kept(STATES)] * len(carried) + [Kept(shape((NC, T, T), BF16)), Kept(HALF_F32)],
+            (core, Kept(q), Kept(k), Kept(v), row, *carried), 2 * SM,
         )
+        if mine:
+            (kept_state,) = moved
 
     gathered, inside[True], inside[False] = lax.optimization_barrier(
         (gathered, inside[True], inside[False])
@@ -535,7 +541,7 @@
         inputs[1] + [small, small, ANY, ANY],
         [wide(False)] * 2 + [pl.BlockSpec((1, 16), lambda i, c: (0, 0))],
         [Kept(WHOLE_BF16)] * 2 + [Kept(shape((1, 16)))],
-        (core, Kept(k), Kept(v), row, Kept(key_inside[False]), Kept(value_inside[False]), later_other,
+        (core, Kept(k), Kept(v), row, key_inside[False], value_inside[False], later_other,
          collected, pair, *[Kept(a) for a in grads]), 4 * MM, aliases={9: 0, 10: 1},
     )
     return query_grad[0], key_grad, value_grad, gain_grad.reshape(16)

time: 143 us -> 142 us (level)
  no operation moved by 1% of the time
where the time goes in v9:
time: 142 us
  Pallas kernels  58.3 us (41%)
  starting transfers between devices  40.4 us (28%)
  waiting for transfers between devices  24.1 us (17%)
  blocking collectives  18 us (13%)
    pallas_call x19, Pallas kernels, call(): pl.pallas_call(kernel, name=name, grid_spec=pltpu.PrefetchScalarGridSpec(...  58.3 us
    all_to_all x3, waiting for transfers between devices, chips_all_to_all(): lax.all_to_all(values, ('x', 'y'), split_axis=0, concat_axis=0, tiled=True)  20.3 us
    all_to_all x1, blocking collectives, chips_all_to_all(): lax.all_to_all(values, ('x', 'y'), split_axis=0, concat_axis=0, tiled=True)  18 us
    ppermute x5, starting transfers between devices, swap_cores(): return lax.ppermute(values, 'core', [(0, 1), (1, 0)])  12.4 us
    all_to_all x3, starting transfers between devices, chips_all_to_all(): lax.all_to_all(values, ('x', 'y'), split_axis=0, concat_axis=0, tiled=True)  12.4 us
    ppermute x2, starting transfers between devices, scan_over_chips(): before = lax.ppermute(total, 'zh', [(0, 1), (1, 0)])  12.4 us
    ppermute x2, waiting for transfers between devices, scan_over_chips(): before = lax.ppermute(total, 'zh', [(0, 1), (1, 0)])  3.52 us
    ppermute x3, starting transfers between devices, per_device(): lax.ppermute(gains[distance], 'dp', [(i, i ^ distance) for i in range(NG)])  3.21 us
  transfers between devices with their start and end apart: 13, of which 6 were waited for; matrix products, arithmetic and copies ran while one was open for 0% of the time, Pallas kernels for 26%

profile of v9, /device:TPU:1, one launch (start us, length us, event | category | flops | bytes accessed | tf_op | source)
XLA Modules:
  0.0 141.8 jit_solution(2461187672767258557)
XLA Ops:
  0.7 2.7 %states_other.1 = (f32[16,136,128]{2,1,0:T(8,128)S(1)}, f32[32,192]{1,0:T(8,128)S(1)}) custom-call(s32[4]{0:T(128)S(1)} %pad_add_fusion.c_ref, bf16[1,192,4096]{2,1,0:T(8,128)(2,1)} %k_ref.15, bf16[1,192,4096]{2,1,0:T(8,128)(2,1)} %v_ref.15, f32[32,192]{1,0:T(8,128)} %bitcast.26), custom_call_target="tpu_custom_call" | custom-call | flops 100663296 | bytes 4308992 | tf_op jit(solution)/shard_map/states_other/pallas_call | solution.py:312
  3.4 3.3 %collective-permute-start = (f32[16,136,128]{2,1,0:T(8,128)S(1)}, f32[16,136,128]{2,1,0:T(8,128)S(1)}, u32[]{:S(2)}, u32[]{:S(2)}) collective-permute-start(f32[16,136,128]{2,1,0:T(8,128)S(1)} %get-tuple-element.56), channel_id=1, source_target_pairs={{0,1},{1,0},{2,3},{3,2},{4,5},{5,4},{6,7},{7,6},{8,9},{9,8},{10,11... | collective-permute-start | bytes 3342344 | tf_op jit(solution)/shard_map/ppermute | solution.py:378
  6.7 2.4 %states_own.1 = (f32[16,128,128]{2,1,0:T(8,128)S(1)}, f32[16,8,128]{2,1,0:T(8,128)S(1)}) custom-call(s32[4]{0:T(128)S(1)} %pad_add_fusion.c_ref, bf16[1,192,4096]{2,1,0:T(8,128)(2,1)} %k_ref.15, bf16[1,192,4096]{2,1,0:T(8,128)(2,1)} %v_ref.15, f32[32,192]{1,0:T(8,128)S(1)} %get-tuple-element.54.row_ref), custom_call_target="tpu_custom_call" | custom-call | flops 100663296 | bytes 4284416 | tf_op jit(solution)/shard_map/states_own/pallas_call | solution.py:312
  11.0 5.0 %all-to-all-start = ((f32[16,136,128]{2,1,0:T(8,128)}), f32[16,136,128]{2,1,0:T(8,128)S(1)}, u32[]{:S(2)}, u32[]{:S(2)}) async-start(f32[16,136,128]{2,1,0:T(8,128)} %get-tuple-element.58), calls=%async_computation | async-start | bytes 2228224 | tf_op jit(solution)/shard_map/all_to_all | solution.py:382
  16.1 4.6 %forward_inside.3 = (bf16[16,192,192]{2,1,0:T(8,128)(2,1)}, f32[192,2048]{1,0:T(8,128)}) custom-call(s32[4]{0:T(128)S(1)} %pad_add_fusion.c_ref, bf16[1,192,4096]{2,1,0:T(8,128)(2,1)} %q_ref.13, bf16[1,192,4096]{2,1,0:T(8,128)(2,1)} %k_ref.15, bf16[1,192,4096]{2,1,0:T(8,128)(2,1)} %v_ref.15, f32[32,192]{1,0:T(8,128)S(1)} %get-tuple-element.54.row_ref), custom_call_target="tpu_custom_call" | custom-call | flops 301989888 | bytes 7495680 | tf_op jit(solution)/shard_map/forward_inside/pallas_call | solution.py:312
  20.7 4.8 %forward_inside.2 = (f32[16,128,128]{2,1,0:T(8,128)}, bf16[16,192,192]{2,1,0:T(8,128)(2,1)}, f32[192,2048]{1,0:T(8,128)}) custom-call(s32[4]{0:T(128)S(1)} %pad_add_fusion.c_ref, bf16[1,192,4096]{2,1,0:T(8,128)(2,1)} %q_ref.13, bf16[1,192,4096]{2,1,0:T(8,128)(2,1)} %k_ref.15, bf16[1,192,4096]{2,1,0:T(8,128)(2,1)} %v_ref.15, ...), custom_call_target="tpu_custom_call" | custom-call | flops 301989888 | bytes 9592832 | tf_op jit(solution)/shard_map/forward_inside/pallas_call | solution.py:312
  25.4 7.1 %all-to-all-done.m_ref.l_ref = f32[16,136,128]{2,1,0:T(8,128)S(1)} async-done(((f32[16,136,128]{2,1,0:T(8,128)}), f32[16,136,128]{2,1,0:T(8,128)S(1)}, u32[]{:S(2)}, u32[]{:S(2)}) %all-to-all-start) | async-done | bytes 1114144 | tf_op jit(solution)/shard_map/all_to_all | solution.py:382
  33.1 7.0 %collective-permute-start.1 = (f32[128,128]{1,0:T(8,128)S(1)}, f32[128,128]{1,0:T(8,128)S(1)}, u32[]{:S(2)}, u32[]{:S(2)}) collective-permute-start(f32[128,128]{1,0:T(8,128)S(1)} %half_total.2), channel_id=1, source_target_pairs={{0,32},{32,0},{1,33},{33,1},{2,34},{34,2},{3,35},{35,3},{4,36},{36... | collective-permute-start | bytes 196616 | tf_op jit(solution)/shard_map/ppermute | solution.py:398
  43.6 18.0 %all_to_all.20.d_ref = f32[16,128,128]{2,1,0:T(8,128)S(1)} all-to-all(f32[16,128,128]{2,1,0:T(8,128)} %get-tuple-element.64), channel_id=1, replica_groups=mesh['dp'=4,'zh'=2,'x'=4,'y'=4,'core'=2] {'x','y'}, dimensions={0} | all-to-all | bytes 2097152 | tf_op jit(solution)/shard_map/all_to_all | solution.py:382
  62.3 5.0 %collective-permute-start.2 = (f32[16,128,128]{2,1,0:T(8,128)S(1)}, f32[16,128,128]{2,1,0:T(8,128)S(1)}, u32[]{:S(2)}, u32[]{:S(2)}) collective-permute-start(f32[16,128,128]{2,1,0:T(8,128)S(1)} %get-tuple-element.67), channel_id=1, source_target_pairs={{0,1},{1,0},{2,3},{3,2},{4,5},{5,4},{6,7},{7,6},{8,9},{9,8},{10,11... | collective-permute-start | bytes 3145736 | tf_op jit(solution)/shard_map/ppermute | solution.py:378
  67.4 2.0 %attend_own.1 = (f32[192,2048]{1,0:T(8,128)S(1)}, f32[192,128]{1,0:T(8,128)S(1)}, f32[192,128]{1,0:T(8,128)S(1)}) custom-call(s32[4]{0:T(128)S(1)} %pad_add_fusion.c_ref, bf16[1,192,4096]{2,1,0:T(8,128)(2,1)S(1)} %copy-done, bf16[1,192,4096]{2,1,0:T(8,128)(2,1)S(1)} %copy-done.1, f32[1,4096]{1,0:T(1,128)S(1)} %bitcast.23, ...), custom_call_target="tpu_custom_call" | custom-call | flops 201326592 | bytes 7577600 | tf_op jit(solution)/shard_map/attend_own/pallas_call | solution.py:312
  69.6 4.1 %attend_other.1 = (bf16[192,2048]{1,0:T(8,128)(2,1)}, f32[16,128,128]{2,1,0:T(8,128)S(1)}, f32[2,8,128]{2,1,0:T(8,128)S(1)}, f32[192,128]{1,0:T(8,128)S(1)}, f32[192,128]{1,0:T(8,128)S(1)}) custom-call(s32[4]{0:T(128)S(1)} %pad_add_fusion.c_ref, bf16[1,192,4096]{2,1,0:T(8,128)(2,1)S(1)} %copy-done, bf16[1,192,4096]{2,1,0:T(8,128)(2,1)S(1)} %copy-done.1, ...), custom_call_target="tpu_custom_call" | custom-call | flops 301989888 | bytes 8044544 | tf_op jit(solution)/shard_map/attend_other/pallas_call | solution.py:312
  74.1 2.5 %delta_own.1 = (bf16[192,2048]{1,0:T(8,128)(2,1)}, f32[16,128,128]{2,1,0:T(8,128)S(1)}, f32[2,8,128]{2,1,0:T(8,128)S(1)}) custom-call(s32[4]{0:T(128)S(1)} %pad_add_fusion.c_ref, bf16[1,192,4096]{2,1,0:T(8,128)(2,1)S(1)} %copy-done, bf16[1,192,4096]{2,1,0:T(8,128)(2,1)S(1)} %copy-done.1, f32[1,4096]{1,0:T(1,128)S(1)} %bitcast.25, ...), custom_call_target="tpu_custom_call" | custom-call | flops 100663296 | bytes 6799360 | tf_op jit(solution)/shard_map/delta_own/pallas_call | solution.py:312
  76.6 2.0 %chip_moment.1 = (f32[16,128,128]{2,1,0:T(8,128)}, f32[16,128,128]{2,1,0:T(8,128)}) custom-call(s32[4]{0:T(128)S(1)} %pad_add_fusion.c_ref, f32[16,128,128]{2,1,0:T(8,128)S(1)} %get-tuple-element.81.own_ref, f32[16,128,128]{2,1,0:T(8,128)S(1)} %collective-permute-done.3.got_ref, f32[16,8,128]{2,1,0:T(8,128)S(1)} %get-tuple-element.57.lo_ref, ...), custom_call_target="tpu_custom_call" | custom-call | bytes 4325376 | tf_op jit(solution)/shard_map/chip_moment/pallas_call | solution.py:312
  78.6 3.7 %all-to-all-start.2 = ((f32[16,128,128]{2,1,0:T(8,128)}), f32[16,128,128]{2,1,0:T(8,128)S(1)}, u32[]{:S(2)}, u32[]{:S(2)}) async-start(f32[16,128,128]{2,1,0:T(8,128)} %get-tuple-element.83), calls=%async_computation.2 | async-start | bytes 2097152 | tf_op jit(solution)/shard_map/all_to_all | solution.py:382
  85.5 8.2 %backward_inside.2 = (bf16[1,192,4096]{2,1,0:T(8,128)(2,1)}, bf16[192,2048]{1,0:T(8,128)(2,1)}, bf16[192,2048]{1,0:T(8,128)(2,1)}) custom-call(s32[4]{0:T(128)S(1)} %pad_add_fusion.c_ref, bf16[192,2048]{1,0:T(8,128)(2,1)} %get-tuple-element.77.od_ref, bf16[1,192,4096]{2,1,0:T(8,128)(2,1)} %q_ref.13, bf16[1,192,4096]{2,1,0:T(8,128)(2,1)} %k_ref.15, ...), custom_call_target="tpu_custom_call" | custom-call | flops 805306368 | bytes 10903552 | tf_op jit(solution)/shard_map/backward_inside/pallas_call | solution.py:312
  93.8 6.0 %all-to-all-done.2.m_ref = f32[16,128,128]{2,1,0:T(8,128)S(1)} async-done(((f32[16,128,128]{2,1,0:T(8,128)}), f32[16,128,128]{2,1,0:T(8,128)S(1)}, u32[]{:S(2)}, u32[]{:S(2)}) %all-to-all-start.2) | async-done | bytes 1048608 | tf_op jit(solution)/shard_map/all_to_all | solution.py:382
  100.4 5.4 %collective-permute-start.7 = (f32[136,128]{1,0:T(8,128)S(1)}, f32[136,128]{1,0:T(8,128)S(1)}, u32[]{:S(2)}, u32[]{:S(2)}) collective-permute-start(f32[136,128]{1,0:T(8,128)S(1)} %half_total.3), channel_id=1, source_target_pairs={{0,32},{32,0},{1,33},{33,1},{2,34},{34,2},{3,35},{35,3},{4,36},{36... | collective-permute-start | bytes 208904 | tf_op jit(solution)/shard_map/ppermute | solution.py:398
  109.3 3.7 %all-to-all-start.3 = ((f32[16,136,128]{2,1,0:T(8,128)}), f32[16,136,128]{2,1,0:T(8,128)S(1)}, u32[]{:S(2)}, u32[]{:S(2)}) async-start(f32[16,136,128]{2,1,0:T(8,128)} %chip_scan.3), calls=%async_computation.3 | async-start | bytes 2228224 | tf_op jit(solution)/shard_map/all_to_all | solution.py:382
  113.0 8.0 %backward_inside.3 = (bf16[1,192,4096]{2,1,0:T(8,128)(2,1)}, bf16[192,2048]{1,0:T(8,128)(2,1)}, bf16[192,2048]{1,0:T(8,128)(2,1)}) custom-call(s32[4]{0:T(128)S(1)} %pad_add_fusion.c_ref, bf16[192,2048]{1,0:T(8,128)(2,1)} %get-tuple-element.72.od_ref, bf16[1,192,4096]{2,1,0:T(8,128)(2,1)} %q_ref.13, ...), custom_call_target="tpu_custom_call", output_to_operand_aliasing={{0}: (8, {})} | custom-call | flops 805306368 | bytes 12476416 | tf_op jit(solution)/shard_map/backward_inside/pallas_call | solution.py:312
  121.0 7.2 %all-to-all-done.3.d_ref.rest_0_ = f32[16,136,128]{2,1,0:T(8,128)S(1)} async-done(((f32[16,136,128]{2,1,0:T(8,128)}), f32[16,136,128]{2,1,0:T(8,128)S(1)}, u32[]{:S(2)}, u32[]{:S(2)}) %all-to-all-start.3) | async-done | bytes 1114144 | tf_op jit(solution)/shard_map/all_to_all | solution.py:382
  130.1 3.6 %collective-permute-start.8 = (f32[16,128,128]{2,1,0:T(8,128)S(1)}, f32[16,128,128]{2,1,0:T(8,128)S(1)}, u32[]{:S(2)}, u32[]{:S(2)}) collective-permute-start(f32[16,128,128]{2,1,0:T(8,128)S(1)} %get-tuple-element.94), channel_id=1, source_target_pairs={{0,1},{1,0},{2,3},{3,2},{4,5},{5,4},{6,7},{7,6},{8,9},{9,8},{10,11... | collective-permute-start | bytes 3145736 | tf_op jit(solution)/shard_map/ppermute | solution.py:378
  133.9 4.0 %finish_own.1 = (bf16[1,192,4096]{2,1,0:T(8,128)(2,1)}, bf16[1,192,4096]{2,1,0:T(8,128)(2,1)}) custom-call(s32[4]{0:T(128)S(1)} %pad_add_fusion.c_ref, bf16[1,192,4096]{2,1,0:T(8,128)(2,1)} %k_ref.15, bf16[1,192,4096]{2,1,0:T(8,128)(2,1)} %v_ref.15, f32[32,192]{1,0:T(8,128)S(1)} %get-tuple-element.54.row_ref, bf16[192,2048]{1,0:T(8,128)(2,1)} %get-tuple-element.96.ki_ref, ...), custom_call_target="tpu_custom_call" | custom-call | flops 402653184 | bytes 8937472 | tf_op jit(solution)/shard_map/finish_own/pallas_call | solution.py:312
  137.9 3.8 %finish_other.1 = (bf16[1,192,4096]{2,1,0:T(8,128)(2,1)}, bf16[1,192,4096]{2,1,0:T(8,128)(2,1)}, f32[1,16]{1,0:T(1,128)}) custom-call(s32[4]{0:T(128)S(1)} %pad_add_fusion.c_ref, bf16[1,192,4096]{2,1,0:T(8,128)(2,1)} %k_ref.15, bf16[1,192,4096]{2,1,0:T(8,128)(2,1)} %v_ref.15, ...), custom_call_target="tpu_custom_call", output_to_operand_aliasing={{0}: (9, {}), {1}: (10, {})} | custom-call | flops 402653184 | bytes 12091456 | tf_op jit(solution)/shard_map/finish_other/pallas_call | solution.py:312
  (45 shorter events, 16.8 us)
Async XLA Ops:
  3.4 5.8 %collective-permute-start = (f32[16,136,128]{2,1,0:T(8,128)S(1)}, f32[16,136,128]{2,1,0:T(8,128)S(1)}, u32[]{:S(2)}, u32[]{:S(2)}) collective-permute-start(f32[16,136,128]{2,1,0:T(8,128)S(1)} %get-tuple-element.56), channel_id=1, source_target_pairs={{0,1},{1,0},{2,3},{3,2},{4,5},{5,4},{6,7},{7,6},{8,9},{9,8},{10,11... | collective-permute-start | bytes 3342344 | tf_op jit(solution)/shard_map/ppermute | solution.py:378
  11.0 21.5 %all-to-all-start = ((f32[16,136,128]{2,1,0:T(8,128)}), f32[16,136,128]{2,1,0:T(8,128)S(1)}, u32[]{:S(2)}, u32[]{:S(2)}) async-start(f32[16,136,128]{2,1,0:T(8,128)} %get-tuple-element.58), calls=%async_computation | async-start | bytes 2228224 | tf_op jit(solution)/shard_map/all_to_all | solution.py:382
  33.1 8.7 %collective-permute-start.1 = (f32[128,128]{1,0:T(8,128)S(1)}, f32[128,128]{1,0:T(8,128)S(1)}, u32[]{:S(2)}, u32[]{:S(2)}) collective-permute-start(f32[128,128]{1,0:T(8,128)S(1)} %half_total.2), channel_id=1, source_target_pairs={{0,32},{32,0},{1,33},{33,1},{2,34},{34,2},{3,35},{35,3},{4,36},{36... | collective-permute-start | bytes 196616 | tf_op jit(solution)/shard_map/ppermute | solution.py:398
  41.9 25.5 %copy-start.4 = (f32[192,2048]{1,0:T(8,128)S(1)}, f32[192,2048]{1,0:T(8,128)}, u32[]{:S(2)}) copy-start(f32[192,2048]{1,0:T(8,128)} %get-tuple-element.68.in_ref) | copy-start | bytes 4718596
  43.6 18.0 %copy-start.5 = (f32[16,128,128]{2,1,0:T(8,128)S(1)}, f32[16,128,128]{2,1,0:T(8,128)}, u32[]{:S(2)}) copy-start(f32[16,128,128]{2,1,0:T(8,128)} %get-tuple-element.65.kept_ref) | copy-start | bytes 3145732
  43.6 23.8 %copy-start.1 = (bf16[1,192,4096]{2,1,0:T(8,128)(2,1)S(1)}, bf16[1,192,4096]{2,1,0:T(8,128)(2,1)}, u32[]{:S(2)}) copy-start(bf16[1,192,4096]{2,1,0:T(8,128)(2,1)} %g_ref.5) | copy-start | bytes 4718596
  61.5 5.8 %copy-start = (bf16[1,192,4096]{2,1,0:T(8,128)(2,1)S(1)}, bf16[1,192,4096]{2,1,0:T(8,128)(2,1)}, u32[]{:S(2)}) copy-start(bf16[1,192,4096]{2,1,0:T(8,128)(2,1)} %q_ref.13) | copy-start | bytes 4718596
  61.5 5.8 %copy-start.8 = (f32[4096]{0:T(1024)S(1)}, f32[4096]{0:T(1024)}, u32[]{:S(2)}) copy-start(f32[4096]{0:T(1024)} %param.11) | copy-start | bytes 49156
  62.3 7.0 %copy-start.2 = (f32[16,128,128]{2,1,0:T(8,128)}, f32[16,128,128]{2,1,0:T(8,128)S(1)}, u32[]{:S(2)}) copy-start(f32[16,128,128]{2,1,0:T(8,128)S(1)} %get-tuple-element.69.x_ref.i_ref) | copy-start | bytes 3145732
  62.3 7.3 %collective-permute-start.2 = (f32[16,128,128]{2,1,0:T(8,128)S(1)}, f32[16,128,128]{2,1,0:T(8,128)S(1)}, u32[]{:S(2)}, u32[]{:S(2)}) collective-permute-start(f32[16,128,128]{2,1,0:T(8,128)S(1)} %get-tuple-element.67), channel_id=1, source_target_pairs={{0,1},{1,0},{2,3},{3,2},{4,5},{5,4},{6,7},{7,6},{8,9},{9,8},{10,11... | collective-permute-start | bytes 3145736 | tf_op jit(solution)/shard_map/ppermute | solution.py:378
  67.4 2.3 %copy-start.3 = (f32[192,2048]{1,0:T(8,128)S(1)}, f32[192,2048]{1,0:T(8,128)}, u32[]{:S(2)}) copy-start(f32[192,2048]{1,0:T(8,128)} %get-tuple-element.62.in_ref) | copy-start | bytes 4718596
  73.7 2.9 %collective-permute-start.3 = (f32[16,128,128]{2,1,0:T(8,128)S(1)}, f32[16,128,128]{2,1,0:T(8,128)S(1)}, u32[]{:S(2)}, u32[]{:S(2)}) collective-permute-start(f32[16,128,128]{2,1,0:T(8,128)S(1)} %get-tuple-element.82), channel_id=1, source_target_pairs={{0,1},{1,0},{2,3},{3,2},{4,5},{5,4},{6,7},{7,6},{8,9},{9,8},{10,11... | collective-permute-start | bytes 3145736 | tf_op jit(solution)/shard_map/ppermute | solution.py:378
  78.6 21.1 %all-to-all-start.2 = ((f32[16,128,128]{2,1,0:T(8,128)}), f32[16,128,128]{2,1,0:T(8,128)S(1)}, u32[]{:S(2)}, u32[]{:S(2)}) async-start(f32[16,128,128]{2,1,0:T(8,128)} %get-tuple-element.83), calls=%async_computation.2 | async-start | bytes 2097152 | tf_op jit(solution)/shard_map/all_to_all | solution.py:382
  82.3 11.4 %collective-permute-start.5 = (f32[8,128]{1,0:T(8,128)S(1)}, f32[8,128]{1,0:T(8,128)S(1)}, u32[]{:S(2)}, u32[]{:S(2)}) collective-permute-start(f32[8,128]{1,0:T(8,128)S(1)} %get-tuple-element.106), channel_id=1, source_target_pairs={{0,128},{64,192},{128,0},{192,64},{1,129},{65,193},{129,1},{193,65... | collective-permute-start | bytes 12296 | tf_op jit(solution)/shard_map/ppermute | solution.py:501
  83.8 9.9 %collective-permute-start.6 = (f32[8,128]{1,0:T(8,128)S(1)}, f32[8,128]{1,0:T(8,128)S(1)}, u32[]{:S(2)}, u32[]{:S(2)}) collective-permute-start(f32[8,128]{1,0:T(8,128)S(1)} %get-tuple-element.107), channel_id=1, source_target_pairs={{0,192},{64,128},{128,64},{192,0},{1,193},{65,129},{129,65},{193,1... | collective-permute-start | bytes 12296 | tf_op jit(solution)/shard_map/ppermute | solution.py:501
  85.4 8.4 %collective-permute-start.4 = (f32[8,128]{1,0:T(8,128)S(1)}, f32[8,128]{1,0:T(8,128)S(1)}, u32[]{:S(2)}, u32[]{:S(2)}) collective-permute-start(f32[8,128]{1,0:T(8,128)S(1)} %slice_bitcast_fusion.2), channel_id=1, source_target_pairs={{0,64},{64,0},{128,192},{192,128},{1,65},{65,1},{129,193},{193,129... | collective-permute-start | bytes 12296 | tf_op jit(solution)/shard_map/ppermute | solution.py:501
  100.4 7.2 %collective-permute-start.7 = (f32[136,128]{1,0:T(8,128)S(1)}, f32[136,128]{1,0:T(8,128)S(1)}, u32[]{:S(2)}, u32[]{:S(2)}) collective-permute-start(f32[136,128]{1,0:T(8,128)S(1)} %half_total.3), channel_id=1, source_target_pairs={{0,32},{32,0},{1,33},{33,1},{2,34},{34,2},{3,35},{35,3},{4,36},{36... | collective-permute-start | bytes 208904 | tf_op jit(solution)/shard_map/ppermute | solution.py:398
  109.3 18.9 %all-to-all-start.3 = ((f32[16,136,128]{2,1,0:T(8,128)}), f32[16,136,128]{2,1,0:T(8,128)S(1)}, u32[]{:S(2)}, u32[]{:S(2)}) async-start(f32[16,136,128]{2,1,0:T(8,128)} %chip_scan.3), calls=%async_computation.3 | async-start | bytes 2228224 | tf_op jit(solution)/shard_map/all_to_all | solution.py:382
  130.1 7.8 %collective-permute-start.8 = (f32[16,128,128]{2,1,0:T(8,128)S(1)}, f32[16,128,128]{2,1,0:T(8,128)S(1)}, u32[]{:S(2)}, u32[]{:S(2)}) collective-permute-start(f32[16,128,128]{2,1,0:T(8,128)S(1)} %get-tuple-element.94), channel_id=1, source_target_pairs={{0,1},{1,0},{2,3},{3,2},{4,5},{5,4},{6,7},{7,6},{8,9},{9,8},{10,11... | collective-permute-start | bytes 3145736 | tf_op jit(solution)/shard_map/ppermute | solution.py:378
  133.8 4.1 %collective-permute-start.9 = (f32[8,128]{1,0:T(8,128)S(1)}, f32[8,128]{1,0:T(8,128)S(1)}, u32[]{:S(2)}, u32[]{:S(2)}) collective-permute-start(f32[8,128]{1,0:T(8,128)S(1)} %get-tuple-element.95.rest_0_), channel_id=1, source_target_pairs={{0,1},{1,0},{2,3},{3,2},{4,5},{5,4},{6,7},{7,6},{8,9},{9,8},{10,11... | collective-permute-start | bytes 12296 | tf_op jit(solution)/shard_map/ppermute | solution.py:378
  133.9 4.0 %copy-start.6 = (bf16[192,2048]{1,0:T(8,128)(2,1)S(1)}, bf16[192,2048]{1,0:T(8,128)(2,1)}, u32[]{:S(2)}) copy-start(bf16[192,2048]{1,0:T(8,128)(2,1)} %get-tuple-element.90.ki_ref) | copy-start | bytes 2359300
  133.9 4.1 %copy-start.7 = (bf16[192,2048]{1,0:T(8,128)(2,1)S(1)}, bf16[192,2048]{1,0:T(8,128)(2,1)}, u32[]{:S(2)}) copy-start(bf16[192,2048]{1,0:T(8,128)(2,1)} %get-tuple-element.91.vi_ref) | copy-start | bytes 2359300

commit v10 on v9

--- a/solution.py
+++ b/solution.py
@@ -123,23 +123,19 @@
 
 def scan_kernel(upward, c_ref, m_ref, l_ref, t_ref, *rest):
     if upward:
-        o_hbm, log_ref, o_buf, sem = rest
+        o_ref, log_ref = rest
         log_ref[...] = l_ref[...]
     else:
-        gain_ref, o_hbm, o_buf, sem = rest
+        gain_ref, o_ref = rest
         both = gain_ref[...] + t_ref[HD:, :]
     run = jnp.where(c_ref[2] == (1 if upward else 0), t_ref[:HD, :], 0.0)
-    copies = [pltpu.make_async_copy(o_buf.at[i], o_hbm.at[i], sem.at[i]) for i in range(NC)]
     for i in range(NC) if upward else reversed(range(NC)):
-        o_buf[i, :HD, :] = run
+        o_ref[i, :HD, :] = run
         if not upward:
             x = i // 4
             row = jnp.where(c_ref[2] == 0, both[x : x + 1, :], both[4 + x : 5 + x, :])
-            o_buf[i, HD:, :] = jnp.broadcast_to(row, (8, HD))
-        copies[i].start()
+            o_ref[i, HD:, :] = jnp.broadcast_to(row, (8, HD))
         run = jnp.exp(l_ref[i, 0:1, :]) * run + m_ref[i]
-    for copy in copies:
-        copy.wait()
 
 
 def hand_on_kernel(upward, c_ref, d_ref, kept_ref, lo_ref, lg_ref, *rest):
@@ -396,12 +392,12 @@
         (place, got, logs, *more), 0,
     )
     before = lax.ppermute(total, "zh", [(0, 1), (1, 0)])
-    outs = [ANY] + [logs_out] * upward
+    outs = [pl.BlockSpec((NC, rows, HD), lambda i, c: (0, 0, 0))] + [logs_out] * upward
+    scanned = shape((NC, rows, HD))
     return call(
         functools.partial(scan_kernel, upward), "chip_scan", (1,),
-        [whole_m, whole_l, whole_t] + more_specs, outs, [Kept(shape((NC, rows, HD))), LOGS][: len(outs)],
+        [whole_m, whole_l, whole_t] + more_specs, outs, [scanned, LOGS] if upward else [Kept(scanned)],
         (place, got, logs, before, *more), 0,
-        scratch=[pltpu.VMEM((NC, rows, HD), F32), pltpu.SemaphoreType.DMA((NC,))],
     )
 
 

time: 142 us -> 141 us (level)
  no operation moved by 1% of the time
where the time goes in v10:
time: 141 us; the launch traced here: 140 us
  Pallas kernels  57.2 us (41%)
  starting transfers between devices  40.4 us (29%)
  waiting for transfers between devices  24.1 us (17%)
  blocking collectives  17.7 us (13%)
    pallas_call x19, Pallas kernels, call(): pl.pallas_call(kernel, name=name, grid_spec=pltpu.PrefetchScalarGridSpec(...  57.2 us
    all_to_all x3, waiting for transfers between devices, chips_all_to_all(): lax.all_to_all(values, ('x', 'y'), split_axis=0, concat_axis=0, tiled=True)  20.2 us
    all_to_all x1, blocking collectives, chips_all_to_all(): lax.all_to_all(values, ('x', 'y'), split_axis=0, concat_axis=0, tiled=True)  17.7 us
    ppermute x5, starting transfers between devices, swap_cores(): return lax.ppermute(values, 'core', [(0, 1), (1, 0)])  12.5 us
    all_to_all x3, starting transfers between devices, chips_all_to_all(): lax.all_to_all(values, ('x', 'y'), split_axis=0, concat_axis=0, tiled=True)  12.4 us
    ppermute x2, starting transfers between devices, scan_over_chips(): before = lax.ppermute(total, 'zh', [(0, 1), (1, 0)])  12.4 us
    ppermute x2, waiting for transfers between devices, scan_over_chips(): before = lax.ppermute(total, 'zh', [(0, 1), (1, 0)])  3.57 us
    ppermute x3, starting transfers between devices, per_device(): lax.ppermute(gains[distance], 'dp', [(i, i ^ distance) for i in range(NG)])  3.21 us
  transfers between devices with their start and end apart: 13, of which 6 were waited for; matrix products, arithmetic and copies ran while one was open for 0% of the time, Pallas kernels for 26%

profile of v10, /device:TPU:1, one launch (start us, length us, event | category | flops | bytes accessed | tf_op | source)
XLA Modules:
  0.0 140.5 jit_solution(6744900349267674746)
XLA Ops:
  0.7 2.7 %states_other.1 = (f32[16,136,128]{2,1,0:T(8,128)S(1)}, f32[32,192]{1,0:T(8,128)S(1)}) custom-call(s32[4]{0:T(128)S(1)} %pad_add_fusion.c_ref, bf16[1,192,4096]{2,1,0:T(8,128)(2,1)} %k_ref.15, bf16[1,192,4096]{2,1,0:T(8,128)(2,1)} %v_ref.15, f32[32,192]{1,0:T(8,128)} %bitcast.26), custom_call_target="tpu_custom_call" | custom-call | flops 100663296 | bytes 4308992 | tf_op jit(solution)/shard_map/states_other/pallas_call | solution.py:308
  3.4 3.3 %collective-permute-start = (f32[16,136,128]{2,1,0:T(8,128)S(1)}, f32[16,136,128]{2,1,0:T(8,128)S(1)}, u32[]{:S(2)}, u32[]{:S(2)}) collective-permute-start(f32[16,136,128]{2,1,0:T(8,128)S(1)} %get-tuple-element.56), channel_id=1, source_target_pairs={{0,1},{1,0},{2,3},{3,2},{4,5},{5,4},{6,7},{7,6},{8,9},{9,8},{10,11... | collective-permute-start | bytes 3342344 | tf_op jit(solution)/shard_map/ppermute | solution.py:374
  6.7 2.4 %states_own.1 = (f32[16,128,128]{2,1,0:T(8,128)S(1)}, f32[16,8,128]{2,1,0:T(8,128)S(1)}) custom-call(s32[4]{0:T(128)S(1)} %pad_add_fusion.c_ref, bf16[1,192,4096]{2,1,0:T(8,128)(2,1)} %k_ref.15, bf16[1,192,4096]{2,1,0:T(8,128)(2,1)} %v_ref.15, f32[32,192]{1,0:T(8,128)S(1)} %get-tuple-element.54.row_ref), custom_call_target="tpu_custom_call" | custom-call | flops 100663296 | bytes 4284416 | tf_op jit(solution)/shard_map/states_own/pallas_call | solution.py:308
  11.0 5.0 %all-to-all-start = ((f32[16,136,128]{2,1,0:T(8,128)}), f32[16,136,128]{2,1,0:T(8,128)S(1)}, u32[]{:S(2)}, u32[]{:S(2)}) async-start(f32[16,136,128]{2,1,0:T(8,128)} %get-tuple-element.58), calls=%async_computation | async-start | bytes 2228224 | tf_op jit(solution)/shard_map/all_to_all | solution.py:378
  16.1 4.6 %forward_inside.3 = (bf16[16,192,192]{2,1,0:T(8,128)(2,1)}, f32[192,2048]{1,0:T(8,128)}) custom-call(s32[4]{0:T(128)S(1)} %pad_add_fusion.c_ref, bf16[1,192,4096]{2,1,0:T(8,128)(2,1)} %q_ref.13, bf16[1,192,4096]{2,1,0:T(8,128)(2,1)} %k_ref.15, bf16[1,192,4096]{2,1,0:T(8,128)(2,1)} %v_ref.15, f32[32,192]{1,0:T(8,128)S(1)} %get-tuple-element.54.row_ref), custom_call_target="tpu_custom_call" | custom-call | flops 301989888 | bytes 7495680 | tf_op jit(solution)/shard_map/forward_inside/pallas_call | solution.py:308
  20.7 4.8 %forward_inside.2 = (f32[16,128,128]{2,1,0:T(8,128)}, bf16[16,192,192]{2,1,0:T(8,128)(2,1)}, f32[192,2048]{1,0:T(8,128)}) custom-call(s32[4]{0:T(128)S(1)} %pad_add_fusion.c_ref, bf16[1,192,4096]{2,1,0:T(8,128)(2,1)} %q_ref.13, bf16[1,192,4096]{2,1,0:T(8,128)(2,1)} %k_ref.15, bf16[1,192,4096]{2,1,0:T(8,128)(2,1)} %v_ref.15, ...), custom_call_target="tpu_custom_call" | custom-call | flops 301989888 | bytes 9592832 | tf_op jit(solution)/shard_map/forward_inside/pallas_call | solution.py:308
  25.4 7.1 %all-to-all-done.m_ref.l_ref = f32[16,136,128]{2,1,0:T(8,128)S(1)} async-done(((f32[16,136,128]{2,1,0:T(8,128)}), f32[16,136,128]{2,1,0:T(8,128)S(1)}, u32[]{:S(2)}, u32[]{:S(2)}) %all-to-all-start) | async-done | bytes 1114144 | tf_op jit(solution)/shard_map/all_to_all | solution.py:378
  33.1 7.0 %collective-permute-start.1 = (f32[128,128]{1,0:T(8,128)S(1)}, f32[128,128]{1,0:T(8,128)S(1)}, u32[]{:S(2)}, u32[]{:S(2)}) collective-permute-start(f32[128,128]{1,0:T(8,128)S(1)} %half_total.2), channel_id=1, source_target_pairs={{0,32},{32,0},{1,33},{33,1},{2,34},{34,2},{3,35},{35,3},{4,36},{36... | collective-permute-start | bytes 196616 | tf_op jit(solution)/shard_map/ppermute | solution.py:394
  42.5 17.7 %all_to_all.20.d_ref = f32[16,128,128]{2,1,0:T(8,128)S(1)} all-to-all(f32[16,128,128]{2,1,0:T(8,128)S(1)} %get-tuple-element.64), channel_id=1, replica_groups=mesh['dp'=4,'zh'=2,'x'=4,'y'=4,'core'=2] {'x','y'}, dimensions={0} | all-to-all | bytes 2097152 | tf_op jit(solution)/shard_map/all_to_all | solution.py:378
  61.1 5.0 %collective-permute-start.2 = (f32[16,128,128]{2,1,0:T(8,128)S(1)}, f32[16,128,128]{2,1,0:T(8,128)S(1)}, u32[]{:S(2)}, u32[]{:S(2)}) collective-permute-start(f32[16,128,128]{2,1,0:T(8,128)S(1)} %get-tuple-element.67), channel_id=1, source_target_pairs={{0,1},{1,0},{2,3},{3,2},{4,5},{5,4},{6,7},{7,6},{8,9},{9,8},{10,11... | collective-permute-start | bytes 3145736 | tf_op jit(solution)/shard_map/ppermute | solution.py:374
  66.1 2.0 %attend_own.1 = (f32[192,2048]{1,0:T(8,128)S(1)}, f32[192,128]{1,0:T(8,128)S(1)}, f32[192,128]{1,0:T(8,128)S(1)}) custom-call(s32[4]{0:T(128)S(1)} %pad_add_fusion.c_ref, bf16[1,192,4096]{2,1,0:T(8,128)(2,1)S(1)} %copy-done, bf16[1,192,4096]{2,1,0:T(8,128)(2,1)S(1)} %copy-done.1, f32[1,4096]{1,0:T(1,128)S(1)} %bitcast.23, ...), custom_call_target="tpu_custom_call" | custom-call | flops 201326592 | bytes 7577600 | tf_op jit(solution)/shard_map/attend_own/pallas_call | solution.py:308
  68.4 4.1 %attend_other.1 = (bf16[192,2048]{1,0:T(8,128)(2,1)}, f32[16,128,128]{2,1,0:T(8,128)S(1)}, f32[2,8,128]{2,1,0:T(8,128)S(1)}, f32[192,128]{1,0:T(8,128)S(1)}, f32[192,128]{1,0:T(8,128)S(1)}) custom-call(s32[4]{0:T(128)S(1)} %pad_add_fusion.c_ref, bf16[1,192,4096]{2,1,0:T(8,128)(2,1)S(1)} %copy-done, bf16[1,192,4096]{2,1,0:T(8,128)(2,1)S(1)} %copy-done.1, ...), custom_call_target="tpu_custom_call" | custom-call | flops 301989888 | bytes 8044544 | tf_op jit(solution)/shard_map/attend_other/pallas_call | solution.py:308
  72.8 2.5 %delta_own.1 = (bf16[192,2048]{1,0:T(8,128)(2,1)}, f32[16,128,128]{2,1,0:T(8,128)S(1)}, f32[2,8,128]{2,1,0:T(8,128)S(1)}) custom-call(s32[4]{0:T(128)S(1)} %pad_add_fusion.c_ref, bf16[1,192,4096]{2,1,0:T(8,128)(2,1)S(1)} %copy-done, bf16[1,192,4096]{2,1,0:T(8,128)(2,1)S(1)} %copy-done.1, f32[1,4096]{1,0:T(1,128)S(1)} %bitcast.25, ...), custom_call_target="tpu_custom_call" | custom-call | flops 100663296 | bytes 6799360 | tf_op jit(solution)/shard_map/delta_own/pallas_call | solution.py:308
  75.4 2.0 %chip_moment.1 = (f32[16,128,128]{2,1,0:T(8,128)}, f32[16,128,128]{2,1,0:T(8,128)}) custom-call(s32[4]{0:T(128)S(1)} %pad_add_fusion.c_ref, f32[16,128,128]{2,1,0:T(8,128)S(1)} %get-tuple-element.81.own_ref, f32[16,128,128]{2,1,0:T(8,128)S(1)} %collective-permute-done.3.got_ref, f32[16,8,128]{2,1,0:T(8,128)S(1)} %get-tuple-element.57.lo_ref, ...), custom_call_target="tpu_custom_call" | custom-call | bytes 4325376 | tf_op jit(solution)/shard_map/chip_moment/pallas_call | solution.py:308
  77.4 3.7 %all-to-all-start.2 = ((f32[16,128,128]{2,1,0:T(8,128)}), f32[16,128,128]{2,1,0:T(8,128)S(1)}, u32[]{:S(2)}, u32[]{:S(2)}) async-start(f32[16,128,128]{2,1,0:T(8,128)} %get-tuple-element.83), calls=%async_computation.2 | async-start | bytes 2097152 | tf_op jit(solution)/shard_map/all_to_all | solution.py:378
  84.3 8.2 %backward_inside.2 = (bf16[1,192,4096]{2,1,0:T(8,128)(2,1)}, bf16[192,2048]{1,0:T(8,128)(2,1)}, bf16[192,2048]{1,0:T(8,128)(2,1)}) custom-call(s32[4]{0:T(128)S(1)} %pad_add_fusion.c_ref, bf16[192,2048]{1,0:T(8,128)(2,1)} %get-tuple-element.77.od_ref, bf16[1,192,4096]{2,1,0:T(8,128)(2,1)} %q_ref.13, bf16[1,192,4096]{2,1,0:T(8,128)(2,1)} %k_ref.15, ...), custom_call_target="tpu_custom_call" | custom-call | flops 805306368 | bytes 10903552 | tf_op jit(solution)/shard_map/backward_inside/pallas_call | solution.py:308
  92.5 6.0 %all-to-all-done.2.m_ref = f32[16,128,128]{2,1,0:T(8,128)S(1)} async-done(((f32[16,128,128]{2,1,0:T(8,128)}), f32[16,128,128]{2,1,0:T(8,128)S(1)}, u32[]{:S(2)}, u32[]{:S(2)}) %all-to-all-start.2) | async-done | bytes 1048608 | tf_op jit(solution)/shard_map/all_to_all | solution.py:378
  99.1 5.4 %collective-permute-start.7 = (f32[136,128]{1,0:T(8,128)S(1)}, f32[136,128]{1,0:T(8,128)S(1)}, u32[]{:S(2)}, u32[]{:S(2)}) collective-permute-start(f32[136,128]{1,0:T(8,128)S(1)} %half_total.3), channel_id=1, source_target_pairs={{0,32},{32,0},{1,33},{33,1},{2,34},{34,2},{3,35},{35,3},{4,36},{36... | collective-permute-start | bytes 208904 | tf_op jit(solution)/shard_map/ppermute | solution.py:394
  108.0 3.7 %all-to-all-start.3 = ((f32[16,136,128]{2,1,0:T(8,128)}), f32[16,136,128]{2,1,0:T(8,128)S(1)}, u32[]{:S(2)}, u32[]{:S(2)}) async-start(f32[16,136,128]{2,1,0:T(8,128)} %chip_scan.3), calls=%async_computation.3 | async-start | bytes 2228224 | tf_op jit(solution)/shard_map/all_to_all | solution.py:378
  111.7 8.0 %backward_inside.3 = (bf16[1,192,4096]{2,1,0:T(8,128)(2,1)}, bf16[192,2048]{1,0:T(8,128)(2,1)}, bf16[192,2048]{1,0:T(8,128)(2,1)}) custom-call(s32[4]{0:T(128)S(1)} %pad_add_fusion.c_ref, bf16[192,2048]{1,0:T(8,128)(2,1)} %get-tuple-element.72.od_ref, bf16[1,192,4096]{2,1,0:T(8,128)(2,1)} %q_ref.13, ...), custom_call_target="tpu_custom_call", output_to_operand_aliasing={{0}: (8, {})} | custom-call | flops 805306368 | bytes 12476416 | tf_op jit(solution)/shard_map/backward_inside/pallas_call | solution.py:308
  119.7 7.2 %all-to-all-done.3.d_ref.rest_0_ = f32[16,136,128]{2,1,0:T(8,128)S(1)} async-done(((f32[16,136,128]{2,1,0:T(8,128)}), f32[16,136,128]{2,1,0:T(8,128)S(1)}, u32[]{:S(2)}, u32[]{:S(2)}) %all-to-all-start.3) | async-done | bytes 1114144 | tf_op jit(solution)/shard_map/all_to_all | solution.py:378
  128.8 3.6 %collective-permute-start.8 = (f32[16,128,128]{2,1,0:T(8,128)S(1)}, f32[16,128,128]{2,1,0:T(8,128)S(1)}, u32[]{:S(2)}, u32[]{:S(2)}) collective-permute-start(f32[16,128,128]{2,1,0:T(8,128)S(1)} %get-tuple-element.94), channel_id=1, source_target_pairs={{0,1},{1,0},{2,3},{3,2},{4,5},{5,4},{6,7},{7,6},{8,9},{9,8},{10,11... | collective-permute-start | bytes 3145736 | tf_op jit(solution)/shard_map/ppermute | solution.py:374
  132.5 4.0 %finish_own.1 = (bf16[1,192,4096]{2,1,0:T(8,128)(2,1)}, bf16[1,192,4096]{2,1,0:T(8,128)(2,1)}) custom-call(s32[4]{0:T(128)S(1)} %pad_add_fusion.c_ref, bf16[1,192,4096]{2,1,0:T(8,128)(2,1)} %k_ref.15, bf16[1,192,4096]{2,1,0:T(8,128)(2,1)} %v_ref.15, f32[32,192]{1,0:T(8,128)S(1)} %get-tuple-element.54.row_ref, bf16[192,2048]{1,0:T(8,128)(2,1)} %get-tuple-element.96.ki_ref, ...), custom_call_target="tpu_custom_call" | custom-call | flops 402653184 | bytes 8937472 | tf_op jit(solution)/shard_map/finish_own/pallas_call | solution.py:308
  136.6 3.8 %finish_other.1 = (bf16[1,192,4096]{2,1,0:T(8,128)(2,1)}, bf16[1,192,4096]{2,1,0:T(8,128)(2,1)}, f32[1,16]{1,0:T(1,128)}) custom-call(s32[4]{0:T(128)S(1)} %pad_add_fusion.c_ref, bf16[1,192,4096]{2,1,0:T(8,128)(2,1)} %k_ref.15, bf16[1,192,4096]{2,1,0:T(8,128)(2,1)} %v_ref.15, ...), custom_call_target="tpu_custom_call", output_to_operand_aliasing={{0}: (9, {}), {1}: (10, {})} | custom-call | flops 402653184 | bytes 12091456 | tf_op jit(solution)/shard_map/finish_other/pallas_call | solution.py:308
  (45 shorter events, 15.7 us)
Async XLA Ops:
  3.4 5.8 %collective-permute-start = (f32[16,136,128]{2,1,0:T(8,128)S(1)}, f32[16,136,128]{2,1,0:T(8,128)S(1)}, u32[]{:S(2)}, u32[]{:S(2)}) collective-permute-start(f32[16,136,128]{2,1,0:T(8,128)S(1)} %get-tuple-element.56), channel_id=1, source_target_pairs={{0,1},{1,0},{2,3},{3,2},{4,5},{5,4},{6,7},{7,6},{8,9},{9,8},{10,11... | collective-permute-start | bytes 3342344 | tf_op jit(solution)/shard_map/ppermute | solution.py:374
  11.0 21.5 %all-to-all-start = ((f32[16,136,128]{2,1,0:T(8,128)}), f32[16,136,128]{2,1,0:T(8,128)S(1)}, u32[]{:S(2)}, u32[]{:S(2)}) async-start(f32[16,136,128]{2,1,0:T(8,128)} %get-tuple-element.58), calls=%async_computation | async-start | bytes 2228224 | tf_op jit(solution)/shard_map/all_to_all | solution.py:378
  33.1 8.7 %collective-permute-start.1 = (f32[128,128]{1,0:T(8,128)S(1)}, f32[128,128]{1,0:T(8,128)S(1)}, u32[]{:S(2)}, u32[]{:S(2)}) collective-permute-start(f32[128,128]{1,0:T(8,128)S(1)} %half_total.2), channel_id=1, source_target_pairs={{0,32},{32,0},{1,33},{33,1},{2,34},{34,2},{3,35},{35,3},{4,36},{36... | collective-permute-start | bytes 196616 | tf_op jit(solution)/shard_map/ppermute | solution.py:394
  41.9 24.2 %copy-start.4 = (f32[192,2048]{1,0:T(8,128)S(1)}, f32[192,2048]{1,0:T(8,128)}, u32[]{:S(2)}) copy-start(f32[192,2048]{1,0:T(8,128)} %get-tuple-element.68.in_ref) | copy-start | bytes 4718596
  42.5 17.8 %copy-start.5 = (f32[16,128,128]{2,1,0:T(8,128)S(1)}, f32[16,128,128]{2,1,0:T(8,128)}, u32[]{:S(2)}) copy-start(f32[16,128,128]{2,1,0:T(8,128)} %get-tuple-element.65.kept_ref) | copy-start | bytes 3145732
  42.5 23.6 %copy-start.1 = (bf16[1,192,4096]{2,1,0:T(8,128)(2,1)S(1)}, bf16[1,192,4096]{2,1,0:T(8,128)(2,1)}, u32[]{:S(2)}) copy-start(bf16[1,192,4096]{2,1,0:T(8,128)(2,1)} %g_ref.5) | copy-start | bytes 4718596
  60.3 5.8 %copy-start = (bf16[1,192,4096]{2,1,0:T(8,128)(2,1)S(1)}, bf16[1,192,4096]{2,1,0:T(8,128)(2,1)}, u32[]{:S(2)}) copy-start(bf16[1,192,4096]{2,1,0:T(8,128)(2,1)} %q_ref.13) | copy-start | bytes 4718596
  60.3 5.8 %copy-start.8 = (f32[4096]{0:T(1024)S(1)}, f32[4096]{0:T(1024)}, u32[]{:S(2)}) copy-start(f32[4096]{0:T(1024)} %param.11) | copy-start | bytes 49156
  61.1 7.0 %copy-start.2 = (f32[16,128,128]{2,1,0:T(8,128)}, f32[16,128,128]{2,1,0:T(8,128)S(1)}, u32[]{:S(2)}) copy-start(f32[16,128,128]{2,1,0:T(8,128)S(1)} %get-tuple-element.69.x_ref.i_ref) | copy-start | bytes 3145732
  61.1 7.3 %collective-permute-start.2 = (f32[16,128,128]{2,1,0:T(8,128)S(1)}, f32[16,128,128]{2,1,0:T(8,128)S(1)}, u32[]{:S(2)}, u32[]{:S(2)}) collective-permute-start(f32[16,128,128]{2,1,0:T(8,128)S(1)} %get-tuple-element.67), channel_id=1, source_target_pairs={{0,1},{1,0},{2,3},{3,2},{4,5},{5,4},{6,7},{7,6},{8,9},{9,8},{10,11... | collective-permute-start | bytes 3145736 | tf_op jit(solution)/shard_map/ppermute | solution.py:374
  66.1 2.3 %copy-start.3 = (f32[192,2048]{1,0:T(8,128)S(1)}, f32[192,2048]{1,0:T(8,128)}, u32[]{:S(2)}) copy-start(f32[192,2048]{1,0:T(8,128)} %get-tuple-element.62.in_ref) | copy-start | bytes 4718596
  72.5 2.9 %collective-permute-start.3 = (f32[16,128,128]{2,1,0:T(8,128)S(1)}, f32[16,128,128]{2,1,0:T(8,128)S(1)}, u32[]{:S(2)}, u32[]{:S(2)}) collective-permute-start(f32[16,128,128]{2,1,0:T(8,128)S(1)} %get-tuple-element.82), channel_id=1, source_target_pairs={{0,1},{1,0},{2,3},{3,2},{4,5},{5,4},{6,7},{7,6},{8,9},{9,8},{10,11... | collective-permute-start | bytes 3145736 | tf_op jit(solution)/shard_map/ppermute | solution.py:374
  77.4 21.1 %all-to-all-start.2 = ((f32[16,128,128]{2,1,0:T(8,128)}), f32[16,128,128]{2,1,0:T(8,128)S(1)}, u32[]{:S(2)}, u32[]{:S(2)}) async-start(f32[16,128,128]{2,1,0:T(8,128)} %get-tuple-element.83), calls=%async_computation.2 | async-start | bytes 2097152 | tf_op jit(solution)/shard_map/all_to_all | solution.py:378
  81.1 11.4 %collective-permute-start.5 = (f32[8,128]{1,0:T(8,128)S(1)}, f32[8,128]{1,0:T(8,128)S(1)}, u32[]{:S(2)}, u32[]{:S(2)}) collective-permute-start(f32[8,128]{1,0:T(8,128)S(1)} %get-tuple-element.106), channel_id=1, source_target_pairs={{0,128},{64,192},{128,0},{192,64},{1,129},{65,193},{129,1},{193,65... | collective-permute-start | bytes 12296 | tf_op jit(solution)/shard_map/ppermute | solution.py:497
  82.5 9.9 %collective-permute-start.6 = (f32[8,128]{1,0:T(8,128)S(1)}, f32[8,128]{1,0:T(8,128)S(1)}, u32[]{:S(2)}, u32[]{:S(2)}) collective-permute-start(f32[8,128]{1,0:T(8,128)S(1)} %get-tuple-element.107), channel_id=1, source_target_pairs={{0,192},{64,128},{128,64},{192,0},{1,193},{65,129},{129,65},{193,1... | collective-permute-start | bytes 12296 | tf_op jit(solution)/shard_map/ppermute | solution.py:497
  84.1 8.4 %collective-permute-start.4 = (f32[8,128]{1,0:T(8,128)S(1)}, f32[8,128]{1,0:T(8,128)S(1)}, u32[]{:S(2)}, u32[]{:S(2)}) collective-permute-start(f32[8,128]{1,0:T(8,128)S(1)} %slice_bitcast_fusion.2), channel_id=1, source_target_pairs={{0,64},{64,0},{128,192},{192,128},{1,65},{65,1},{129,193},{193,129... | collective-permute-start | bytes 12296 | tf_op jit(solution)/shard_map/ppermute | solution.py:497
  99.1 7.2 %collective-permute-start.7 = (f32[136,128]{1,0:T(8,128)S(1)}, f32[136,128]{1,0:T(8,128)S(1)}, u32[]{:S(2)}, u32[]{:S(2)}) collective-permute-start(f32[136,128]{1,0:T(8,128)S(1)} %half_total.3), channel_id=1, source_target_pairs={{0,32},{32,0},{1,33},{33,1},{2,34},{34,2},{3,35},{35,3},{4,36},{36... | collective-permute-start | bytes 208904 | tf_op jit(solution)/shard_map/ppermute | solution.py:394
  108.0 18.9 %all-to-all-start.3 = ((f32[16,136,128]{2,1,0:T(8,128)}), f32[16,136,128]{2,1,0:T(8,128)S(1)}, u32[]{:S(2)}, u32[]{:S(2)}) async-start(f32[16,136,128]{2,1,0:T(8,128)} %chip_scan.3), calls=%async_computation.3 | async-start | bytes 2228224 | tf_op jit(solution)/shard_map/all_to_all | solution.py:378
  128.8 7.8 %collective-permute-start.8 = (f32[16,128,128]{2,1,0:T(8,128)S(1)}, f32[16,128,128]{2,1,0:T(8,128)S(1)}, u32[]{:S(2)}, u32[]{:S(2)}) collective-permute-start(f32[16,128,128]{2,1,0:T(8,128)S(1)} %get-tuple-element.94), channel_id=1, source_target_pairs={{0,1},{1,0},{2,3},{3,2},{4,5},{5,4},{6,7},{7,6},{8,9},{9,8},{10,11... | collective-permute-start | bytes 3145736 | tf_op jit(solution)/shard_map/ppermute | solution.py:374
  132.4 4.1 %collective-permute-start.9 = (f32[8,128]{1,0:T(8,128)S(1)}, f32[8,128]{1,0:T(8,128)S(1)}, u32[]{:S(2)}, u32[]{:S(2)}) collective-permute-start(f32[8,128]{1,0:T(8,128)S(1)} %get-tuple-element.95.rest_0_), channel_id=1, source_target_pairs={{0,1},{1,0},{2,3},{3,2},{4,5},{5,4},{6,7},{7,6},{8,9},{9,8},{10,11... | collective-permute-start | bytes 12296 | tf_op jit(solution)/shard_map/ppermute | solution.py:374
  132.5 4.0 %copy-start.6 = (bf16[192,2048]{1,0:T(8,128)(2,1)S(1)}, bf16[192,2048]{1,0:T(8,128)(2,1)}, u32[]{:S(2)}) copy-start(bf16[192,2048]{1,0:T(8,128)(2,1)} %get-tuple-element.90.ki_ref) | copy-start | bytes 2359300
  132.5 4.1 %copy-start.7 = (bf16[192,2048]{1,0:T(8,128)(2,1)S(1)}, bf16[192,2048]{1,0:T(8,128)(2,1)}, u32[]{:S(2)}) copy-start(bf16[192,2048]{1,0:T(8,128)(2,1)} %get-tuple-element.91.vi_ref) | copy-start | bytes 2359300
